TPU v7x, 32 devices: a whole 2x2x4 slice. The times are simulated.
32 devices in a mesh: groups: 2 (over y), tiles: 4 (over z), views: 2 (over x), gz: 2 (over core).
Axes of the slice: x: 2, y: 2, z: 4, core: 2. Of those that a mesh axis runs over, the one named last changes fastest.
Arguments:
- view_data: bfloat16 [4, 4, 16, 128, 128], P(('groups', 'views'), 'tiles', 'gz'), parts along dimension 0, may hold values from 0.19921875 to 2
- estimate: float32 [32, 512, 128], P(('groups', 'gz'), 'tiles'), parts along dimension 0, may hold values from 0.5 to 1.5
- psf_taps: float32 [2, 2, 2, 9], P('views'), may hold values from 0.02 to 0.3
- offsets: int32 [2, 8], P('views'), may hold values from 0 to 3, as said below
Outputs:
- updated_estimate: float32 [32, 512, 128], P(('groups', 'gz'), 'tiles'), parts along dimension 0
There are 2 independent parts, one for each index of `groups`. A program takes and returns all parts, laid end to end along the dimension named above; an argument that names none is the same for every part. Nothing has to cross between parts.
Inputs may be any that keep to these rules, and one draw needn't show every extreme that they name: `offsets`: in each view's row no value appears more than 4 times, and one value appears exactly 4 times.
All inputs are finite; a program needn't handle non-finite values.
Results may differ from a plain program's by a relative error of at most 0.0022.
The roundings to bfloat16 on the way count: a program that leaves them out, or rounds other values in their place, can miss the bound.
Values may be sent and summed in bfloat16 or wider, within the bound.
No kernel may reach another device: no remote copies, remote signals or barrier semaphores. Data moves between devices by JAX's collectives and lax.ppermute only.
A program may use at most 64 MiB of HBM per device.

v0:
```python
import functools

import jax
import jax.numpy as jnp
from jax import lax
from jax.experimental import pallas as pl
from jax.experimental.pallas import tpu as pltpu
from jax.sharding import PartitionSpec as P


ITERS = 2
CAP = 4


TV_WEIGHT = 0.1
SMOOTH_SQUARE = 0.0025


def with_halo(cells, sides, width):
    for axis, dim in sides:
        count = lax.axis_size(axis)
        ends = count - 1
        head = lax.slice_in_dim(cells, 0, width, axis=dim)
        tail = lax.slice_in_dim(cells, cells.shape[dim] - width, cells.shape[dim], axis=dim)
        cells = jnp.concatenate(
            [
                lax.ppermute(tail, axis, [(i, (i + 1) % count) for i in range(ends)]),
                cells,
                lax.ppermute(head, axis, [((i + 1) % count, i) for i in range(ends)]),
            ],
            axis=dim,
        )
    return cells


def toeplitz_matrix(profile, length):
    half_width = (profile.shape[0] - 1) // 2
    position = jnp.arange(length, dtype=jnp.int32)
    offset = position[None, :] - position[:, None] + half_width
    tap_index = jnp.arange(profile.shape[0], dtype=jnp.int32)
    picked = (offset[:, :, None] == tap_index[None, None, :]).astype(jnp.float32)
    return jnp.sum(picked * profile[None, None, :], axis=2).astype(jnp.bfloat16)


def curvature(padded):
    anchor = padded[:-1, :-1, :-1]
    grad_z = padded[1:, :-1, :-1] - anchor
    grad_y = padded[:-1, 1:, :-1] - anchor
    grad_x = padded[:-1, :-1, 1:] - anchor
    magnitude = jnp.sqrt(grad_z * grad_z + grad_y * grad_y + grad_x * grad_x + SMOOTH_SQUARE)
    unit_z = grad_z / magnitude
    unit_y = grad_y / magnitude
    unit_x = grad_x / magnitude
    return (
        unit_z[1:, 1:, 1:]
        - unit_z[:-1, 1:, 1:]
        + (unit_y[1:, 1:, 1:] - unit_y[1:, :-1, 1:])
        + (unit_x[1:, 1:, 1:] - unit_x[1:, 1:, :-1])
    )


def view_correction(view_tile, observed, kernel_y, kernel_x):
    blurred = jnp.zeros(view_tile.shape, jnp.float32)
    for term_index in range(2):
        half_blur = jnp.einsum(
            "yk,zkx->zyx", kernel_y[term_index], view_tile, preferred_element_type=jnp.float32
        ).astype(jnp.bfloat16)
        blurred = blurred + jnp.einsum(
            "zyk,xk->zyx", half_blur, kernel_x[term_index], preferred_element_type=jnp.float32
        )
    quotient = (observed.astype(jnp.float32) / blurred).astype(jnp.bfloat16)
    log_sum = jnp.zeros(view_tile.shape, jnp.float32)
    for term_index in range(2):
        half_back = jnp.einsum(
            "ky,zkx->zyx", kernel_y[term_index], quotient, preferred_element_type=jnp.float32
        ).astype(jnp.bfloat16)
        log_sum = log_sum + jnp.einsum(
            "zyk,kx->zyx", half_back, kernel_x[term_index], preferred_element_type=jnp.float32
        )
    return log_sum.astype(jnp.bfloat16)


def shards(view_data, estimate, psf_taps, offsets):
    owners = lax.axis_size("tiles")
    view_count = lax.axis_size("views")
    observed = view_data[0, 0]
    planes, height, columns = estimate.shape
    view_shift = offsets[0]
    blocks = view_shift.shape[0]
    block_rows = height // blocks
    slot_count = owners * CAP
    kernel_y = jnp.stack(
        [toeplitz_matrix(psf_taps[0, term_index, 0], height) for term_index in range(2)]
    )
    kernel_x = jnp.stack(
        [toeplitz_matrix(psf_taps[0, term_index, 1], columns) for term_index in range(2)]
    )
    position = jnp.arange(blocks, dtype=jnp.int32)
    same_owner = view_shift[:, None] == view_shift[None, :]
    before = position[None, :] < position[:, None]
    slot_rank = jnp.sum((same_owner & before).astype(jnp.int32), axis=1)
    member = lax.axis_index("tiles")
    target = (member + view_shift) % owners
    source_tile = (member - view_shift) % owners
    slot_index = jnp.arange(slot_count, dtype=jnp.int32)
    to_owner = ((target * CAP + slot_rank)[:, None] == slot_index[None, :]).astype(jnp.bfloat16)
    from_tile = ((source_tile * CAP + slot_rank)[:, None] == slot_index[None, :]).astype(
        jnp.bfloat16
    )
    current = estimate
    for _ in range(ITERS):
        padded = with_halo(current, (("tiles", 1), ("gz", 0)), 1)
        padded = jnp.pad(padded, ((0, 0), (0, 0), (1, 1)))
        owned_blocks = current.astype(jnp.bfloat16).reshape(planes, blocks, block_rows, columns)
        outgoing = jnp.einsum(
            "sk,zsrx->kzrx", from_tile, owned_blocks, preferred_element_type=jnp.float32
        ).astype(jnp.bfloat16)
        incoming = lax.all_to_all(
            outgoing.reshape(owners, CAP, planes, block_rows, columns),
            "tiles",
            split_axis=0,
            concat_axis=0,
            tiled=True,
        )
        view_tile = jnp.einsum(
            "sk,kzrx->zsrx",
            to_owner,
            incoming.reshape(slot_count, planes, block_rows, columns),
            preferred_element_type=jnp.float32,
        ).astype(jnp.bfloat16)
        view_tile = view_tile.reshape(planes, height, columns)
        correction = view_correction(view_tile, observed, kernel_y, kernel_x)
        correction = correction.reshape(planes, blocks, block_rows, columns)
        returned = jnp.einsum(
            "sk,zsrx->kzrx", to_owner, correction, preferred_element_type=jnp.float32
        ).astype(jnp.bfloat16)
        gathered = lax.all_to_all(
            returned.reshape(owners, CAP, planes, block_rows, columns),
            "tiles",
            split_axis=0,
            concat_axis=0,
            tiled=True,
        )
        owned_rows = jnp.einsum(
            "sk,kzrx->zsrx",
            from_tile,
            gathered.reshape(slot_count, planes, block_rows, columns),
            preferred_element_type=jnp.float32,
        ).reshape(planes, height, columns)
        log_values = jnp.log(owned_rows)
        share_rows = height // view_count
        log_part = lax.psum_scatter(log_values, "views", scatter_dimension=1, tiled=True)
        first_row = lax.axis_index("views") * share_rows
        window = lax.dynamic_slice_in_dim(padded, first_row, share_rows + 2, 1)
        damping = 1.0 - TV_WEIGHT * curvature(window)
        rows_now = lax.dynamic_slice_in_dim(current, first_row, share_rows, 1)
        updated = rows_now * jnp.exp(log_part / view_count) / damping
        current = lax.all_gather(updated, "views", axis=1, tiled=True)
    return current


INFO_ROWS = 16
CHUNK = 32
ANY = pl.BlockSpec(memory_space=pl.ANY)
VMEM = pl.BlockSpec(memory_space=pltpu.VMEM)
SMEM = pl.BlockSpec(memory_space=pltpu.SMEM)
LIMIT = pltpu.CompilerParams(vmem_limit_bytes=16 * 2**20)


def split_kernel(core_ref, wide_ref, narrow_ref, *refs):
    outs, sems = refs[:-1], refs[-1]
    core = core_ref[0]
    copies = []
    for n, (source, pick) in enumerate(
        [(wide_ref, 1 - core), (narrow_ref, 1 - core), (wide_ref, core), (narrow_ref, core)]
    ):
        copies.append(pltpu.make_async_copy(source.at[:, pick], outs[n], sems.at[n]))
    for copy in copies:
        copy.start()
    for copy in copies:
        copy.wait()


def split_by_core(core, wide, narrow):
    pairs = [x.reshape(x.shape[0] // 2, 2, *x.shape[1:]) for x in (wide, narrow)]
    shapes = [jax.ShapeDtypeStruct((x.shape[0], *x.shape[2:]), x.dtype) for x in pairs]
    return pl.pallas_call(
        split_kernel,
        out_shape=shapes * 2,
        in_specs=[SMEM, ANY, ANY],
        out_specs=[VMEM] * 4,
        scratch_shapes=[pltpu.SemaphoreType.DMA((4,))],
        compiler_params=LIMIT,
        name="split_by_core",
    )(core, *pairs)


def matrices_kernel(taps, info_ref, out_ref):
    views, columns = info_ref.shape
    length = out_ref.shape[-2] // 2
    half_width = (taps - 1) // 2
    row = lax.broadcasted_iota(jnp.int32, (length, columns), 0)
    column = lax.broadcasted_iota(jnp.int32, (length, columns), 1)
    band = jnp.abs(row - column) <= half_width
    for v in range(views):
        profile = jnp.broadcast_to(info_ref[v : v + 1, :], (8, columns))
        for kind, (flipped, axis) in enumerate([(0, 0), (1, 1), (1, 0), (0, 1)]):
            for r in range(2):
                lane = (4 * flipped + 2 * r + axis) * taps + half_width
                spread = jnp.broadcast_to(pltpu.roll(profile, columns - lane, 1)[0:1], (length, columns))
                rolled = pltpu.roll(spread, 0, 1, stride=1, stride_axis=0)
                rolled = jnp.where(band, rolled, 0.0).astype(out_ref.dtype)
                out_ref[v, kind, r * length : (r + 1) * length, :] = rolled


def blur_matrices(taps, length, info):
    views, columns = info.shape
    return pl.pallas_call(
        functools.partial(matrices_kernel, taps),
        out_shape=jax.ShapeDtypeStruct((views, 4, 2 * length, columns), jnp.bfloat16),
        in_specs=[VMEM],
        out_specs=VMEM,
        compiler_params=LIMIT,
        name="blur_matrices",
    )(info)


def gather_kernel(tiles, tile_ref, *refs):
    pieces, (wide_ref, narrow_ref) = refs[:tiles], refs[tiles:]
    for k in range(tiles):
        owner = lax.bitwise_xor(tile_ref[0], k)
        wide_ref[owner] = pieces[k][...]
        narrow_ref[owner] = pieces[k][...].astype(narrow_ref.dtype)


def gather_plane(tile, pieces):
    shape = (len(pieces), *pieces[0].shape)
    return pl.pallas_call(
        functools.partial(gather_kernel, len(pieces)),
        out_shape=(jax.ShapeDtypeStruct(shape, jnp.float32), jax.ShapeDtypeStruct(shape, jnp.bfloat16)),
        in_specs=[SMEM] + [VMEM] * len(pieces),
        out_specs=[VMEM] * 2,
        compiler_params=LIMIT,
        name="gather_plane",
    )(tile, *pieces)


def correction_kernel(tiles, tile_ref, offsets_ref, current_ref, matrices_ref, *refs):
    data, log_ref = refs[:tiles], refs[tiles]
    work = refs[tiles + 1 :]
    views, blocks = offsets_ref.shape
    height, columns = data[0].shape[-2:]
    rows = height // blocks
    me = tile_ref[0]
    shift = [[offsets_ref[w, s] for s in range(blocks)] for w in range(views)]
    planes = [work[3 * w] for w in range(views)]
    halves = [work[3 * w + 1] for w in range(views)]
    logs = [work[3 * w + 2] for w in range(views)]

    def first(w, kind):
        half = jnp.dot(matrices_ref[w, kind], planes[w][...], preferred_element_type=jnp.float32)
        half = half.astype(jnp.bfloat16)
        for k in range(tiles):
            for r in range(2):
                halves[w][k * height : (k + 1) * height, r * columns : (r + 1) * columns] = half[
                    r * height : (r + 1) * height, k * columns : (k + 1) * columns
                ]

    for w in range(views):
        for k in range(tiles):
            tile = lax.bitwise_xor(me, k)
            for s in range(blocks):
                owner = lax.rem(tile + shift[w][s], tiles)
                planes[w][s * rows : (s + 1) * rows, k * columns : (k + 1) * columns] = current_ref[
                    owner, s * rows : (s + 1) * rows, :
                ]
    for w in range(views):
        first(w, 0)
    for w in range(views):
        blurred = jnp.dot(halves[w][...], matrices_ref[w, 1], preferred_element_type=jnp.float32)
        for k in range(tiles):
            quotient = data[k][w].astype(jnp.float32) / blurred[k * height : (k + 1) * height]
            planes[w][:, k * columns : (k + 1) * columns] = quotient.astype(jnp.bfloat16)
    for w in range(views):
        first(w, 2)
    for w in range(views):
        back = jnp.dot(halves[w][...], matrices_ref[w, 3], preferred_element_type=jnp.float32)
        logs[w][...] = jnp.log(back.astype(jnp.bfloat16).astype(jnp.float32))
    for o in range(tiles):
        for s in range(blocks):
            total = None
            for w in range(views):
                tile = lax.rem(o - shift[w][s] + tiles, tiles)
                start = pl.multiple_of(lax.bitwise_xor(tile, me) * height + s * rows, rows)
                part = logs[w][pl.ds(start, rows), :]
                total = part if total is None else total + part
            log_ref[o * height + s * rows : o * height + (s + 1) * rows, :] = total


def correction_logs(tile, offsets, current, matrices, data):
    tiles, height, columns = current.shape
    scratch = [
        pltpu.VMEM((height, tiles * columns), jnp.bfloat16),
        pltpu.VMEM((tiles * height, 2 * columns), jnp.bfloat16),
        pltpu.VMEM((tiles * height, columns), jnp.float32),
    ]
    return pl.pallas_call(
        functools.partial(correction_kernel, tiles),
        out_shape=jax.ShapeDtypeStruct((tiles * height, columns), jnp.float32),
        in_specs=[SMEM, SMEM] + [VMEM] * (2 + tiles),
        out_specs=VMEM,
        scratch_shapes=scratch * offsets.shape[0],
        cost_estimate=pl.CostEstimate(flops=300_000_000, bytes_accessed=1_500_000, transcendentals=0),
        compiler_params=LIMIT,
        name="correction",
    )(tile, offsets, current, matrices, *data)


def update_kernel(views, core_ref, current_ref, twin_ref, other_ref, log_ref, new_ref, narrow_ref):
    total, columns = current_ref.shape
    first = core_ref[0] == 0
    row = lax.broadcasted_iota(jnp.int32, (CHUNK, columns), 0)
    column = lax.broadcasted_iota(jnp.int32, (CHUNK, columns), 1)

    def scale(z, y, x):
        return lax.rsqrt(z * z + y * y + x * x + SMOOTH_SQUARE)

    def pick(low, high, start, size):
        return jnp.where(first, low[start : start + size, :], high[start : start + size, :])

    def next_row(x, following):
        return jnp.where(row == CHUNK - 1, following, pltpu.roll(x, CHUNK - 1, 0))

    def next_column(x):
        return jnp.where(column == columns - 1, 0.0, pltpu.roll(x, columns - 1, 1))

    def edge(x):
        return x * lax.rsqrt(x * x + SMOOTH_SQUARE)

    carry = edge(current_ref[0:1, :])
    for start in range(0, total, CHUNK):
        stop = start + CHUNK
        current = current_ref[start:stop, :]
        above = pick(twin_ref, other_ref, start, CHUNK)
        below = pick(other_ref, twin_ref, start, CHUNK)
        if stop < total:
            current_next, below_next = current_ref[stop : stop + 1, :], pick(other_ref, twin_ref, stop, 1)
        else:
            current_next = below_next = jnp.zeros((1, columns), jnp.float32)
        grad_z = above - current
        grad_y = next_row(current, current_next) - current
        grad_x = next_column(current) - current
        inverse = scale(grad_z, grad_y, grad_x)
        unit_y, unit_x = grad_y * inverse, grad_x * inverse
        before_y = jnp.where(row == 0, carry, pltpu.roll(unit_y, 1, 0))
        before_x = jnp.where(column == 0, edge(current), pltpu.roll(unit_x, 1, 1))
        carry = unit_y[CHUNK - 1 : CHUNK, :]
        lower_z = current - below
        lower = lower_z * scale(lower_z, next_row(below, below_next) - below, next_column(below) - below)
        divergence = grad_z * inverse - lower + (unit_y - before_y) + (unit_x - before_x)
        damping = 1.0 - TV_WEIGHT * divergence
        new = current * jnp.exp(log_ref[start:stop, :] * (1.0 / views)) / damping
        new_ref[start:stop, :] = new
        narrow_ref[start:stop, :] = new.astype(narrow_ref.dtype)


def update(views, core, current, twin, other, logs):
    return pl.pallas_call(
        functools.partial(update_kernel, views),
        out_shape=(
            jax.ShapeDtypeStruct(current.shape, jnp.float32),
            jax.ShapeDtypeStruct(current.shape, jnp.bfloat16),
        ),
        in_specs=[SMEM] + [VMEM] * 4,
        out_specs=[VMEM] * 2,
        compiler_params=LIMIT,
        name="update",
    )(core, current, twin, other, logs)


def plane_shards(view_data, estimate, psf_taps, offsets):
    tiles, views = lax.axis_size("tiles"), lax.axis_size("views")
    square = ("tiles", "views", "gz")
    _, height, columns = estimate.shape
    blocks = offsets.shape[1]
    taps = psf_taps.shape[-1]
    tile, view, core = lax.axis_index("tiles"), lax.axis_index("views"), lax.axis_index("gz")
    straight = view == core
    swap = [(0, 1), (1, 0)]

    def device(t, v, g):
        return (t * views + v) * 2 + g

    def place(chain, t):
        return jnp.where(chain == 0, t, tiles - 1 - t)

    def over_tiles(pick):
        return [pick(tile)] + [
            lax.ppermute(pick(lax.bitwise_xor(tile, k)), "tiles", [(t, t ^ k) for t in range(tiles)])
            for k in range(1, tiles)
        ]

    me = tile.reshape(1).astype(jnp.int32)
    flag = core.reshape(1).astype(jnp.int32)
    give, give_data, keep, keep_data = split_by_core(flag, estimate, view_data[0, 0])

    chain = jnp.where(straight, keep, lax.ppermute(give, "gz", swap))
    pieces = over_tiles(lambda t: lax.dynamic_index_in_dim(chain, place(view, t), 0, keepdims=False))

    got_data = lax.ppermute(give_data, "gz", swap)
    mine = jnp.where(straight, keep_data, got_data)
    profiles = [psf_taps.reshape(-1), psf_taps[..., ::-1].reshape(-1)]
    info = jnp.concatenate([*profiles, offsets.reshape(-1).astype(jnp.float32)])
    info = jnp.pad(info, (0, columns - info.shape[0])).astype(jnp.bfloat16)
    sent = jnp.concatenate(
        [
            jnp.where(straight, got_data, keep_data).reshape(tiles * height, columns),
            jnp.broadcast_to(info, (INFO_ROWS, columns)),
        ]
    )
    came = lax.ppermute(sent, "views", swap)
    both = jnp.stack([mine, came[: tiles * height].reshape(tiles, height, columns)], axis=1)
    data = over_tiles(lambda t: lax.dynamic_index_in_dim(both, place(view, t), 0, keepdims=False))

    info = jnp.stack([info, came[tiles * height]]).astype(jnp.float32)
    shifts = info[:, 8 * taps : 8 * taps + blocks].astype(jnp.int32)
    matrices = blur_matrices(taps, height, info)

    path = [(t, 0) for t in range(tiles)] + [(t, 1) for t in reversed(range(tiles))]
    hops = []
    for here, there in zip(path[:-1], path[1:]):
        one, two = device(*here, 1), device(*there, 0)
        hops += [(one, two), (two, one)]

    current, narrow = gather_plane(me, pieces)
    current = current.reshape(tiles * height, columns)
    for _ in range(ITERS):
        other = lax.ppermute(current, square, hops)
        twin = lax.ppermute(current, "gz", swap)
        logs = correction_logs(me, shifts, narrow, matrices, data)
        current, narrow = update(views, flag, current, twin, other, logs)
        narrow = narrow.reshape(tiles, height, columns)

    result = current.astype(jnp.float16).reshape(tiles, height, columns)
    result = jnp.stack(over_tiles(lambda t: lax.dynamic_index_in_dim(result, t, 0, keepdims=False)))
    crossed = lax.ppermute(result, "views", swap)
    twin = lax.ppermute(jnp.where(straight, crossed, result), "gz", swap)
    same = jnp.where(straight, result, crossed)
    ordered = []
    for i in range(tiles):
        k = lax.bitwise_xor(place(core, i), tile)
        same_i = lax.dynamic_index_in_dim(same, k, 0, keepdims=False)
        twin_i = lax.dynamic_index_in_dim(twin, k, 0, keepdims=False)
        ordered += [jnp.where(core == 0, same_i, twin_i), jnp.where(core == 0, twin_i, same_i)]
    return jnp.stack(ordered).astype(jnp.float32)


def one_plane_each(mesh, view_data, estimate, psf_taps, offsets):
    tiles, views, depth = mesh.shape["tiles"], mesh.shape["views"], mesh.shape["gz"]
    planes = estimate.shape[0] // (mesh.shape["groups"] * depth)
    height, columns = estimate.shape[1] // tiles, estimate.shape[2]
    return (
        depth == 2
        and views == 2
        and planes == 2 * tiles
        and tiles & (tiles - 1) == 0
        and height == columns
        and height % (16 * offsets.shape[1]) == 0
        and columns == 128
        and 8 * psf_taps.shape[-1] + offsets.shape[1] <= columns
    )


def solution(mesh):
    in_specs = (
        P(("groups", "views"), "tiles", "gz", None, None),
        P(("groups", "gz"), "tiles", None),
        P("views", None, None, None),
        P("views", None),
    )
    out_specs = P(("groups", "gz"), "tiles", None)

    def step(*arrays):
        if not one_plane_each(mesh, *arrays):
            return jax.shard_map(shards, mesh=mesh, in_specs=in_specs, out_specs=out_specs, check_vma=False)(*arrays)
        body = jax.shard_map(plane_shards, mesh=mesh, in_specs=in_specs, out_specs=out_specs, check_vma=False)
        return body(*arrays)

    return step
```

profile of v0, /device:TPU:0, one launch (start us, length us, event | category | flops | bytes accessed | tf_op | source)
XLA Modules:
  0.0 54.2 jit_solution(4737880321478624220)
XLA Ops:
  0.0 1.0 %copy-done = f32[8,128,128]{2,1,0:T(8,128)S(1)} copy-done((f32[8,128,128]{2,1,0:T(8,128)S(1)}, f32[8,128,128]{2,1,0:T(8,128)}, u32[]{:S(2)}) %copy-start) | copy-done | bytes 524312
  1.0 0.9 %copy-done.1 = bf16[1,1,8,128,128]{4,3,2,1,0:T(8,128)(2,1)S(1)} copy-done((bf16[1,1,8,128,128]{4,3,2,1,0:T(8,128)(2,1)S(1)}, bf16[1,1,8,128,128]{4,3,2,1,0:T(8,128)(2,1)}, u32[]{:S(2)}) %copy-start.1) | copy-done | bytes 262168
  3.9 3.0 %collective-permute-start.7 = (bf16[528,128]{1,0:T(8,128)(2,1)S(1)}, bf16[528,128]{1,0:T(8,128)(2,1)S(1)}, u32[]{:S(2)}, u32[]{:S(2)}) collective-permute-start(bf16[528,128]{1,0:T(8,128)(2,1)S(1)} %pad_maximum_fusion), channel_id=1, source_target_pairs={{0,2},{2,0},{1,3},{3,1},{4,6},{6,4},{5,7},{7,5},{8,10},{10,8},{9,1... | collective-permute-start | bytes 405512 | tf_op jit(solution)/shard_map/ppermute | solution.py:421
  7.0 1.6 %collective-permute-start.1 = (f32[128,128]{1,0:T(8,128)S(1)}, f32[128,128]{1,0:T(8,128)S(1)}, u32[]{:S(2)}, u32[]{:S(2)}) collective-permute-start(f32[128,128]{1,0:T(8,128)S(1)} %get-tuple-element.33), channel_id=1, source_target_pairs={{0,4},{4,0},{8,12},{12,8},{1,5},{5,1},{9,13},{13,9},{2,6},{6,2},{1... | collective-permute-start | bytes 196616 | tf_op jit(solution)/shard_map/ppermute | solution.py:399
  8.7 2.6 %collective-permute-start.2 = (f32[128,128]{1,0:T(8,128)S(1)}, f32[128,128]{1,0:T(8,128)S(1)}, u32[]{:S(2)}, u32[]{:S(2)}) collective-permute-start(f32[128,128]{1,0:T(8,128)S(1)} %get-tuple-element.32), channel_id=1, source_target_pairs={{0,8},{4,12},{8,0},{12,4},{1,9},{5,13},{9,1},{13,5},{2,10},{6,14},... | collective-permute-start | bytes 196616 | tf_op jit(solution)/shard_map/ppermute | solution.py:399
  11.5 3.7 %collective-permute-start.10 = (bf16[2,128,128]{2,1,0:T(8,128)(2,1)S(1)}, bf16[2,128,128]{2,1,0:T(8,128)(2,1)S(1)}, u32[]{:S(2)}, u32[]{:S(2)}) collective-permute-start(bf16[2,128,128]{2,1,0:T(8,128)(2,1)S(1)} %get-tuple-element.25), channel_id=1, source_target_pairs={{0,12},{4,8},{8,4},{12,0},{1,13},{5,9},{9,5},{13,1},{2,14},{6,10},... | collective-permute-start | bytes 196616 | tf_op jit(solution)/shard_map/ppermute | solution.py:399
  15.2 0.8 %collective-permute-start.9 = (bf16[2,128,128]{2,1,0:T(8,128)(2,1)S(1)}, bf16[2,128,128]{2,1,0:T(8,128)(2,1)S(1)}, u32[]{:S(2)}, u32[]{:S(2)}) collective-permute-start(bf16[2,128,128]{2,1,0:T(8,128)(2,1)S(1)} %get-tuple-element.28), channel_id=1, source_target_pairs={{0,8},{4,12},{8,0},{12,4},{1,9},{5,13},{9,1},{13,5},{2,10},{6,14},... | collective-permute-start | bytes 196616 | tf_op jit(solution)/shard_map/ppermute | solution.py:399
  16.0 0.7 %collective-permute-done.2.refs_2_ = f32[128,128]{1,0:T(8,128)S(1)} collective-permute-done((f32[128,128]{1,0:T(8,128)S(1)}, f32[128,128]{1,0:T(8,128)S(1)}, u32[]{:S(2)}, u32[]{:S(2)}) %collective-permute-start.2) | collective-permute-done | bytes 65568 | tf_op jit(solution)/shard_map/ppermute | solution.py:399
  16.7 0.9 %collective-permute-done.3.refs_3_ = f32[128,128]{1,0:T(8,128)S(1)} collective-permute-done((f32[128,128]{1,0:T(8,128)S(1)}, f32[128,128]{1,0:T(8,128)S(1)}, u32[]{:S(2)}, u32[]{:S(2)}) %collective-permute-start.3) | collective-permute-done | bytes 65568 | tf_op jit(solution)/shard_map/ppermute | solution.py:399
  17.8 0.7 %collective-permute-start.5 = (f32[512,128]{1,0:T(8,128)S(1)}, f32[512,128]{1,0:T(8,128)S(1)}, u32[]{:S(2)}, u32[]{:S(2)}) collective-permute-start(f32[512,128]{1,0:T(8,128)S(1)} %bitcast.43), channel_id=1, source_target_pairs={{1,4},{4,1},{5,8},{8,5},{9,12},{12,9},{13,14},{14,13},{15,10},{10,... | collective-permute-start | bytes 786440 | tf_op jit(solution)/shard_map/ppermute | solution.py:438
  18.5 1.0 %blur_matrices.1.matrices_ref = bf16[2,4,256,128]{3,2,1,0:T(8,128)(2,1)S(1)} custom-call(f32[2,128]{1,0:T(2,128)S(1)} %maximum_convert_fusion.info_ref), custom_call_target="tpu_custom_call" | custom-call | tf_op jit(solution)/shard_map/blur_matrices/pallas_call | solution.py:218
  19.5 3.3 %collective-permute-done.9.refs_2_ = bf16[2,128,128]{2,1,0:T(8,128)(2,1)S(1)} collective-permute-done((bf16[2,128,128]{2,1,0:T(8,128)(2,1)S(1)}, bf16[2,128,128]{2,1,0:T(8,128)(2,1)S(1)}, u32[]{:S(2)}, u32[]{:S(2)}) %collective-permute-start.9) | collective-permute-done | bytes 65568 | tf_op jit(solution)/shard_map/ppermute | solution.py:399
  22.8 1.7 %correction.2.log_ref = f32[512,128]{1,0:T(8,128)S(1)} custom-call(s32[1]{0:T(128)} %bitcast.1.tile_ref, s32[2,8]{1,0:T(2,128)S(1)} %slice_convert_fusion.offsets_ref, bf16[4,128,128]{2,1,0:T(8,128)(2,1)S(1)} %get-tuple-element.19.current_ref, bf16[2,4,256,128]{3,2,1,0:T(8,128)(2,1)S(1)} %blur_matrices.1.matrices_ref, ...), custom_call_target="tpu_custom_call" | custom-call | flops 300000000 | bytes 1500000 | tf_op jit(solution)/shard_map/correction/pallas_call | solution.py:307
  25.1 2.4 %collective-permute-start.11 = (f32[512,128]{1,0:T(8,128)S(1)}, f32[512,128]{1,0:T(8,128)S(1)}, u32[]{:S(2)}, u32[]{:S(2)}) collective-permute-start(f32[512,128]{1,0:T(8,128)S(1)} %get-tuple-element.20.current_ref), channel_id=1, source_target_pairs={{0,1},{1,0},{2,3},{3,2},{4,5},{5,4},{6,7},{7,6},{8,9},{9,8},{10,11... | collective-permute-start | bytes 786440 | tf_op jit(solution)/shard_map/ppermute | solution.py:439
  28.3 1.7 %correction.3.log_ref = f32[512,128]{1,0:T(8,128)S(1)} custom-call(s32[1]{0:T(128)} %bitcast.1.tile_ref, s32[2,8]{1,0:T(2,128)S(1)} %slice_convert_fusion.offsets_ref, bf16[4,128,128]{2,1,0:T(8,128)(2,1)S(1)} %bitcast.45, bf16[2,4,256,128]{3,2,1,0:T(8,128)(2,1)S(1)} %blur_matrices.1.matrices_ref, bf16[2,128,128]{2,1,0:T(8,128)(2,1)S(1)} %get-tuple-element.26.refs_0_, ...), custom_call_target="tpu_custom_call" | custom-call | flops 300000000 | bytes 1500000 | tf_op jit(solution)/shard_map/correction/pallas_call | solution.py:307
  30.0 1.2 %update.3 = (f32[512,128]{1,0:T(8,128)S(1)}, bf16[512,128]{1,0:T(8,128)(2,1)}) custom-call(s32[1]{0:T(128)} %bitcast.core_ref, f32[512,128]{1,0:T(8,128)S(1)} %get-tuple-element.20.current_ref, f32[512,128]{1,0:T(8,128)S(1)} %collective-permute-done.11.twin_ref, f32[512,128]{1,0:T(8,128)S(1)} %collective-permute-done.12.other_ref, ...), custom_call_target="tpu_custom_call" | custom-call | tf_op jit(solution)/shard_map/update/pallas_call | solution.py:368
  31.3 7.9 %collective-permute-start.13 = (f16[128,128]{1,0:T(8,128)(2,1)S(1)}, f16[128,128]{1,0:T(8,128)(2,1)S(1)}, u32[]{:S(2)}, u32[]{:S(2)}) collective-permute-start(f16[128,128]{1,0:T(8,128)(2,1)S(1)} %get-tuple-element.38), channel_id=1, source_target_pairs={{0,4},{4,0},{8,12},{12,8},{1,5},{5,1},{9,13},{13,9},{2,6},{6,2},{1... | collective-permute-start | bytes 98312 | tf_op jit(solution)/shard_map/ppermute | solution.py:399
  39.2 1.6 %collective-permute-start.14 = (f16[128,128]{1,0:T(8,128)(2,1)S(1)}, f16[128,128]{1,0:T(8,128)(2,1)S(1)}, u32[]{:S(2)}, u32[]{:S(2)}) collective-permute-start(f16[128,128]{1,0:T(8,128)(2,1)S(1)} %get-tuple-element.37), channel_id=1, source_target_pairs={{0,8},{4,12},{8,0},{12,4},{1,9},{5,13},{9,1},{13,5},{2,10},{6,14},... | collective-permute-start | bytes 98312 | tf_op jit(solution)/shard_map/ppermute | solution.py:399
  40.8 1.4 %collective-permute-start.15 = (f16[128,128]{1,0:T(8,128)(2,1)S(1)}, f16[128,128]{1,0:T(8,128)(2,1)S(1)}, u32[]{:S(2)}, u32[]{:S(2)}) collective-permute-start(f16[128,128]{1,0:T(8,128)(2,1)S(1)} %get-tuple-element.36), channel_id=1, source_target_pairs={{0,12},{4,8},{8,4},{12,0},{1,13},{5,9},{9,5},{13,1},{2,14},{6,10},... | collective-permute-start | bytes 98312 | tf_op jit(solution)/shard_map/ppermute | solution.py:399
  42.2 1.8 %collective-permute-done.14 = f16[128,128]{1,0:T(8,128)(2,1)S(1)} collective-permute-done((f16[128,128]{1,0:T(8,128)(2,1)S(1)}, f16[128,128]{1,0:T(8,128)(2,1)S(1)}, u32[]{:S(2)}, u32[]{:S(2)}) %collective-permute-start.14) | collective-permute-done | bytes 32800 | tf_op jit(solution)/shard_map/ppermute | solution.py:399
  44.0 2.5 %collective-permute-done.15 = f16[128,128]{1,0:T(8,128)(2,1)S(1)} collective-permute-done((f16[128,128]{1,0:T(8,128)(2,1)S(1)}, f16[128,128]{1,0:T(8,128)(2,1)S(1)}, u32[]{:S(2)}, u32[]{:S(2)}) %collective-permute-start.15) | collective-permute-done | bytes 32800 | tf_op jit(solution)/shard_map/ppermute | solution.py:399
  47.2 4.4 %collective-permute-done.16 = f16[4,128,128]{2,1,0:T(8,128)(2,1)S(1)} collective-permute-done((f16[4,128,128]{2,1,0:T(8,128)(2,1)S(1)}, f16[4,128,128]{2,1,0:T(8,128)(2,1)S(1)}, u32[]{:S(2)}, u32[]{:S(2)}) %collective-permute-start.16) | collective-permute-done | bytes 131104 | tf_op jit(solution)/shard_map/ppermute | solution.py:446
  51.8 1.3 %collective-permute-done.17 = f16[4,128,128]{2,1,0:T(8,128)(2,1)S(1)} collective-permute-done((f16[4,128,128]{2,1,0:T(8,128)(2,1)S(1)}, f16[4,128,128]{2,1,0:T(8,128)(2,1)S(1)}, u32[]{:S(2)}, u32[]{:S(2)}) %collective-permute-start.17) | collective-permute-done | bytes 131104 | tf_op jit(solution)/shard_map/ppermute | solution.py:447
  53.4 0.8 %convert_element_type.26 = f32[8,128,128]{2,1,0:T(8,128)} convert(f16[8,128,128]{2,1,0:T(8,128)(2,1)S(1)} %select_dynamic-update-slice_fusion) | non-fusion elementwise | flops 131072 | bytes 786432 | tf_op jit(solution)/shard_map/convert_element_type | solution.py:455
  (57 shorter events, 4.9 us)
Async XLA Ops:
  0.0 1.0 %copy-start = (f32[8,128,128]{2,1,0:T(8,128)S(1)}, f32[8,128,128]{2,1,0:T(8,128)}, u32[]{:S(2)}) copy-start(f32[8,128,128]{2,1,0:T(8,128)} %param.5) | copy-start | bytes 1572868
  1.0 0.9 %copy-start.1 = (bf16[1,1,8,128,128]{4,3,2,1,0:T(8,128)(2,1)S(1)}, bf16[1,1,8,128,128]{4,3,2,1,0:T(8,128)(2,1)}, u32[]{:S(2)}) copy-start(bf16[1,1,8,128,128]{4,3,2,1,0:T(8,128)(2,1)} %param.4) | copy-start | bytes 786436
  2.2 0.7 %copy-start.2 = (f32[1,2,2,9]{3,2,1,0:T(2,128)S(1)}, f32[1,2,2,9]{3,2,1,0:T(2,128)}, u32[]{:S(2)}) copy-start(f32[1,2,2,9]{3,2,1,0:T(2,128)} %param.6) | copy-start | bytes 436
  2.2 1.7 %collective-permute-start.6 = (bf16[4,128,128]{2,1,0:T(8,128)(2,1)S(1)}, bf16[4,128,128]{2,1,0:T(8,128)(2,1)S(1)}, u32[]{:S(2)}, u32[]{:S(2)}) collective-permute-start(bf16[4,128,128]{2,1,0:T(8,128)(2,1)S(1)} %get-tuple-element.17), channel_id=1, source_target_pairs={{0,1},{1,0},{2,3},{3,2},{4,5},{5,4},{6,7},{7,6},{8,9},{9,8},{10,11... | collective-permute-start | bytes 393224 | tf_op jit(solution)/shard_map/ppermute | solution.py:410
  2.7 4.2 %collective-permute-start = (f32[4,128,128]{2,1,0:T(8,128)S(1)}, f32[4,128,128]{2,1,0:T(8,128)S(1)}, u32[]{:S(2)}, u32[]{:S(2)}) collective-permute-start(f32[4,128,128]{2,1,0:T(8,128)S(1)} %get-tuple-element.15), channel_id=1, source_target_pairs={{0,1},{1,0},{2,3},{3,2},{4,5},{5,4},{6,7},{7,6},{8,9},{9,8},{10,11... | collective-permute-start | bytes 786440 | tf_op jit(solution)/shard_map/ppermute | solution.py:407
  3.0 0.7 %copy-start.3 = (s32[1,8]{1,0:T(1,128)S(1)}, s32[1,8]{1,0:T(1,128)}, u32[]{:S(2)}) copy-start(s32[1,8]{1,0:T(1,128)} %param.7) | copy-start | bytes 100
  3.9 7.6 %collective-permute-start.7 = (bf16[528,128]{1,0:T(8,128)(2,1)S(1)}, bf16[528,128]{1,0:T(8,128)(2,1)S(1)}, u32[]{:S(2)}, u32[]{:S(2)}) collective-permute-start(bf16[528,128]{1,0:T(8,128)(2,1)S(1)} %pad_maximum_fusion), channel_id=1, source_target_pairs={{0,2},{2,0},{1,3},{3,1},{4,6},{6,4},{5,7},{7,5},{8,10},{10,8},{9,1... | collective-permute-start | bytes 405512 | tf_op jit(solution)/shard_map/ppermute | solution.py:421
  7.0 8.2 %collective-permute-start.1 = (f32[128,128]{1,0:T(8,128)S(1)}, f32[128,128]{1,0:T(8,128)S(1)}, u32[]{:S(2)}, u32[]{:S(2)}) collective-permute-start(f32[128,128]{1,0:T(8,128)S(1)} %get-tuple-element.33), channel_id=1, source_target_pairs={{0,4},{4,0},{8,12},{12,8},{1,5},{5,1},{9,13},{13,9},{2,6},{6,2},{1... | collective-permute-start | bytes 196616 | tf_op jit(solution)/shard_map/ppermute | solution.py:399
  8.7 8.1 %collective-permute-start.2 = (f32[128,128]{1,0:T(8,128)S(1)}, f32[128,128]{1,0:T(8,128)S(1)}, u32[]{:S(2)}, u32[]{:S(2)}) collective-permute-start(f32[128,128]{1,0:T(8,128)S(1)} %get-tuple-element.32), channel_id=1, source_target_pairs={{0,8},{4,12},{8,0},{12,4},{1,9},{5,13},{9,1},{13,5},{2,10},{6,14},... | collective-permute-start | bytes 196616 | tf_op jit(solution)/shard_map/ppermute | solution.py:399
  11.3 6.4 %collective-permute-start.3 = (f32[128,128]{1,0:T(8,128)S(1)}, f32[128,128]{1,0:T(8,128)S(1)}, u32[]{:S(2)}, u32[]{:S(2)}) collective-permute-start(f32[128,128]{1,0:T(8,128)S(1)} %get-tuple-element.31), channel_id=1, source_target_pairs={{0,12},{4,8},{8,4},{12,0},{1,13},{5,9},{9,5},{13,1},{2,14},{6,10},... | collective-permute-start | bytes 196616 | tf_op jit(solution)/shard_map/ppermute | solution.py:399
  11.5 8.0 %collective-permute-start.10 = (bf16[2,128,128]{2,1,0:T(8,128)(2,1)S(1)}, bf16[2,128,128]{2,1,0:T(8,128)(2,1)S(1)}, u32[]{:S(2)}, u32[]{:S(2)}) collective-permute-start(bf16[2,128,128]{2,1,0:T(8,128)(2,1)S(1)} %get-tuple-element.25), channel_id=1, source_target_pairs={{0,12},{4,8},{8,4},{12,0},{1,13},{5,9},{9,5},{13,1},{2,14},{6,10},... | collective-permute-start | bytes 196616 | tf_op jit(solution)/shard_map/ppermute | solution.py:399
  15.2 4.3 %collective-permute-start.8 = (bf16[2,128,128]{2,1,0:T(8,128)(2,1)S(1)}, bf16[2,128,128]{2,1,0:T(8,128)(2,1)S(1)}, u32[]{:S(2)}, u32[]{:S(2)}) collective-permute-start(bf16[2,128,128]{2,1,0:T(8,128)(2,1)S(1)} %get-tuple-element.27), channel_id=1, source_target_pairs={{0,4},{4,0},{8,12},{12,8},{1,5},{5,1},{9,13},{13,9},{2,6},{6,2},{1... | collective-permute-start | bytes 196616 | tf_op jit(solution)/shard_map/ppermute | solution.py:399
  15.2 7.6 %collective-permute-start.9 = (bf16[2,128,128]{2,1,0:T(8,128)(2,1)S(1)}, bf16[2,128,128]{2,1,0:T(8,128)(2,1)S(1)}, u32[]{:S(2)}, u32[]{:S(2)}) collective-permute-start(bf16[2,128,128]{2,1,0:T(8,128)(2,1)S(1)} %get-tuple-element.28), channel_id=1, source_target_pairs={{0,8},{4,12},{8,0},{12,4},{1,9},{5,13},{9,1},{13,5},{2,10},{6,14},... | collective-permute-start | bytes 196616 | tf_op jit(solution)/shard_map/ppermute | solution.py:399
  17.7 6.8 %collective-permute-start.4 = (f32[512,128]{1,0:T(8,128)S(1)}, f32[512,128]{1,0:T(8,128)S(1)}, u32[]{:S(2)}, u32[]{:S(2)}) collective-permute-start(f32[512,128]{1,0:T(8,128)S(1)} %bitcast.42), channel_id=1, source_target_pairs={{0,1},{1,0},{2,3},{3,2},{4,5},{5,4},{6,7},{7,6},{8,9},{9,8},{10,11... | collective-permute-start | bytes 786440 | tf_op jit(solution)/shard_map/ppermute | solution.py:439
  17.8 6.8 %collective-permute-start.5 = (f32[512,128]{1,0:T(8,128)S(1)}, f32[512,128]{1,0:T(8,128)S(1)}, u32[]{:S(2)}, u32[]{:S(2)}) collective-permute-start(f32[512,128]{1,0:T(8,128)S(1)} %bitcast.43), channel_id=1, source_target_pairs={{1,4},{4,1},{5,8},{8,5},{9,12},{12,9},{13,14},{14,13},{15,10},{10,... | collective-permute-start | bytes 786440 | tf_op jit(solution)/shard_map/ppermute | solution.py:438
  25.1 4.8 %collective-permute-start.11 = (f32[512,128]{1,0:T(8,128)S(1)}, f32[512,128]{1,0:T(8,128)S(1)}, u32[]{:S(2)}, u32[]{:S(2)}) collective-permute-start(f32[512,128]{1,0:T(8,128)S(1)} %get-tuple-element.20.current_ref), channel_id=1, source_target_pairs={{0,1},{1,0},{2,3},{3,2},{4,5},{5,4},{6,7},{7,6},{8,9},{9,8},{10,11... | collective-permute-start | bytes 786440 | tf_op jit(solution)/shard_map/ppermute | solution.py:439
  27.6 2.4 %collective-permute-start.12 = (f32[512,128]{1,0:T(8,128)S(1)}, f32[512,128]{1,0:T(8,128)S(1)}, u32[]{:S(2)}, u32[]{:S(2)}) collective-permute-start(f32[512,128]{1,0:T(8,128)S(1)} %get-tuple-element.20.current_ref), channel_id=1, source_target_pairs={{1,4},{4,1},{5,8},{8,5},{9,12},{12,9},{13,14},{14,13},{15,10},{10,... | collective-permute-start | bytes 786440 | tf_op jit(solution)/shard_map/ppermute | solution.py:438
  31.3 10.9 %collective-permute-start.13 = (f16[128,128]{1,0:T(8,128)(2,1)S(1)}, f16[128,128]{1,0:T(8,128)(2,1)S(1)}, u32[]{:S(2)}, u32[]{:S(2)}) collective-permute-start(f16[128,128]{1,0:T(8,128)(2,1)S(1)} %get-tuple-element.38), channel_id=1, source_target_pairs={{0,4},{4,0},{8,12},{12,8},{1,5},{5,1},{9,13},{13,9},{2,6},{6,2},{1... | collective-permute-start | bytes 98312 | tf_op jit(solution)/shard_map/ppermute | solution.py:399
  39.2 4.8 %collective-permute-start.14 = (f16[128,128]{1,0:T(8,128)(2,1)S(1)}, f16[128,128]{1,0:T(8,128)(2,1)S(1)}, u32[]{:S(2)}, u32[]{:S(2)}) collective-permute-start(f16[128,128]{1,0:T(8,128)(2,1)S(1)} %get-tuple-element.37), channel_id=1, source_target_pairs={{0,8},{4,12},{8,0},{12,4},{1,9},{5,13},{9,1},{13,5},{2,10},{6,14},... | collective-permute-start | bytes 98312 | tf_op jit(solution)/shard_map/ppermute | solution.py:399
  40.8 5.7 %collective-permute-start.15 = (f16[128,128]{1,0:T(8,128)(2,1)S(1)}, f16[128,128]{1,0:T(8,128)(2,1)S(1)}, u32[]{:S(2)}, u32[]{:S(2)}) collective-permute-start(f16[128,128]{1,0:T(8,128)(2,1)S(1)} %get-tuple-element.36), channel_id=1, source_target_pairs={{0,12},{4,8},{8,4},{12,0},{1,13},{5,9},{9,5},{13,1},{2,14},{6,10},... | collective-permute-start | bytes 98312 | tf_op jit(solution)/shard_map/ppermute | solution.py:399
  46.5 5.0 %collective-permute-start.16 = (f16[4,128,128]{2,1,0:T(8,128)(2,1)S(1)}, f16[4,128,128]{2,1,0:T(8,128)(2,1)S(1)}, u32[]{:S(2)}, u32[]{:S(2)}) collective-permute-start(f16[4,128,128]{2,1,0:T(8,128)(2,1)S(1)} %pad_maximum_fusion.1), channel_id=1, source_target_pairs={{0,2},{2,0},{1,3},{3,1},{4,6},{6,4},{5,7},{7,5},{8,10},{10,8},{9,1... | collective-permute-start | bytes 393224 | tf_op jit(solution)/shard_map/ppermute | solution.py:446
  51.7 1.4 %collective-permute-start.17 = (f16[4,128,128]{2,1,0:T(8,128)(2,1)S(1)}, f16[4,128,128]{2,1,0:T(8,128)(2,1)S(1)}, u32[]{:S(2)}, u32[]{:S(2)}) collective-permute-start(f16[4,128,128]{2,1,0:T(8,128)(2,1)S(1)} %get-tuple-element.24), channel_id=1, source_target_pairs={{0,1},{1,0},{2,3},{3,2},{4,5},{5,4},{6,7},{7,6},{8,9},{9,8},{10,11... | collective-permute-start | bytes 393224 | tf_op jit(solution)/shard_map/ppermute | solution.py:447
where the time goes:
time: 54.4 us; the launch traced here: 54.2 us
  starting transfers between devices  28 us (51%)
  waiting for transfers between devices  14.9 us (27%)
  Pallas kernels  6.4 us (12%)
  local copies, waits for them, and re-layouts  2.95 us (5%)
  other arithmetic  1.58 us (3%)
    ppermute x9, starting transfers between devices, over_tiles(): lax.ppermute(pick(lax.bitwise_xor(tile, k)), 'tiles', [(t, t ^ k) for t i...  19.8 us
    ppermute x9, waiting for transfers between devices, over_tiles(): lax.ppermute(pick(lax.bitwise_xor(tile, k)), 'tiles', [(t, t ^ k) for t i...  9.25 us
    ppermute x1, waiting for transfers between devices, plane_shards(): crossed = lax.ppermute(result, 'views', swap)  4.37 us
    pallas_call x2, Pallas kernels, correction_logs(): pl.pallas_call(functools.partial(correction_kernel, tiles), out_shape=jax...  3.38 us
    ppermute x1, starting transfers between devices, plane_shards(): came = lax.ppermute(sent, 'views', swap)  3.03 us
    unnamed x8, local copies, waits for them, and re-layouts  2.6 us
    ppermute x2, starting transfers between devices, plane_shards(): twin = lax.ppermute(current, 'gz', swap)  2.49 us
    pallas_call x2, Pallas kernels, update(): pl.pallas_call(functools.partial(update_kernel, views), out_shape=(jax.Sh...  1.85 us
  transfers between devices with their start and end apart: 18, of which 7 were waited for; matrix products, arithmetic and copies ran while one was open for 1% of the time, Pallas kernels for 8%

commit v1 on v0

--- a/solution.py
+++ b/solution.py
@@ -161,38 +161,9 @@
 
 INFO_ROWS = 16
 CHUNK = 32
-ANY = pl.BlockSpec(memory_space=pl.ANY)
 VMEM = pl.BlockSpec(memory_space=pltpu.VMEM)
 SMEM = pl.BlockSpec(memory_space=pltpu.SMEM)
 LIMIT = pltpu.CompilerParams(vmem_limit_bytes=16 * 2**20)
-
-
-def split_kernel(core_ref, wide_ref, narrow_ref, *refs):
-    outs, sems = refs[:-1], refs[-1]
-    core = core_ref[0]
-    copies = []
-    for n, (source, pick) in enumerate(
-        [(wide_ref, 1 - core), (narrow_ref, 1 - core), (wide_ref, core), (narrow_ref, core)]
-    ):
-        copies.append(pltpu.make_async_copy(source.at[:, pick], outs[n], sems.at[n]))
-    for copy in copies:
-        copy.start()
-    for copy in copies:
-        copy.wait()
-
-
-def split_by_core(core, wide, narrow):
-    pairs = [x.reshape(x.shape[0] // 2, 2, *x.shape[1:]) for x in (wide, narrow)]
-    shapes = [jax.ShapeDtypeStruct((x.shape[0], *x.shape[2:]), x.dtype) for x in pairs]
-    return pl.pallas_call(
-        split_kernel,
-        out_shape=shapes * 2,
-        in_specs=[SMEM, ANY, ANY],
-        out_specs=[VMEM] * 4,
-        scratch_shapes=[pltpu.SemaphoreType.DMA((4,))],
-        compiler_params=LIMIT,
-        name="split_by_core",
-    )(core, *pairs)
 
 
 def matrices_kernel(taps, info_ref, out_ref):
@@ -225,31 +196,10 @@
     )(info)
 
 
-def gather_kernel(tiles, tile_ref, *refs):
-    pieces, (wide_ref, narrow_ref) = refs[:tiles], refs[tiles:]
-    for k in range(tiles):
-        owner = lax.bitwise_xor(tile_ref[0], k)
-        wide_ref[owner] = pieces[k][...]
-        narrow_ref[owner] = pieces[k][...].astype(narrow_ref.dtype)
-
-
-def gather_plane(tile, pieces):
-    shape = (len(pieces), *pieces[0].shape)
-    return pl.pallas_call(
-        functools.partial(gather_kernel, len(pieces)),
-        out_shape=(jax.ShapeDtypeStruct(shape, jnp.float32), jax.ShapeDtypeStruct(shape, jnp.bfloat16)),
-        in_specs=[SMEM] + [VMEM] * len(pieces),
-        out_specs=[VMEM] * 2,
-        compiler_params=LIMIT,
-        name="gather_plane",
-    )(tile, *pieces)
-
-
 def correction_kernel(tiles, tile_ref, offsets_ref, current_ref, matrices_ref, *refs):
-    data, log_ref = refs[:tiles], refs[tiles]
-    work = refs[tiles + 1 :]
     views, blocks = offsets_ref.shape
-    height, columns = data[0].shape[-2:]
+    data, log_ref, work = refs[: views * tiles], refs[views * tiles], refs[views * tiles + 1 :]
+    height, columns = data[0].shape
     rows = height // blocks
     me = tile_ref[0]
     shift = [[offsets_ref[w, s] for s in range(blocks)] for w in range(views)]
@@ -279,7 +229,7 @@
     for w in range(views):
         blurred = jnp.dot(halves[w][...], matrices_ref[w, 1], preferred_element_type=jnp.float32)
         for k in range(tiles):
-            quotient = data[k][w].astype(jnp.float32) / blurred[k * height : (k + 1) * height]
+            quotient = data[w * tiles + k][...].astype(jnp.float32) / blurred[k * height : (k + 1) * height]
             planes[w][:, k * columns : (k + 1) * columns] = quotient.astype(jnp.bfloat16)
     for w in range(views):
         first(w, 2)
@@ -307,7 +257,7 @@
     return pl.pallas_call(
         functools.partial(correction_kernel, tiles),
         out_shape=jax.ShapeDtypeStruct((tiles * height, columns), jnp.float32),
-        in_specs=[SMEM, SMEM] + [VMEM] * (2 + tiles),
+        in_specs=[SMEM, SMEM] + [VMEM] * (2 + len(data)),
         out_specs=VMEM,
         scratch_shapes=scratch * offsets.shape[0],
         cost_estimate=pl.CostEstimate(flops=300_000_000, bytes_accessed=1_500_000, transcendentals=0),
@@ -316,7 +266,7 @@
     )(tile, offsets, current, matrices, *data)
 
 
-def update_kernel(views, core_ref, current_ref, twin_ref, other_ref, log_ref, new_ref, narrow_ref):
+def update_kernel(views, core_ref, current_ref, twin_ref, other_ref, log_ref, *new_refs):
     total, columns = current_ref.shape
     first = core_ref[0] == 0
     row = lax.broadcasted_iota(jnp.int32, (CHUNK, columns), 0)
@@ -360,19 +310,16 @@
         divergence = grad_z * inverse - lower + (unit_y - before_y) + (unit_x - before_x)
         damping = 1.0 - TV_WEIGHT * divergence
         new = current * jnp.exp(log_ref[start:stop, :] * (1.0 / views)) / damping
-        new_ref[start:stop, :] = new
-        narrow_ref[start:stop, :] = new.astype(narrow_ref.dtype)
-
-
-def update(views, core, current, twin, other, logs):
+        for ref in new_refs:
+            ref[start:stop, :] = new.astype(ref.dtype)
+
+
+def update(views, core, current, twin, other, logs, dtypes):
     return pl.pallas_call(
         functools.partial(update_kernel, views),
-        out_shape=(
-            jax.ShapeDtypeStruct(current.shape, jnp.float32),
-            jax.ShapeDtypeStruct(current.shape, jnp.bfloat16),
-        ),
+        out_shape=[jax.ShapeDtypeStruct(current.shape, dtype) for dtype in dtypes],
         in_specs=[SMEM] + [VMEM] * 4,
-        out_specs=[VMEM] * 2,
+        out_specs=[VMEM] * len(dtypes),
         compiler_params=LIMIT,
         name="update",
     )(core, current, twin, other, logs)
@@ -395,32 +342,40 @@
         return jnp.where(chain == 0, t, tiles - 1 - t)
 
     def over_tiles(pick):
-        return [pick(tile)] + [
-            lax.ppermute(pick(lax.bitwise_xor(tile, k)), "tiles", [(t, t ^ k) for t in range(tiles)])
-            for k in range(1, tiles)
-        ]
+        pieces = [pick(tile)]
+        for k in range(1, tiles):
+            pieces.append(
+                lax.ppermute(pick(lax.bitwise_xor(tile, k)), "tiles", [(t, t ^ k) for t in range(tiles)])
+            )
+        return pieces
 
     me = tile.reshape(1).astype(jnp.int32)
     flag = core.reshape(1).astype(jnp.int32)
-    give, give_data, keep, keep_data = split_by_core(flag, estimate, view_data[0, 0])
-
-    chain = jnp.where(straight, keep, lax.ppermute(give, "gz", swap))
-    pieces = over_tiles(lambda t: lax.dynamic_index_in_dim(chain, place(view, t), 0, keepdims=False))
-
-    got_data = lax.ppermute(give_data, "gz", swap)
-    mine = jnp.where(straight, keep_data, got_data)
+
+    def coded(parity):
+        planes, data = (
+            lax.dynamic_index_in_dim(x.reshape(tiles, 2, height, columns), parity, 1, keepdims=False)
+            for x in (estimate, view_data)
+        )
+        return jnp.stack([(planes - 1.0).astype(jnp.float16), data.astype(jnp.float16)])
+
+    keep = coded(core)
+    got = lax.ppermute(coded(1 - core), "gz", swap)
+    mine = jnp.where(straight, keep, got)
     profiles = [psf_taps.reshape(-1), psf_taps[..., ::-1].reshape(-1)]
     info = jnp.concatenate([*profiles, offsets.reshape(-1).astype(jnp.float32)])
-    info = jnp.pad(info, (0, columns - info.shape[0])).astype(jnp.bfloat16)
+    info = jnp.pad(info, (0, columns - info.shape[0])).astype(jnp.bfloat16).astype(jnp.float16)
     sent = jnp.concatenate(
         [
-            jnp.where(straight, got_data, keep_data).reshape(tiles * height, columns),
+            jnp.where(straight, got[1], keep[1]).reshape(tiles * height, columns),
             jnp.broadcast_to(info, (INFO_ROWS, columns)),
         ]
     )
     came = lax.ppermute(sent, "views", swap)
-    both = jnp.stack([mine, came[: tiles * height].reshape(tiles, height, columns)], axis=1)
-    data = over_tiles(lambda t: lax.dynamic_index_in_dim(both, place(view, t), 0, keepdims=False))
+    theirs = came[: tiles * height].reshape(tiles, height, columns)
+    pieces = over_tiles(lambda t: lax.dynamic_index_in_dim(mine, place(view, t), 1, keepdims=False))
+    others = over_tiles(lambda t: lax.dynamic_index_in_dim(theirs, place(view, t), 0, keepdims=False))
+    data = [piece[1].astype(jnp.bfloat16) for piece in pieces] + [x.astype(jnp.bfloat16) for x in others]
 
     info = jnp.stack([info, came[tiles * height]]).astype(jnp.float32)
     shifts = info[:, 8 * taps : 8 * taps + blocks].astype(jnp.int32)
@@ -432,20 +387,41 @@
         one, two = device(*here, 1), device(*there, 0)
         hops += [(one, two), (two, one)]
 
-    current, narrow = gather_plane(me, pieces)
-    current = current.reshape(tiles * height, columns)
-    for _ in range(ITERS):
-        other = lax.ppermute(current, square, hops)
-        twin = lax.ppermute(current, "gz", swap)
-        logs = correction_logs(me, shifts, narrow, matrices, data)
-        current, narrow = update(views, flag, current, twin, other, logs)
-        narrow = narrow.reshape(tiles, height, columns)
+    def owned_by(o):
+        chosen = pieces[o][0]
+        for t in range(1, tiles):
+            chosen = jnp.where(tile == t, pieces[o ^ t][0], chosen)
+        return chosen
+
+    plane = jnp.concatenate([owned_by(o) for o in range(tiles)])
+    current = plane.astype(jnp.float32) + 1.0
+    narrow = current.astype(jnp.bfloat16)
+    at_end = jnp.where(view == 0, (tile == 0) & (core == 0), (tile == 0) & (core == 1))
+    for iteration in range(ITERS):
+        last = iteration == ITERS - 1
+        other = lax.ppermute(plane, square, hops)
+        twin = lax.ppermute(plane, "gz", swap)
+        other = jnp.where(at_end, 0.0, other.astype(jnp.float32) + 1.0)
+        twin = twin.astype(jnp.float32) + 1.0
+        logs = correction_logs(me, shifts, narrow.reshape(tiles, height, columns), matrices, data)
+        current, *rest = update(
+            views, flag, current, twin, other, logs, [jnp.float32] if last else [jnp.float32, jnp.bfloat16]
+        )
+        if not last:
+            narrow = rest[0]
+            plane = (current - 1.0).astype(jnp.float16)
 
     result = current.astype(jnp.float16).reshape(tiles, height, columns)
     result = jnp.stack(over_tiles(lambda t: lax.dynamic_index_in_dim(result, t, 0, keepdims=False)))
-    crossed = lax.ppermute(result, "views", swap)
-    twin = lax.ppermute(jnp.where(straight, crossed, result), "gz", swap)
-    same = jnp.where(straight, result, crossed)
+    turn, across = [], []
+    for t in range(tiles):
+        for v in range(2):
+            turn += [(device(t, v, 1 - v), device(t, v, v)), (device(t, v, v), device(t, 1 - v, v))]
+            across += [(device(t, v, 1 - v), device(t, 1 - v, v))]
+    turned = lax.ppermute(result, square, turn)
+    crossed = lax.ppermute(result, square, across)
+    same = jnp.where(straight, result, turned)
+    twin = jnp.where(straight, turned, crossed)
     ordered = []
     for i in range(tiles):
         k = lax.bitwise_xor(place(core, i), tile)

time: 54.4 us -> 52.8 us (0.971)
  the two profiles are of different devices: /device:TPU:0 before, /device:TPU:1 now
where the time goes in v1:
time: 52.8 us; the launch traced here: 52.6 us
  starting transfers between devices  25.6 us (48%)
  waiting for transfers between devices  16.6 us (31%)
  Pallas kernels  5.56 us (11%)
  other arithmetic  3.37 us (6%)
  local copies, waits for them, and re-layouts  1.02 us (2%)
    ppermute x9, starting transfers between devices, over_tiles(): lax.ppermute(pick(lax.bitwise_xor(tile, k)), 'tiles', [(t, t ^ k) for t i...  11 us
    ppermute x9, waiting for transfers between devices, over_tiles(): lax.ppermute(pick(lax.bitwise_xor(tile, k)), 'tiles', [(t, t ^ k) for t i...  10.7 us
    ppermute x2, starting transfers between devices, plane_shards(): other = lax.ppermute(plane, square, hops)  6.76 us
    ppermute x1, waiting for transfers between devices, plane_shards(): crossed = lax.ppermute(result, square, across)  4.31 us
    pallas_call x2, Pallas kernels, correction_logs(): pl.pallas_call(functools.partial(correction_kernel, tiles), out_shape=jax...  3.39 us
    ppermute x1, starting transfers between devices, plane_shards(): turned = lax.ppermute(result, square, turn)  3.35 us
    ppermute x1, starting transfers between devices, plane_shards(): came = lax.ppermute(sent, 'views', swap)  2.4 us
    ppermute x1, starting transfers between devices, plane_shards(): crossed = lax.ppermute(result, square, across)  1.91 us
  transfers between devices with their start and end apart: 17, of which 8 were waited for; matrix products, arithmetic and copies ran while one was open for 2% of the time, Pallas kernels for 8%

profile of v1, /device:TPU:1, one launch (start us, length us, event | category | flops | bytes accessed | tf_op | source)
XLA Modules:
  0.0 52.6 jit_solution(9548948186273632418)
XLA Ops:
  0.0 1.1 %fusion.2 = (f16[1,4,128,128]{3,2,1,0:T(8,128)(2,1)S(1)}, f16[1,4,128,128]{3,2,1,0:T(8,128)(2,1)S(1)}) fusion(f32[4,2,128,128]{3,2,1,0:T(8,128)} %bitcast.116, s32[]{:T(128)S(6)} %select_n.231, s32[]{:T(128)S(6)} %select_n.232), kind=kLoop, calls=%fused_computation.13 | loop fusion | flops 262144 | bytes 786440 | tf_op jit(solution)/shard_map/convert_element_type | solution.py:360
  3.1 2.4 %collective-permute-start.6 = (f16[528,128]{1,0:T(8,128)(2,1)S(1)}, f16[528,128]{1,0:T(8,128)(2,1)S(1)}, u32[]{:S(2)}, u32[]{:S(2)}) collective-permute-start(f16[528,128]{1,0:T(8,128)(2,1)S(1)} %pad_maximum_fusion.1), channel_id=1, source_target_pairs={{0,2},{2,0},{1,3},{3,1},{4,6},{6,4},{5,7},{7,5},{8,10},{10,8},{9,1... | collective-permute-start | bytes 405512 | tf_op jit(solution)/shard_map/ppermute | solution.py:374
  5.7 3.4 %collective-permute-start.1 = (f16[2,128,128]{2,1,0:T(8,128)(2,1)S(1)}, f16[2,128,128]{2,1,0:T(8,128)(2,1)S(1)}, u32[]{:S(2)}, u32[]{:S(2)}) collective-permute-start(f16[2,128,128]{2,1,0:T(8,128)(2,1)S(1)} %get-tuple-element.17), channel_id=1, source_target_pairs={{0,12},{4,8},{8,4},{12,0},{1,13},{5,9},{9,5},{13,1},{2,14},{6,10},... | collective-permute-start | bytes 196616 | tf_op jit(solution)/shard_map/ppermute | solution.py:348
  9.4 1.3 %collective-permute-done.1 = f16[2,128,128]{2,1,0:T(8,128)(2,1)S(1)} collective-permute-done((f16[2,128,128]{2,1,0:T(8,128)(2,1)S(1)}, f16[2,128,128]{2,1,0:T(8,128)(2,1)S(1)}, u32[]{:S(2)}, u32[]{:S(2)}) %collective-permute-start.1) | collective-permute-done | bytes 65568 | tf_op jit(solution)/shard_map/ppermute | solution.py:348
  10.7 4.1 %collective-permute-done.2 = f16[2,128,128]{2,1,0:T(8,128)(2,1)S(1)} collective-permute-done((f16[2,128,128]{2,1,0:T(8,128)(2,1)S(1)}, f16[2,128,128]{2,1,0:T(8,128)(2,1)S(1)}, u32[]{:S(2)}, u32[]{:S(2)}) %collective-permute-start.2) | collective-permute-done | bytes 65568 | tf_op jit(solution)/shard_map/ppermute | solution.py:348
  15.0 3.3 %collective-permute-start.5 = (f16[512,128]{1,0:T(8,128)(2,1)S(1)}, f16[512,128]{1,0:T(8,128)(2,1)S(1)}, u32[]{:S(2)}, u32[]{:S(2)}) collective-permute-start(f16[512,128]{1,0:T(8,128)(2,1)S(1)} %pad_maximum_fusion.2), channel_id=1, source_target_pairs={{1,4},{4,1},{5,8},{8,5},{9,12},{12,9},{13,14},{14,13},{15,10},{10,... | collective-permute-start | bytes 393224 | tf_op jit(solution)/shard_map/ppermute | solution.py:402
  18.6 0.8 %collective-permute-start.7 = (f16[128,128]{1,0:T(8,128)(2,1)S(1)}, f16[128,128]{1,0:T(8,128)(2,1)S(1)}, u32[]{:S(2)}, u32[]{:S(2)}) collective-permute-start(f16[128,128]{1,0:T(8,128)(2,1)S(1)} %get-tuple-element.28), channel_id=1, source_target_pairs={{0,4},{4,0},{8,12},{12,8},{1,5},{5,1},{9,13},{13,9},{2,6},{6,2},{1... | collective-permute-start | bytes 98312 | tf_op jit(solution)/shard_map/ppermute | solution.py:348
  19.4 1.4 %collective-permute-start.8 = (f16[128,128]{1,0:T(8,128)(2,1)S(1)}, f16[128,128]{1,0:T(8,128)(2,1)S(1)}, u32[]{:S(2)}, u32[]{:S(2)}) collective-permute-start(f16[128,128]{1,0:T(8,128)(2,1)S(1)} %get-tuple-element.27), channel_id=1, source_target_pairs={{0,8},{4,12},{8,0},{12,4},{1,9},{5,13},{9,1},{13,5},{2,10},{6,14},... | collective-permute-start | bytes 98312 | tf_op jit(solution)/shard_map/ppermute | solution.py:348
  20.8 1.4 %collective-permute-start.9 = (f16[128,128]{1,0:T(8,128)(2,1)S(1)}, f16[128,128]{1,0:T(8,128)(2,1)S(1)}, u32[]{:S(2)}, u32[]{:S(2)}) collective-permute-start(f16[128,128]{1,0:T(8,128)(2,1)S(1)} %get-tuple-element.26), channel_id=1, source_target_pairs={{0,12},{4,8},{8,4},{12,0},{1,13},{5,9},{9,5},{13,1},{2,14},{6,10},... | collective-permute-start | bytes 98312 | tf_op jit(solution)/shard_map/ppermute | solution.py:348
  22.3 1.0 %blur_matrices.1.matrices_ref = bf16[2,4,256,128]{3,2,1,0:T(8,128)(2,1)S(1)} custom-call(f32[2,128]{1,0:T(2,128)S(1)} %maximum_convert_fusion.info_ref), custom_call_target="tpu_custom_call" | custom-call | tf_op jit(solution)/shard_map/blur_matrices/pallas_call | solution.py:189
  23.4 2.1 %collective-permute-done.9 = f16[128,128]{1,0:T(8,128)(2,1)S(1)} collective-permute-done((f16[128,128]{1,0:T(8,128)(2,1)S(1)}, f16[128,128]{1,0:T(8,128)(2,1)S(1)}, u32[]{:S(2)}, u32[]{:S(2)}) %collective-permute-start.9) | collective-permute-done | bytes 32800 | tf_op jit(solution)/shard_map/ppermute | solution.py:348
  25.4 1.7 %correction.2.log_ref = f32[512,128]{1,0:T(8,128)S(1)} custom-call(s32[1]{0:T(128)} %bitcast.14.tile_ref, s32[2,8]{1,0:T(2,128)S(1)} %slice_convert_fusion.3.offsets_ref, bf16[4,128,128]{2,1,0:T(8,128)(2,1)S(1)} %bitcast.112, bf16[2,4,256,128]{3,2,1,0:T(8,128)(2,1)S(1)} %blur_matrices.1.matrices_ref, bf16[128,128]{1,0:T(8,128)(2,1)S(1)} %fusion.9.refs_0_, ...), custom_call_target="tpu_custom_call" | custom-call | flops 300000000 | bytes 1500000 | tf_op jit(solution)/shard_map/correction/pallas_call | solution.py:257
  27.9 3.4 %collective-permute-start.11 = (f16[512,128]{1,0:T(8,128)(2,1)S(1)}, f16[512,128]{1,0:T(8,128)(2,1)S(1)}, u32[]{:S(2)}, u32[]{:S(2)}) collective-permute-start(f16[512,128]{1,0:T(8,128)(2,1)S(1)} %add_convert_fusion), channel_id=1, source_target_pairs={{1,4},{4,1},{5,8},{8,5},{9,12},{12,9},{13,14},{14,13},{15,10},{10,... | collective-permute-start | bytes 393224 | tf_op jit(solution)/shard_map/ppermute | solution.py:402
  31.4 1.7 %correction.3.log_ref = f32[512,128]{1,0:T(8,128)S(1)} custom-call(s32[1]{0:T(128)} %bitcast.14.tile_ref, s32[2,8]{1,0:T(2,128)S(1)} %slice_convert_fusion.3.offsets_ref, bf16[4,128,128]{2,1,0:T(8,128)(2,1)S(1)} %bitcast.113, bf16[2,4,256,128]{3,2,1,0:T(8,128)(2,1)S(1)} %blur_matrices.1.matrices_ref, bf16[128,128]{1,0:T(8,128)(2,1)S(1)} %fusion.9.refs_0_, ...), custom_call_target="tpu_custom_call" | custom-call | flops 300000000 | bytes 1500000 | tf_op jit(solution)/shard_map/correction/pallas_call | solution.py:257
  33.1 1.1 %collective-permute-done.11 = f16[512,128]{1,0:T(8,128)(2,1)S(1)} collective-permute-done((f16[512,128]{1,0:T(8,128)(2,1)S(1)}, f16[512,128]{1,0:T(8,128)(2,1)S(1)}, u32[]{:S(2)}, u32[]{:S(2)}) %collective-permute-start.11) | collective-permute-done | bytes 131104 | tf_op jit(solution)/shard_map/ppermute | solution.py:402
  34.9 0.9 %collective-permute-start.12 = (f16[128,128]{1,0:T(8,128)(2,1)S(1)}, f16[128,128]{1,0:T(8,128)(2,1)S(1)}, u32[]{:S(2)}, u32[]{:S(2)}) collective-permute-start(f16[128,128]{1,0:T(8,128)(2,1)S(1)} %get-tuple-element.25), channel_id=1, source_target_pairs={{0,4},{4,0},{8,12},{12,8},{1,5},{5,1},{9,13},{13,9},{2,6},{6,2},{1... | collective-permute-start | bytes 98312 | tf_op jit(solution)/shard_map/ppermute | solution.py:348
  35.8 1.4 %collective-permute-start.13 = (f16[128,128]{1,0:T(8,128)(2,1)S(1)}, f16[128,128]{1,0:T(8,128)(2,1)S(1)}, u32[]{:S(2)}, u32[]{:S(2)}) collective-permute-start(f16[128,128]{1,0:T(8,128)(2,1)S(1)} %get-tuple-element.24), channel_id=1, source_target_pairs={{0,8},{4,12},{8,0},{12,4},{1,9},{5,13},{9,1},{13,5},{2,10},{6,14},... | collective-permute-start | bytes 98312 | tf_op jit(solution)/shard_map/ppermute | solution.py:348
  37.2 1.3 %collective-permute-start.14 = (f16[128,128]{1,0:T(8,128)(2,1)S(1)}, f16[128,128]{1,0:T(8,128)(2,1)S(1)}, u32[]{:S(2)}, u32[]{:S(2)}) collective-permute-start(f16[128,128]{1,0:T(8,128)(2,1)S(1)} %get-tuple-element.23), channel_id=1, source_target_pairs={{0,12},{4,8},{8,4},{12,0},{1,13},{5,9},{9,5},{13,1},{2,14},{6,10},... | collective-permute-start | bytes 98312 | tf_op jit(solution)/shard_map/ppermute | solution.py:348
  38.5 0.9 %collective-permute-done.13 = f16[128,128]{1,0:T(8,128)(2,1)S(1)} collective-permute-done((f16[128,128]{1,0:T(8,128)(2,1)S(1)}, f16[128,128]{1,0:T(8,128)(2,1)S(1)}, u32[]{:S(2)}, u32[]{:S(2)}) %collective-permute-start.13) | collective-permute-done | bytes 32800 | tf_op jit(solution)/shard_map/ppermute | solution.py:348
  39.4 2.3 %collective-permute-done.14 = f16[128,128]{1,0:T(8,128)(2,1)S(1)} collective-permute-done((f16[128,128]{1,0:T(8,128)(2,1)S(1)}, f16[128,128]{1,0:T(8,128)(2,1)S(1)}, u32[]{:S(2)}, u32[]{:S(2)}) %collective-permute-start.14) | collective-permute-done | bytes 32800 | tf_op jit(solution)/shard_map/ppermute | solution.py:348
  41.8 3.4 %collective-permute-start.15 = (f16[4,128,128]{2,1,0:T(8,128)(2,1)S(1)}, f16[4,128,128]{2,1,0:T(8,128)(2,1)S(1)}, u32[]{:S(2)}, u32[]{:S(2)}) collective-permute-start(f16[4,128,128]{2,1,0:T(8,128)(2,1)S(1)} %pad_maximum_fusion.3), channel_id=1, source_target_pairs={{1,0},{0,2},{2,3},{3,1},{5,4},{4,6},{6,7},{7,5},{9,8},{8,10},{10,1... | collective-permute-start | bytes 393224 | tf_op jit(solution)/shard_map/ppermute | solution.py:421
  45.1 1.9 %collective-permute-start.16 = (f16[4,128,128]{2,1,0:T(8,128)(2,1)S(1)}, f16[4,128,128]{2,1,0:T(8,128)(2,1)S(1)}, u32[]{:S(2)}, u32[]{:S(2)}) collective-permute-start(f16[4,128,128]{2,1,0:T(8,128)(2,1)S(1)} %pad_maximum_fusion.3), channel_id=1, source_target_pairs={{1,2},{2,1},{5,6},{6,5},{9,10},{10,9},{13,14},{14,13},{17,18},{18,... | collective-permute-start | bytes 393224 | tf_op jit(solution)/shard_map/ppermute | solution.py:422
  47.1 4.3 %collective-permute-done.16 = f16[4,128,128]{2,1,0:T(8,128)(2,1)S(1)} collective-permute-done((f16[4,128,128]{2,1,0:T(8,128)(2,1)S(1)}, f16[4,128,128]{2,1,0:T(8,128)(2,1)S(1)}, u32[]{:S(2)}, u32[]{:S(2)}) %collective-permute-start.16) | collective-permute-done | bytes 131104 | tf_op jit(solution)/shard_map/ppermute | solution.py:422
  51.8 0.8 %convert_element_type.177 = f32[8,128,128]{2,1,0:T(8,128)} convert(f16[8,128,128]{2,1,0:T(8,128)(2,1)S(1)} %select_dynamic-update-slice_fusion) | non-fusion elementwise | flops 131072 | bytes 786432 | tf_op jit(solution)/shard_map/convert_element_type | solution.py:431
  (70 shorter events, 4.7 us)
Async XLA Ops:
  0.0 1.1 %copy-start = (bf16[1,1,8,128,128]{4,3,2,1,0:T(8,128)(2,1)S(1)}, bf16[1,1,8,128,128]{4,3,2,1,0:T(8,128)(2,1)}, u32[]{:S(2)}) copy-start(bf16[1,1,8,128,128]{4,3,2,1,0:T(8,128)(2,1)} %param.4) | copy-start | bytes 786436
  1.2 0.7 %copy-start.2 = (s32[1,8]{1,0:T(1,128)S(1)}, s32[1,8]{1,0:T(1,128)}, u32[]{:S(2)}) copy-start(s32[1,8]{1,0:T(1,128)} %param.7) | copy-start | bytes 100
  1.3 0.7 %copy-start.1 = (f32[1,2,2,9]{3,2,1,0:T(2,128)S(1)}, f32[1,2,2,9]{3,2,1,0:T(2,128)}, u32[]{:S(2)}) copy-start(f32[1,2,2,9]{3,2,1,0:T(2,128)} %param.6) | copy-start | bytes 436
  1.3 1.6 %collective-permute-start = (f16[2,4,128,128]{3,2,1,0:T(8,128)(2,1)S(1)}, f16[2,4,128,128]{3,2,1,0:T(8,128)(2,1)S(1)}, u32[]{:S(2)}, u32[]{:S(2)}) collective-permute-start(f16[2,4,128,128]{3,2,1,0:T(8,128)(2,1)S(1)} %pad_maximum_fusion), channel_id=1, source_target_pairs={{0,1},{1,0},{2,3},{3,2},{4,5},{5,4},{6,7},{7,6},{8,9},{9,8},{10,11... | collective-permute-start | bytes 786440 | tf_op jit(solution)/shard_map/ppermute | solution.py:363
  3.1 15.4 %collective-permute-start.6 = (f16[528,128]{1,0:T(8,128)(2,1)S(1)}, f16[528,128]{1,0:T(8,128)(2,1)S(1)}, u32[]{:S(2)}, u32[]{:S(2)}) collective-permute-start(f16[528,128]{1,0:T(8,128)(2,1)S(1)} %pad_maximum_fusion.1), channel_id=1, source_target_pairs={{0,2},{2,0},{1,3},{3,1},{4,6},{6,4},{5,7},{7,5},{8,10},{10,8},{9,1... | collective-permute-start | bytes 405512 | tf_op jit(solution)/shard_map/ppermute | solution.py:374
  5.7 5.1 %collective-permute-start.1 = (f16[2,128,128]{2,1,0:T(8,128)(2,1)S(1)}, f16[2,128,128]{2,1,0:T(8,128)(2,1)S(1)}, u32[]{:S(2)}, u32[]{:S(2)}) collective-permute-start(f16[2,128,128]{2,1,0:T(8,128)(2,1)S(1)} %get-tuple-element.17), channel_id=1, source_target_pairs={{0,12},{4,8},{8,4},{12,0},{1,13},{5,9},{9,5},{13,1},{2,14},{6,10},... | collective-permute-start | bytes 196616 | tf_op jit(solution)/shard_map/ppermute | solution.py:348
  9.0 5.8 %collective-permute-start.2 = (f16[2,128,128]{2,1,0:T(8,128)(2,1)S(1)}, f16[2,128,128]{2,1,0:T(8,128)(2,1)S(1)}, u32[]{:S(2)}, u32[]{:S(2)}) collective-permute-start(f16[2,128,128]{2,1,0:T(8,128)(2,1)S(1)} %get-tuple-element.16), channel_id=1, source_target_pairs={{0,8},{4,12},{8,0},{12,4},{1,9},{5,13},{9,1},{13,5},{2,10},{6,14},... | collective-permute-start | bytes 196616 | tf_op jit(solution)/shard_map/ppermute | solution.py:348
  9.0 5.8 %collective-permute-start.3 = (f16[2,128,128]{2,1,0:T(8,128)(2,1)S(1)}, f16[2,128,128]{2,1,0:T(8,128)(2,1)S(1)}, u32[]{:S(2)}, u32[]{:S(2)}) collective-permute-start(f16[2,128,128]{2,1,0:T(8,128)(2,1)S(1)} %get-tuple-element.15), channel_id=1, source_target_pairs={{0,4},{4,0},{8,12},{12,8},{1,5},{5,1},{9,13},{13,9},{2,6},{6,2},{1... | collective-permute-start | bytes 196616 | tf_op jit(solution)/shard_map/ppermute | solution.py:348
  15.0 12.2 %collective-permute-start.5 = (f16[512,128]{1,0:T(8,128)(2,1)S(1)}, f16[512,128]{1,0:T(8,128)(2,1)S(1)}, u32[]{:S(2)}, u32[]{:S(2)}) collective-permute-start(f16[512,128]{1,0:T(8,128)(2,1)S(1)} %pad_maximum_fusion.2), channel_id=1, source_target_pairs={{1,4},{4,1},{5,8},{8,5},{9,12},{12,9},{13,14},{14,13},{15,10},{10,... | collective-permute-start | bytes 393224 | tf_op jit(solution)/shard_map/ppermute | solution.py:402
  18.3 8.8 %collective-permute-start.4 = (f16[512,128]{1,0:T(8,128)(2,1)S(1)}, f16[512,128]{1,0:T(8,128)(2,1)S(1)}, u32[]{:S(2)}, u32[]{:S(2)}) collective-permute-start(f16[512,128]{1,0:T(8,128)(2,1)S(1)} %pad_maximum_fusion.2), channel_id=1, source_target_pairs={{0,1},{1,0},{2,3},{3,2},{4,5},{5,4},{6,7},{7,6},{8,9},{9,8},{10,11... | collective-permute-start | bytes 393224 | tf_op jit(solution)/shard_map/ppermute | solution.py:403
  18.6 4.7 %collective-permute-start.7 = (f16[128,128]{1,0:T(8,128)(2,1)S(1)}, f16[128,128]{1,0:T(8,128)(2,1)S(1)}, u32[]{:S(2)}, u32[]{:S(2)}) collective-permute-start(f16[128,128]{1,0:T(8,128)(2,1)S(1)} %get-tuple-element.28), channel_id=1, source_target_pairs={{0,4},{4,0},{8,12},{12,8},{1,5},{5,1},{9,13},{13,9},{2,6},{6,2},{1... | collective-permute-start | bytes 98312 | tf_op jit(solution)/shard_map/ppermute | solution.py:348
  19.4 3.9 %collective-permute-start.8 = (f16[128,128]{1,0:T(8,128)(2,1)S(1)}, f16[128,128]{1,0:T(8,128)(2,1)S(1)}, u32[]{:S(2)}, u32[]{:S(2)}) collective-permute-start(f16[128,128]{1,0:T(8,128)(2,1)S(1)} %get-tuple-element.27), channel_id=1, source_target_pairs={{0,8},{4,12},{8,0},{12,4},{1,9},{5,13},{9,1},{13,5},{2,10},{6,14},... | collective-permute-start | bytes 98312 | tf_op jit(solution)/shard_map/ppermute | solution.py:348
  20.8 4.6 %collective-permute-start.9 = (f16[128,128]{1,0:T(8,128)(2,1)S(1)}, f16[128,128]{1,0:T(8,128)(2,1)S(1)}, u32[]{:S(2)}, u32[]{:S(2)}) collective-permute-start(f16[128,128]{1,0:T(8,128)(2,1)S(1)} %get-tuple-element.26), channel_id=1, source_target_pairs={{0,12},{4,8},{8,4},{12,0},{1,13},{5,9},{9,5},{13,1},{2,14},{6,10},... | collective-permute-start | bytes 98312 | tf_op jit(solution)/shard_map/ppermute | solution.py:348
  27.9 6.3 %collective-permute-start.11 = (f16[512,128]{1,0:T(8,128)(2,1)S(1)}, f16[512,128]{1,0:T(8,128)(2,1)S(1)}, u32[]{:S(2)}, u32[]{:S(2)}) collective-permute-start(f16[512,128]{1,0:T(8,128)(2,1)S(1)} %add_convert_fusion), channel_id=1, source_target_pairs={{1,4},{4,1},{5,8},{8,5},{9,12},{12,9},{13,14},{14,13},{15,10},{10,... | collective-permute-start | bytes 393224 | tf_op jit(solution)/shard_map/ppermute | solution.py:402
  31.3 2.9 %collective-permute-start.10 = (f16[512,128]{1,0:T(8,128)(2,1)S(1)}, f16[512,128]{1,0:T(8,128)(2,1)S(1)}, u32[]{:S(2)}, u32[]{:S(2)}) collective-permute-start(f16[512,128]{1,0:T(8,128)(2,1)S(1)} %add_convert_fusion), channel_id=1, source_target_pairs={{0,1},{1,0},{2,3},{3,2},{4,5},{5,4},{6,7},{7,6},{8,9},{9,8},{10,11... | collective-permute-start | bytes 393224 | tf_op jit(solution)/shard_map/ppermute | solution.py:403
  34.9 3.6 %collective-permute-start.12 = (f16[128,128]{1,0:T(8,128)(2,1)S(1)}, f16[128,128]{1,0:T(8,128)(2,1)S(1)}, u32[]{:S(2)}, u32[]{:S(2)}) collective-permute-start(f16[128,128]{1,0:T(8,128)(2,1)S(1)} %get-tuple-element.25), channel_id=1, source_target_pairs={{0,4},{4,0},{8,12},{12,8},{1,5},{5,1},{9,13},{13,9},{2,6},{6,2},{1... | collective-permute-start | bytes 98312 | tf_op jit(solution)/shard_map/ppermute | solution.py:348
  35.8 3.7 %collective-permute-start.13 = (f16[128,128]{1,0:T(8,128)(2,1)S(1)}, f16[128,128]{1,0:T(8,128)(2,1)S(1)}, u32[]{:S(2)}, u32[]{:S(2)}) collective-permute-start(f16[128,128]{1,0:T(8,128)(2,1)S(1)} %get-tuple-element.24), channel_id=1, source_target_pairs={{0,8},{4,12},{8,0},{12,4},{1,9},{5,13},{9,1},{13,5},{2,10},{6,14},... | collective-permute-start | bytes 98312 | tf_op jit(solution)/shard_map/ppermute | solution.py:348
  37.2 4.6 %collective-permute-start.14 = (f16[128,128]{1,0:T(8,128)(2,1)S(1)}, f16[128,128]{1,0:T(8,128)(2,1)S(1)}, u32[]{:S(2)}, u32[]{:S(2)}) collective-permute-start(f16[128,128]{1,0:T(8,128)(2,1)S(1)} %get-tuple-element.23), channel_id=1, source_target_pairs={{0,12},{4,8},{8,4},{12,0},{1,13},{5,9},{9,5},{13,1},{2,14},{6,10},... | collective-permute-start | bytes 98312 | tf_op jit(solution)/shard_map/ppermute | solution.py:348
  41.8 5.3 %collective-permute-start.15 = (f16[4,128,128]{2,1,0:T(8,128)(2,1)S(1)}, f16[4,128,128]{2,1,0:T(8,128)(2,1)S(1)}, u32[]{:S(2)}, u32[]{:S(2)}) collective-permute-start(f16[4,128,128]{2,1,0:T(8,128)(2,1)S(1)} %pad_maximum_fusion.3), channel_id=1, source_target_pairs={{1,0},{0,2},{2,3},{3,1},{5,4},{4,6},{6,7},{7,5},{9,8},{8,10},{10,1... | collective-permute-start | bytes 393224 | tf_op jit(solution)/shard_map/ppermute | solution.py:421
  45.1 6.3 %collective-permute-start.16 = (f16[4,128,128]{2,1,0:T(8,128)(2,1)S(1)}, f16[4,128,128]{2,1,0:T(8,128)(2,1)S(1)}, u32[]{:S(2)}, u32[]{:S(2)}) collective-permute-start(f16[4,128,128]{2,1,0:T(8,128)(2,1)S(1)} %pad_maximum_fusion.3), channel_id=1, source_target_pairs={{1,2},{2,1},{5,6},{6,5},{9,10},{10,9},{13,14},{14,13},{17,18},{18,... | collective-permute-start | bytes 393224 | tf_op jit(solution)/shard_map/ppermute | solution.py:422

commit v2 on v1

--- a/solution.py
+++ b/solution.py
@@ -160,6 +160,9 @@
 
 
 INFO_ROWS = 16
+PLANE_UNIT = 65534.0
+DATA_UNIT = 1024.0
+TAP_UNIT = 8192.0
 CHUNK = 32
 VMEM = pl.BlockSpec(memory_space=pltpu.VMEM)
 SMEM = pl.BlockSpec(memory_space=pltpu.SMEM)
@@ -328,58 +331,69 @@
 def plane_shards(view_data, estimate, psf_taps, offsets):
     tiles, views = lax.axis_size("tiles"), lax.axis_size("views")
     square = ("tiles", "views", "gz")
-    _, height, columns = estimate.shape
+    planes, height, columns = estimate.shape
     blocks = offsets.shape[1]
     taps = psf_taps.shape[-1]
     tile, view, core = lax.axis_index("tiles"), lax.axis_index("views"), lax.axis_index("gz")
-    straight = view == core
     swap = [(0, 1), (1, 0)]
 
     def device(t, v, g):
         return (t * views + v) * 2 + g
 
-    def place(chain, t):
-        return jnp.where(chain == 0, t, tiles - 1 - t)
-
-    def over_tiles(pick):
-        pieces = [pick(tile)]
-        for k in range(1, tiles):
-            pieces.append(
-                lax.ppermute(pick(lax.bitwise_xor(tile, k)), "tiles", [(t, t ^ k) for t in range(tiles)])
-            )
+    def ordered(pieces, shift):
+        placed = []
+        for i in range(tiles):
+            chosen = pieces[i]
+            for s in range(1, tiles):
+                chosen = jnp.where(shift == s, pieces[i ^ s], chosen)
+            placed.append(chosen)
+        return placed
+
+    def exchange(pick):
+        pieces = []
+        for k in range(tiles):
+            pairs = [(device(t, v, g), device(t ^ k, g, v)) for t in range(tiles) for v in range(2) for g in range(2)]
+            pieces.append(lax.ppermute(pick(lax.bitwise_xor(tile, k)), square, pairs))
         return pieces
+
+    def end_of(chain):
+        return jnp.where(chain == 0, 0, tiles - 1)
 
     me = tile.reshape(1).astype(jnp.int32)
     flag = core.reshape(1).astype(jnp.int32)
-
-    def coded(parity):
-        planes, data = (
-            lax.dynamic_index_in_dim(x.reshape(tiles, 2, height, columns), parity, 1, keepdims=False)
-            for x in (estimate, view_data)
-        )
-        return jnp.stack([(planes - 1.0).astype(jnp.float16), data.astype(jnp.float16)])
-
-    keep = coded(core)
-    got = lax.ppermute(coded(1 - core), "gz", swap)
-    mine = jnp.where(straight, keep, got)
     profiles = [psf_taps.reshape(-1), psf_taps[..., ::-1].reshape(-1)]
-    info = jnp.concatenate([*profiles, offsets.reshape(-1).astype(jnp.float32)])
-    info = jnp.pad(info, (0, columns - info.shape[0])).astype(jnp.bfloat16).astype(jnp.float16)
-    sent = jnp.concatenate(
-        [
-            jnp.where(straight, got[1], keep[1]).reshape(tiles * height, columns),
-            jnp.broadcast_to(info, (INFO_ROWS, columns)),
-        ]
-    )
-    came = lax.ppermute(sent, "views", swap)
-    theirs = came[: tiles * height].reshape(tiles, height, columns)
-    pieces = over_tiles(lambda t: lax.dynamic_index_in_dim(mine, place(view, t), 1, keepdims=False))
-    others = over_tiles(lambda t: lax.dynamic_index_in_dim(theirs, place(view, t), 0, keepdims=False))
-    data = [piece[1].astype(jnp.bfloat16) for piece in pieces] + [x.astype(jnp.bfloat16) for x in others]
-
-    info = jnp.stack([info, came[tiles * height]]).astype(jnp.float32)
+    info = [lax.reduce_precision(p, 8, 7) * TAP_UNIT for p in profiles]
+    info = jnp.concatenate([*info, offsets.reshape(-1).astype(jnp.float32)])
+    info = jnp.pad(info, (0, columns - info.shape[0])).astype(jnp.int16)
+
+    wide = estimate.reshape(tiles, 2, height, columns)
+    wide = lax.dynamic_index_in_dim(wide, view, 1, keepdims=True)
+    wide = jnp.round((wide - 1.0) * PLANE_UNIT).astype(jnp.int16)
+    data = view_data.reshape(tiles, 2, height, columns).astype(jnp.float32)
+    data = (data * DATA_UNIT).astype(jnp.int16)
+    payload = jnp.concatenate([wide, data], axis=1).reshape(tiles, 3 * height, columns)
+    note = jnp.broadcast_to(info, (tiles, INFO_ROWS, columns))
+    payload = jnp.concatenate([payload, note], axis=1)
+
+    def for_tile(t):
+        return lax.dynamic_index_in_dim(payload, lax.bitwise_xor(t, end_of(core)), 0, keepdims=False)
+
+    pieces = exchange(for_tile)
+    planes = [piece[:height] for piece in pieces]
+    pairs = [piece[height : 3 * height].reshape(2, height, columns) for piece in pieces]
+    keep = [lax.dynamic_index_in_dim(pair, core, 0, keepdims=False) for pair in pairs]
+    give = [lax.dynamic_index_in_dim(pair, 1 - core, 0, keepdims=False) for pair in pairs]
+    note = pieces[0][3 * height :]
+    got = lax.ppermute(jnp.concatenate([*planes, *give, note]), "gz", swap)
+    length = tiles * height
+    twin = got[:length].reshape(tiles, height, columns)
+    take = got[length : 2 * length].reshape(tiles, height, columns)
+    data = [x.astype(jnp.float32) * (1.0 / DATA_UNIT) for x in [*keep, *[take[k] for k in range(tiles)]]]
+    data = [x.astype(jnp.bfloat16) for x in data]
+
+    info = jnp.stack([note[0], got[2 * length]]).astype(jnp.float32)
     shifts = info[:, 8 * taps : 8 * taps + blocks].astype(jnp.int32)
-    matrices = blur_matrices(taps, height, info)
+    matrices = blur_matrices(taps, height, info * (1.0 / TAP_UNIT))
 
     path = [(t, 0) for t in range(tiles)] + [(t, 1) for t in reversed(range(tiles))]
     hops = []
@@ -387,22 +401,20 @@
         one, two = device(*here, 1), device(*there, 0)
         hops += [(one, two), (two, one)]
 
-    def owned_by(o):
-        chosen = pieces[o][0]
-        for t in range(1, tiles):
-            chosen = jnp.where(tile == t, pieces[o ^ t][0], chosen)
-        return chosen
-
-    plane = jnp.concatenate([owned_by(o) for o in range(tiles)])
-    current = plane.astype(jnp.float32) + 1.0
+    def plane_of(coded):
+        return coded.astype(jnp.float32) * (1.0 / PLANE_UNIT) + 1.0
+
+    plane = jnp.concatenate(ordered(planes, tile))
+    twin = plane_of(jnp.concatenate(ordered([twin[k] for k in range(tiles)], tile)))
+    current = plane_of(plane)
     narrow = current.astype(jnp.bfloat16)
-    at_end = jnp.where(view == 0, (tile == 0) & (core == 0), (tile == 0) & (core == 1))
+    at_end = (tile == 0) & (core == view)
     for iteration in range(ITERS):
-        last = iteration == ITERS - 1
+        first, last = iteration == 0, iteration == ITERS - 1
         other = lax.ppermute(plane, square, hops)
-        twin = lax.ppermute(plane, "gz", swap)
-        other = jnp.where(at_end, 0.0, other.astype(jnp.float32) + 1.0)
-        twin = twin.astype(jnp.float32) + 1.0
+        if not first:
+            twin = lax.ppermute(current, "gz", swap)
+        other = jnp.where(at_end, 0.0, plane_of(other) if first else other.astype(jnp.float32) + 1.0)
         logs = correction_logs(me, shifts, narrow.reshape(tiles, height, columns), matrices, data)
         current, *rest = update(
             views, flag, current, twin, other, logs, [jnp.float32] if last else [jnp.float32, jnp.bfloat16]
@@ -412,23 +424,11 @@
             plane = (current - 1.0).astype(jnp.float16)
 
     result = current.astype(jnp.float16).reshape(tiles, height, columns)
-    result = jnp.stack(over_tiles(lambda t: lax.dynamic_index_in_dim(result, t, 0, keepdims=False)))
-    turn, across = [], []
-    for t in range(tiles):
-        for v in range(2):
-            turn += [(device(t, v, 1 - v), device(t, v, v)), (device(t, v, v), device(t, 1 - v, v))]
-            across += [(device(t, v, 1 - v), device(t, 1 - v, v))]
-    turned = lax.ppermute(result, square, turn)
-    crossed = lax.ppermute(result, square, across)
-    same = jnp.where(straight, result, turned)
-    twin = jnp.where(straight, turned, crossed)
-    ordered = []
-    for i in range(tiles):
-        k = lax.bitwise_xor(place(core, i), tile)
-        same_i = lax.dynamic_index_in_dim(same, k, 0, keepdims=False)
-        twin_i = lax.dynamic_index_in_dim(twin, k, 0, keepdims=False)
-        ordered += [jnp.where(core == 0, same_i, twin_i), jnp.where(core == 0, twin_i, same_i)]
-    return jnp.stack(ordered).astype(jnp.float32)
+    twin = lax.ppermute(result, "gz", swap)
+    both = jnp.stack([jnp.where(core == 0, result, twin), jnp.where(core == 0, twin, result)], axis=1)
+    pieces = exchange(lambda t: lax.dynamic_index_in_dim(both, t, 0, keepdims=False))
+    result = jnp.concatenate(ordered(pieces, lax.bitwise_xor(tile, end_of(core))))
+    return result.astype(jnp.float32)
 
 
 def one_plane_each(mesh, view_data, estimate, psf_taps, offsets):

time: 52.8 us -> 53.1 us (level)
  starting transfers between devices: 25.6 us -> 22.1 us
  waiting for transfers between devices: 16.6 us -> 19.3 us
  local copies, waits for them, and re-layouts: 1.02 us -> 1.73 us
    ppermute x2, waiting for transfers between devices: 1.06 us -> 6.32 us  [plane_shards(): other = lax.ppermute(plane, square, hops)]
    ppermute x15 -> x11, waiting for transfers between devices: 15.6 us -> 13 us  [the longest x8 11.6 us: exchange(): pieces.append(lax.ppermute(pick(lax.bitwise_xor(tile, k)), square, pairs))]
    ppermute x2, starting transfers between devices: 6.76 us -> 4.35 us  [plane_shards(): other = lax.ppermute(plane, square, hops)]
    ppermute x15 -> x11, starting transfers between devices: 18.9 us -> 17.8 us  [the longest x8 17.6 us: exchange(): pieces.append(lax.ppermute(pick(lax.bitwise_xor(tile, k)), square, pairs))]
    rev x1, local copies, waits for them, and re-layouts: 0.1 us -> 0.83 us  [plane_shards(): profiles = [psf_taps.reshape(-1), psf_taps[..., ::-1].reshape(-1)]]
    another operation x1 -> x2, other arithmetic: 0.01 us -> 0.7 us  [step(): return body(*arrays)]
    convert_element_type x13 -> x8, other arithmetic: 2.17 us -> 2.15 us  [the longest x1 1.07 us: plane_shards(): data = (data * DATA_UNIT).astype(jnp.int16)]
  transfers between devices with their start and end apart: 17 -> 13, of which waited for: 8 -> 8; matrix products, arithmetic and copies ran while one was open for 2% -> 0% of each run, Pallas kernels for 8% -> 3%
where the time goes in v2:
time: 53.1 us; the launch traced here: 52.8 us
  starting transfers between devices  22.1 us (42%)
  waiting for transfers between devices  19.3 us (36%)
  Pallas kernels  5.59 us (11%)
  other arithmetic  3.72 us (7%)
  local copies, waits for them, and re-layouts  1.73 us (3%)
    ppermute x8, starting transfers between devices, exchange(): pieces.append(lax.ppermute(pick(lax.bitwise_xor(tile, k)), square, pairs))  17.6 us
    ppermute x8, waiting for transfers between devices, exchange(): pieces.append(lax.ppermute(pick(lax.bitwise_xor(tile, k)), square, pairs))  11.6 us
    ppermute x2, waiting for transfers between devices, plane_shards(): other = lax.ppermute(plane, square, hops)  6.32 us
    ppermute x2, starting transfers between devices, plane_shards(): other = lax.ppermute(plane, square, hops)  4.35 us
    pallas_call x2, Pallas kernels, correction_logs(): pl.pallas_call(functools.partial(correction_kernel, tiles), out_shape=jax...  3.41 us
    ppermute x1, waiting for transfers between devices, plane_shards(): twin = lax.ppermute(result, 'gz', swap)  1.31 us
    pallas_call x2, Pallas kernels, update(): pl.pallas_call(functools.partial(update_kernel, views), out_shape=[jax.Sh...  1.19 us
    convert_element_type x1, other arithmetic, plane_shards(): data = (data * DATA_UNIT).astype(jnp.int16)  1.07 us
  transfers between devices with their start and end apart: 13, of which 8 were waited for; matrix products, arithmetic and copies ran while one was open for 0% of the time, Pallas kernels for 3%

profile of v2, /device:TPU:1, one launch (start us, length us, event | category | flops | bytes accessed | tf_op | source)
XLA Modules:
  0.0 52.8 jit_solution(10435474213022494331)
XLA Ops:
  0.0 0.8 %rev.3 = f32[1,2,2,9]{3,2,1,0:T(2,128)S(1)} reverse(f32[1,2,2,9]{3,2,1,0:T(2,128)} %param.6), dimensions={3} | reverse | bytes 288 | tf_op jit(solution)/shard_map/rev | solution.py:364
  0.8 0.7 %multiply_convert_fusion.10 = s16[1,2,2,9]{3,2,1,0:T(2,128)(2,1)S(1)} fusion(f32[1,2,2,9]{3,2,1,0:T(2,128)} %param.6), kind=kLoop, calls=%fused_computation.79 | loop fusion | flops 108 | bytes 216 | tf_op jit(solution)/shard_map/convert.7 | solution.py:463
  1.5 1.1 %multiply_convert_fusion = s16[1,1,8,128,128]{4,3,2,1,0:T(8,128)(2,1)S(1)} fusion(bf16[1,1,8,128,128]{4,3,2,1,0:T(8,128)(2,1)} %param.4), kind=kLoop, calls=%fused_computation.4 | loop fusion | flops 393216 | bytes 524288 | tf_op jit(solution)/shard_map/convert_element_type | solution.py:373
  2.8 0.6 %copy-done.1 = s32[1,8]{1,0:T(1,128)S(1)} copy-done((s32[1,8]{1,0:T(1,128)S(1)}, s32[1,8]{1,0:T(1,128)}, u32[]{:S(2)}) %copy-start.1) | copy-done | bytes 56
  3.6 4.5 %collective-permute-start.3 = (s16[400,128]{1,0:T(8,128)(2,1)S(1)}, s16[400,128]{1,0:T(8,128)(2,1)S(1)}, u32[]{:S(2)}, u32[]{:S(2)}) collective-permute-start(s16[400,128]{1,0:T(8,128)(2,1)S(1)} %get-tuple-element.16), channel_id=1, source_target_pairs={{0,0},{1,2},{2,1},{3,3},{4,4},{5,6},{6,5},{7,7},{8,8},{9,10},{10,9... | collective-permute-start | bytes 307208 | tf_op jit(solution)/shard_map/ppermute | solution.py:356
  8.1 1.1 %collective-permute-start.2 = (s16[400,128]{1,0:T(8,128)(2,1)S(1)}, s16[400,128]{1,0:T(8,128)(2,1)S(1)}, u32[]{:S(2)}, u32[]{:S(2)}) collective-permute-start(s16[400,128]{1,0:T(8,128)(2,1)S(1)} %get-tuple-element.15), channel_id=1, source_target_pairs={{0,4},{1,6},{2,5},{3,7},{4,0},{5,2},{6,1},{7,3},{8,12},{9,14},{10,... | collective-permute-start | bytes 307208 | tf_op jit(solution)/shard_map/ppermute | solution.py:356
  9.2 3.8 %collective-permute-start.1 = (s16[400,128]{1,0:T(8,128)(2,1)S(1)}, s16[400,128]{1,0:T(8,128)(2,1)S(1)}, u32[]{:S(2)}, u32[]{:S(2)}) collective-permute-start(s16[400,128]{1,0:T(8,128)(2,1)S(1)} %get-tuple-element.14), channel_id=1, source_target_pairs={{0,8},{1,10},{2,9},{3,11},{4,12},{5,14},{6,13},{7,15},{8,0},{9,2},... | collective-permute-start | bytes 307208 | tf_op jit(solution)/shard_map/ppermute | solution.py:356
  13.5 3.8 %collective-permute-done.1 = s16[400,128]{1,0:T(8,128)(2,1)S(1)} collective-permute-done((s16[400,128]{1,0:T(8,128)(2,1)S(1)}, s16[400,128]{1,0:T(8,128)(2,1)S(1)}, u32[]{:S(2)}, u32[]{:S(2)}) %collective-permute-start.1) | collective-permute-done | bytes 102432 | tf_op jit(solution)/shard_map/ppermute | solution.py:356
  17.3 2.5 %collective-permute-done = s16[400,128]{1,0:T(8,128)(2,1)S(1)} collective-permute-done((s16[400,128]{1,0:T(8,128)(2,1)S(1)}, s16[400,128]{1,0:T(8,128)(2,1)S(1)}, u32[]{:S(2)}, u32[]{:S(2)}) %collective-permute-start) | collective-permute-done | bytes 102432 | tf_op jit(solution)/shard_map/ppermute | solution.py:356
  20.2 2.2 %collective-permute-start.5 = (s16[512,128]{1,0:T(8,128)(2,1)S(1)}, s16[512,128]{1,0:T(8,128)(2,1)S(1)}, u32[]{:S(2)}, u32[]{:S(2)}) collective-permute-start(s16[512,128]{1,0:T(8,128)(2,1)S(1)} %pad_add_fusion.1), channel_id=1, source_target_pairs={{1,4},{4,1},{5,8},{8,5},{9,12},{12,9},{13,14},{14,13},{15,10},{10,... | collective-permute-start | bytes 393224 | tf_op jit(solution)/shard_map/ppermute | solution.py:414
  22.5 4.0 %collective-permute-done.5 = s16[512,128]{1,0:T(8,128)(2,1)S(1)} collective-permute-done((s16[512,128]{1,0:T(8,128)(2,1)S(1)}, s16[512,128]{1,0:T(8,128)(2,1)S(1)}, u32[]{:S(2)}, u32[]{:S(2)}) %collective-permute-start.5) | collective-permute-done | bytes 131104 | tf_op jit(solution)/shard_map/ppermute | solution.py:414
  26.6 1.0 %blur_matrices.1.matrices_ref = bf16[2,4,256,128]{3,2,1,0:T(8,128)(2,1)S(1)} custom-call(f32[2,128]{1,0:T(2,128)S(1)} %broadcast_multiply_fusion.info_ref), custom_call_target="tpu_custom_call" | custom-call | tf_op jit(solution)/shard_map/blur_matrices/pallas_call | solution.py:192
  27.9 1.7 %correction.2.log_ref = f32[512,128]{1,0:T(8,128)S(1)} custom-call(s32[1]{0:T(128)} %bitcast.17.tile_ref, s32[2,8]{1,0:T(2,128)S(1)} %slice_convert_fusion.offsets_ref, bf16[4,128,128]{2,1,0:T(8,128)(2,1)S(1)} %bitcast.50, bf16[2,4,256,128]{3,2,1,0:T(8,128)(2,1)S(1)} %blur_matrices.1.matrices_ref, bf16[128,128]{1,0:T(8,128)(2,1)S(1)} %get-tuple-element.37.refs_0_, ...), custom_call_target="tpu_custom_call" | custom-call | flops 300000000 | bytes 1500000 | tf_op jit(solution)/shard_map/correction/pallas_call | solution.py:260
  29.6 0.6 %update.2 = (f32[512,128]{1,0:T(8,128)S(1)}, bf16[512,128]{1,0:T(8,128)(2,1)S(1)}) custom-call(s32[1]{0:T(128)} %bitcast.core_ref, f32[512,128]{1,0:T(8,128)S(1)} %get-tuple-element.36.current_ref, f32[512,128]{1,0:T(8,128)S(1)} %multiply_add_fusion.twin_ref, f32[512,128]{1,0:T(8,128)S(1)} %add_select_fusion.1.other_ref, f32[512,128]{1,0:T(8,128)S(1)} %correction.2.log_ref), custom_call_target="tpu_custom_call" | custom-call | tf_op jit(solution)/shard_map/update/pallas_call | solution.py:321
  30.2 2.2 %collective-permute-start.7 = (f16[512,128]{1,0:T(8,128)(2,1)S(1)}, f16[512,128]{1,0:T(8,128)(2,1)S(1)}, u32[]{:S(2)}, u32[]{:S(2)}) collective-permute-start(f16[512,128]{1,0:T(8,128)(2,1)S(1)} %add_convert_fusion), channel_id=1, source_target_pairs={{1,4},{4,1},{5,8},{8,5},{9,12},{12,9},{13,14},{14,13},{15,10},{10,... | collective-permute-start | bytes 393224 | tf_op jit(solution)/shard_map/ppermute | solution.py:414
  32.5 1.7 %correction.3.log_ref = f32[512,128]{1,0:T(8,128)S(1)} custom-call(s32[1]{0:T(128)} %bitcast.17.tile_ref, s32[2,8]{1,0:T(2,128)S(1)} %slice_convert_fusion.offsets_ref, bf16[4,128,128]{2,1,0:T(8,128)(2,1)S(1)} %bitcast.51, bf16[2,4,256,128]{3,2,1,0:T(8,128)(2,1)S(1)} %blur_matrices.1.matrices_ref, bf16[128,128]{1,0:T(8,128)(2,1)S(1)} %get-tuple-element.37.refs_0_, ...), custom_call_target="tpu_custom_call" | custom-call | flops 300000000 | bytes 1500000 | tf_op jit(solution)/shard_map/correction/pallas_call | solution.py:260
  34.2 2.3 %collective-permute-done.7 = f16[512,128]{1,0:T(8,128)(2,1)S(1)} collective-permute-done((f16[512,128]{1,0:T(8,128)(2,1)S(1)}, f16[512,128]{1,0:T(8,128)(2,1)S(1)}, u32[]{:S(2)}, u32[]{:S(2)}) %collective-permute-start.7) | collective-permute-done | bytes 131104 | tf_op jit(solution)/shard_map/ppermute | solution.py:414
  36.5 0.6 %update.3 = f32[512,128]{1,0:T(8,128)S(1)} custom-call(s32[1]{0:T(128)} %bitcast.core_ref, f32[512,128]{1,0:T(8,128)S(1)} %get-tuple-element.7.current_ref, f32[512,128]{1,0:T(8,128)S(1)} %collective-permute-done.6.twin_ref, f32[512,128]{1,0:T(8,128)S(1)} %add_select_fusion.other_ref, f32[512,128]{1,0:T(8,128)S(1)} %correction.3.log_ref), custom_call_target="tpu_custom_call" | custom-call | tf_op jit(solution)/shard_map/update/pallas_call | solution.py:321
  37.3 1.3 %collective-permute-done.8 = f16[4,128,128]{2,1,0:T(8,128)(2,1)S(1)} collective-permute-done((f16[4,128,128]{2,1,0:T(8,128)(2,1)S(1)}, f16[4,128,128]{2,1,0:T(8,128)(2,1)S(1)}, u32[]{:S(2)}, u32[]{:S(2)}) %collective-permute-start.8) | collective-permute-done | bytes 131104 | tf_op jit(solution)/shard_map/ppermute | solution.py:427
  38.8 3.2 %collective-permute-start.10 = (f16[2,128,128]{2,1,0:T(8,128)(2,1)S(1)}, f16[2,128,128]{2,1,0:T(8,128)(2,1)S(1)}, u32[]{:S(2)}, u32[]{:S(2)}) collective-permute-start(f16[2,128,128]{2,1,0:T(8,128)(2,1)S(1)} %get-tuple-element.30), channel_id=1, source_target_pairs={{0,8},{1,10},{2,9},{3,11},{4,12},{5,14},{6,13},{7,15},{8,0},{9,2},... | collective-permute-start | bytes 196616 | tf_op jit(solution)/shard_map/ppermute | solution.py:356
  41.9 3.5 %collective-permute-start.12 = (f16[2,128,128]{2,1,0:T(8,128)(2,1)S(1)}, f16[2,128,128]{2,1,0:T(8,128)(2,1)S(1)}, u32[]{:S(2)}, u32[]{:S(2)}) collective-permute-start(f16[2,128,128]{2,1,0:T(8,128)(2,1)S(1)} %get-tuple-element.32), channel_id=1, source_target_pairs={{0,0},{1,2},{2,1},{3,3},{4,4},{5,6},{6,5},{7,7},{8,8},{9,10},{10,9... | collective-permute-start | bytes 196616 | tf_op jit(solution)/shard_map/ppermute | solution.py:356
  45.4 1.6 %collective-permute-start.9 = (f16[2,128,128]{2,1,0:T(8,128)(2,1)S(1)}, f16[2,128,128]{2,1,0:T(8,128)(2,1)S(1)}, u32[]{:S(2)}, u32[]{:S(2)}) collective-permute-start(f16[2,128,128]{2,1,0:T(8,128)(2,1)S(1)} %get-tuple-element.29), channel_id=1, source_target_pairs={{0,12},{1,14},{2,13},{3,15},{4,8},{5,10},{6,9},{7,11},{8,4},{9,6},... | collective-permute-start | bytes 196616 | tf_op jit(solution)/shard_map/ppermute | solution.py:356
  47.6 4.3 %collective-permute-done.9 = f16[2,128,128]{2,1,0:T(8,128)(2,1)S(1)} collective-permute-done((f16[2,128,128]{2,1,0:T(8,128)(2,1)S(1)}, f16[2,128,128]{2,1,0:T(8,128)(2,1)S(1)}, u32[]{:S(2)}, u32[]{:S(2)}) %collective-permute-start.9) | collective-permute-done | bytes 65568 | tf_op jit(solution)/shard_map/ppermute | solution.py:356
  52.0 0.9 %maximum_convert_fusion = f32[8,128,128]{2,1,0:T(8,128)} fusion(f16[2,128,128]{2,1,0:T(8,128)(2,1)S(1)} %get-tuple-element.26, f16[2,128,128]{2,1,0:T(8,128)(2,1)S(1)} %get-tuple-element.27, f16[2,128,128]{2,1,0:T(8,128)(2,1)S(1)} %get-tuple-element.28, f16[2,128,128]{2,1,0:T(8,128)(2,1)S(1)} %get-tuple-element.25), kind=kLoop, calls=%fused_computation.18 | loop fusion | flops 524288 | bytes 786432 | tf_op jit(solution)/shard_map/convert_element_type | solution.py:431
  (58 shorter events, 2.8 us)
Async XLA Ops:
  0.0 3.4 %copy-start = (f32[8,128,128]{2,1,0:T(8,128)S(1)}, f32[8,128,128]{2,1,0:T(8,128)}, u32[]{:S(2)}) copy-start(f32[8,128,128]{2,1,0:T(8,128)} %param.5) | copy-start | bytes 1572868
  2.7 0.7 %copy-start.1 = (s32[1,8]{1,0:T(1,128)S(1)}, s32[1,8]{1,0:T(1,128)}, u32[]{:S(2)}) copy-start(s32[1,8]{1,0:T(1,128)} %param.7) | copy-start | bytes 100
  3.6 9.4 %collective-permute-start.3 = (s16[400,128]{1,0:T(8,128)(2,1)S(1)}, s16[400,128]{1,0:T(8,128)(2,1)S(1)}, u32[]{:S(2)}, u32[]{:S(2)}) collective-permute-start(s16[400,128]{1,0:T(8,128)(2,1)S(1)} %get-tuple-element.16), channel_id=1, source_target_pairs={{0,0},{1,2},{2,1},{3,3},{4,4},{5,6},{6,5},{7,7},{8,8},{9,10},{10,9... | collective-permute-start | bytes 307208 | tf_op jit(solution)/shard_map/ppermute | solution.py:356
  8.1 5.4 %collective-permute-start.2 = (s16[400,128]{1,0:T(8,128)(2,1)S(1)}, s16[400,128]{1,0:T(8,128)(2,1)S(1)}, u32[]{:S(2)}, u32[]{:S(2)}) collective-permute-start(s16[400,128]{1,0:T(8,128)(2,1)S(1)} %get-tuple-element.15), channel_id=1, source_target_pairs={{0,4},{1,6},{2,5},{3,7},{4,0},{5,2},{6,1},{7,3},{8,12},{9,14},{10,... | collective-permute-start | bytes 307208 | tf_op jit(solution)/shard_map/ppermute | solution.py:356
  9.2 8.1 %collective-permute-start.1 = (s16[400,128]{1,0:T(8,128)(2,1)S(1)}, s16[400,128]{1,0:T(8,128)(2,1)S(1)}, u32[]{:S(2)}, u32[]{:S(2)}) collective-permute-start(s16[400,128]{1,0:T(8,128)(2,1)S(1)} %get-tuple-element.14), channel_id=1, source_target_pairs={{0,8},{1,10},{2,9},{3,11},{4,12},{5,14},{6,13},{7,15},{8,0},{9,2},... | collective-permute-start | bytes 307208 | tf_op jit(solution)/shard_map/ppermute | solution.py:356
  13.0 6.8 %collective-permute-start = (s16[400,128]{1,0:T(8,128)(2,1)S(1)}, s16[400,128]{1,0:T(8,128)(2,1)S(1)}, u32[]{:S(2)}, u32[]{:S(2)}) collective-permute-start(s16[400,128]{1,0:T(8,128)(2,1)S(1)} %get-tuple-element.13), channel_id=1, source_target_pairs={{0,12},{1,14},{2,13},{3,15},{4,8},{5,10},{6,9},{7,11},{8,4},{9,6},... | collective-permute-start | bytes 307208 | tf_op jit(solution)/shard_map/ppermute | solution.py:356
  20.1 6.4 %collective-permute-start.4 = (s16[1040,128]{1,0:T(8,128)(2,1)S(1)}, s16[1040,128]{1,0:T(8,128)(2,1)S(1)}, u32[]{:S(2)}, u32[]{:S(2)}) collective-permute-start(s16[1040,128]{1,0:T(8,128)(2,1)S(1)} %constant_dynamic-update-slice_fusion), channel_id=1, source_target_pairs={{0,1},{1,0},{2,3},{3,2},{4,5},{5,4},{6,7},{7,6},{8,9},{9,8},{10,11... | collective-permute-start | bytes 798728 | tf_op jit(solution)/shard_map/ppermute | solution.py:387
  20.2 6.3 %collective-permute-start.5 = (s16[512,128]{1,0:T(8,128)(2,1)S(1)}, s16[512,128]{1,0:T(8,128)(2,1)S(1)}, u32[]{:S(2)}, u32[]{:S(2)}) collective-permute-start(s16[512,128]{1,0:T(8,128)(2,1)S(1)} %pad_add_fusion.1), channel_id=1, source_target_pairs={{1,4},{4,1},{5,8},{8,5},{9,12},{12,9},{13,14},{14,13},{15,10},{10,... | collective-permute-start | bytes 393224 | tf_op jit(solution)/shard_map/ppermute | solution.py:414
  30.2 6.3 %collective-permute-start.7 = (f16[512,128]{1,0:T(8,128)(2,1)S(1)}, f16[512,128]{1,0:T(8,128)(2,1)S(1)}, u32[]{:S(2)}, u32[]{:S(2)}) collective-permute-start(f16[512,128]{1,0:T(8,128)(2,1)S(1)} %add_convert_fusion), channel_id=1, source_target_pairs={{1,4},{4,1},{5,8},{8,5},{9,12},{12,9},{13,14},{14,13},{15,10},{10,... | collective-permute-start | bytes 393224 | tf_op jit(solution)/shard_map/ppermute | solution.py:414
  32.4 4.1 %collective-permute-start.6 = (f32[512,128]{1,0:T(8,128)S(1)}, f32[512,128]{1,0:T(8,128)S(1)}, u32[]{:S(2)}, u32[]{:S(2)}) collective-permute-start(f32[512,128]{1,0:T(8,128)S(1)} %get-tuple-element.7.current_ref), channel_id=1, source_target_pairs={{0,1},{1,0},{2,3},{3,2},{4,5},{5,4},{6,7},{7,6},{8,9},{9,8},{10,11... | collective-permute-start | bytes 786440 | tf_op jit(solution)/shard_map/ppermute | solution.py:416
  37.2 1.4 %collective-permute-start.8 = (f16[4,128,128]{2,1,0:T(8,128)(2,1)S(1)}, f16[4,128,128]{2,1,0:T(8,128)(2,1)S(1)}, u32[]{:S(2)}, u32[]{:S(2)}) collective-permute-start(f16[4,128,128]{2,1,0:T(8,128)(2,1)S(1)} %bitcast.54), channel_id=1, source_target_pairs={{0,1},{1,0},{2,3},{3,2},{4,5},{5,4},{6,7},{7,6},{8,9},{9,8},{10,11... | collective-permute-start | bytes 393224 | tf_op jit(solution)/shard_map/ppermute | solution.py:427
  38.8 8.2 %collective-permute-start.10 = (f16[2,128,128]{2,1,0:T(8,128)(2,1)S(1)}, f16[2,128,128]{2,1,0:T(8,128)(2,1)S(1)}, u32[]{:S(2)}, u32[]{:S(2)}) collective-permute-start(f16[2,128,128]{2,1,0:T(8,128)(2,1)S(1)} %get-tuple-element.30), channel_id=1, source_target_pairs={{0,8},{1,10},{2,9},{3,11},{4,12},{5,14},{6,13},{7,15},{8,0},{9,2},... | collective-permute-start | bytes 196616 | tf_op jit(solution)/shard_map/ppermute | solution.py:356
  41.9 5.1 %collective-permute-start.11 = (f16[2,128,128]{2,1,0:T(8,128)(2,1)S(1)}, f16[2,128,128]{2,1,0:T(8,128)(2,1)S(1)}, u32[]{:S(2)}, u32[]{:S(2)}) collective-permute-start(f16[2,128,128]{2,1,0:T(8,128)(2,1)S(1)} %get-tuple-element.31), channel_id=1, source_target_pairs={{0,4},{1,6},{2,5},{3,7},{4,0},{5,2},{6,1},{7,3},{8,12},{9,14},{10,... | collective-permute-start | bytes 196616 | tf_op jit(solution)/shard_map/ppermute | solution.py:356
  41.9 5.6 %collective-permute-start.12 = (f16[2,128,128]{2,1,0:T(8,128)(2,1)S(1)}, f16[2,128,128]{2,1,0:T(8,128)(2,1)S(1)}, u32[]{:S(2)}, u32[]{:S(2)}) collective-permute-start(f16[2,128,128]{2,1,0:T(8,128)(2,1)S(1)} %get-tuple-element.32), channel_id=1, source_target_pairs={{0,0},{1,2},{2,1},{3,3},{4,4},{5,6},{6,5},{7,7},{8,8},{9,10},{10,9... | collective-permute-start | bytes 196616 | tf_op jit(solution)/shard_map/ppermute | solution.py:356
  45.4 6.5 %collective-permute-start.9 = (f16[2,128,128]{2,1,0:T(8,128)(2,1)S(1)}, f16[2,128,128]{2,1,0:T(8,128)(2,1)S(1)}, u32[]{:S(2)}, u32[]{:S(2)}) collective-permute-start(f16[2,128,128]{2,1,0:T(8,128)(2,1)S(1)} %get-tuple-element.29), channel_id=1, source_target_pairs={{0,12},{1,14},{2,13},{3,15},{4,8},{5,10},{6,9},{7,11},{8,4},{9,6},... | collective-permute-start | bytes 196616 | tf_op jit(solution)/shard_map/ppermute | solution.py:356

commit v3 on v2

--- a/solution.py
+++ b/solution.py
@@ -353,7 +353,7 @@
         pieces = []
         for k in range(tiles):
             pairs = [(device(t, v, g), device(t ^ k, g, v)) for t in range(tiles) for v in range(2) for g in range(2)]
-            pieces.append(lax.ppermute(pick(lax.bitwise_xor(tile, k)), square, pairs))
+            pieces.append(lax.ppermute(pick(k), square, pairs))
         return pieces
 
     def end_of(chain):
@@ -361,10 +361,6 @@
 
     me = tile.reshape(1).astype(jnp.int32)
     flag = core.reshape(1).astype(jnp.int32)
-    profiles = [psf_taps.reshape(-1), psf_taps[..., ::-1].reshape(-1)]
-    info = [lax.reduce_precision(p, 8, 7) * TAP_UNIT for p in profiles]
-    info = jnp.concatenate([*info, offsets.reshape(-1).astype(jnp.float32)])
-    info = jnp.pad(info, (0, columns - info.shape[0])).astype(jnp.int16)
 
     wide = estimate.reshape(tiles, 2, height, columns)
     wide = lax.dynamic_index_in_dim(wide, view, 1, keepdims=True)
@@ -372,28 +368,34 @@
     data = view_data.reshape(tiles, 2, height, columns).astype(jnp.float32)
     data = (data * DATA_UNIT).astype(jnp.int16)
     payload = jnp.concatenate([wide, data], axis=1).reshape(tiles, 3 * height, columns)
-    note = jnp.broadcast_to(info, (tiles, INFO_ROWS, columns))
-    payload = jnp.concatenate([payload, note], axis=1)
-
-    def for_tile(t):
-        return lax.dynamic_index_in_dim(payload, lax.bitwise_xor(t, end_of(core)), 0, keepdims=False)
+    payload, psf_taps, offsets = lax.optimization_barrier((payload, psf_taps, offsets))
+    profiles = [psf_taps.reshape(-1), psf_taps[..., ::-1].reshape(-1)]
+    info = [lax.reduce_precision(p, 8, 7) * TAP_UNIT for p in profiles]
+    info = jnp.concatenate([*info, offsets.reshape(-1).astype(jnp.float32)])
+    info = jnp.pad(info, (0, columns - info.shape[0])).astype(jnp.int16)
+    info = jnp.broadcast_to(info, (INFO_ROWS, columns))
+
+    def for_tile(k):
+        place = lax.bitwise_xor(lax.bitwise_xor(tile, k), end_of(core))
+        piece = lax.dynamic_index_in_dim(payload, place, 0, keepdims=False)
+        return piece if k else jnp.concatenate([piece, info])
 
     pieces = exchange(for_tile)
+    note = pieces[0][3 * height :]
+    notes = jnp.stack([note[0], lax.ppermute(note, "gz", swap)[0]]).astype(jnp.float32)
+    shifts = notes[:, 8 * taps : 8 * taps + blocks].astype(jnp.int32)
+    matrices = blur_matrices(taps, height, notes * (1.0 / TAP_UNIT))
+
     planes = [piece[:height] for piece in pieces]
     pairs = [piece[height : 3 * height].reshape(2, height, columns) for piece in pieces]
     keep = [lax.dynamic_index_in_dim(pair, core, 0, keepdims=False) for pair in pairs]
     give = [lax.dynamic_index_in_dim(pair, 1 - core, 0, keepdims=False) for pair in pairs]
-    note = pieces[0][3 * height :]
-    got = lax.ppermute(jnp.concatenate([*planes, *give, note]), "gz", swap)
+    got = lax.ppermute(jnp.concatenate([*planes, *give]), "gz", swap)
     length = tiles * height
     twin = got[:length].reshape(tiles, height, columns)
-    take = got[length : 2 * length].reshape(tiles, height, columns)
+    take = got[length:].reshape(tiles, height, columns)
     data = [x.astype(jnp.float32) * (1.0 / DATA_UNIT) for x in [*keep, *[take[k] for k in range(tiles)]]]
     data = [x.astype(jnp.bfloat16) for x in data]
-
-    info = jnp.stack([note[0], got[2 * length]]).astype(jnp.float32)
-    shifts = info[:, 8 * taps : 8 * taps + blocks].astype(jnp.int32)
-    matrices = blur_matrices(taps, height, info * (1.0 / TAP_UNIT))
 
     path = [(t, 0) for t in range(tiles)] + [(t, 1) for t in reversed(range(tiles))]
     hops = []
@@ -424,10 +426,20 @@
             plane = (current - 1.0).astype(jnp.float16)
 
     result = current.astype(jnp.float16).reshape(tiles, height, columns)
-    twin = lax.ppermute(result, "gz", swap)
-    both = jnp.stack([jnp.where(core == 0, result, twin), jnp.where(core == 0, twin, result)], axis=1)
-    pieces = exchange(lambda t: lax.dynamic_index_in_dim(both, t, 0, keepdims=False))
-    result = jnp.concatenate(ordered(pieces, lax.bitwise_xor(tile, end_of(core))))
+    pieces = []
+    for k in range(tiles):
+        piece = lax.dynamic_index_in_dim(result, lax.bitwise_xor(tile, k), 0)
+        pieces.append(lax.ppermute(piece, "tiles", [(t, t ^ k) for t in range(tiles)]) if k else piece)
+    mine = jnp.concatenate(pieces)
+    crossed = [lax.ppermute(pieces[0], "views", swap)]
+    crossed.append(lax.ppermute(mine[1:], "views", swap))
+    crossed = jnp.concatenate(crossed)
+    straight = view == core
+    same = jnp.where(straight, mine, crossed)
+    twin = lax.ppermute(jnp.where(straight, crossed, mine), "gz", swap)
+    even, odd = jnp.where(core == 0, same, twin), jnp.where(core == 0, twin, same)
+    result = [jnp.stack([even[k], odd[k]]) for k in range(tiles)]
+    result = jnp.concatenate(ordered(result, lax.bitwise_xor(tile, end_of(core))))
     return result.astype(jnp.float32)
 
 

time: 53.1 us -> 49.2 us (0.927)
  the two profiles are of different devices: /device:TPU:1 before, /device:TPU:0 now
where the time goes in v3:
time: 49.2 us; the launch traced here: 49 us
  starting transfers between devices  24.7 us (50%)
  waiting for transfers between devices  13.9 us (28%)
  Pallas kernels  5.56 us (11%)
  other arithmetic  3.2 us (7%)
  local copies, waits for them, and re-layouts  1.18 us (2%)
  between operations  0.5 us (1%)
    ppermute x1, starting transfers between devices, plane_shards(): twin = lax.ppermute(current, 'gz', swap)  7.62 us
    ppermute x4, waiting for transfers between devices, exchange(): pieces.append(lax.ppermute(pick(k), square, pairs))  6.47 us
    ppermute x4, starting transfers between devices, exchange(): pieces.append(lax.ppermute(pick(k), square, pairs))  6.38 us
    ppermute x3, starting transfers between devices, plane_shards(): lax.ppermute(piece, 'tiles', [(t, t ^ k) for t in range(tiles)])  4.88 us
    pallas_call x2, Pallas kernels, correction_logs(): pl.pallas_call(functools.partial(correction_kernel, tiles), out_shape=jax...  3.39 us
    ppermute x1, waiting for transfers between devices, plane_shards(): crossed.append(lax.ppermute(mine[1:], 'views', swap))  3.16 us
    ppermute x3, waiting for transfers between devices, plane_shards(): lax.ppermute(piece, 'tiles', [(t, t ^ k) for t in range(tiles)])  2.88 us
    ppermute x1, starting transfers between devices, plane_shards(): crossed.append(lax.ppermute(mine[1:], 'views', swap))  1.5 us
  transfers between devices with their start and end apart: 15, of which 4 were waited for; matrix products, arithmetic and copies ran while one was open for 1% of the time, Pallas kernels for 5%

profile of v3, /device:TPU:0, one launch (start us, length us, event | category | flops | bytes accessed | tf_op | source)
XLA Modules:
  0.0 49.0 jit_solution(2997322204313116001)
XLA Ops:
  0.0 1.1 %multiply_convert_fusion = s16[1,1,8,128,128]{4,3,2,1,0:T(8,128)(2,1)S(1)} fusion(bf16[1,1,8,128,128]{4,3,2,1,0:T(8,128)(2,1)} %param.4), kind=kLoop, calls=%fused_computation | loop fusion | flops 393216 | bytes 524288 | tf_op jit(solution)/shard_map/convert_element_type | solution.py:369
  1.3 3.1 %collective-permute-start.2 = (s16[384,128]{1,0:T(8,128)(2,1)S(1)}, s16[384,128]{1,0:T(8,128)(2,1)S(1)}, u32[]{:S(2)}, u32[]{:S(2)}) collective-permute-start(s16[384,128]{1,0:T(8,128)(2,1)S(1)} %get-tuple-element.23), channel_id=1, source_target_pairs={{0,4},{1,6},{2,5},{3,7},{4,0},{5,2},{6,1},{7,3},{8,12},{9,14},{10,... | collective-permute-start | bytes 294920 | tf_op jit(solution)/shard_map/ppermute | solution.py:356
  4.5 2.6 %collective-permute-start.1 = (s16[384,128]{1,0:T(8,128)(2,1)S(1)}, s16[384,128]{1,0:T(8,128)(2,1)S(1)}, u32[]{:S(2)}, u32[]{:S(2)}) collective-permute-start(s16[384,128]{1,0:T(8,128)(2,1)S(1)} %get-tuple-element.24), channel_id=1, source_target_pairs={{0,8},{1,10},{2,9},{3,11},{4,12},{5,14},{6,13},{7,15},{8,0},{9,2},... | collective-permute-start | bytes 294920 | tf_op jit(solution)/shard_map/ppermute | solution.py:356
  7.3 0.6 %copy-done.2 = s32[1,8]{1,0:T(1,128)S(1)} copy-done((s32[1,8]{1,0:T(1,128)S(1)}, s32[1,8]{1,0:T(1,128)}, u32[]{:S(2)}) %copy-start.2) | copy-done | bytes 56
  8.0 0.7 %collective-permute-start.3 = (s16[400,128]{1,0:T(8,128)(2,1)S(1)}, s16[400,128]{1,0:T(8,128)(2,1)S(1)}, u32[]{:S(2)}, u32[]{:S(2)}) collective-permute-start(s16[400,128]{1,0:T(8,128)(2,1)S(1)} %pad_add_fusion.2), channel_id=1, source_target_pairs={{0,0},{1,2},{2,1},{3,3},{4,4},{5,6},{6,5},{7,7},{8,8},{9,10},{10,9... | collective-permute-start | bytes 307208 | tf_op jit(solution)/shard_map/ppermute | solution.py:356
  8.8 6.5 %collective-permute-done.1 = s16[384,128]{1,0:T(8,128)(2,1)S(1)} collective-permute-done((s16[384,128]{1,0:T(8,128)(2,1)S(1)}, s16[384,128]{1,0:T(8,128)(2,1)S(1)}, u32[]{:S(2)}, u32[]{:S(2)}) %collective-permute-start.1) | collective-permute-done | bytes 98336 | tf_op jit(solution)/shard_map/ppermute | solution.py:356
  15.6 1.4 %collective-permute-start.6 = (s16[16,128]{1,0:T(8,128)(2,1)S(1)}, s16[16,128]{1,0:T(8,128)(2,1)S(1)}, u32[]{:S(2)}, u32[]{:S(2)}) collective-permute-start(s16[16,128]{1,0:T(8,128)(2,1)S(1)} %slice.146), channel_id=1, source_target_pairs={{0,1},{1,0},{2,3},{3,2},{4,5},{5,4},{6,7},{7,6},{8,9},{9,8},{10,11... | collective-permute-start | bytes 12296 | tf_op jit(solution)/shard_map/ppermute | solution.py:385
  17.1 0.7 %collective-permute-start.5 = (s16[512,128]{1,0:T(8,128)(2,1)S(1)}, s16[512,128]{1,0:T(8,128)(2,1)S(1)}, u32[]{:S(2)}, u32[]{:S(2)}) collective-permute-start(s16[512,128]{1,0:T(8,128)(2,1)S(1)} %pad_add_fusion.1), channel_id=1, source_target_pairs={{1,4},{4,1},{5,8},{8,5},{9,12},{12,9},{13,14},{14,13},{15,10},{10,... | collective-permute-start | bytes 393224 | tf_op jit(solution)/shard_map/ppermute | solution.py:416
  17.9 1.0 %blur_matrices.1.matrices_ref = bf16[2,4,256,128]{3,2,1,0:T(8,128)(2,1)S(1)} custom-call(f32[2,128]{1,0:T(2,128)S(1)} %broadcast_multiply_fusion.info_ref), custom_call_target="tpu_custom_call" | custom-call | tf_op jit(solution)/shard_map/blur_matrices/pallas_call | solution.py:192
  19.2 1.7 %correction.2.log_ref = f32[512,128]{1,0:T(8,128)S(1)} custom-call(s32[1]{0:T(128)} %bitcast.17.tile_ref, s32[2,8]{1,0:T(2,128)S(1)} %slice_convert_fusion.offsets_ref, bf16[4,128,128]{2,1,0:T(8,128)(2,1)S(1)} %bitcast.38, bf16[2,4,256,128]{3,2,1,0:T(8,128)(2,1)S(1)} %blur_matrices.1.matrices_ref, bf16[128,128]{1,0:T(8,128)(2,1)S(1)} %get-tuple-element.51.refs_0_, ...), custom_call_target="tpu_custom_call" | custom-call | flops 300000000 | bytes 1500000 | tf_op jit(solution)/shard_map/correction/pallas_call | solution.py:260
  20.9 0.6 %update.2 = (f32[512,128]{1,0:T(8,128)S(1)}, bf16[512,128]{1,0:T(8,128)(2,1)S(1)}) custom-call(s32[1]{0:T(128)} %bitcast.core_ref, f32[512,128]{1,0:T(8,128)S(1)} %get-tuple-element.50.current_ref, f32[512,128]{1,0:T(8,128)S(1)} %multiply_add_fusion.twin_ref, f32[512,128]{1,0:T(8,128)S(1)} %add_select_fusion.1.other_ref, f32[512,128]{1,0:T(8,128)S(1)} %correction.2.log_ref), custom_call_target="tpu_custom_call" | custom-call | tf_op jit(solution)/shard_map/update/pallas_call | solution.py:321
  21.6 0.7 %collective-permute-start.8 = (f16[512,128]{1,0:T(8,128)(2,1)S(1)}, f16[512,128]{1,0:T(8,128)(2,1)S(1)}, u32[]{:S(2)}, u32[]{:S(2)}) collective-permute-start(f16[512,128]{1,0:T(8,128)(2,1)S(1)} %add_convert_fusion), channel_id=1, source_target_pairs={{1,4},{4,1},{5,8},{8,5},{9,12},{12,9},{13,14},{14,13},{15,10},{10,... | collective-permute-start | bytes 393224 | tf_op jit(solution)/shard_map/ppermute | solution.py:416
  22.3 7.6 %collective-permute-start.7 = (f32[512,128]{1,0:T(8,128)S(1)}, f32[512,128]{1,0:T(8,128)S(1)}, u32[]{:S(2)}, u32[]{:S(2)}) collective-permute-start(f32[512,128]{1,0:T(8,128)S(1)} %get-tuple-element.13.current_ref), channel_id=1, source_target_pairs={{0,1},{1,0},{2,3},{3,2},{4,5},{5,4},{6,7},{7,6},{8,9},{9,8},{10,11... | collective-permute-start | bytes 786440 | tf_op jit(solution)/shard_map/ppermute | solution.py:418
  29.9 1.7 %correction.3.log_ref = f32[512,128]{1,0:T(8,128)S(1)} custom-call(s32[1]{0:T(128)} %bitcast.17.tile_ref, s32[2,8]{1,0:T(2,128)S(1)} %slice_convert_fusion.offsets_ref, bf16[4,128,128]{2,1,0:T(8,128)(2,1)S(1)} %bitcast.39, bf16[2,4,256,128]{3,2,1,0:T(8,128)(2,1)S(1)} %blur_matrices.1.matrices_ref, bf16[128,128]{1,0:T(8,128)(2,1)S(1)} %get-tuple-element.51.refs_0_, ...), custom_call_target="tpu_custom_call" | custom-call | flops 300000000 | bytes 1500000 | tf_op jit(solution)/shard_map/correction/pallas_call | solution.py:260
  31.6 0.6 %update.3 = f32[512,128]{1,0:T(8,128)S(1)} custom-call(s32[1]{0:T(128)} %bitcast.core_ref, f32[512,128]{1,0:T(8,128)S(1)} %get-tuple-element.13.current_ref, f32[512,128]{1,0:T(8,128)S(1)} %collective-permute-done.7.twin_ref, f32[512,128]{1,0:T(8,128)S(1)} %add_select_fusion.other_ref, f32[512,128]{1,0:T(8,128)S(1)} %correction.3.log_ref), custom_call_target="tpu_custom_call" | custom-call | tf_op jit(solution)/shard_map/update/pallas_call | solution.py:321
  32.3 3.5 %collective-permute-start.10 = (f16[1,128,128]{2,1,0:T(8,128)(2,1)S(1)}, f16[1,128,128]{2,1,0:T(8,128)(2,1)S(1)}, u32[]{:S(2)}, u32[]{:S(2)}) collective-permute-start(f16[1,128,128]{2,1,0:T(8,128)(2,1)S(1)} %get-tuple-element.47), channel_id=1, source_target_pairs={{0,8},{4,12},{8,0},{12,4},{1,9},{5,13},{9,1},{13,5},{2,10},{6,14},... | collective-permute-start | bytes 98312 | tf_op jit(solution)/shard_map/ppermute | solution.py:432
  35.8 1.4 %collective-permute-start.11 = (f16[1,128,128]{2,1,0:T(8,128)(2,1)S(1)}, f16[1,128,128]{2,1,0:T(8,128)(2,1)S(1)}, u32[]{:S(2)}, u32[]{:S(2)}) collective-permute-start(f16[1,128,128]{2,1,0:T(8,128)(2,1)S(1)} %get-tuple-element.46), channel_id=1, source_target_pairs={{0,12},{4,8},{8,4},{12,0},{1,13},{5,9},{9,5},{13,1},{2,14},{6,10},... | collective-permute-start | bytes 98312 | tf_op jit(solution)/shard_map/ppermute | solution.py:432
  37.2 1.5 %collective-permute-start.12 = (f16[1,128,128]{2,1,0:T(8,128)(2,1)S(1)}, f16[1,128,128]{2,1,0:T(8,128)(2,1)S(1)}, u32[]{:S(2)}, u32[]{:S(2)}) collective-permute-start(f16[1,128,128]{2,1,0:T(8,128)(2,1)S(1)} %get-tuple-element.48), channel_id=1, source_target_pairs={{0,2},{2,0},{1,3},{3,1},{4,6},{6,4},{5,7},{7,5},{8,10},{10,8},{9,1... | collective-permute-start | bytes 98312 | tf_op jit(solution)/shard_map/ppermute | solution.py:434
  38.7 2.9 %collective-permute-done.11 = f16[1,128,128]{2,1,0:T(8,128)(2,1)S(1)} collective-permute-done((f16[1,128,128]{2,1,0:T(8,128)(2,1)S(1)}, f16[1,128,128]{2,1,0:T(8,128)(2,1)S(1)}, u32[]{:S(2)}, u32[]{:S(2)}) %collective-permute-start.11) | collective-permute-done | bytes 32800 | tf_op jit(solution)/shard_map/ppermute | solution.py:432
  41.6 1.5 %collective-permute-start.13 = (f16[3,128,128]{2,1,0:T(8,128)(2,1)S(1)}, f16[3,128,128]{2,1,0:T(8,128)(2,1)S(1)}, u32[]{:S(2)}, u32[]{:S(2)}) collective-permute-start(f16[3,128,128]{2,1,0:T(8,128)(2,1)S(1)} %pad_maximum_fusion.1), channel_id=1, source_target_pairs={{0,2},{2,0},{1,3},{3,1},{4,6},{6,4},{5,7},{7,5},{8,10},{10,8},{9,1... | collective-permute-start | bytes 294920 | tf_op jit(solution)/shard_map/ppermute | solution.py:435
  43.1 3.2 %collective-permute-done.13 = f16[3,128,128]{2,1,0:T(8,128)(2,1)S(1)} collective-permute-done((f16[3,128,128]{2,1,0:T(8,128)(2,1)S(1)}, f16[3,128,128]{2,1,0:T(8,128)(2,1)S(1)}, u32[]{:S(2)}, u32[]{:S(2)}) %collective-permute-start.13) | collective-permute-done | bytes 98336 | tf_op jit(solution)/shard_map/ppermute | solution.py:435
  46.5 1.3 %collective-permute-done.14 = f16[4,128,128]{2,1,0:T(8,128)(2,1)S(1)} collective-permute-done((f16[4,128,128]{2,1,0:T(8,128)(2,1)S(1)}, f16[4,128,128]{2,1,0:T(8,128)(2,1)S(1)}, u32[]{:S(2)}, u32[]{:S(2)}) %collective-permute-start.14) | collective-permute-done | bytes 131104 | tf_op jit(solution)/shard_map/ppermute | solution.py:439
  47.8 0.1 broadcast_select_fusion.3
  48.2 0.9 %maximum_convert_fusion = f32[8,128,128]{2,1,0:T(8,128)} fusion(f16[2,128,128]{2,1,0:T(8,128)(2,1)S(1)} %get-tuple-element.28, f16[2,128,128]{2,1,0:T(8,128)(2,1)S(1)} %get-tuple-element.27, f16[2,128,128]{2,1,0:T(8,128)(2,1)S(1)} %get-tuple-element.26, f16[2,128,128]{2,1,0:T(8,128)(2,1)S(1)} %get-tuple-element.25), kind=kLoop, calls=%fused_computation.2 | loop fusion | flops 524288 | bytes 786432 | tf_op jit(solution)/shard_map/convert_element_type | solution.py:443
  (72 shorter events, 1.9 us)
Async XLA Ops:
  0.0 1.1 %copy-start = (f32[8,128,128]{2,1,0:T(8,128)S(1)}, f32[8,128,128]{2,1,0:T(8,128)}, u32[]{:S(2)}) copy-start(f32[8,128,128]{2,1,0:T(8,128)} %param.5) | copy-start | bytes 1572868
  1.3 5.7 %copy-start.1 = (f32[1,2,2,9]{3,2,1,0:T(2,128)S(1)}, f32[1,2,2,9]{3,2,1,0:T(2,128)}, u32[]{:S(2)}) copy-start(f32[1,2,2,9]{3,2,1,0:T(2,128)} %param.6) | copy-start | bytes 436
  1.3 7.4 %collective-permute-start.2 = (s16[384,128]{1,0:T(8,128)(2,1)S(1)}, s16[384,128]{1,0:T(8,128)(2,1)S(1)}, u32[]{:S(2)}, u32[]{:S(2)}) collective-permute-start(s16[384,128]{1,0:T(8,128)(2,1)S(1)} %get-tuple-element.23), channel_id=1, source_target_pairs={{0,4},{1,6},{2,5},{3,7},{4,0},{5,2},{6,1},{7,3},{8,12},{9,14},{10,... | collective-permute-start | bytes 294920 | tf_op jit(solution)/shard_map/ppermute | solution.py:356
  4.5 10.8 %collective-permute-start.1 = (s16[384,128]{1,0:T(8,128)(2,1)S(1)}, s16[384,128]{1,0:T(8,128)(2,1)S(1)}, u32[]{:S(2)}, u32[]{:S(2)}) collective-permute-start(s16[384,128]{1,0:T(8,128)(2,1)S(1)} %get-tuple-element.24), channel_id=1, source_target_pairs={{0,8},{1,10},{2,9},{3,11},{4,12},{5,14},{6,13},{7,15},{8,0},{9,2},... | collective-permute-start | bytes 294920 | tf_op jit(solution)/shard_map/ppermute | solution.py:356
  7.0 8.2 %collective-permute-start = (s16[384,128]{1,0:T(8,128)(2,1)S(1)}, s16[384,128]{1,0:T(8,128)(2,1)S(1)}, u32[]{:S(2)}, u32[]{:S(2)}) collective-permute-start(s16[384,128]{1,0:T(8,128)(2,1)S(1)} %get-tuple-element.21), channel_id=1, source_target_pairs={{0,12},{1,14},{2,13},{3,15},{4,8},{5,10},{6,9},{7,11},{8,4},{9,6},... | collective-permute-start | bytes 294920 | tf_op jit(solution)/shard_map/ppermute | solution.py:356
  7.3 0.7 %copy-start.2 = (s32[1,8]{1,0:T(1,128)S(1)}, s32[1,8]{1,0:T(1,128)}, u32[]{:S(2)}) copy-start(s32[1,8]{1,0:T(1,128)} %param.7) | copy-start | bytes 100
  8.0 7.3 %collective-permute-start.3 = (s16[400,128]{1,0:T(8,128)(2,1)S(1)}, s16[400,128]{1,0:T(8,128)(2,1)S(1)}, u32[]{:S(2)}, u32[]{:S(2)}) collective-permute-start(s16[400,128]{1,0:T(8,128)(2,1)S(1)} %pad_add_fusion.2), channel_id=1, source_target_pairs={{0,0},{1,2},{2,1},{3,3},{4,4},{5,6},{6,5},{7,7},{8,8},{9,10},{10,9... | collective-permute-start | bytes 307208 | tf_op jit(solution)/shard_map/ppermute | solution.py:356
  15.6 2.2 %collective-permute-start.6 = (s16[16,128]{1,0:T(8,128)(2,1)S(1)}, s16[16,128]{1,0:T(8,128)(2,1)S(1)}, u32[]{:S(2)}, u32[]{:S(2)}) collective-permute-start(s16[16,128]{1,0:T(8,128)(2,1)S(1)} %slice.146), channel_id=1, source_target_pairs={{0,1},{1,0},{2,3},{3,2},{4,5},{5,4},{6,7},{7,6},{8,9},{9,8},{10,11... | collective-permute-start | bytes 12296 | tf_op jit(solution)/shard_map/ppermute | solution.py:385
  17.0 2.0 %collective-permute-start.4 = (s16[1024,128]{1,0:T(8,128)(2,1)S(1)}, s16[1024,128]{1,0:T(8,128)(2,1)S(1)}, u32[]{:S(2)}, u32[]{:S(2)}) collective-permute-start(s16[1024,128]{1,0:T(8,128)(2,1)S(1)} %bitcast_dynamic-update-slice_fusion), channel_id=1, source_target_pairs={{0,1},{1,0},{2,3},{3,2},{4,5},{5,4},{6,7},{7,6},{8,9},{9,8},{10,11... | collective-permute-start | bytes 786440 | tf_op jit(solution)/shard_map/ppermute | solution.py:393
  17.1 1.8 %collective-permute-start.5 = (s16[512,128]{1,0:T(8,128)(2,1)S(1)}, s16[512,128]{1,0:T(8,128)(2,1)S(1)}, u32[]{:S(2)}, u32[]{:S(2)}) collective-permute-start(s16[512,128]{1,0:T(8,128)(2,1)S(1)} %pad_add_fusion.1), channel_id=1, source_target_pairs={{1,4},{4,1},{5,8},{8,5},{9,12},{12,9},{13,14},{14,13},{15,10},{10,... | collective-permute-start | bytes 393224 | tf_op jit(solution)/shard_map/ppermute | solution.py:416
  21.6 10.0 %collective-permute-start.8 = (f16[512,128]{1,0:T(8,128)(2,1)S(1)}, f16[512,128]{1,0:T(8,128)(2,1)S(1)}, u32[]{:S(2)}, u32[]{:S(2)}) collective-permute-start(f16[512,128]{1,0:T(8,128)(2,1)S(1)} %add_convert_fusion), channel_id=1, source_target_pairs={{1,4},{4,1},{5,8},{8,5},{9,12},{12,9},{13,14},{14,13},{15,10},{10,... | collective-permute-start | bytes 393224 | tf_op jit(solution)/shard_map/ppermute | solution.py:416
  22.3 9.4 %collective-permute-start.7 = (f32[512,128]{1,0:T(8,128)S(1)}, f32[512,128]{1,0:T(8,128)S(1)}, u32[]{:S(2)}, u32[]{:S(2)}) collective-permute-start(f32[512,128]{1,0:T(8,128)S(1)} %get-tuple-element.13.current_ref), channel_id=1, source_target_pairs={{0,1},{1,0},{2,3},{3,2},{4,5},{5,4},{6,7},{7,6},{8,9},{9,8},{10,11... | collective-permute-start | bytes 786440 | tf_op jit(solution)/shard_map/ppermute | solution.py:418
  32.3 6.4 %collective-permute-start.10 = (f16[1,128,128]{2,1,0:T(8,128)(2,1)S(1)}, f16[1,128,128]{2,1,0:T(8,128)(2,1)S(1)}, u32[]{:S(2)}, u32[]{:S(2)}) collective-permute-start(f16[1,128,128]{2,1,0:T(8,128)(2,1)S(1)} %get-tuple-element.47), channel_id=1, source_target_pairs={{0,8},{4,12},{8,0},{12,4},{1,9},{5,13},{9,1},{13,5},{2,10},{6,14},... | collective-permute-start | bytes 98312 | tf_op jit(solution)/shard_map/ppermute | solution.py:432
  35.8 5.7 %collective-permute-start.11 = (f16[1,128,128]{2,1,0:T(8,128)(2,1)S(1)}, f16[1,128,128]{2,1,0:T(8,128)(2,1)S(1)}, u32[]{:S(2)}, u32[]{:S(2)}) collective-permute-start(f16[1,128,128]{2,1,0:T(8,128)(2,1)S(1)} %get-tuple-element.46), channel_id=1, source_target_pairs={{0,12},{4,8},{8,4},{12,0},{1,13},{5,9},{9,5},{13,1},{2,14},{6,10},... | collective-permute-start | bytes 98312 | tf_op jit(solution)/shard_map/ppermute | solution.py:432
  37.2 4.4 %collective-permute-start.9 = (f16[1,128,128]{2,1,0:T(8,128)(2,1)S(1)}, f16[1,128,128]{2,1,0:T(8,128)(2,1)S(1)}, u32[]{:S(2)}, u32[]{:S(2)}) collective-permute-start(f16[1,128,128]{2,1,0:T(8,128)(2,1)S(1)} %get-tuple-element.45), channel_id=1, source_target_pairs={{0,4},{4,0},{8,12},{12,8},{1,5},{5,1},{9,13},{13,9},{2,6},{6,2},{1... | collective-permute-start | bytes 98312 | tf_op jit(solution)/shard_map/ppermute | solution.py:432
  37.2 5.9 %collective-permute-start.12 = (f16[1,128,128]{2,1,0:T(8,128)(2,1)S(1)}, f16[1,128,128]{2,1,0:T(8,128)(2,1)S(1)}, u32[]{:S(2)}, u32[]{:S(2)}) collective-permute-start(f16[1,128,128]{2,1,0:T(8,128)(2,1)S(1)} %get-tuple-element.48), channel_id=1, source_target_pairs={{0,2},{2,0},{1,3},{3,1},{4,6},{6,4},{5,7},{7,5},{8,10},{10,8},{9,1... | collective-permute-start | bytes 98312 | tf_op jit(solution)/shard_map/ppermute | solution.py:434
  41.6 4.7 %collective-permute-start.13 = (f16[3,128,128]{2,1,0:T(8,128)(2,1)S(1)}, f16[3,128,128]{2,1,0:T(8,128)(2,1)S(1)}, u32[]{:S(2)}, u32[]{:S(2)}) collective-permute-start(f16[3,128,128]{2,1,0:T(8,128)(2,1)S(1)} %pad_maximum_fusion.1), channel_id=1, source_target_pairs={{0,2},{2,0},{1,3},{3,1},{4,6},{6,4},{5,7},{7,5},{8,10},{10,8},{9,1... | collective-permute-start | bytes 294920 | tf_op jit(solution)/shard_map/ppermute | solution.py:435
  46.4 1.4 %collective-permute-start.14 = (f16[4,128,128]{2,1,0:T(8,128)(2,1)S(1)}, f16[4,128,128]{2,1,0:T(8,128)(2,1)S(1)}, u32[]{:S(2)}, u32[]{:S(2)}) collective-permute-start(f16[4,128,128]{2,1,0:T(8,128)(2,1)S(1)} %broadcast_select_fusion), channel_id=1, source_target_pairs={{0,1},{1,0},{2,3},{3,2},{4,5},{5,4},{6,7},{7,6},{8,9},{9,8},{10,11... | collective-permute-start | bytes 393224 | tf_op jit(solution)/shard_map/ppermute | solution.py:439

commit v4 on v3

--- a/solution.py
+++ b/solution.py
@@ -369,20 +369,22 @@
     data = (data * DATA_UNIT).astype(jnp.int16)
     payload = jnp.concatenate([wide, data], axis=1).reshape(tiles, 3 * height, columns)
     payload, psf_taps, offsets = lax.optimization_barrier((payload, psf_taps, offsets))
+
+    def for_tile(k):
+        place = lax.bitwise_xor(lax.bitwise_xor(tile, k), end_of(core))
+        return lax.dynamic_index_in_dim(payload, place, 0, keepdims=False)
+
+    pieces = exchange(for_tile)
+
     profiles = [psf_taps.reshape(-1), psf_taps[..., ::-1].reshape(-1)]
     info = [lax.reduce_precision(p, 8, 7) * TAP_UNIT for p in profiles]
     info = jnp.concatenate([*info, offsets.reshape(-1).astype(jnp.float32)])
     info = jnp.pad(info, (0, columns - info.shape[0])).astype(jnp.int16)
     info = jnp.broadcast_to(info, (INFO_ROWS, columns))
-
-    def for_tile(k):
-        place = lax.bitwise_xor(lax.bitwise_xor(tile, k), end_of(core))
-        piece = lax.dynamic_index_in_dim(payload, place, 0, keepdims=False)
-        return piece if k else jnp.concatenate([piece, info])
-
-    pieces = exchange(for_tile)
-    note = pieces[0][3 * height :]
-    notes = jnp.stack([note[0], lax.ppermute(note, "gz", swap)[0]]).astype(jnp.float32)
+    note = lax.ppermute(info, "views", swap)
+    straight = view == core
+    notes = jnp.stack([jnp.where(straight, info[0], note[0]), jnp.where(straight, note[0], info[0])])
+    notes = notes.astype(jnp.float32)
     shifts = notes[:, 8 * taps : 8 * taps + blocks].astype(jnp.int32)
     matrices = blur_matrices(taps, height, notes * (1.0 / TAP_UNIT))
 
@@ -434,7 +436,6 @@
     crossed = [lax.ppermute(pieces[0], "views", swap)]
     crossed.append(lax.ppermute(mine[1:], "views", swap))
     crossed = jnp.concatenate(crossed)
-    straight = view == core
     same = jnp.where(straight, mine, crossed)
     twin = lax.ppermute(jnp.where(straight, crossed, mine), "gz", swap)
     even, odd = jnp.where(core == 0, same, twin), jnp.where(core == 0, twin, same)

time: 49.2 us -> 52 us (1.057)
  starting transfers between devices: 24.7 us -> 29.2 us
  waiting for transfers between devices: 13.9 us -> 11.6 us
  local copies, waits for them, and re-layouts: 1.18 us -> 1.8 us
    ppermute x1, starting transfers between devices: 0.09 us -> 2.63 us  [plane_shards(): got = lax.ppermute(jnp.concatenate([*planes, *give]), 'gz', swap)]
    ppermute x1, starting transfers between devices: 1.36 us -> 3.03 us  [plane_shards(): note = lax.ppermute(info, 'views', swap)]
    ppermute x4, starting transfers between devices: 6.38 us -> 5.12 us  [exchange(): pieces.append(lax.ppermute(pick(k), square, pairs))]
    ppermute x4, waiting for transfers between devices: 6.47 us -> 5.34 us  [exchange(): pieces.append(lax.ppermute(pick(k), square, pairs))]
    ppermute x1, starting transfers between devices: 1.5 us -> 2.45 us  [plane_shards(): crossed.append(lax.ppermute(mine[1:], 'views', swap))]
    ppermute x3, waiting for transfers between devices: 2.88 us -> 2.03 us  [plane_shards(): lax.ppermute(piece, 'tiles', [(t, t ^ k) for t in range(tiles)])]
    ppermute x1, starting transfers between devices: 1.47 us -> 2.23 us  [plane_shards(): crossed = [lax.ppermute(pieces[0], 'views', swap)]]
    unnamed x14, local copies, waits for them, and re-layouts: 0.68 us -> 1.32 us
  transfers between devices with their start and end apart: 15 -> 15, of which waited for: 4 -> 7; matrix products, arithmetic and copies ran while one was open for 1% -> 1% of each run, Pallas kernels for 5% -> 5%
where the time goes in v4:
time: 52 us; the launch traced here: 51.8 us
  starting transfers between devices  29.2 us (56%)
  waiting for transfers between devices  11.6 us (22%)
  Pallas kernels  5.57 us (11%)
  other arithmetic  3.19 us (6%)
  local copies, waits for them, and re-layouts  1.8 us (3%)
    ppermute x1, starting transfers between devices, plane_shards(): twin = lax.ppermute(current, 'gz', swap)  7.49 us
    ppermute x4, waiting for transfers between devices, exchange(): pieces.append(lax.ppermute(pick(k), square, pairs))  5.34 us
    ppermute x4, starting transfers between devices, exchange(): pieces.append(lax.ppermute(pick(k), square, pairs))  5.12 us
    ppermute x3, starting transfers between devices, plane_shards(): lax.ppermute(piece, 'tiles', [(t, t ^ k) for t in range(tiles)])  4.87 us
    pallas_call x2, Pallas kernels, correction_logs(): pl.pallas_call(functools.partial(correction_kernel, tiles), out_shape=jax...  3.39 us
    ppermute x1, starting transfers between devices, plane_shards(): note = lax.ppermute(info, 'views', swap)  3.03 us
    ppermute x1, starting transfers between devices, plane_shards(): got = lax.ppermute(jnp.concatenate([*planes, *give]), 'gz', swap)  2.63 us
    ppermute x1, waiting for transfers between devices, plane_shards(): crossed.append(lax.ppermute(mine[1:], 'views', swap))  2.58 us
  transfers between devices with their start and end apart: 15, of which 7 were waited for; matrix products, arithmetic and copies ran while one was open for 1% of the time, Pallas kernels for 5%

profile of v4, /device:TPU:0, one launch (start us, length us, event | category | flops | bytes accessed | tf_op | source)
XLA Modules:
  0.0 51.8 jit_solution(879176016891278381)
XLA Ops:
  0.0 1.1 %multiply_convert_fusion = s16[1,1,8,128,128]{4,3,2,1,0:T(8,128)(2,1)S(1)} fusion(bf16[1,1,8,128,128]{4,3,2,1,0:T(8,128)(2,1)} %param.4), kind=kLoop, calls=%fused_computation | loop fusion | flops 393216 | bytes 524288 | tf_op jit(solution)/shard_map/convert_element_type | solution.py:369
  1.3 0.6 %copy-done.1 = f32[1,2,2,9]{3,2,1,0:T(2,128)S(1)} copy-done((f32[1,2,2,9]{3,2,1,0:T(2,128)S(1)}, f32[1,2,2,9]{3,2,1,0:T(2,128)}, u32[]{:S(2)}) %copy-start.1) | copy-done | bytes 168
  2.9 3.0 %collective-permute-start.6 = (s16[16,128]{1,0:T(8,128)(2,1)S(1)}, s16[16,128]{1,0:T(8,128)(2,1)S(1)}, u32[]{:S(2)}, u32[]{:S(2)}) collective-permute-start(s16[16,128]{1,0:T(8,128)(2,1)S(1)} %broadcast_in_dim.9), channel_id=1, source_target_pairs={{0,2},{2,0},{1,3},{3,1},{4,6},{6,4},{5,7},{7,5},{8,10},{10,8},{9,1... | collective-permute-start | bytes 12296 | tf_op jit(solution)/shard_map/ppermute | solution.py:384
  5.9 0.7 %collective-permute-start.3 = (s16[384,128]{1,0:T(8,128)(2,1)S(1)}, s16[384,128]{1,0:T(8,128)(2,1)S(1)}, u32[]{:S(2)}, u32[]{:S(2)}) collective-permute-start(s16[384,128]{1,0:T(8,128)(2,1)S(1)} %get-tuple-element.22), channel_id=1, source_target_pairs={{0,0},{1,2},{2,1},{3,3},{4,4},{5,6},{6,5},{7,7},{8,8},{9,10},{10,9... | collective-permute-start | bytes 294920 | tf_op jit(solution)/shard_map/ppermute | solution.py:356
  6.6 1.6 %collective-permute-start.2 = (s16[384,128]{1,0:T(8,128)(2,1)S(1)}, s16[384,128]{1,0:T(8,128)(2,1)S(1)}, u32[]{:S(2)}, u32[]{:S(2)}) collective-permute-start(s16[384,128]{1,0:T(8,128)(2,1)S(1)} %get-tuple-element.23), channel_id=1, source_target_pairs={{0,4},{1,6},{2,5},{3,7},{4,0},{5,2},{6,1},{7,3},{8,12},{9,14},{10,... | collective-permute-start | bytes 294920 | tf_op jit(solution)/shard_map/ppermute | solution.py:356
  8.2 2.6 %collective-permute-start.1 = (s16[384,128]{1,0:T(8,128)(2,1)S(1)}, s16[384,128]{1,0:T(8,128)(2,1)S(1)}, u32[]{:S(2)}, u32[]{:S(2)}) collective-permute-start(s16[384,128]{1,0:T(8,128)(2,1)S(1)} %get-tuple-element.24), channel_id=1, source_target_pairs={{0,8},{1,10},{2,9},{3,11},{4,12},{5,14},{6,13},{7,15},{8,0},{9,2},... | collective-permute-start | bytes 294920 | tf_op jit(solution)/shard_map/ppermute | solution.py:356
  11.2 1.0 %blur_matrices.1.matrices_ref = bf16[2,4,256,128]{3,2,1,0:T(8,128)(2,1)S(1)} custom-call(f32[2,128]{1,0:T(2,128)S(1)} %broadcast_multiply_fusion.info_ref), custom_call_target="tpu_custom_call" | custom-call | tf_op jit(solution)/shard_map/blur_matrices/pallas_call | solution.py:192
  12.2 2.2 %collective-permute-done.1 = s16[384,128]{1,0:T(8,128)(2,1)S(1)} collective-permute-done((s16[384,128]{1,0:T(8,128)(2,1)S(1)}, s16[384,128]{1,0:T(8,128)(2,1)S(1)}, u32[]{:S(2)}, u32[]{:S(2)}) %collective-permute-start.1) | collective-permute-done | bytes 98336 | tf_op jit(solution)/shard_map/ppermute | solution.py:356
  14.4 3.1 %collective-permute-done = s16[384,128]{1,0:T(8,128)(2,1)S(1)} collective-permute-done((s16[384,128]{1,0:T(8,128)(2,1)S(1)}, s16[384,128]{1,0:T(8,128)(2,1)S(1)}, u32[]{:S(2)}, u32[]{:S(2)}) %collective-permute-start) | collective-permute-done | bytes 98336 | tf_op jit(solution)/shard_map/ppermute | solution.py:356
  17.9 2.6 %collective-permute-start.4 = (s16[1024,128]{1,0:T(8,128)(2,1)S(1)}, s16[1024,128]{1,0:T(8,128)(2,1)S(1)}, u32[]{:S(2)}, u32[]{:S(2)}) collective-permute-start(s16[1024,128]{1,0:T(8,128)(2,1)S(1)} %bitcast_dynamic-update-slice_fusion), channel_id=1, source_target_pairs={{0,1},{1,0},{2,3},{3,2},{4,5},{5,4},{6,7},{7,6},{8,9},{9,8},{10,11... | collective-permute-start | bytes 786440 | tf_op jit(solution)/shard_map/ppermute | solution.py:395
  20.5 0.7 %collective-permute-start.5 = (s16[512,128]{1,0:T(8,128)(2,1)S(1)}, s16[512,128]{1,0:T(8,128)(2,1)S(1)}, u32[]{:S(2)}, u32[]{:S(2)}) collective-permute-start(s16[512,128]{1,0:T(8,128)(2,1)S(1)} %pad_add_fusion.1), channel_id=1, source_target_pairs={{1,4},{4,1},{5,8},{8,5},{9,12},{12,9},{13,14},{14,13},{15,10},{10,... | collective-permute-start | bytes 393224 | tf_op jit(solution)/shard_map/ppermute | solution.py:418
  21.8 1.7 %correction.2.log_ref = f32[512,128]{1,0:T(8,128)S(1)} custom-call(s32[1]{0:T(128)} %bitcast.16.tile_ref, s32[2,8]{1,0:T(2,128)S(1)} %slice_convert_fusion.offsets_ref, bf16[4,128,128]{2,1,0:T(8,128)(2,1)S(1)} %bitcast.48, bf16[2,4,256,128]{3,2,1,0:T(8,128)(2,1)S(1)} %blur_matrices.1.matrices_ref, bf16[128,128]{1,0:T(8,128)(2,1)S(1)} %get-tuple-element.53.refs_0_, ...), custom_call_target="tpu_custom_call" | custom-call | flops 300000000 | bytes 1500000 | tf_op jit(solution)/shard_map/correction/pallas_call | solution.py:260
  23.5 0.6 %update.2 = (f32[512,128]{1,0:T(8,128)S(1)}, bf16[512,128]{1,0:T(8,128)(2,1)S(1)}) custom-call(s32[1]{0:T(128)} %bitcast.core_ref, f32[512,128]{1,0:T(8,128)S(1)} %get-tuple-element.50.current_ref, f32[512,128]{1,0:T(8,128)S(1)} %multiply_add_fusion.twin_ref, f32[512,128]{1,0:T(8,128)S(1)} %add_select_fusion.1.other_ref, f32[512,128]{1,0:T(8,128)S(1)} %correction.2.log_ref), custom_call_target="tpu_custom_call" | custom-call | tf_op jit(solution)/shard_map/update/pallas_call | solution.py:321
  24.2 0.7 %collective-permute-start.8 = (f16[512,128]{1,0:T(8,128)(2,1)S(1)}, f16[512,128]{1,0:T(8,128)(2,1)S(1)}, u32[]{:S(2)}, u32[]{:S(2)}) collective-permute-start(f16[512,128]{1,0:T(8,128)(2,1)S(1)} %add_convert_fusion), channel_id=1, source_target_pairs={{1,4},{4,1},{5,8},{8,5},{9,12},{12,9},{13,14},{14,13},{15,10},{10,... | collective-permute-start | bytes 393224 | tf_op jit(solution)/shard_map/ppermute | solution.py:418
  24.9 7.5 %collective-permute-start.7 = (f32[512,128]{1,0:T(8,128)S(1)}, f32[512,128]{1,0:T(8,128)S(1)}, u32[]{:S(2)}, u32[]{:S(2)}) collective-permute-start(f32[512,128]{1,0:T(8,128)S(1)} %get-tuple-element.13.current_ref), channel_id=1, source_target_pairs={{0,1},{1,0},{2,3},{3,2},{4,5},{5,4},{6,7},{7,6},{8,9},{9,8},{10,11... | collective-permute-start | bytes 786440 | tf_op jit(solution)/shard_map/ppermute | solution.py:420
  32.4 1.7 %correction.3.log_ref = f32[512,128]{1,0:T(8,128)S(1)} custom-call(s32[1]{0:T(128)} %bitcast.16.tile_ref, s32[2,8]{1,0:T(2,128)S(1)} %slice_convert_fusion.offsets_ref, bf16[4,128,128]{2,1,0:T(8,128)(2,1)S(1)} %bitcast.49, bf16[2,4,256,128]{3,2,1,0:T(8,128)(2,1)S(1)} %blur_matrices.1.matrices_ref, bf16[128,128]{1,0:T(8,128)(2,1)S(1)} %get-tuple-element.53.refs_0_, ...), custom_call_target="tpu_custom_call" | custom-call | flops 300000000 | bytes 1500000 | tf_op jit(solution)/shard_map/correction/pallas_call | solution.py:260
  34.8 3.3 %collective-permute-start.10 = (f16[1,128,128]{2,1,0:T(8,128)(2,1)S(1)}, f16[1,128,128]{2,1,0:T(8,128)(2,1)S(1)}, u32[]{:S(2)}, u32[]{:S(2)}) collective-permute-start(f16[1,128,128]{2,1,0:T(8,128)(2,1)S(1)} %get-tuple-element.47), channel_id=1, source_target_pairs={{0,8},{4,12},{8,0},{12,4},{1,9},{5,13},{9,1},{13,5},{2,10},{6,14},... | collective-permute-start | bytes 98312 | tf_op jit(solution)/shard_map/ppermute | solution.py:434
  38.1 1.6 %collective-permute-start.11 = (f16[1,128,128]{2,1,0:T(8,128)(2,1)S(1)}, f16[1,128,128]{2,1,0:T(8,128)(2,1)S(1)}, u32[]{:S(2)}, u32[]{:S(2)}) collective-permute-start(f16[1,128,128]{2,1,0:T(8,128)(2,1)S(1)} %get-tuple-element.46), channel_id=1, source_target_pairs={{0,12},{4,8},{8,4},{12,0},{1,13},{5,9},{9,5},{13,1},{2,14},{6,10},... | collective-permute-start | bytes 98312 | tf_op jit(solution)/shard_map/ppermute | solution.py:434
  39.7 2.2 %collective-permute-start.12 = (f16[1,128,128]{2,1,0:T(8,128)(2,1)S(1)}, f16[1,128,128]{2,1,0:T(8,128)(2,1)S(1)}, u32[]{:S(2)}, u32[]{:S(2)}) collective-permute-start(f16[1,128,128]{2,1,0:T(8,128)(2,1)S(1)} %get-tuple-element.48), channel_id=1, source_target_pairs={{0,2},{2,0},{1,3},{3,1},{4,6},{6,4},{5,7},{7,5},{8,10},{10,8},{9,1... | collective-permute-start | bytes 98312 | tf_op jit(solution)/shard_map/ppermute | solution.py:436
  41.9 2.0 %collective-permute-done.11 = f16[1,128,128]{2,1,0:T(8,128)(2,1)S(1)} collective-permute-done((f16[1,128,128]{2,1,0:T(8,128)(2,1)S(1)}, f16[1,128,128]{2,1,0:T(8,128)(2,1)S(1)}, u32[]{:S(2)}, u32[]{:S(2)}) %collective-permute-start.11) | collective-permute-done | bytes 32800 | tf_op jit(solution)/shard_map/ppermute | solution.py:434
  44.0 2.5 %collective-permute-start.13 = (f16[3,128,128]{2,1,0:T(8,128)(2,1)S(1)}, f16[3,128,128]{2,1,0:T(8,128)(2,1)S(1)}, u32[]{:S(2)}, u32[]{:S(2)}) collective-permute-start(f16[3,128,128]{2,1,0:T(8,128)(2,1)S(1)} %pad_maximum_fusion.1), channel_id=1, source_target_pairs={{0,2},{2,0},{1,3},{3,1},{4,6},{6,4},{5,7},{7,5},{8,10},{10,8},{9,1... | collective-permute-start | bytes 294920 | tf_op jit(solution)/shard_map/ppermute | solution.py:437
  46.5 2.6 %collective-permute-done.13 = f16[3,128,128]{2,1,0:T(8,128)(2,1)S(1)} collective-permute-done((f16[3,128,128]{2,1,0:T(8,128)(2,1)S(1)}, f16[3,128,128]{2,1,0:T(8,128)(2,1)S(1)}, u32[]{:S(2)}, u32[]{:S(2)}) %collective-permute-start.13) | collective-permute-done | bytes 98336 | tf_op jit(solution)/shard_map/ppermute | solution.py:437
  49.2 1.3 %collective-permute-done.14 = f16[4,128,128]{2,1,0:T(8,128)(2,1)S(1)} collective-permute-done((f16[4,128,128]{2,1,0:T(8,128)(2,1)S(1)}, f16[4,128,128]{2,1,0:T(8,128)(2,1)S(1)}, u32[]{:S(2)}, u32[]{:S(2)}) %collective-permute-start.14) | collective-permute-done | bytes 131104 | tf_op jit(solution)/shard_map/ppermute | solution.py:440
  50.9 0.9 %maximum_convert_fusion = f32[8,128,128]{2,1,0:T(8,128)} fusion(f16[2,128,128]{2,1,0:T(8,128)(2,1)S(1)} %get-tuple-element.28, f16[2,128,128]{2,1,0:T(8,128)(2,1)S(1)} %get-tuple-element.27, f16[2,128,128]{2,1,0:T(8,128)(2,1)S(1)} %get-tuple-element.26, f16[2,128,128]{2,1,0:T(8,128)(2,1)S(1)} %get-tuple-element.25), kind=kLoop, calls=%fused_computation.2 | loop fusion | flops 524288 | bytes 786432 | tf_op jit(solution)/shard_map/convert_element_type | solution.py:444
  (69 shorter events, 3.6 us)
Async XLA Ops:
  0.0 1.1 %copy-start = (f32[8,128,128]{2,1,0:T(8,128)S(1)}, f32[8,128,128]{2,1,0:T(8,128)}, u32[]{:S(2)}) copy-start(f32[8,128,128]{2,1,0:T(8,128)} %param.5) | copy-start | bytes 1572868
  1.2 0.7 %copy-start.1 = (f32[1,2,2,9]{3,2,1,0:T(2,128)S(1)}, f32[1,2,2,9]{3,2,1,0:T(2,128)}, u32[]{:S(2)}) copy-start(f32[1,2,2,9]{3,2,1,0:T(2,128)} %param.6) | copy-start | bytes 436
  2.1 0.7 %copy-start.2 = (s32[1,8]{1,0:T(1,128)S(1)}, s32[1,8]{1,0:T(1,128)}, u32[]{:S(2)}) copy-start(s32[1,8]{1,0:T(1,128)} %param.7) | copy-start | bytes 100
  2.9 8.2 %collective-permute-start.6 = (s16[16,128]{1,0:T(8,128)(2,1)S(1)}, s16[16,128]{1,0:T(8,128)(2,1)S(1)}, u32[]{:S(2)}, u32[]{:S(2)}) collective-permute-start(s16[16,128]{1,0:T(8,128)(2,1)S(1)} %broadcast_in_dim.9), channel_id=1, source_target_pairs={{0,2},{2,0},{1,3},{3,1},{4,6},{6,4},{5,7},{7,5},{8,10},{10,8},{9,1... | collective-permute-start | bytes 12296 | tf_op jit(solution)/shard_map/ppermute | solution.py:384
  5.9 6.2 %collective-permute-start.3 = (s16[384,128]{1,0:T(8,128)(2,1)S(1)}, s16[384,128]{1,0:T(8,128)(2,1)S(1)}, u32[]{:S(2)}, u32[]{:S(2)}) collective-permute-start(s16[384,128]{1,0:T(8,128)(2,1)S(1)} %get-tuple-element.22), channel_id=1, source_target_pairs={{0,0},{1,2},{2,1},{3,3},{4,4},{5,6},{6,5},{7,7},{8,8},{9,10},{10,9... | collective-permute-start | bytes 294920 | tf_op jit(solution)/shard_map/ppermute | solution.py:356
  6.6 5.6 %collective-permute-start.2 = (s16[384,128]{1,0:T(8,128)(2,1)S(1)}, s16[384,128]{1,0:T(8,128)(2,1)S(1)}, u32[]{:S(2)}, u32[]{:S(2)}) collective-permute-start(s16[384,128]{1,0:T(8,128)(2,1)S(1)} %get-tuple-element.23), channel_id=1, source_target_pairs={{0,4},{1,6},{2,5},{3,7},{4,0},{5,2},{6,1},{7,3},{8,12},{9,14},{10,... | collective-permute-start | bytes 294920 | tf_op jit(solution)/shard_map/ppermute | solution.py:356
  8.2 6.2 %collective-permute-start.1 = (s16[384,128]{1,0:T(8,128)(2,1)S(1)}, s16[384,128]{1,0:T(8,128)(2,1)S(1)}, u32[]{:S(2)}, u32[]{:S(2)}) collective-permute-start(s16[384,128]{1,0:T(8,128)(2,1)S(1)} %get-tuple-element.24), channel_id=1, source_target_pairs={{0,8},{1,10},{2,9},{3,11},{4,12},{5,14},{6,13},{7,15},{8,0},{9,2},... | collective-permute-start | bytes 294920 | tf_op jit(solution)/shard_map/ppermute | solution.py:356
  10.8 6.7 %collective-permute-start = (s16[384,128]{1,0:T(8,128)(2,1)S(1)}, s16[384,128]{1,0:T(8,128)(2,1)S(1)}, u32[]{:S(2)}, u32[]{:S(2)}) collective-permute-start(s16[384,128]{1,0:T(8,128)(2,1)S(1)} %get-tuple-element.21), channel_id=1, source_target_pairs={{0,12},{1,14},{2,13},{3,15},{4,8},{5,10},{6,9},{7,11},{8,4},{9,6},... | collective-permute-start | bytes 294920 | tf_op jit(solution)/shard_map/ppermute | solution.py:356
  17.9 3.8 %collective-permute-start.4 = (s16[1024,128]{1,0:T(8,128)(2,1)S(1)}, s16[1024,128]{1,0:T(8,128)(2,1)S(1)}, u32[]{:S(2)}, u32[]{:S(2)}) collective-permute-start(s16[1024,128]{1,0:T(8,128)(2,1)S(1)} %bitcast_dynamic-update-slice_fusion), channel_id=1, source_target_pairs={{0,1},{1,0},{2,3},{3,2},{4,5},{5,4},{6,7},{7,6},{8,9},{9,8},{10,11... | collective-permute-start | bytes 786440 | tf_op jit(solution)/shard_map/ppermute | solution.py:395
  20.5 0.8 %collective-permute-start.5 = (s16[512,128]{1,0:T(8,128)(2,1)S(1)}, s16[512,128]{1,0:T(8,128)(2,1)S(1)}, u32[]{:S(2)}, u32[]{:S(2)}) collective-permute-start(s16[512,128]{1,0:T(8,128)(2,1)S(1)} %pad_add_fusion.1), channel_id=1, source_target_pairs={{1,4},{4,1},{5,8},{8,5},{9,12},{12,9},{13,14},{14,13},{15,10},{10,... | collective-permute-start | bytes 393224 | tf_op jit(solution)/shard_map/ppermute | solution.py:418
  24.2 9.9 %collective-permute-start.8 = (f16[512,128]{1,0:T(8,128)(2,1)S(1)}, f16[512,128]{1,0:T(8,128)(2,1)S(1)}, u32[]{:S(2)}, u32[]{:S(2)}) collective-permute-start(f16[512,128]{1,0:T(8,128)(2,1)S(1)} %add_convert_fusion), channel_id=1, source_target_pairs={{1,4},{4,1},{5,8},{8,5},{9,12},{12,9},{13,14},{14,13},{15,10},{10,... | collective-permute-start | bytes 393224 | tf_op jit(solution)/shard_map/ppermute | solution.py:418
  24.9 9.3 %collective-permute-start.7 = (f32[512,128]{1,0:T(8,128)S(1)}, f32[512,128]{1,0:T(8,128)S(1)}, u32[]{:S(2)}, u32[]{:S(2)}) collective-permute-start(f32[512,128]{1,0:T(8,128)S(1)} %get-tuple-element.13.current_ref), channel_id=1, source_target_pairs={{0,1},{1,0},{2,3},{3,2},{4,5},{5,4},{6,7},{7,6},{8,9},{9,8},{10,11... | collective-permute-start | bytes 786440 | tf_op jit(solution)/shard_map/ppermute | solution.py:420
  34.8 7.1 %collective-permute-start.10 = (f16[1,128,128]{2,1,0:T(8,128)(2,1)S(1)}, f16[1,128,128]{2,1,0:T(8,128)(2,1)S(1)}, u32[]{:S(2)}, u32[]{:S(2)}) collective-permute-start(f16[1,128,128]{2,1,0:T(8,128)(2,1)S(1)} %get-tuple-element.47), channel_id=1, source_target_pairs={{0,8},{4,12},{8,0},{12,4},{1,9},{5,13},{9,1},{13,5},{2,10},{6,14},... | collective-permute-start | bytes 98312 | tf_op jit(solution)/shard_map/ppermute | solution.py:434
  38.1 5.8 %collective-permute-start.11 = (f16[1,128,128]{2,1,0:T(8,128)(2,1)S(1)}, f16[1,128,128]{2,1,0:T(8,128)(2,1)S(1)}, u32[]{:S(2)}, u32[]{:S(2)}) collective-permute-start(f16[1,128,128]{2,1,0:T(8,128)(2,1)S(1)} %get-tuple-element.46), channel_id=1, source_target_pairs={{0,12},{4,8},{8,4},{12,0},{1,13},{5,9},{9,5},{13,1},{2,14},{6,10},... | collective-permute-start | bytes 98312 | tf_op jit(solution)/shard_map/ppermute | solution.py:434
  39.7 4.3 %collective-permute-start.9 = (f16[1,128,128]{2,1,0:T(8,128)(2,1)S(1)}, f16[1,128,128]{2,1,0:T(8,128)(2,1)S(1)}, u32[]{:S(2)}, u32[]{:S(2)}) collective-permute-start(f16[1,128,128]{2,1,0:T(8,128)(2,1)S(1)} %get-tuple-element.45), channel_id=1, source_target_pairs={{0,4},{4,0},{8,12},{12,8},{1,5},{5,1},{9,13},{13,9},{2,6},{6,2},{1... | collective-permute-start | bytes 98312 | tf_op jit(solution)/shard_map/ppermute | solution.py:434
  39.7 6.8 %collective-permute-start.12 = (f16[1,128,128]{2,1,0:T(8,128)(2,1)S(1)}, f16[1,128,128]{2,1,0:T(8,128)(2,1)S(1)}, u32[]{:S(2)}, u32[]{:S(2)}) collective-permute-start(f16[1,128,128]{2,1,0:T(8,128)(2,1)S(1)} %get-tuple-element.48), channel_id=1, source_target_pairs={{0,2},{2,0},{1,3},{3,1},{4,6},{6,4},{5,7},{7,5},{8,10},{10,8},{9,1... | collective-permute-start | bytes 98312 | tf_op jit(solution)/shard_map/ppermute | solution.py:436
  44.0 5.0 %collective-permute-start.13 = (f16[3,128,128]{2,1,0:T(8,128)(2,1)S(1)}, f16[3,128,128]{2,1,0:T(8,128)(2,1)S(1)}, u32[]{:S(2)}, u32[]{:S(2)}) collective-permute-start(f16[3,128,128]{2,1,0:T(8,128)(2,1)S(1)} %pad_maximum_fusion.1), channel_id=1, source_target_pairs={{0,2},{2,0},{1,3},{3,1},{4,6},{6,4},{5,7},{7,5},{8,10},{10,8},{9,1... | collective-permute-start | bytes 294920 | tf_op jit(solution)/shard_map/ppermute | solution.py:437
  49.2 1.4 %collective-permute-start.14 = (f16[4,128,128]{2,1,0:T(8,128)(2,1)S(1)}, f16[4,128,128]{2,1,0:T(8,128)(2,1)S(1)}, u32[]{:S(2)}, u32[]{:S(2)}) collective-permute-start(f16[4,128,128]{2,1,0:T(8,128)(2,1)S(1)} %broadcast_select_fusion), channel_id=1, source_target_pairs={{0,1},{1,0},{2,3},{3,2},{4,5},{5,4},{6,7},{7,6},{8,9},{9,8},{10,11... | collective-permute-start | bytes 393224 | tf_op jit(solution)/shard_map/ppermute | solution.py:440

commit v5 on v4

--- a/solution.py
+++ b/solution.py
@@ -328,10 +328,39 @@
     )(core, current, twin, other, logs)
 
 
+def write_kernel(where_ref, *refs):
+    sources, out_ref, sems = refs[:-2], refs[-2], refs[-1]
+    tiles = out_ref.shape[0] // 2
+    copies = []
+    for parity, pair in enumerate((sources[:2], sources[2:])):
+        q = where_ref[0] if parity == 0 else 1 - where_ref[0]
+        for k in range(tiles):
+            source = pair[0].at[0] if k == 0 else pair[1].at[k - 1]
+            target = 2 * lax.bitwise_xor(where_ref[1], k) + q
+            copies.append(pltpu.make_async_copy(source, out_ref.at[target], sems.at[parity, k]))
+    for copy in copies:
+        copy.start()
+    for copy in copies:
+        copy.wait()
+
+
+def write_planes(where, sources):
+    tiles = 1 + sources[1].shape[0]
+    return pl.pallas_call(
+        write_kernel,
+        out_shape=jax.ShapeDtypeStruct((2 * tiles, *sources[0].shape[1:]), jnp.float32),
+        in_specs=[SMEM] + [VMEM] * 4,
+        out_specs=pl.BlockSpec(memory_space=pl.ANY),
+        scratch_shapes=[pltpu.SemaphoreType.DMA((2, tiles))],
+        compiler_params=LIMIT,
+        name="write_planes",
+    )(where, *sources)
+
+
 def plane_shards(view_data, estimate, psf_taps, offsets):
     tiles, views = lax.axis_size("tiles"), lax.axis_size("views")
     square = ("tiles", "views", "gz")
-    planes, height, columns = estimate.shape
+    _, height, columns = estimate.shape
     blocks = offsets.shape[1]
     taps = psf_taps.shape[-1]
     tile, view, core = lax.axis_index("tiles"), lax.axis_index("views"), lax.axis_index("gz")
@@ -388,16 +417,17 @@
     shifts = notes[:, 8 * taps : 8 * taps + blocks].astype(jnp.int32)
     matrices = blur_matrices(taps, height, notes * (1.0 / TAP_UNIT))
 
-    planes = [piece[:height] for piece in pieces]
-    pairs = [piece[height : 3 * height].reshape(2, height, columns) for piece in pieces]
-    keep = [lax.dynamic_index_in_dim(pair, core, 0, keepdims=False) for pair in pairs]
-    give = [lax.dynamic_index_in_dim(pair, 1 - core, 0, keepdims=False) for pair in pairs]
-    got = lax.ppermute(jnp.concatenate([*planes, *give]), "gz", swap)
-    length = tiles * height
-    twin = got[:length].reshape(tiles, height, columns)
-    take = got[length:].reshape(tiles, height, columns)
-    data = [x.astype(jnp.float32) * (1.0 / DATA_UNIT) for x in [*keep, *[take[k] for k in range(tiles)]]]
-    data = [x.astype(jnp.bfloat16) for x in data]
+    swapped = []
+    for piece in pieces:
+        swapped.append(lax.ppermute(piece, "gz", swap))
+
+    def view_part(piece):
+        part = lax.dynamic_slice_in_dim(piece, (1 + core) * height, height).astype(jnp.float32)
+        return (part * (1.0 / DATA_UNIT)).astype(jnp.bfloat16)
+
+    data = [view_part(piece) for piece in pieces]
+    for piece in swapped:
+        data.append(view_part(piece))
 
     path = [(t, 0) for t in range(tiles)] + [(t, 1) for t in reversed(range(tiles))]
     hops = []
@@ -408,8 +438,8 @@
     def plane_of(coded):
         return coded.astype(jnp.float32) * (1.0 / PLANE_UNIT) + 1.0
 
-    plane = jnp.concatenate(ordered(planes, tile))
-    twin = plane_of(jnp.concatenate(ordered([twin[k] for k in range(tiles)], tile)))
+    plane = jnp.concatenate(ordered([piece[:height] for piece in pieces], tile))
+    twin = plane_of(jnp.concatenate(ordered([piece[:height] for piece in swapped], tile)))
     current = plane_of(plane)
     narrow = current.astype(jnp.bfloat16)
     at_end = (tile == 0) & (core == view)
@@ -435,13 +465,12 @@
     mine = jnp.concatenate(pieces)
     crossed = [lax.ppermute(pieces[0], "views", swap)]
     crossed.append(lax.ppermute(mine[1:], "views", swap))
-    crossed = jnp.concatenate(crossed)
-    same = jnp.where(straight, mine, crossed)
-    twin = lax.ppermute(jnp.where(straight, crossed, mine), "gz", swap)
-    even, odd = jnp.where(core == 0, same, twin), jnp.where(core == 0, twin, same)
-    result = [jnp.stack([even[k], odd[k]]) for k in range(tiles)]
-    result = jnp.concatenate(ordered(result, lax.bitwise_xor(tile, end_of(core))))
-    return result.astype(jnp.float32)
+    halves = [mine[:1], mine[1:]]
+    twins = [lax.ppermute(jnp.where(straight, c, m), "gz", swap) for c, m in zip(crossed, halves)]
+    same = [jnp.where(straight, m, c).astype(jnp.float32) for c, m in zip(crossed, halves)]
+    twins = [x.astype(jnp.float32) for x in twins]
+    where = jnp.stack([core, lax.bitwise_xor(tile, end_of(core))]).astype(jnp.int32)
+    return write_planes(where, same + twins)
 
 
 def one_plane_each(mesh, view_data, estimate, psf_taps, offsets):

time: 52 us -> 49.6 us (0.954)
  starting transfers between devices: 29.2 us -> 22.6 us
  waiting for transfers between devices: 11.6 us -> 15.8 us
  Pallas kernels: 5.57 us -> 6.96 us
  other arithmetic: 3.19 us -> 2.14 us
    ppermute x1, starting transfers between devices: 7.49 us -> 2.06 us  [plane_shards(): twin = lax.ppermute(current, 'gz', swap)]
    ppermute x3, waiting for transfers between devices: 2.03 us -> 3.78 us  [plane_shards(): lax.ppermute(piece, 'tiles', [(t, t ^ k) for t in range(tiles)])]
    ppermute x1, starting transfers between devices: 2.45 us -> 1.06 us  [plane_shards(): crossed.append(lax.ppermute(mine[1:], 'views', swap))]
    pallas_call x0 -> x1, Pallas kernels: none -> 1.39 us  [write_planes(): pl.pallas_call(write_kernel, out_shape=jax.ShapeDtypeStruct((2 * tiles, *...]
    ppermute x3, starting transfers between devices: 4.87 us -> 5.85 us  [plane_shards(): lax.ppermute(piece, 'tiles', [(t, t ^ k) for t in range(tiles)])]
    ppermute x1, waiting for transfers between devices: 2.58 us -> 3.52 us  [plane_shards(): crossed.append(lax.ppermute(mine[1:], 'views', swap))]
    ppermute x4, waiting for transfers between devices: 5.34 us -> 6.2 us  [exchange(): pieces.append(lax.ppermute(pick(k), square, pairs))]
    convert_element_type x4 -> x10, other arithmetic: 0.99 us -> 0.18 us  [the longest x8 0.16 us: view_part(): return (part * (1.0 / DATA_UNIT)).astype(jnp.bfloat16)]
  transfers between devices with their start and end apart: 15 -> 19, of which waited for: 7 -> 10; matrix products, arithmetic and copies ran while one was open for 1% -> 1% of each run, Pallas kernels for 5% -> 9%
where the time goes in v5:
time: 49.6 us; the launch traced here: 49.4 us
  starting transfers between devices  22.6 us (46%)
  waiting for transfers between devices  15.8 us (32%)
  Pallas kernels  6.96 us (14%)
  other arithmetic  2.14 us (4%)
  local copies, waits for them, and re-layouts  1.61 us (3%)
    ppermute x4, waiting for transfers between devices, exchange(): pieces.append(lax.ppermute(pick(k), square, pairs))  6.2 us
    ppermute x3, starting transfers between devices, plane_shards(): lax.ppermute(piece, 'tiles', [(t, t ^ k) for t in range(tiles)])  5.85 us
    ppermute x4, starting transfers between devices, exchange(): pieces.append(lax.ppermute(pick(k), square, pairs))  5.11 us
    ppermute x3, waiting for transfers between devices, plane_shards(): lax.ppermute(piece, 'tiles', [(t, t ^ k) for t in range(tiles)])  3.78 us
    ppermute x1, waiting for transfers between devices, plane_shards(): crossed.append(lax.ppermute(mine[1:], 'views', swap))  3.52 us
    pallas_call x2, Pallas kernels, correction_logs(): pl.pallas_call(functools.partial(correction_kernel, tiles), out_shape=jax...  3.39 us
    ppermute x1, starting transfers between devices, plane_shards(): note = lax.ppermute(info, 'views', swap)  3.03 us
    ppermute x4, starting transfers between devices, plane_shards(): swapped.append(lax.ppermute(piece, 'gz', swap))  2.53 us
  transfers between devices with their start and end apart: 19, of which 10 were waited for; matrix products, arithmetic and copies ran while one was open for 1% of the time, Pallas kernels for 9%

profile of v5, /device:TPU:0, one launch (start us, length us, event | category | flops | bytes accessed | tf_op | source)
XLA Modules:
  0.0 49.4 jit_solution(11805820779055998020)
XLA Ops:
  0.0 1.1 %multiply_convert_fusion = s16[1,1,8,128,128]{4,3,2,1,0:T(8,128)(2,1)S(1)} fusion(bf16[1,1,8,128,128]{4,3,2,1,0:T(8,128)(2,1)} %param.4), kind=kLoop, calls=%fused_computation | loop fusion | flops 393216 | bytes 524288 | tf_op jit(solution)/shard_map/convert_element_type | solution.py:398
  1.3 0.6 %copy-done.1 = f32[1,2,2,9]{3,2,1,0:T(2,128)S(1)} copy-done((f32[1,2,2,9]{3,2,1,0:T(2,128)S(1)}, f32[1,2,2,9]{3,2,1,0:T(2,128)}, u32[]{:S(2)}) %copy-start.1) | copy-done | bytes 168
  2.9 3.0 %collective-permute-start.9 = (s16[16,128]{1,0:T(8,128)(2,1)S(1)}, s16[16,128]{1,0:T(8,128)(2,1)S(1)}, u32[]{:S(2)}, u32[]{:S(2)}) collective-permute-start(s16[16,128]{1,0:T(8,128)(2,1)S(1)} %broadcast_in_dim.9), channel_id=1, source_target_pairs={{0,2},{2,0},{1,3},{3,1},{4,6},{6,4},{5,7},{7,5},{8,10},{10,8},{9,1... | collective-permute-start | bytes 12296 | tf_op jit(solution)/shard_map/ppermute | solution.py:413
  5.9 3.7 %collective-permute-start = (s16[384,128]{1,0:T(8,128)(2,1)S(1)}, s16[384,128]{1,0:T(8,128)(2,1)S(1)}, u32[]{:S(2)}, u32[]{:S(2)}) collective-permute-start(s16[384,128]{1,0:T(8,128)(2,1)S(1)} %get-tuple-element.23), channel_id=1, source_target_pairs={{0,12},{1,14},{2,13},{3,15},{4,8},{5,10},{6,9},{7,11},{8,4},{9,6},... | collective-permute-start | bytes 294920 | tf_op jit(solution)/shard_map/ppermute | solution.py:385
  9.6 0.8 %collective-permute-start.2 = (s16[384,128]{1,0:T(8,128)(2,1)S(1)}, s16[384,128]{1,0:T(8,128)(2,1)S(1)}, u32[]{:S(2)}, u32[]{:S(2)}) collective-permute-start(s16[384,128]{1,0:T(8,128)(2,1)S(1)} %get-tuple-element.25), channel_id=1, source_target_pairs={{0,4},{1,6},{2,5},{3,7},{4,0},{5,2},{6,1},{7,3},{8,12},{9,14},{10,... | collective-permute-start | bytes 294920 | tf_op jit(solution)/shard_map/ppermute | solution.py:385
  10.4 0.7 %collective-permute-start.3 = (s16[384,128]{1,0:T(8,128)(2,1)S(1)}, s16[384,128]{1,0:T(8,128)(2,1)S(1)}, u32[]{:S(2)}, u32[]{:S(2)}) collective-permute-start(s16[384,128]{1,0:T(8,128)(2,1)S(1)} %get-tuple-element.24), channel_id=1, source_target_pairs={{0,0},{1,2},{2,1},{3,3},{4,4},{5,6},{6,5},{7,7},{8,8},{9,10},{10,9... | collective-permute-start | bytes 294920 | tf_op jit(solution)/shard_map/ppermute | solution.py:385
  11.2 1.0 %blur_matrices.1.matrices_ref = bf16[2,4,256,128]{3,2,1,0:T(8,128)(2,1)S(1)} custom-call(f32[2,128]{1,0:T(2,128)S(1)} %broadcast_multiply_fusion.info_ref), custom_call_target="tpu_custom_call" | custom-call | tf_op jit(solution)/shard_map/blur_matrices/pallas_call | solution.py:192
  12.2 0.6 %collective-permute-done = s16[384,128]{1,0:T(8,128)(2,1)S(1)} collective-permute-done((s16[384,128]{1,0:T(8,128)(2,1)S(1)}, s16[384,128]{1,0:T(8,128)(2,1)S(1)}, u32[]{:S(2)}, u32[]{:S(2)}) %collective-permute-start) | collective-permute-done | bytes 98336 | tf_op jit(solution)/shard_map/ppermute | solution.py:385
  12.8 5.6 %collective-permute-done.1 = s16[384,128]{1,0:T(8,128)(2,1)S(1)} collective-permute-done((s16[384,128]{1,0:T(8,128)(2,1)S(1)}, s16[384,128]{1,0:T(8,128)(2,1)S(1)}, u32[]{:S(2)}, u32[]{:S(2)}) %collective-permute-start.1) | collective-permute-done | bytes 98336 | tf_op jit(solution)/shard_map/ppermute | solution.py:385
  18.5 0.7 %collective-permute-start.8 = (s16[512,128]{1,0:T(8,128)(2,1)S(1)}, s16[512,128]{1,0:T(8,128)(2,1)S(1)}, u32[]{:S(2)}, u32[]{:S(2)}) collective-permute-start(s16[512,128]{1,0:T(8,128)(2,1)S(1)} %pad_add_fusion.1), channel_id=1, source_target_pairs={{1,4},{4,1},{5,8},{8,5},{9,12},{12,9},{13,14},{14,13},{15,10},{10,... | collective-permute-start | bytes 393224 | tf_op jit(solution)/shard_map/ppermute | solution.py:448
  19.2 1.9 %collective-permute-start.4 = (s16[384,128]{1,0:T(8,128)(2,1)S(1)}, s16[384,128]{1,0:T(8,128)(2,1)S(1)}, u32[]{:S(2)}, u32[]{:S(2)}) collective-permute-start(s16[384,128]{1,0:T(8,128)(2,1)S(1)} %collective-permute-done), channel_id=1, source_target_pairs={{0,1},{1,0},{2,3},{3,2},{4,5},{5,4},{6,7},{7,6},{8,9},{9,8},{10,11... | collective-permute-start | bytes 294920 | tf_op jit(solution)/shard_map/ppermute | solution.py:422
  23.1 1.7 %correction.2.log_ref = f32[512,128]{1,0:T(8,128)S(1)} custom-call(s32[1]{0:T(128)} %bitcast.9.tile_ref, s32[2,8]{1,0:T(2,128)S(1)} %slice_convert_fusion.offsets_ref, bf16[4,128,128]{2,1,0:T(8,128)(2,1)S(1)} %bitcast.29, bf16[2,4,256,128]{3,2,1,0:T(8,128)(2,1)S(1)} %blur_matrices.1.matrices_ref, bf16[128,128]{1,0:T(8,128)(2,1)S(1)} %multiply_convert_fusion.8.refs_0_, ...), custom_call_target="tpu_custom_call" | custom-call | flops 300000000 | bytes 1500000 | tf_op jit(solution)/shard_map/correction/pallas_call | solution.py:260
  24.9 0.6 %update.2 = (f32[512,128]{1,0:T(8,128)S(1)}, bf16[512,128]{1,0:T(8,128)(2,1)S(1)}) custom-call(s32[1]{0:T(128)} %bitcast.core_ref, f32[512,128]{1,0:T(8,128)S(1)} %get-tuple-element.34.current_ref, f32[512,128]{1,0:T(8,128)S(1)} %multiply_add_fusion.twin_ref, f32[512,128]{1,0:T(8,128)S(1)} %add_select_fusion.1.other_ref, f32[512,128]{1,0:T(8,128)S(1)} %correction.2.log_ref), custom_call_target="tpu_custom_call" | custom-call | tf_op jit(solution)/shard_map/update/pallas_call | solution.py:321
  25.6 0.7 %collective-permute-start.11 = (f16[512,128]{1,0:T(8,128)(2,1)S(1)}, f16[512,128]{1,0:T(8,128)(2,1)S(1)}, u32[]{:S(2)}, u32[]{:S(2)}) collective-permute-start(f16[512,128]{1,0:T(8,128)(2,1)S(1)} %add_convert_fusion), channel_id=1, source_target_pairs={{1,4},{4,1},{5,8},{8,5},{9,12},{12,9},{13,14},{14,13},{15,10},{10,... | collective-permute-start | bytes 393224 | tf_op jit(solution)/shard_map/ppermute | solution.py:448
  26.3 2.1 %collective-permute-start.10 = (f32[512,128]{1,0:T(8,128)S(1)}, f32[512,128]{1,0:T(8,128)S(1)}, u32[]{:S(2)}, u32[]{:S(2)}) collective-permute-start(f32[512,128]{1,0:T(8,128)S(1)} %get-tuple-element.13.current_ref), channel_id=1, source_target_pairs={{0,1},{1,0},{2,3},{3,2},{4,5},{5,4},{6,7},{7,6},{8,9},{9,8},{10,11... | collective-permute-start | bytes 786440 | tf_op jit(solution)/shard_map/ppermute | solution.py:450
  28.3 1.7 %correction.3.log_ref = f32[512,128]{1,0:T(8,128)S(1)} custom-call(s32[1]{0:T(128)} %bitcast.9.tile_ref, s32[2,8]{1,0:T(2,128)S(1)} %slice_convert_fusion.offsets_ref, bf16[4,128,128]{2,1,0:T(8,128)(2,1)S(1)} %bitcast.30, bf16[2,4,256,128]{3,2,1,0:T(8,128)(2,1)S(1)} %blur_matrices.1.matrices_ref, bf16[128,128]{1,0:T(8,128)(2,1)S(1)} %multiply_convert_fusion.8.refs_0_, ...), custom_call_target="tpu_custom_call" | custom-call | flops 300000000 | bytes 1500000 | tf_op jit(solution)/shard_map/correction/pallas_call | solution.py:260
  30.8 2.5 %collective-permute-start.13 = (f16[1,128,128]{2,1,0:T(8,128)(2,1)S(1)}, f16[1,128,128]{2,1,0:T(8,128)(2,1)S(1)}, u32[]{:S(2)}, u32[]{:S(2)}) collective-permute-start(f16[1,128,128]{2,1,0:T(8,128)(2,1)S(1)} %get-tuple-element.31), channel_id=1, source_target_pairs={{0,4},{4,0},{8,12},{12,8},{1,5},{5,1},{9,13},{13,9},{2,6},{6,2},{1... | collective-permute-start | bytes 98312 | tf_op jit(solution)/shard_map/ppermute | solution.py:464
  33.3 2.9 %collective-permute-start.14 = (f16[1,128,128]{2,1,0:T(8,128)(2,1)S(1)}, f16[1,128,128]{2,1,0:T(8,128)(2,1)S(1)}, u32[]{:S(2)}, u32[]{:S(2)}) collective-permute-start(f16[1,128,128]{2,1,0:T(8,128)(2,1)S(1)} %get-tuple-element.30), channel_id=1, source_target_pairs={{0,8},{4,12},{8,0},{12,4},{1,9},{5,13},{9,1},{13,5},{2,10},{6,14},... | collective-permute-start | bytes 98312 | tf_op jit(solution)/shard_map/ppermute | solution.py:464
  36.6 1.4 %collective-permute-start.12 = (f16[1,128,128]{2,1,0:T(8,128)(2,1)S(1)}, f16[1,128,128]{2,1,0:T(8,128)(2,1)S(1)}, u32[]{:S(2)}, u32[]{:S(2)}) collective-permute-start(f16[1,128,128]{2,1,0:T(8,128)(2,1)S(1)} %get-tuple-element.32), channel_id=1, source_target_pairs={{0,2},{2,0},{1,3},{3,1},{4,6},{6,4},{5,7},{7,5},{8,10},{10,8},{9,1... | collective-permute-start | bytes 98312 | tf_op jit(solution)/shard_map/ppermute | solution.py:466
  38.4 3.5 %collective-permute-done.15 = f16[1,128,128]{2,1,0:T(8,128)(2,1)S(1)} collective-permute-done((f16[1,128,128]{2,1,0:T(8,128)(2,1)S(1)}, f16[1,128,128]{2,1,0:T(8,128)(2,1)S(1)}, u32[]{:S(2)}, u32[]{:S(2)}) %collective-permute-start.15) | collective-permute-done | bytes 32800 | tf_op jit(solution)/shard_map/ppermute | solution.py:464
  41.9 1.1 %collective-permute-start.16 = (f16[3,128,128]{2,1,0:T(8,128)(2,1)S(1)}, f16[3,128,128]{2,1,0:T(8,128)(2,1)S(1)}, u32[]{:S(2)}, u32[]{:S(2)}) collective-permute-start(f16[3,128,128]{2,1,0:T(8,128)(2,1)S(1)} %constant_dynamic-update-slice_fusion), channel_id=1, source_target_pairs={{0,2},{2,0},{1,3},{3,1},{4,6},{6,4},{5,7},{7,5},{8,10},{10,8},{9,1... | collective-permute-start | bytes 294920 | tf_op jit(solution)/shard_map/ppermute | solution.py:467
  43.0 3.5 %collective-permute-done.16 = f16[3,128,128]{2,1,0:T(8,128)(2,1)S(1)} collective-permute-done((f16[3,128,128]{2,1,0:T(8,128)(2,1)S(1)}, f16[3,128,128]{2,1,0:T(8,128)(2,1)S(1)}, u32[]{:S(2)}, u32[]{:S(2)}) %collective-permute-start.16) | collective-permute-done | bytes 98336 | tf_op jit(solution)/shard_map/ppermute | solution.py:467
  46.8 1.2 %collective-permute-done.18 = f16[3,128,128]{2,1,0:T(8,128)(2,1)S(1)} collective-permute-done((f16[3,128,128]{2,1,0:T(8,128)(2,1)S(1)}, f16[3,128,128]{2,1,0:T(8,128)(2,1)S(1)}, u32[]{:S(2)}, u32[]{:S(2)}) %collective-permute-start.18) | collective-permute-done | bytes 98336 | tf_op jit(solution)/shard_map/ppermute | solution.py:469
  48.0 1.4 %write_planes.1 = f32[8,128,128]{2,1,0:T(8,128)} custom-call(s32[2]{0:T(128)S(1)} %pad_add_fusion.2.where_ref, f32[1,128,128]{2,1,0:T(8,128)S(1)} %get-tuple-element.36.refs_0_, f32[3,128,128]{2,1,0:T(8,128)S(1)} %get-tuple-element.28.refs_1_, f32[1,128,128]{2,1,0:T(8,128)S(1)} %convert_element_type.149.refs_2_, f32[3,128,128]{2,1,0:T(8,128)S(1)} %convert_element_type.150.refs_3_), custom_call_target="tpu_custom_call" | custom-call | tf_op jit(solution)/shard_map/write_planes/pallas_call | solution.py:349
  (69 shorter events, 5.1 us)
Async XLA Ops:
  0.0 1.1 %copy-start = (f32[8,128,128]{2,1,0:T(8,128)S(1)}, f32[8,128,128]{2,1,0:T(8,128)}, u32[]{:S(2)}) copy-start(f32[8,128,128]{2,1,0:T(8,128)} %param.5) | copy-start | bytes 1572868
  1.2 0.7 %copy-start.1 = (f32[1,2,2,9]{3,2,1,0:T(2,128)S(1)}, f32[1,2,2,9]{3,2,1,0:T(2,128)}, u32[]{:S(2)}) copy-start(f32[1,2,2,9]{3,2,1,0:T(2,128)} %param.6) | copy-start | bytes 436
  2.1 0.7 %copy-start.2 = (s32[1,8]{1,0:T(1,128)S(1)}, s32[1,8]{1,0:T(1,128)}, u32[]{:S(2)}) copy-start(s32[1,8]{1,0:T(1,128)} %param.7) | copy-start | bytes 100
  2.9 8.2 %collective-permute-start.9 = (s16[16,128]{1,0:T(8,128)(2,1)S(1)}, s16[16,128]{1,0:T(8,128)(2,1)S(1)}, u32[]{:S(2)}, u32[]{:S(2)}) collective-permute-start(s16[16,128]{1,0:T(8,128)(2,1)S(1)} %broadcast_in_dim.9), channel_id=1, source_target_pairs={{0,2},{2,0},{1,3},{3,1},{4,6},{6,4},{5,7},{7,5},{8,10},{10,8},{9,1... | collective-permute-start | bytes 12296 | tf_op jit(solution)/shard_map/ppermute | solution.py:413
  5.9 6.9 %collective-permute-start = (s16[384,128]{1,0:T(8,128)(2,1)S(1)}, s16[384,128]{1,0:T(8,128)(2,1)S(1)}, u32[]{:S(2)}, u32[]{:S(2)}) collective-permute-start(s16[384,128]{1,0:T(8,128)(2,1)S(1)} %get-tuple-element.23), channel_id=1, source_target_pairs={{0,12},{1,14},{2,13},{3,15},{4,8},{5,10},{6,9},{7,11},{8,4},{9,6},... | collective-permute-start | bytes 294920 | tf_op jit(solution)/shard_map/ppermute | solution.py:385
  9.6 8.8 %collective-permute-start.1 = (s16[384,128]{1,0:T(8,128)(2,1)S(1)}, s16[384,128]{1,0:T(8,128)(2,1)S(1)}, u32[]{:S(2)}, u32[]{:S(2)}) collective-permute-start(s16[384,128]{1,0:T(8,128)(2,1)S(1)} %get-tuple-element.26), channel_id=1, source_target_pairs={{0,8},{1,10},{2,9},{3,11},{4,12},{5,14},{6,13},{7,15},{8,0},{9,2},... | collective-permute-start | bytes 294920 | tf_op jit(solution)/shard_map/ppermute | solution.py:385
  9.6 8.8 %collective-permute-start.2 = (s16[384,128]{1,0:T(8,128)(2,1)S(1)}, s16[384,128]{1,0:T(8,128)(2,1)S(1)}, u32[]{:S(2)}, u32[]{:S(2)}) collective-permute-start(s16[384,128]{1,0:T(8,128)(2,1)S(1)} %get-tuple-element.25), channel_id=1, source_target_pairs={{0,4},{1,6},{2,5},{3,7},{4,0},{5,2},{6,1},{7,3},{8,12},{9,14},{10,... | collective-permute-start | bytes 294920 | tf_op jit(solution)/shard_map/ppermute | solution.py:385
  10.4 8.0 %collective-permute-start.3 = (s16[384,128]{1,0:T(8,128)(2,1)S(1)}, s16[384,128]{1,0:T(8,128)(2,1)S(1)}, u32[]{:S(2)}, u32[]{:S(2)}) collective-permute-start(s16[384,128]{1,0:T(8,128)(2,1)S(1)} %get-tuple-element.24), channel_id=1, source_target_pairs={{0,0},{1,2},{2,1},{3,3},{4,4},{5,6},{6,5},{7,7},{8,8},{9,10},{10,9... | collective-permute-start | bytes 294920 | tf_op jit(solution)/shard_map/ppermute | solution.py:385
  18.5 6.3 %collective-permute-start.8 = (s16[512,128]{1,0:T(8,128)(2,1)S(1)}, s16[512,128]{1,0:T(8,128)(2,1)S(1)}, u32[]{:S(2)}, u32[]{:S(2)}) collective-permute-start(s16[512,128]{1,0:T(8,128)(2,1)S(1)} %pad_add_fusion.1), channel_id=1, source_target_pairs={{1,4},{4,1},{5,8},{8,5},{9,12},{12,9},{13,14},{14,13},{15,10},{10,... | collective-permute-start | bytes 393224 | tf_op jit(solution)/shard_map/ppermute | solution.py:448
  19.2 2.9 %collective-permute-start.4 = (s16[384,128]{1,0:T(8,128)(2,1)S(1)}, s16[384,128]{1,0:T(8,128)(2,1)S(1)}, u32[]{:S(2)}, u32[]{:S(2)}) collective-permute-start(s16[384,128]{1,0:T(8,128)(2,1)S(1)} %collective-permute-done), channel_id=1, source_target_pairs={{0,1},{1,0},{2,3},{3,2},{4,5},{5,4},{6,7},{7,6},{8,9},{9,8},{10,11... | collective-permute-start | bytes 294920 | tf_op jit(solution)/shard_map/ppermute | solution.py:422
  21.2 1.3 %collective-permute-start.5 = (s16[384,128]{1,0:T(8,128)(2,1)S(1)}, s16[384,128]{1,0:T(8,128)(2,1)S(1)}, u32[]{:S(2)}, u32[]{:S(2)}) collective-permute-start(s16[384,128]{1,0:T(8,128)(2,1)S(1)} %collective-permute-done.1), channel_id=1, source_target_pairs={{0,1},{1,0},{2,3},{3,2},{4,5},{5,4},{6,7},{7,6},{8,9},{9,8},{10,11... | collective-permute-start | bytes 294920 | tf_op jit(solution)/shard_map/ppermute | solution.py:422
  21.2 1.4 %collective-permute-start.6 = (s16[384,128]{1,0:T(8,128)(2,1)S(1)}, s16[384,128]{1,0:T(8,128)(2,1)S(1)}, u32[]{:S(2)}, u32[]{:S(2)}) collective-permute-start(s16[384,128]{1,0:T(8,128)(2,1)S(1)} %collective-permute-done.2), channel_id=1, source_target_pairs={{0,1},{1,0},{2,3},{3,2},{4,5},{5,4},{6,7},{7,6},{8,9},{9,8},{10,11... | collective-permute-start | bytes 294920 | tf_op jit(solution)/shard_map/ppermute | solution.py:422
  21.7 1.3 %collective-permute-start.7 = (s16[384,128]{1,0:T(8,128)(2,1)S(1)}, s16[384,128]{1,0:T(8,128)(2,1)S(1)}, u32[]{:S(2)}, u32[]{:S(2)}) collective-permute-start(s16[384,128]{1,0:T(8,128)(2,1)S(1)} %collective-permute-done.3), channel_id=1, source_target_pairs={{0,1},{1,0},{2,3},{3,2},{4,5},{5,4},{6,7},{7,6},{8,9},{9,8},{10,11... | collective-permute-start | bytes 294920 | tf_op jit(solution)/shard_map/ppermute | solution.py:422
  25.6 4.5 %collective-permute-start.11 = (f16[512,128]{1,0:T(8,128)(2,1)S(1)}, f16[512,128]{1,0:T(8,128)(2,1)S(1)}, u32[]{:S(2)}, u32[]{:S(2)}) collective-permute-start(f16[512,128]{1,0:T(8,128)(2,1)S(1)} %add_convert_fusion), channel_id=1, source_target_pairs={{1,4},{4,1},{5,8},{8,5},{9,12},{12,9},{13,14},{14,13},{15,10},{10,... | collective-permute-start | bytes 393224 | tf_op jit(solution)/shard_map/ppermute | solution.py:448
  26.3 3.8 %collective-permute-start.10 = (f32[512,128]{1,0:T(8,128)S(1)}, f32[512,128]{1,0:T(8,128)S(1)}, u32[]{:S(2)}, u32[]{:S(2)}) collective-permute-start(f32[512,128]{1,0:T(8,128)S(1)} %get-tuple-element.13.current_ref), channel_id=1, source_target_pairs={{0,1},{1,0},{2,3},{3,2},{4,5},{5,4},{6,7},{7,6},{8,9},{9,8},{10,11... | collective-permute-start | bytes 786440 | tf_op jit(solution)/shard_map/ppermute | solution.py:450
  30.8 7.3 %collective-permute-start.13 = (f16[1,128,128]{2,1,0:T(8,128)(2,1)S(1)}, f16[1,128,128]{2,1,0:T(8,128)(2,1)S(1)}, u32[]{:S(2)}, u32[]{:S(2)}) collective-permute-start(f16[1,128,128]{2,1,0:T(8,128)(2,1)S(1)} %get-tuple-element.31), channel_id=1, source_target_pairs={{0,4},{4,0},{8,12},{12,8},{1,5},{5,1},{9,13},{13,9},{2,6},{6,2},{1... | collective-permute-start | bytes 98312 | tf_op jit(solution)/shard_map/ppermute | solution.py:464
  33.3 5.1 %collective-permute-start.14 = (f16[1,128,128]{2,1,0:T(8,128)(2,1)S(1)}, f16[1,128,128]{2,1,0:T(8,128)(2,1)S(1)}, u32[]{:S(2)}, u32[]{:S(2)}) collective-permute-start(f16[1,128,128]{2,1,0:T(8,128)(2,1)S(1)} %get-tuple-element.30), channel_id=1, source_target_pairs={{0,8},{4,12},{8,0},{12,4},{1,9},{5,13},{9,1},{13,5},{2,10},{6,14},... | collective-permute-start | bytes 98312 | tf_op jit(solution)/shard_map/ppermute | solution.py:464
  36.1 5.7 %collective-permute-start.15 = (f16[1,128,128]{2,1,0:T(8,128)(2,1)S(1)}, f16[1,128,128]{2,1,0:T(8,128)(2,1)S(1)}, u32[]{:S(2)}, u32[]{:S(2)}) collective-permute-start(f16[1,128,128]{2,1,0:T(8,128)(2,1)S(1)} %get-tuple-element.29), channel_id=1, source_target_pairs={{0,12},{4,8},{8,4},{12,0},{1,13},{5,9},{9,5},{13,1},{2,14},{6,10},... | collective-permute-start | bytes 98312 | tf_op jit(solution)/shard_map/ppermute | solution.py:464
  36.6 6.3 %collective-permute-start.12 = (f16[1,128,128]{2,1,0:T(8,128)(2,1)S(1)}, f16[1,128,128]{2,1,0:T(8,128)(2,1)S(1)}, u32[]{:S(2)}, u32[]{:S(2)}) collective-permute-start(f16[1,128,128]{2,1,0:T(8,128)(2,1)S(1)} %get-tuple-element.32), channel_id=1, source_target_pairs={{0,2},{2,0},{1,3},{3,1},{4,6},{6,4},{5,7},{7,5},{8,10},{10,8},{9,1... | collective-permute-start | bytes 98312 | tf_op jit(solution)/shard_map/ppermute | solution.py:466
  41.9 4.7 %collective-permute-start.16 = (f16[3,128,128]{2,1,0:T(8,128)(2,1)S(1)}, f16[3,128,128]{2,1,0:T(8,128)(2,1)S(1)}, u32[]{:S(2)}, u32[]{:S(2)}) collective-permute-start(f16[3,128,128]{2,1,0:T(8,128)(2,1)S(1)} %constant_dynamic-update-slice_fusion), channel_id=1, source_target_pairs={{0,2},{2,0},{1,3},{3,1},{4,6},{6,4},{5,7},{7,5},{8,10},{10,8},{9,1... | collective-permute-start | bytes 294920 | tf_op jit(solution)/shard_map/ppermute | solution.py:467
  43.0 3.8 %collective-permute-start.17 = (f16[1,128,128]{2,1,0:T(8,128)(2,1)S(1)}, f16[1,128,128]{2,1,0:T(8,128)(2,1)S(1)}, u32[]{:S(2)}, u32[]{:S(2)}) collective-permute-start(f16[1,128,128]{2,1,0:T(8,128)(2,1)S(1)} %get-tuple-element.35), channel_id=1, source_target_pairs={{0,1},{1,0},{2,3},{3,2},{4,5},{5,4},{6,7},{7,6},{8,9},{9,8},{10,11... | collective-permute-start | bytes 98312 | tf_op jit(solution)/shard_map/ppermute | solution.py:469
  46.6 1.4 %collective-permute-start.18 = (f16[3,128,128]{2,1,0:T(8,128)(2,1)S(1)}, f16[3,128,128]{2,1,0:T(8,128)(2,1)S(1)}, u32[]{:S(2)}, u32[]{:S(2)}) collective-permute-start(f16[3,128,128]{2,1,0:T(8,128)(2,1)S(1)} %get-tuple-element.27), channel_id=1, source_target_pairs={{0,1},{1,0},{2,3},{3,2},{4,5},{5,4},{6,7},{7,6},{8,9},{9,8},{10,11... | collective-permute-start | bytes 294920 | tf_op jit(solution)/shard_map/ppermute | solution.py:469

commit v6 on v4

--- a/solution.py
+++ b/solution.py
@@ -199,12 +199,40 @@
     )(info)
 
 
-def correction_kernel(tiles, tile_ref, offsets_ref, current_ref, matrices_ref, *refs):
+def pack_kernel(where_ref, *refs):
+    pieces, (plane_ref, give_ref) = refs[:-2], refs[-2:]
+    height = plane_ref.shape[1]
+    other = pl.multiple_of((2 - where_ref[1]) * height, height)
+    for k, piece in enumerate(pieces):
+        plane = piece[0:height, :]
+        plane_ref[lax.bitwise_xor(where_ref[0], k)] = plane
+        give_ref[k, 0] = plane
+        give_ref[k, 1] = piece[pl.ds(other, height), :]
+
+
+def pack(where, pieces):
+    rows, columns = pieces[0].shape
+    shape = (len(pieces), rows // 3, columns)
+    return pl.pallas_call(
+        pack_kernel,
+        out_shape=[
+            jax.ShapeDtypeStruct(shape, pieces[0].dtype),
+            jax.ShapeDtypeStruct((shape[0], 2, *shape[1:]), pieces[0].dtype),
+        ],
+        in_specs=[SMEM] + [VMEM] * len(pieces),
+        out_specs=[VMEM] * 2,
+        compiler_params=LIMIT,
+        name="pack",
+    )(where, *pieces)
+
+
+def correction_kernel(where_ref, offsets_ref, current_ref, matrices_ref, *refs):
     views, blocks = offsets_ref.shape
-    data, log_ref, work = refs[: views * tiles], refs[views * tiles], refs[views * tiles + 1 :]
-    height, columns = data[0].shape
+    tiles, height, columns = current_ref.shape
+    pieces, swapped_ref, log_ref, work = refs[:tiles], refs[tiles], refs[tiles + 1], refs[tiles + 2 :]
     rows = height // blocks
-    me = tile_ref[0]
+    me = where_ref[0]
+    own = pl.multiple_of((1 + where_ref[1]) * height, height)
     shift = [[offsets_ref[w, s] for s in range(blocks)] for w in range(views)]
     planes = [work[3 * w] for w in range(views)]
     halves = [work[3 * w + 1] for w in range(views)]
@@ -232,7 +260,9 @@
     for w in range(views):
         blurred = jnp.dot(halves[w][...], matrices_ref[w, 1], preferred_element_type=jnp.float32)
         for k in range(tiles):
-            quotient = data[w * tiles + k][...].astype(jnp.float32) / blurred[k * height : (k + 1) * height]
+            observed = pieces[k][pl.ds(own, height), :] if w == 0 else swapped_ref[k, 1]
+            observed = observed.astype(jnp.float32) * (1.0 / DATA_UNIT)
+            quotient = observed / blurred[k * height : (k + 1) * height]
             planes[w][:, k * columns : (k + 1) * columns] = quotient.astype(jnp.bfloat16)
     for w in range(views):
         first(w, 2)
@@ -250,7 +280,7 @@
             log_ref[o * height + s * rows : o * height + (s + 1) * rows, :] = total
 
 
-def correction_logs(tile, offsets, current, matrices, data):
+def correction_logs(where, offsets, current, matrices, pieces, swapped):
     tiles, height, columns = current.shape
     scratch = [
         pltpu.VMEM((height, tiles * columns), jnp.bfloat16),
@@ -258,15 +288,15 @@
         pltpu.VMEM((tiles * height, columns), jnp.float32),
     ]
     return pl.pallas_call(
-        functools.partial(correction_kernel, tiles),
+        correction_kernel,
         out_shape=jax.ShapeDtypeStruct((tiles * height, columns), jnp.float32),
-        in_specs=[SMEM, SMEM] + [VMEM] * (2 + len(data)),
+        in_specs=[SMEM, SMEM] + [VMEM] * (3 + tiles),
         out_specs=VMEM,
         scratch_shapes=scratch * offsets.shape[0],
         cost_estimate=pl.CostEstimate(flops=300_000_000, bytes_accessed=1_500_000, transcendentals=0),
         compiler_params=LIMIT,
         name="correction",
-    )(tile, offsets, current, matrices, *data)
+    )(where, offsets, current, matrices, *pieces, swapped)
 
 
 def update_kernel(views, core_ref, current_ref, twin_ref, other_ref, log_ref, *new_refs):
@@ -331,7 +361,7 @@
 def plane_shards(view_data, estimate, psf_taps, offsets):
     tiles, views = lax.axis_size("tiles"), lax.axis_size("views")
     square = ("tiles", "views", "gz")
-    planes, height, columns = estimate.shape
+    _, height, columns = estimate.shape
     blocks = offsets.shape[1]
     taps = psf_taps.shape[-1]
     tile, view, core = lax.axis_index("tiles"), lax.axis_index("views"), lax.axis_index("gz")
@@ -359,7 +389,7 @@
     def end_of(chain):
         return jnp.where(chain == 0, 0, tiles - 1)
 
-    me = tile.reshape(1).astype(jnp.int32)
+    where = jnp.stack([tile, core]).astype(jnp.int32)
     flag = core.reshape(1).astype(jnp.int32)
 
     wide = estimate.reshape(tiles, 2, height, columns)
@@ -388,16 +418,8 @@
     shifts = notes[:, 8 * taps : 8 * taps + blocks].astype(jnp.int32)
     matrices = blur_matrices(taps, height, notes * (1.0 / TAP_UNIT))
 
-    planes = [piece[:height] for piece in pieces]
-    pairs = [piece[height : 3 * height].reshape(2, height, columns) for piece in pieces]
-    keep = [lax.dynamic_index_in_dim(pair, core, 0, keepdims=False) for pair in pairs]
-    give = [lax.dynamic_index_in_dim(pair, 1 - core, 0, keepdims=False) for pair in pairs]
-    got = lax.ppermute(jnp.concatenate([*planes, *give]), "gz", swap)
-    length = tiles * height
-    twin = got[:length].reshape(tiles, height, columns)
-    take = got[length:].reshape(tiles, height, columns)
-    data = [x.astype(jnp.float32) * (1.0 / DATA_UNIT) for x in [*keep, *[take[k] for k in range(tiles)]]]
-    data = [x.astype(jnp.bfloat16) for x in data]
+    plane, give = pack(where, pieces)
+    swapped = lax.ppermute(give, "gz", swap)
 
     path = [(t, 0) for t in range(tiles)] + [(t, 1) for t in reversed(range(tiles))]
     hops = []
@@ -408,8 +430,8 @@
     def plane_of(coded):
         return coded.astype(jnp.float32) * (1.0 / PLANE_UNIT) + 1.0
 
-    plane = jnp.concatenate(ordered(planes, tile))
-    twin = plane_of(jnp.concatenate(ordered([twin[k] for k in range(tiles)], tile)))
+    plane = plane.reshape(tiles * height, columns)
+    twin = plane_of(jnp.concatenate(ordered([swapped[k, 0] for k in range(tiles)], tile)))
     current = plane_of(plane)
     narrow = current.astype(jnp.bfloat16)
     at_end = (tile == 0) & (core == view)
@@ -419,7 +441,7 @@
         if not first:
             twin = lax.ppermute(current, "gz", swap)
         other = jnp.where(at_end, 0.0, plane_of(other) if first else other.astype(jnp.float32) + 1.0)
-        logs = correction_logs(me, shifts, narrow.reshape(tiles, height, columns), matrices, data)
+        logs = correction_logs(where, shifts, narrow.reshape(tiles, height, columns), matrices, pieces, swapped)
         current, *rest = update(
             views, flag, current, twin, other, logs, [jnp.float32] if last else [jnp.float32, jnp.bfloat16]
         )

time: 52 us -> 52.2 us (level)
  Pallas kernels: 5.57 us -> 6.16 us
    pallas_call x2 -> x3, Pallas kernels: 3.39 us -> 3.98 us  [the longest x2 3.39 us: correction_logs(): pl.pallas_call(correction_kernel, out_shape=jax.ShapeDtypeStruct((tiles *...]
    unnamed x14 -> x7, local copies, waits for them, and re-layouts: 1.32 us -> 1.23 us
where the time goes in v6:
time: 52.2 us; the launch traced here: 52 us
  starting transfers between devices  29.3 us (56%)
  waiting for transfers between devices  11.5 us (22%)
  Pallas kernels  6.16 us (12%)
  other arithmetic  3.13 us (6%)
  local copies, waits for them, and re-layouts  1.67 us (3%)
    ppermute x1, starting transfers between devices, plane_shards(): twin = lax.ppermute(current, 'gz', swap)  7.56 us
    ppermute x4, waiting for transfers between devices, exchange(): pieces.append(lax.ppermute(pick(k), square, pairs))  5.26 us
    ppermute x4, starting transfers between devices, exchange(): pieces.append(lax.ppermute(pick(k), square, pairs))  5.12 us
    ppermute x3, starting transfers between devices, plane_shards(): lax.ppermute(piece, 'tiles', [(t, t ^ k) for t in range(tiles)])  4.88 us
    pallas_call x2, Pallas kernels, correction_logs(): pl.pallas_call(correction_kernel, out_shape=jax.ShapeDtypeStruct((tiles *...  3.39 us
    ppermute x1, starting transfers between devices, plane_shards(): note = lax.ppermute(info, 'views', swap)  3.03 us
    ppermute x1, starting transfers between devices, plane_shards(): swapped = lax.ppermute(give, 'gz', swap)  2.63 us
    ppermute x1, waiting for transfers between devices, plane_shards(): crossed.append(lax.ppermute(mine[1:], 'views', swap))  2.58 us
  transfers between devices with their start and end apart: 15, of which 7 were waited for; matrix products, arithmetic and copies ran while one was open for 1% of the time, Pallas kernels for 5%

profile of v6, /device:TPU:0, one launch (start us, length us, event | category | flops | bytes accessed | tf_op | source)
XLA Modules:
  0.0 52.0 jit_solution(3186797246389748957)
XLA Ops:
  0.0 1.1 %multiply_convert_fusion = s16[1,1,8,128,128]{4,3,2,1,0:T(8,128)(2,1)S(1)} fusion(bf16[1,1,8,128,128]{4,3,2,1,0:T(8,128)(2,1)} %param.4), kind=kLoop, calls=%fused_computation | loop fusion | flops 393216 | bytes 524288 | tf_op jit(solution)/shard_map/convert_element_type | solution.py:399
  1.3 0.6 %copy-done.1 = f32[1,2,2,9]{3,2,1,0:T(2,128)S(1)} copy-done((f32[1,2,2,9]{3,2,1,0:T(2,128)S(1)}, f32[1,2,2,9]{3,2,1,0:T(2,128)}, u32[]{:S(2)}) %copy-start.1) | copy-done | bytes 168
  2.9 3.0 %collective-permute-start.6 = (s16[16,128]{1,0:T(8,128)(2,1)S(1)}, s16[16,128]{1,0:T(8,128)(2,1)S(1)}, u32[]{:S(2)}, u32[]{:S(2)}) collective-permute-start(s16[16,128]{1,0:T(8,128)(2,1)S(1)} %broadcast_in_dim.9), channel_id=1, source_target_pairs={{0,2},{2,0},{1,3},{3,1},{4,6},{6,4},{5,7},{7,5},{8,10},{10,8},{9,1... | collective-permute-start | bytes 12296 | tf_op jit(solution)/shard_map/ppermute | solution.py:414
  5.9 0.7 %collective-permute-start = (s16[384,128]{1,0:T(8,128)(2,1)S(1)}, s16[384,128]{1,0:T(8,128)(2,1)S(1)}, u32[]{:S(2)}, u32[]{:S(2)}) collective-permute-start(s16[384,128]{1,0:T(8,128)(2,1)S(1)} %get-tuple-element.24), channel_id=1, source_target_pairs={{0,0},{1,2},{2,1},{3,3},{4,4},{5,6},{6,5},{7,7},{8,8},{9,10},{10,9... | collective-permute-start | bytes 294920 | tf_op jit(solution)/shard_map/ppermute | solution.py:386
  6.6 1.6 %collective-permute-start.1 = (s16[384,128]{1,0:T(8,128)(2,1)S(1)}, s16[384,128]{1,0:T(8,128)(2,1)S(1)}, u32[]{:S(2)}, u32[]{:S(2)}) collective-permute-start(s16[384,128]{1,0:T(8,128)(2,1)S(1)} %get-tuple-element.23), channel_id=1, source_target_pairs={{0,4},{1,6},{2,5},{3,7},{4,0},{5,2},{6,1},{7,3},{8,12},{9,14},{10,... | collective-permute-start | bytes 294920 | tf_op jit(solution)/shard_map/ppermute | solution.py:386
  8.2 2.6 %collective-permute-start.2 = (s16[384,128]{1,0:T(8,128)(2,1)S(1)}, s16[384,128]{1,0:T(8,128)(2,1)S(1)}, u32[]{:S(2)}, u32[]{:S(2)}) collective-permute-start(s16[384,128]{1,0:T(8,128)(2,1)S(1)} %get-tuple-element.22), channel_id=1, source_target_pairs={{0,8},{1,10},{2,9},{3,11},{4,12},{5,14},{6,13},{7,15},{8,0},{9,2},... | collective-permute-start | bytes 294920 | tf_op jit(solution)/shard_map/ppermute | solution.py:386
  11.2 1.0 %blur_matrices.1.matrices_ref = bf16[2,4,256,128]{3,2,1,0:T(8,128)(2,1)S(1)} custom-call(f32[2,128]{1,0:T(2,128)S(1)} %broadcast_multiply_fusion.info_ref), custom_call_target="tpu_custom_call" | custom-call | tf_op jit(solution)/shard_map/blur_matrices/pallas_call | solution.py:192
  12.3 2.2 %collective-permute-done.2.refs_2_ = s16[384,128]{1,0:T(8,128)(2,1)S(1)} collective-permute-done((s16[384,128]{1,0:T(8,128)(2,1)S(1)}, s16[384,128]{1,0:T(8,128)(2,1)S(1)}, u32[]{:S(2)}, u32[]{:S(2)}) %collective-permute-start.2) | collective-permute-done | bytes 98336 | tf_op jit(solution)/shard_map/ppermute | solution.py:386
  14.4 3.1 %collective-permute-done.3.refs_3_ = s16[384,128]{1,0:T(8,128)(2,1)S(1)} collective-permute-done((s16[384,128]{1,0:T(8,128)(2,1)S(1)}, s16[384,128]{1,0:T(8,128)(2,1)S(1)}, u32[]{:S(2)}, u32[]{:S(2)}) %collective-permute-start.3) | collective-permute-done | bytes 98336 | tf_op jit(solution)/shard_map/ppermute | solution.py:386
  18.1 2.6 %collective-permute-start.4 = (s16[4,2,128,128]{3,2,1,0:T(8,128)(2,1)S(1)}, s16[4,2,128,128]{3,2,1,0:T(8,128)(2,1)S(1)}, u32[]{:S(2)}, u32[]{:S(2)}) collective-permute-start(s16[4,2,128,128]{3,2,1,0:T(8,128)(2,1)S(1)} %get-tuple-element.14), channel_id=1, source_target_pairs={{0,1},{1,0},{2,3},{3,2},{4,5},{5,4},{6,7},{7,6},{8,9},{9,8},{10,11... | collective-permute-start | bytes 786440 | tf_op jit(solution)/shard_map/ppermute | solution.py:422
  20.8 0.7 %collective-permute-start.5 = (s16[512,128]{1,0:T(8,128)(2,1)S(1)}, s16[512,128]{1,0:T(8,128)(2,1)S(1)}, u32[]{:S(2)}, u32[]{:S(2)}) collective-permute-start(s16[512,128]{1,0:T(8,128)(2,1)S(1)} %bitcast.69), channel_id=1, source_target_pairs={{1,4},{4,1},{5,8},{8,5},{9,12},{12,9},{13,14},{14,13},{15,10},{10,... | collective-permute-start | bytes 393224 | tf_op jit(solution)/shard_map/ppermute | solution.py:440
  22.0 1.7 %correction.2.log_ref = f32[512,128]{1,0:T(8,128)S(1)} custom-call(s32[2]{0:T(128)S(1)} %pad_add_fusion.1.where_ref, s32[2,8]{1,0:T(2,128)S(1)} %slice_convert_fusion.offsets_ref, bf16[4,128,128]{2,1,0:T(8,128)(2,1)S(1)} %add_convert_fusion.1.current_ref, bf16[2,4,256,128]{3,2,1,0:T(8,128)(2,1)S(1)} %blur_matrices.1.matrices_ref, ...), custom_call_target="tpu_custom_call" | custom-call | flops 300000000 | bytes 1500000 | tf_op jit(solution)/shard_map/correction/pallas_call | solution.py:290
  23.7 0.6 %update.2 = (f32[512,128]{1,0:T(8,128)S(1)}, bf16[512,128]{1,0:T(8,128)(2,1)S(1)}) custom-call(s32[1]{0:T(128)} %bitcast.core_ref, f32[512,128]{1,0:T(8,128)S(1)} %multiply_add_fusion.1.current_ref, f32[512,128]{1,0:T(8,128)S(1)} %multiply_add_fusion.twin_ref, f32[512,128]{1,0:T(8,128)S(1)} %add_select_fusion.1.other_ref, f32[512,128]{1,0:T(8,128)S(1)} %correction.2.log_ref), custom_call_target="tpu_custom_call" | custom-call | tf_op jit(solution)/shard_map/update/pallas_call | solution.py:351
  24.4 0.7 %collective-permute-start.8 = (f16[512,128]{1,0:T(8,128)(2,1)S(1)}, f16[512,128]{1,0:T(8,128)(2,1)S(1)}, u32[]{:S(2)}, u32[]{:S(2)}) collective-permute-start(f16[512,128]{1,0:T(8,128)(2,1)S(1)} %add_convert_fusion), channel_id=1, source_target_pairs={{1,4},{4,1},{5,8},{8,5},{9,12},{12,9},{13,14},{14,13},{15,10},{10,... | collective-permute-start | bytes 393224 | tf_op jit(solution)/shard_map/ppermute | solution.py:440
  25.1 7.6 %collective-permute-start.7 = (f32[512,128]{1,0:T(8,128)S(1)}, f32[512,128]{1,0:T(8,128)S(1)}, u32[]{:S(2)}, u32[]{:S(2)}) collective-permute-start(f32[512,128]{1,0:T(8,128)S(1)} %get-tuple-element.17.current_ref), channel_id=1, source_target_pairs={{0,1},{1,0},{2,3},{3,2},{4,5},{5,4},{6,7},{7,6},{8,9},{9,8},{10,11... | collective-permute-start | bytes 786440 | tf_op jit(solution)/shard_map/ppermute | solution.py:442
  32.6 1.7 %correction.3.log_ref = f32[512,128]{1,0:T(8,128)S(1)} custom-call(s32[2]{0:T(128)S(1)} %pad_add_fusion.1.where_ref, s32[2,8]{1,0:T(2,128)S(1)} %slice_convert_fusion.offsets_ref, bf16[4,128,128]{2,1,0:T(8,128)(2,1)S(1)} %bitcast.70, bf16[2,4,256,128]{3,2,1,0:T(8,128)(2,1)S(1)} %blur_matrices.1.matrices_ref, ...), custom_call_target="tpu_custom_call" | custom-call | flops 300000000 | bytes 1500000 | tf_op jit(solution)/shard_map/correction/pallas_call | solution.py:290
  35.1 3.3 %collective-permute-start.10 = (f16[1,128,128]{2,1,0:T(8,128)(2,1)S(1)}, f16[1,128,128]{2,1,0:T(8,128)(2,1)S(1)}, u32[]{:S(2)}, u32[]{:S(2)}) collective-permute-start(f16[1,128,128]{2,1,0:T(8,128)(2,1)S(1)} %get-tuple-element.43), channel_id=1, source_target_pairs={{0,8},{4,12},{8,0},{12,4},{1,9},{5,13},{9,1},{13,5},{2,10},{6,14},... | collective-permute-start | bytes 98312 | tf_op jit(solution)/shard_map/ppermute | solution.py:456
  38.3 1.6 %collective-permute-start.11 = (f16[1,128,128]{2,1,0:T(8,128)(2,1)S(1)}, f16[1,128,128]{2,1,0:T(8,128)(2,1)S(1)}, u32[]{:S(2)}, u32[]{:S(2)}) collective-permute-start(f16[1,128,128]{2,1,0:T(8,128)(2,1)S(1)} %get-tuple-element.42), channel_id=1, source_target_pairs={{0,12},{4,8},{8,4},{12,0},{1,13},{5,9},{9,5},{13,1},{2,14},{6,10},... | collective-permute-start | bytes 98312 | tf_op jit(solution)/shard_map/ppermute | solution.py:456
  39.9 2.2 %collective-permute-start.12 = (f16[1,128,128]{2,1,0:T(8,128)(2,1)S(1)}, f16[1,128,128]{2,1,0:T(8,128)(2,1)S(1)}, u32[]{:S(2)}, u32[]{:S(2)}) collective-permute-start(f16[1,128,128]{2,1,0:T(8,128)(2,1)S(1)} %get-tuple-element.44), channel_id=1, source_target_pairs={{0,2},{2,0},{1,3},{3,1},{4,6},{6,4},{5,7},{7,5},{8,10},{10,8},{9,1... | collective-permute-start | bytes 98312 | tf_op jit(solution)/shard_map/ppermute | solution.py:458
  42.2 2.0 %collective-permute-done.11 = f16[1,128,128]{2,1,0:T(8,128)(2,1)S(1)} collective-permute-done((f16[1,128,128]{2,1,0:T(8,128)(2,1)S(1)}, f16[1,128,128]{2,1,0:T(8,128)(2,1)S(1)}, u32[]{:S(2)}, u32[]{:S(2)}) %collective-permute-start.11) | collective-permute-done | bytes 32800 | tf_op jit(solution)/shard_map/ppermute | solution.py:456
  44.2 2.4 %collective-permute-start.13 = (f16[3,128,128]{2,1,0:T(8,128)(2,1)S(1)}, f16[3,128,128]{2,1,0:T(8,128)(2,1)S(1)}, u32[]{:S(2)}, u32[]{:S(2)}) collective-permute-start(f16[3,128,128]{2,1,0:T(8,128)(2,1)S(1)} %pad_maximum_fusion.1), channel_id=1, source_target_pairs={{0,2},{2,0},{1,3},{3,1},{4,6},{6,4},{5,7},{7,5},{8,10},{10,8},{9,1... | collective-permute-start | bytes 294920 | tf_op jit(solution)/shard_map/ppermute | solution.py:459
  46.7 2.6 %collective-permute-done.13 = f16[3,128,128]{2,1,0:T(8,128)(2,1)S(1)} collective-permute-done((f16[3,128,128]{2,1,0:T(8,128)(2,1)S(1)}, f16[3,128,128]{2,1,0:T(8,128)(2,1)S(1)}, u32[]{:S(2)}, u32[]{:S(2)}) %collective-permute-start.13) | collective-permute-done | bytes 98336 | tf_op jit(solution)/shard_map/ppermute | solution.py:459
  49.5 1.3 %collective-permute-done.14 = f16[4,128,128]{2,1,0:T(8,128)(2,1)S(1)} collective-permute-done((f16[4,128,128]{2,1,0:T(8,128)(2,1)S(1)}, f16[4,128,128]{2,1,0:T(8,128)(2,1)S(1)}, u32[]{:S(2)}, u32[]{:S(2)}) %collective-permute-start.14) | collective-permute-done | bytes 131104 | tf_op jit(solution)/shard_map/ppermute | solution.py:462
  51.2 0.9 %maximum_convert_fusion = f32[8,128,128]{2,1,0:T(8,128)} fusion(f16[2,128,128]{2,1,0:T(8,128)(2,1)S(1)} %get-tuple-element.28, f16[2,128,128]{2,1,0:T(8,128)(2,1)S(1)} %get-tuple-element.27, f16[2,128,128]{2,1,0:T(8,128)(2,1)S(1)} %get-tuple-element.26, f16[2,128,128]{2,1,0:T(8,128)(2,1)S(1)} %get-tuple-element.25), kind=kLoop, calls=%fused_computation.2 | loop fusion | flops 524288 | bytes 786432 | tf_op jit(solution)/shard_map/convert_element_type | solution.py:466
  (54 shorter events, 4.0 us)
Async XLA Ops:
  0.0 1.1 %copy-start = (f32[8,128,128]{2,1,0:T(8,128)S(1)}, f32[8,128,128]{2,1,0:T(8,128)}, u32[]{:S(2)}) copy-start(f32[8,128,128]{2,1,0:T(8,128)} %param.5) | copy-start | bytes 1572868
  1.2 0.7 %copy-start.1 = (f32[1,2,2,9]{3,2,1,0:T(2,128)S(1)}, f32[1,2,2,9]{3,2,1,0:T(2,128)}, u32[]{:S(2)}) copy-start(f32[1,2,2,9]{3,2,1,0:T(2,128)} %param.6) | copy-start | bytes 436
  2.1 0.7 %copy-start.2 = (s32[1,8]{1,0:T(1,128)S(1)}, s32[1,8]{1,0:T(1,128)}, u32[]{:S(2)}) copy-start(s32[1,8]{1,0:T(1,128)} %param.7) | copy-start | bytes 100
  2.9 8.3 %collective-permute-start.6 = (s16[16,128]{1,0:T(8,128)(2,1)S(1)}, s16[16,128]{1,0:T(8,128)(2,1)S(1)}, u32[]{:S(2)}, u32[]{:S(2)}) collective-permute-start(s16[16,128]{1,0:T(8,128)(2,1)S(1)} %broadcast_in_dim.9), channel_id=1, source_target_pairs={{0,2},{2,0},{1,3},{3,1},{4,6},{6,4},{5,7},{7,5},{8,10},{10,8},{9,1... | collective-permute-start | bytes 12296 | tf_op jit(solution)/shard_map/ppermute | solution.py:414
  5.9 6.3 %collective-permute-start = (s16[384,128]{1,0:T(8,128)(2,1)S(1)}, s16[384,128]{1,0:T(8,128)(2,1)S(1)}, u32[]{:S(2)}, u32[]{:S(2)}) collective-permute-start(s16[384,128]{1,0:T(8,128)(2,1)S(1)} %get-tuple-element.24), channel_id=1, source_target_pairs={{0,0},{1,2},{2,1},{3,3},{4,4},{5,6},{6,5},{7,7},{8,8},{9,10},{10,9... | collective-permute-start | bytes 294920 | tf_op jit(solution)/shard_map/ppermute | solution.py:386
  6.6 5.7 %collective-permute-start.1 = (s16[384,128]{1,0:T(8,128)(2,1)S(1)}, s16[384,128]{1,0:T(8,128)(2,1)S(1)}, u32[]{:S(2)}, u32[]{:S(2)}) collective-permute-start(s16[384,128]{1,0:T(8,128)(2,1)S(1)} %get-tuple-element.23), channel_id=1, source_target_pairs={{0,4},{1,6},{2,5},{3,7},{4,0},{5,2},{6,1},{7,3},{8,12},{9,14},{10,... | collective-permute-start | bytes 294920 | tf_op jit(solution)/shard_map/ppermute | solution.py:386
  8.2 6.2 %collective-permute-start.2 = (s16[384,128]{1,0:T(8,128)(2,1)S(1)}, s16[384,128]{1,0:T(8,128)(2,1)S(1)}, u32[]{:S(2)}, u32[]{:S(2)}) collective-permute-start(s16[384,128]{1,0:T(8,128)(2,1)S(1)} %get-tuple-element.22), channel_id=1, source_target_pairs={{0,8},{1,10},{2,9},{3,11},{4,12},{5,14},{6,13},{7,15},{8,0},{9,2},... | collective-permute-start | bytes 294920 | tf_op jit(solution)/shard_map/ppermute | solution.py:386
  10.8 6.7 %collective-permute-start.3 = (s16[384,128]{1,0:T(8,128)(2,1)S(1)}, s16[384,128]{1,0:T(8,128)(2,1)S(1)}, u32[]{:S(2)}, u32[]{:S(2)}) collective-permute-start(s16[384,128]{1,0:T(8,128)(2,1)S(1)} %get-tuple-element.21), channel_id=1, source_target_pairs={{0,12},{1,14},{2,13},{3,15},{4,8},{5,10},{6,9},{7,11},{8,4},{9,6},... | collective-permute-start | bytes 294920 | tf_op jit(solution)/shard_map/ppermute | solution.py:386
  18.1 3.8 %collective-permute-start.4 = (s16[4,2,128,128]{3,2,1,0:T(8,128)(2,1)S(1)}, s16[4,2,128,128]{3,2,1,0:T(8,128)(2,1)S(1)}, u32[]{:S(2)}, u32[]{:S(2)}) collective-permute-start(s16[4,2,128,128]{3,2,1,0:T(8,128)(2,1)S(1)} %get-tuple-element.14), channel_id=1, source_target_pairs={{0,1},{1,0},{2,3},{3,2},{4,5},{5,4},{6,7},{7,6},{8,9},{9,8},{10,11... | collective-permute-start | bytes 786440 | tf_op jit(solution)/shard_map/ppermute | solution.py:422
  20.8 0.8 %collective-permute-start.5 = (s16[512,128]{1,0:T(8,128)(2,1)S(1)}, s16[512,128]{1,0:T(8,128)(2,1)S(1)}, u32[]{:S(2)}, u32[]{:S(2)}) collective-permute-start(s16[512,128]{1,0:T(8,128)(2,1)S(1)} %bitcast.69), channel_id=1, source_target_pairs={{1,4},{4,1},{5,8},{8,5},{9,12},{12,9},{13,14},{14,13},{15,10},{10,... | collective-permute-start | bytes 393224 | tf_op jit(solution)/shard_map/ppermute | solution.py:440
  24.4 10.0 %collective-permute-start.8 = (f16[512,128]{1,0:T(8,128)(2,1)S(1)}, f16[512,128]{1,0:T(8,128)(2,1)S(1)}, u32[]{:S(2)}, u32[]{:S(2)}) collective-permute-start(f16[512,128]{1,0:T(8,128)(2,1)S(1)} %add_convert_fusion), channel_id=1, source_target_pairs={{1,4},{4,1},{5,8},{8,5},{9,12},{12,9},{13,14},{14,13},{15,10},{10,... | collective-permute-start | bytes 393224 | tf_op jit(solution)/shard_map/ppermute | solution.py:440
  25.1 9.3 %collective-permute-start.7 = (f32[512,128]{1,0:T(8,128)S(1)}, f32[512,128]{1,0:T(8,128)S(1)}, u32[]{:S(2)}, u32[]{:S(2)}) collective-permute-start(f32[512,128]{1,0:T(8,128)S(1)} %get-tuple-element.17.current_ref), channel_id=1, source_target_pairs={{0,1},{1,0},{2,3},{3,2},{4,5},{5,4},{6,7},{7,6},{8,9},{9,8},{10,11... | collective-permute-start | bytes 786440 | tf_op jit(solution)/shard_map/ppermute | solution.py:442
  35.1 7.1 %collective-permute-start.10 = (f16[1,128,128]{2,1,0:T(8,128)(2,1)S(1)}, f16[1,128,128]{2,1,0:T(8,128)(2,1)S(1)}, u32[]{:S(2)}, u32[]{:S(2)}) collective-permute-start(f16[1,128,128]{2,1,0:T(8,128)(2,1)S(1)} %get-tuple-element.43), channel_id=1, source_target_pairs={{0,8},{4,12},{8,0},{12,4},{1,9},{5,13},{9,1},{13,5},{2,10},{6,14},... | collective-permute-start | bytes 98312 | tf_op jit(solution)/shard_map/ppermute | solution.py:456
  38.3 5.8 %collective-permute-start.11 = (f16[1,128,128]{2,1,0:T(8,128)(2,1)S(1)}, f16[1,128,128]{2,1,0:T(8,128)(2,1)S(1)}, u32[]{:S(2)}, u32[]{:S(2)}) collective-permute-start(f16[1,128,128]{2,1,0:T(8,128)(2,1)S(1)} %get-tuple-element.42), channel_id=1, source_target_pairs={{0,12},{4,8},{8,4},{12,0},{1,13},{5,9},{9,5},{13,1},{2,14},{6,10},... | collective-permute-start | bytes 98312 | tf_op jit(solution)/shard_map/ppermute | solution.py:456
  39.9 4.3 %collective-permute-start.9 = (f16[1,128,128]{2,1,0:T(8,128)(2,1)S(1)}, f16[1,128,128]{2,1,0:T(8,128)(2,1)S(1)}, u32[]{:S(2)}, u32[]{:S(2)}) collective-permute-start(f16[1,128,128]{2,1,0:T(8,128)(2,1)S(1)} %get-tuple-element.41), channel_id=1, source_target_pairs={{0,4},{4,0},{8,12},{12,8},{1,5},{5,1},{9,13},{13,9},{2,6},{6,2},{1... | collective-permute-start | bytes 98312 | tf_op jit(solution)/shard_map/ppermute | solution.py:456
  39.9 6.7 %collective-permute-start.12 = (f16[1,128,128]{2,1,0:T(8,128)(2,1)S(1)}, f16[1,128,128]{2,1,0:T(8,128)(2,1)S(1)}, u32[]{:S(2)}, u32[]{:S(2)}) collective-permute-start(f16[1,128,128]{2,1,0:T(8,128)(2,1)S(1)} %get-tuple-element.44), channel_id=1, source_target_pairs={{0,2},{2,0},{1,3},{3,1},{4,6},{6,4},{5,7},{7,5},{8,10},{10,8},{9,1... | collective-permute-start | bytes 98312 | tf_op jit(solution)/shard_map/ppermute | solution.py:458
  44.2 5.0 %collective-permute-start.13 = (f16[3,128,128]{2,1,0:T(8,128)(2,1)S(1)}, f16[3,128,128]{2,1,0:T(8,128)(2,1)S(1)}, u32[]{:S(2)}, u32[]{:S(2)}) collective-permute-start(f16[3,128,128]{2,1,0:T(8,128)(2,1)S(1)} %pad_maximum_fusion.1), channel_id=1, source_target_pairs={{0,2},{2,0},{1,3},{3,1},{4,6},{6,4},{5,7},{7,5},{8,10},{10,8},{9,1... | collective-permute-start | bytes 294920 | tf_op jit(solution)/shard_map/ppermute | solution.py:459
  49.4 1.4 %collective-permute-start.14 = (f16[4,128,128]{2,1,0:T(8,128)(2,1)S(1)}, f16[4,128,128]{2,1,0:T(8,128)(2,1)S(1)}, u32[]{:S(2)}, u32[]{:S(2)}) collective-permute-start(f16[4,128,128]{2,1,0:T(8,128)(2,1)S(1)} %broadcast_select_fusion), channel_id=1, source_target_pairs={{0,1},{1,0},{2,3},{3,2},{4,5},{5,4},{6,7},{7,6},{8,9},{9,8},{10,11... | collective-permute-start | bytes 393224 | tf_op jit(solution)/shard_map/ppermute | solution.py:462

commit v7 on v4

--- a/solution.py
+++ b/solution.py
@@ -432,16 +432,18 @@
     for k in range(tiles):
         piece = lax.dynamic_index_in_dim(result, lax.bitwise_xor(tile, k), 0)
         pieces.append(lax.ppermute(piece, "tiles", [(t, t ^ k) for t in range(tiles)]) if k else piece)
-    mine = jnp.concatenate(pieces)
-    crossed = [lax.ppermute(pieces[0], "views", swap)]
-    crossed.append(lax.ppermute(mine[1:], "views", swap))
-    crossed = jnp.concatenate(crossed)
-    same = jnp.where(straight, mine, crossed)
-    twin = lax.ppermute(jnp.where(straight, crossed, mine), "gz", swap)
-    even, odd = jnp.where(core == 0, same, twin), jnp.where(core == 0, twin, same)
-    result = [jnp.stack([even[k], odd[k]]) for k in range(tiles)]
-    result = jnp.concatenate(ordered(result, lax.bitwise_xor(tile, end_of(core))))
-    return result.astype(jnp.float32)
+    mine = ordered([piece[0] for piece in pieces], lax.bitwise_xor(tile, end_of(core)))
+    mine, turned = jnp.stack(mine), jnp.stack(mine[::-1])
+    one_way = [(device(t, v, v), device(t, 1 - v, v)) for t in range(tiles) for v in range(2)]
+    across = [(device(t, v, 1 - v), device(t, 1 - v, v)) for t in range(tiles) for v in range(2)]
+    far_twin = lax.ppermute(turned, square, across)
+    far_same = lax.ppermute(mine, square, one_way)
+    near_twin = lax.ppermute(turned, "gz", swap)
+    same = jnp.where(straight, mine, far_same)
+    twin = jnp.where(straight, near_twin, far_twin)
+    parity = lax.broadcasted_iota(jnp.int32, (tiles, 2, height, columns), 1)
+    result = jnp.where(parity == core, same[:, None], twin[:, None])
+    return result.astype(jnp.float32).reshape(2 * tiles, height, columns)
 
 
 def one_plane_each(mesh, view_data, estimate, psf_taps, offsets):

time: 52 us -> 59.3 us (1.14)
  the two profiles are of different devices: /device:TPU:0 before, /device:TPU:1 now
where the time goes in v7:
time: 59.3 us; the launch traced here: 59 us
  starting transfers between devices  27.5 us (46%)
  waiting for transfers between devices  20.6 us (35%)
  Pallas kernels  5.57 us (9%)
  other arithmetic  3.12 us (5%)
  local copies, waits for them, and re-layouts  1.78 us (3%)
    ppermute x4, starting transfers between devices, exchange(): pieces.append(lax.ppermute(pick(k), square, pairs))  8.16 us
    ppermute x2, starting transfers between devices, plane_shards(): other = lax.ppermute(plane, square, hops)  5.74 us
    ppermute x4, waiting for transfers between devices, exchange(): pieces.append(lax.ppermute(pick(k), square, pairs))  5.3 us
    ppermute x2, waiting for transfers between devices, plane_shards(): other = lax.ppermute(plane, square, hops)  4.91 us
    ppermute x1, waiting for transfers between devices, plane_shards(): far_same = lax.ppermute(mine, square, one_way)  4.41 us
    ppermute x1, starting transfers between devices, plane_shards(): far_twin = lax.ppermute(turned, square, across)  3.97 us
    ppermute x3, starting transfers between devices, plane_shards(): lax.ppermute(piece, 'tiles', [(t, t ^ k) for t in range(tiles)])  3.61 us
    ppermute x3, waiting for transfers between devices, plane_shards(): lax.ppermute(piece, 'tiles', [(t, t ^ k) for t in range(tiles)])  3.49 us
  transfers between devices with their start and end apart: 15, of which 9 were waited for; matrix products, arithmetic and copies ran while one was open for 1% of the time, Pallas kernels for 5%

profile of v7, /device:TPU:1, one launch (start us, length us, event | category | flops | bytes accessed | tf_op | source)
XLA Modules:
  0.0 59.0 jit_solution(3696105486803046668)
XLA Ops:
  0.0 1.1 %multiply_convert_fusion = s16[1,1,8,128,128]{4,3,2,1,0:T(8,128)(2,1)S(1)} fusion(bf16[1,1,8,128,128]{4,3,2,1,0:T(8,128)(2,1)} %param.4), kind=kLoop, calls=%fused_computation | loop fusion | flops 393216 | bytes 524288 | tf_op jit(solution)/shard_map/convert_element_type | solution.py:369
  2.9 2.1 %collective-permute-start.6 = (s16[16,128]{1,0:T(8,128)(2,1)S(1)}, s16[16,128]{1,0:T(8,128)(2,1)S(1)}, u32[]{:S(2)}, u32[]{:S(2)}) collective-permute-start(s16[16,128]{1,0:T(8,128)(2,1)S(1)} %broadcast_in_dim.31), channel_id=1, source_target_pairs={{0,2},{2,0},{1,3},{3,1},{4,6},{6,4},{5,7},{7,5},{8,10},{10,8},{9,1... | collective-permute-start | bytes 12296 | tf_op jit(solution)/shard_map/ppermute | solution.py:384
  5.0 2.5 %collective-permute-start.3 = (s16[384,128]{1,0:T(8,128)(2,1)S(1)}, s16[384,128]{1,0:T(8,128)(2,1)S(1)}, u32[]{:S(2)}, u32[]{:S(2)}) collective-permute-start(s16[384,128]{1,0:T(8,128)(2,1)S(1)} %get-tuple-element.20), channel_id=1, source_target_pairs={{0,0},{1,2},{2,1},{3,3},{4,4},{5,6},{6,5},{7,7},{8,8},{9,10},{10,9... | collective-permute-start | bytes 294920 | tf_op jit(solution)/shard_map/ppermute | solution.py:356
  7.5 2.2 %collective-permute-start.2 = (s16[384,128]{1,0:T(8,128)(2,1)S(1)}, s16[384,128]{1,0:T(8,128)(2,1)S(1)}, u32[]{:S(2)}, u32[]{:S(2)}) collective-permute-start(s16[384,128]{1,0:T(8,128)(2,1)S(1)} %get-tuple-element.21), channel_id=1, source_target_pairs={{0,4},{1,6},{2,5},{3,7},{4,0},{5,2},{6,1},{7,3},{8,12},{9,14},{10,... | collective-permute-start | bytes 294920 | tf_op jit(solution)/shard_map/ppermute | solution.py:356
  9.7 3.1 %collective-permute-start.1 = (s16[384,128]{1,0:T(8,128)(2,1)S(1)}, s16[384,128]{1,0:T(8,128)(2,1)S(1)}, u32[]{:S(2)}, u32[]{:S(2)}) collective-permute-start(s16[384,128]{1,0:T(8,128)(2,1)S(1)} %get-tuple-element.22), channel_id=1, source_target_pairs={{0,8},{1,10},{2,9},{3,11},{4,12},{5,14},{6,13},{7,15},{8,0},{9,2},... | collective-permute-start | bytes 294920 | tf_op jit(solution)/shard_map/ppermute | solution.py:356
  13.3 1.0 %blur_matrices.1.matrices_ref = bf16[2,4,256,128]{3,2,1,0:T(8,128)(2,1)S(1)} custom-call(f32[2,128]{1,0:T(2,128)S(1)} %broadcast_multiply_fusion.info_ref), custom_call_target="tpu_custom_call" | custom-call | tf_op jit(solution)/shard_map/blur_matrices/pallas_call | solution.py:192
  14.3 2.9 %collective-permute-done.1 = s16[384,128]{1,0:T(8,128)(2,1)S(1)} collective-permute-done((s16[384,128]{1,0:T(8,128)(2,1)S(1)}, s16[384,128]{1,0:T(8,128)(2,1)S(1)}, u32[]{:S(2)}, u32[]{:S(2)}) %collective-permute-start.1) | collective-permute-done | bytes 98336 | tf_op jit(solution)/shard_map/ppermute | solution.py:356
  17.1 2.4 %collective-permute-done = s16[384,128]{1,0:T(8,128)(2,1)S(1)} collective-permute-done((s16[384,128]{1,0:T(8,128)(2,1)S(1)}, s16[384,128]{1,0:T(8,128)(2,1)S(1)}, u32[]{:S(2)}, u32[]{:S(2)}) %collective-permute-start) | collective-permute-done | bytes 98336 | tf_op jit(solution)/shard_map/ppermute | solution.py:356
  20.0 2.9 %collective-permute-start.5 = (s16[512,128]{1,0:T(8,128)(2,1)S(1)}, s16[512,128]{1,0:T(8,128)(2,1)S(1)}, u32[]{:S(2)}, u32[]{:S(2)}) collective-permute-start(s16[512,128]{1,0:T(8,128)(2,1)S(1)} %pad_add_fusion.1), channel_id=1, source_target_pairs={{1,4},{4,1},{5,8},{8,5},{9,12},{12,9},{13,14},{14,13},{15,10},{10,... | collective-permute-start | bytes 393224 | tf_op jit(solution)/shard_map/ppermute | solution.py:418
  23.0 3.3 %collective-permute-done.5 = s16[512,128]{1,0:T(8,128)(2,1)S(1)} collective-permute-done((s16[512,128]{1,0:T(8,128)(2,1)S(1)}, s16[512,128]{1,0:T(8,128)(2,1)S(1)}, u32[]{:S(2)}, u32[]{:S(2)}) %collective-permute-start.5) | collective-permute-done | bytes 131104 | tf_op jit(solution)/shard_map/ppermute | solution.py:418
  26.6 1.7 %correction.2.log_ref = f32[512,128]{1,0:T(8,128)S(1)} custom-call(s32[1]{0:T(128)} %bitcast.16.tile_ref, s32[2,8]{1,0:T(2,128)S(1)} %slice_convert_fusion.offsets_ref, bf16[4,128,128]{2,1,0:T(8,128)(2,1)S(1)} %bitcast.54, bf16[2,4,256,128]{3,2,1,0:T(8,128)(2,1)S(1)} %blur_matrices.1.matrices_ref, bf16[128,128]{1,0:T(8,128)(2,1)S(1)} %get-tuple-element.44.refs_0_, ...), custom_call_target="tpu_custom_call" | custom-call | flops 300000000 | bytes 1500000 | tf_op jit(solution)/shard_map/correction/pallas_call | solution.py:260
  28.9 2.9 %collective-permute-start.8 = (f16[512,128]{1,0:T(8,128)(2,1)S(1)}, f16[512,128]{1,0:T(8,128)(2,1)S(1)}, u32[]{:S(2)}, u32[]{:S(2)}) collective-permute-start(f16[512,128]{1,0:T(8,128)(2,1)S(1)} %add_convert_fusion), channel_id=1, source_target_pairs={{1,4},{4,1},{5,8},{8,5},{9,12},{12,9},{13,14},{14,13},{15,10},{10,... | collective-permute-start | bytes 393224 | tf_op jit(solution)/shard_map/ppermute | solution.py:418
  31.9 1.7 %correction.3.log_ref = f32[512,128]{1,0:T(8,128)S(1)} custom-call(s32[1]{0:T(128)} %bitcast.16.tile_ref, s32[2,8]{1,0:T(2,128)S(1)} %slice_convert_fusion.offsets_ref, bf16[4,128,128]{2,1,0:T(8,128)(2,1)S(1)} %bitcast.55, bf16[2,4,256,128]{3,2,1,0:T(8,128)(2,1)S(1)} %blur_matrices.1.matrices_ref, bf16[128,128]{1,0:T(8,128)(2,1)S(1)} %get-tuple-element.44.refs_0_, ...), custom_call_target="tpu_custom_call" | custom-call | flops 300000000 | bytes 1500000 | tf_op jit(solution)/shard_map/correction/pallas_call | solution.py:260
  33.6 1.6 %collective-permute-done.8 = f16[512,128]{1,0:T(8,128)(2,1)S(1)} collective-permute-done((f16[512,128]{1,0:T(8,128)(2,1)S(1)}, f16[512,128]{1,0:T(8,128)(2,1)S(1)}, u32[]{:S(2)}, u32[]{:S(2)}) %collective-permute-start.8) | collective-permute-done | bytes 131104 | tf_op jit(solution)/shard_map/ppermute | solution.py:418
  35.9 1.9 %collective-permute-start.10 = (f16[1,128,128]{2,1,0:T(8,128)(2,1)S(1)}, f16[1,128,128]{2,1,0:T(8,128)(2,1)S(1)}, u32[]{:S(2)}, u32[]{:S(2)}) collective-permute-start(f16[1,128,128]{2,1,0:T(8,128)(2,1)S(1)} %get-tuple-element.38), channel_id=1, source_target_pairs={{0,8},{4,12},{8,0},{12,4},{1,9},{5,13},{9,1},{13,5},{2,10},{6,14},... | collective-permute-start | bytes 98312 | tf_op jit(solution)/shard_map/ppermute | solution.py:434
  38.3 1.2 %collective-permute-start.9 = (f16[1,128,128]{2,1,0:T(8,128)(2,1)S(1)}, f16[1,128,128]{2,1,0:T(8,128)(2,1)S(1)}, u32[]{:S(2)}, u32[]{:S(2)}) collective-permute-start(f16[1,128,128]{2,1,0:T(8,128)(2,1)S(1)} %get-tuple-element.39), channel_id=1, source_target_pairs={{0,12},{4,8},{8,4},{12,0},{1,13},{5,9},{9,5},{13,1},{2,14},{6,10},... | collective-permute-start | bytes 98312 | tf_op jit(solution)/shard_map/ppermute | solution.py:434
  39.7 0.9 %collective-permute-done.11 = f16[1,128,128]{2,1,0:T(8,128)(2,1)S(1)} collective-permute-done((f16[1,128,128]{2,1,0:T(8,128)(2,1)S(1)}, f16[1,128,128]{2,1,0:T(8,128)(2,1)S(1)}, u32[]{:S(2)}, u32[]{:S(2)}) %collective-permute-start.11) | collective-permute-done | bytes 32800 | tf_op jit(solution)/shard_map/ppermute | solution.py:434
  40.6 2.5 %collective-permute-done.9 = f16[1,128,128]{2,1,0:T(8,128)(2,1)S(1)} collective-permute-done((f16[1,128,128]{2,1,0:T(8,128)(2,1)S(1)}, f16[1,128,128]{2,1,0:T(8,128)(2,1)S(1)}, u32[]{:S(2)}, u32[]{:S(2)}) %collective-permute-start.9) | collective-permute-done | bytes 32800 | tf_op jit(solution)/shard_map/ppermute | solution.py:434
  43.1 1.3 %collective-permute-start.12 = (f16[4,128,128]{2,1,0:T(8,128)(2,1)S(1)}, f16[4,128,128]{2,1,0:T(8,128)(2,1)S(1)}, u32[]{:S(2)}, u32[]{:S(2)}) collective-permute-start(f16[4,128,128]{2,1,0:T(8,128)(2,1)S(1)} %pad_maximum_fusion), channel_id=1, source_target_pairs={{0,2},{3,1},{4,6},{7,5},{8,10},{11,9},{12,14},{15,13},{16,18},{19,... | collective-permute-start | bytes 393224 | tf_op jit(solution)/shard_map/ppermute | solution.py:440
  44.4 4.4 %collective-permute-done.12 = f16[4,128,128]{2,1,0:T(8,128)(2,1)S(1)} collective-permute-done((f16[4,128,128]{2,1,0:T(8,128)(2,1)S(1)}, f16[4,128,128]{2,1,0:T(8,128)(2,1)S(1)}, u32[]{:S(2)}, u32[]{:S(2)}) %collective-permute-start.12) | collective-permute-done | bytes 131104 | tf_op jit(solution)/shard_map/ppermute | solution.py:440
  48.9 2.5 %collective-permute-start.13 = (f16[4,128,128]{2,1,0:T(8,128)(2,1)S(1)}, f16[4,128,128]{2,1,0:T(8,128)(2,1)S(1)}, u32[]{:S(2)}, u32[]{:S(2)}) collective-permute-start(f16[4,128,128]{2,1,0:T(8,128)(2,1)S(1)} %get-tuple-element.36), channel_id=1, source_target_pairs={{0,1},{1,0},{2,3},{3,2},{4,5},{5,4},{6,7},{7,6},{8,9},{9,8},{10,11... | collective-permute-start | bytes 393224 | tf_op jit(solution)/shard_map/ppermute | solution.py:441
  51.4 4.0 %collective-permute-start.14 = (f16[4,128,128]{2,1,0:T(8,128)(2,1)S(1)}, f16[4,128,128]{2,1,0:T(8,128)(2,1)S(1)}, u32[]{:S(2)}, u32[]{:S(2)}) collective-permute-start(f16[4,128,128]{2,1,0:T(8,128)(2,1)S(1)} %get-tuple-element.36), channel_id=1, source_target_pairs={{1,2},{2,1},{5,6},{6,5},{9,10},{10,9},{13,14},{14,13},{17,18},{18,... | collective-permute-start | bytes 393224 | tf_op jit(solution)/shard_map/ppermute | solution.py:439
  55.5 2.5 %collective-permute-done.14 = f16[4,128,128]{2,1,0:T(8,128)(2,1)S(1)} collective-permute-done((f16[4,128,128]{2,1,0:T(8,128)(2,1)S(1)}, f16[4,128,128]{2,1,0:T(8,128)(2,1)S(1)}, u32[]{:S(2)}, u32[]{:S(2)}) %collective-permute-start.14) | collective-permute-done | bytes 131104 | tf_op jit(solution)/shard_map/ppermute | solution.py:439
  58.1 0.9 %fusion = f32[8,128,128]{2,1,0:T(8,128)} fusion(pred[8]{0:T(512)(128)(4,1)S(1)} %iota.12, f16[4,128,128]{2,1,0:T(8,128)(2,1)S(1)} %broadcast_select_fusion, f16[4,128,128]{2,1,0:T(8,128)(2,1)S(1)} %get-tuple-element.35), kind=kLoop, calls=%fused_computation.3 | loop fusion | flops 262144 | bytes 786440 | tf_op jit(solution)/shard_map/convert_element_type | solution.py:446
  (67 shorter events, 5.2 us)
Async XLA Ops:
  0.0 1.1 %copy-start = (f32[8,128,128]{2,1,0:T(8,128)S(1)}, f32[8,128,128]{2,1,0:T(8,128)}, u32[]{:S(2)}) copy-start(f32[8,128,128]{2,1,0:T(8,128)} %param.5) | copy-start | bytes 1572868
  1.2 0.7 %copy-start.1 = (f32[1,2,2,9]{3,2,1,0:T(2,128)S(1)}, f32[1,2,2,9]{3,2,1,0:T(2,128)}, u32[]{:S(2)}) copy-start(f32[1,2,2,9]{3,2,1,0:T(2,128)} %param.6) | copy-start | bytes 436
  2.1 0.7 %copy-start.2 = (s32[1,8]{1,0:T(1,128)S(1)}, s32[1,8]{1,0:T(1,128)}, u32[]{:S(2)}) copy-start(s32[1,8]{1,0:T(1,128)} %param.7) | copy-start | bytes 100
  2.9 10.3 %collective-permute-start.6 = (s16[16,128]{1,0:T(8,128)(2,1)S(1)}, s16[16,128]{1,0:T(8,128)(2,1)S(1)}, u32[]{:S(2)}, u32[]{:S(2)}) collective-permute-start(s16[16,128]{1,0:T(8,128)(2,1)S(1)} %broadcast_in_dim.31), channel_id=1, source_target_pairs={{0,2},{2,0},{1,3},{3,1},{4,6},{6,4},{5,7},{7,5},{8,10},{10,8},{9,1... | collective-permute-start | bytes 12296 | tf_op jit(solution)/shard_map/ppermute | solution.py:384
  5.0 9.3 %collective-permute-start.3 = (s16[384,128]{1,0:T(8,128)(2,1)S(1)}, s16[384,128]{1,0:T(8,128)(2,1)S(1)}, u32[]{:S(2)}, u32[]{:S(2)}) collective-permute-start(s16[384,128]{1,0:T(8,128)(2,1)S(1)} %get-tuple-element.20), channel_id=1, source_target_pairs={{0,0},{1,2},{2,1},{3,3},{4,4},{5,6},{6,5},{7,7},{8,8},{9,10},{10,9... | collective-permute-start | bytes 294920 | tf_op jit(solution)/shard_map/ppermute | solution.py:356
  7.5 6.8 %collective-permute-start.2 = (s16[384,128]{1,0:T(8,128)(2,1)S(1)}, s16[384,128]{1,0:T(8,128)(2,1)S(1)}, u32[]{:S(2)}, u32[]{:S(2)}) collective-permute-start(s16[384,128]{1,0:T(8,128)(2,1)S(1)} %get-tuple-element.21), channel_id=1, source_target_pairs={{0,4},{1,6},{2,5},{3,7},{4,0},{5,2},{6,1},{7,3},{8,12},{9,14},{10,... | collective-permute-start | bytes 294920 | tf_op jit(solution)/shard_map/ppermute | solution.py:356
  9.7 7.4 %collective-permute-start.1 = (s16[384,128]{1,0:T(8,128)(2,1)S(1)}, s16[384,128]{1,0:T(8,128)(2,1)S(1)}, u32[]{:S(2)}, u32[]{:S(2)}) collective-permute-start(s16[384,128]{1,0:T(8,128)(2,1)S(1)} %get-tuple-element.22), channel_id=1, source_target_pairs={{0,8},{1,10},{2,9},{3,11},{4,12},{5,14},{6,13},{7,15},{8,0},{9,2},... | collective-permute-start | bytes 294920 | tf_op jit(solution)/shard_map/ppermute | solution.py:356
  12.9 6.7 %collective-permute-start = (s16[384,128]{1,0:T(8,128)(2,1)S(1)}, s16[384,128]{1,0:T(8,128)(2,1)S(1)}, u32[]{:S(2)}, u32[]{:S(2)}) collective-permute-start(s16[384,128]{1,0:T(8,128)(2,1)S(1)} %get-tuple-element.19), channel_id=1, source_target_pairs={{0,12},{1,14},{2,13},{3,15},{4,8},{5,10},{6,9},{7,11},{8,4},{9,6},... | collective-permute-start | bytes 294920 | tf_op jit(solution)/shard_map/ppermute | solution.py:356
  19.9 6.4 %collective-permute-start.4 = (s16[1024,128]{1,0:T(8,128)(2,1)S(1)}, s16[1024,128]{1,0:T(8,128)(2,1)S(1)}, u32[]{:S(2)}, u32[]{:S(2)}) collective-permute-start(s16[1024,128]{1,0:T(8,128)(2,1)S(1)} %bitcast_dynamic-update-slice_fusion), channel_id=1, source_target_pairs={{0,1},{1,0},{2,3},{3,2},{4,5},{5,4},{6,7},{7,6},{8,9},{9,8},{10,11... | collective-permute-start | bytes 786440 | tf_op jit(solution)/shard_map/ppermute | solution.py:395
  20.0 6.3 %collective-permute-start.5 = (s16[512,128]{1,0:T(8,128)(2,1)S(1)}, s16[512,128]{1,0:T(8,128)(2,1)S(1)}, u32[]{:S(2)}, u32[]{:S(2)}) collective-permute-start(s16[512,128]{1,0:T(8,128)(2,1)S(1)} %pad_add_fusion.1), channel_id=1, source_target_pairs={{1,4},{4,1},{5,8},{8,5},{9,12},{12,9},{13,14},{14,13},{15,10},{10,... | collective-permute-start | bytes 393224 | tf_op jit(solution)/shard_map/ppermute | solution.py:418
  28.9 6.3 %collective-permute-start.8 = (f16[512,128]{1,0:T(8,128)(2,1)S(1)}, f16[512,128]{1,0:T(8,128)(2,1)S(1)}, u32[]{:S(2)}, u32[]{:S(2)}) collective-permute-start(f16[512,128]{1,0:T(8,128)(2,1)S(1)} %add_convert_fusion), channel_id=1, source_target_pairs={{1,4},{4,1},{5,8},{8,5},{9,12},{12,9},{13,14},{14,13},{15,10},{10,... | collective-permute-start | bytes 393224 | tf_op jit(solution)/shard_map/ppermute | solution.py:418
  31.8 3.4 %collective-permute-start.7 = (f32[512,128]{1,0:T(8,128)S(1)}, f32[512,128]{1,0:T(8,128)S(1)}, u32[]{:S(2)}, u32[]{:S(2)}) collective-permute-start(f32[512,128]{1,0:T(8,128)S(1)} %get-tuple-element.13.current_ref), channel_id=1, source_target_pairs={{0,1},{1,0},{2,3},{3,2},{4,5},{5,4},{6,7},{7,6},{8,9},{9,8},{10,11... | collective-permute-start | bytes 786440 | tf_op jit(solution)/shard_map/ppermute | solution.py:420
  35.9 3.7 %collective-permute-start.10 = (f16[1,128,128]{2,1,0:T(8,128)(2,1)S(1)}, f16[1,128,128]{2,1,0:T(8,128)(2,1)S(1)}, u32[]{:S(2)}, u32[]{:S(2)}) collective-permute-start(f16[1,128,128]{2,1,0:T(8,128)(2,1)S(1)} %get-tuple-element.38), channel_id=1, source_target_pairs={{0,8},{4,12},{8,0},{12,4},{1,9},{5,13},{9,1},{13,5},{2,10},{6,14},... | collective-permute-start | bytes 98312 | tf_op jit(solution)/shard_map/ppermute | solution.py:434
  37.8 2.8 %collective-permute-start.11 = (f16[1,128,128]{2,1,0:T(8,128)(2,1)S(1)}, f16[1,128,128]{2,1,0:T(8,128)(2,1)S(1)}, u32[]{:S(2)}, u32[]{:S(2)}) collective-permute-start(f16[1,128,128]{2,1,0:T(8,128)(2,1)S(1)} %get-tuple-element.37), channel_id=1, source_target_pairs={{0,4},{4,0},{8,12},{12,8},{1,5},{5,1},{9,13},{13,9},{2,6},{6,2},{1... | collective-permute-start | bytes 98312 | tf_op jit(solution)/shard_map/ppermute | solution.py:434
  38.3 4.7 %collective-permute-start.9 = (f16[1,128,128]{2,1,0:T(8,128)(2,1)S(1)}, f16[1,128,128]{2,1,0:T(8,128)(2,1)S(1)}, u32[]{:S(2)}, u32[]{:S(2)}) collective-permute-start(f16[1,128,128]{2,1,0:T(8,128)(2,1)S(1)} %get-tuple-element.39), channel_id=1, source_target_pairs={{0,12},{4,8},{8,4},{12,0},{1,13},{5,9},{9,5},{13,1},{2,14},{6,10},... | collective-permute-start | bytes 98312 | tf_op jit(solution)/shard_map/ppermute | solution.py:434
  43.1 5.7 %collective-permute-start.12 = (f16[4,128,128]{2,1,0:T(8,128)(2,1)S(1)}, f16[4,128,128]{2,1,0:T(8,128)(2,1)S(1)}, u32[]{:S(2)}, u32[]{:S(2)}) collective-permute-start(f16[4,128,128]{2,1,0:T(8,128)(2,1)S(1)} %pad_maximum_fusion), channel_id=1, source_target_pairs={{0,2},{3,1},{4,6},{7,5},{8,10},{11,9},{12,14},{15,13},{16,18},{19,... | collective-permute-start | bytes 393224 | tf_op jit(solution)/shard_map/ppermute | solution.py:440
  48.9 6.6 %collective-permute-start.13 = (f16[4,128,128]{2,1,0:T(8,128)(2,1)S(1)}, f16[4,128,128]{2,1,0:T(8,128)(2,1)S(1)}, u32[]{:S(2)}, u32[]{:S(2)}) collective-permute-start(f16[4,128,128]{2,1,0:T(8,128)(2,1)S(1)} %get-tuple-element.36), channel_id=1, source_target_pairs={{0,1},{1,0},{2,3},{3,2},{4,5},{5,4},{6,7},{7,6},{8,9},{9,8},{10,11... | collective-permute-start | bytes 393224 | tf_op jit(solution)/shard_map/ppermute | solution.py:441
  51.4 6.6 %collective-permute-start.14 = (f16[4,128,128]{2,1,0:T(8,128)(2,1)S(1)}, f16[4,128,128]{2,1,0:T(8,128)(2,1)S(1)}, u32[]{:S(2)}, u32[]{:S(2)}) collective-permute-start(f16[4,128,128]{2,1,0:T(8,128)(2,1)S(1)} %get-tuple-element.36), channel_id=1, source_target_pairs={{1,2},{2,1},{5,6},{6,5},{9,10},{10,9},{13,14},{14,13},{17,18},{18,... | collective-permute-start | bytes 393224 | tf_op jit(solution)/shard_map/ppermute | solution.py:439

commit v8 on v4

--- a/solution.py
+++ b/solution.py
@@ -349,12 +349,9 @@
             placed.append(chosen)
         return placed
 
-    def exchange(pick):
-        pieces = []
-        for k in range(tiles):
-            pairs = [(device(t, v, g), device(t ^ k, g, v)) for t in range(tiles) for v in range(2) for g in range(2)]
-            pieces.append(lax.ppermute(pick(k), square, pairs))
-        return pieces
+    def transfer(piece, k):
+        pairs = [(device(t, v, g), device(t ^ k, g, v)) for t in range(tiles) for v in range(2) for g in range(2)]
+        return lax.ppermute(piece, square, pairs)
 
     def end_of(chain):
         return jnp.where(chain == 0, 0, tiles - 1)
@@ -370,11 +367,17 @@
     payload = jnp.concatenate([wide, data], axis=1).reshape(tiles, 3 * height, columns)
     payload, psf_taps, offsets = lax.optimization_barrier((payload, psf_taps, offsets))
 
-    def for_tile(k):
+    planes, pairs = [], []
+    for k in range(tiles):
         place = lax.bitwise_xor(lax.bitwise_xor(tile, k), end_of(core))
-        return lax.dynamic_index_in_dim(payload, place, 0, keepdims=False)
-
-    pieces = exchange(for_tile)
+        piece = lax.dynamic_index_in_dim(payload, place, 0, keepdims=False)
+        if k > 1:
+            planes.append(transfer(piece[:height], k))
+            pairs.append(transfer(piece[height:], k))
+        else:
+            piece = transfer(piece, k)
+            planes.append(piece[:height])
+            pairs.append(piece[height:])
 
     profiles = [psf_taps.reshape(-1), psf_taps[..., ::-1].reshape(-1)]
     info = [lax.reduce_precision(p, 8, 7) * TAP_UNIT for p in profiles]
@@ -388,8 +391,7 @@
     shifts = notes[:, 8 * taps : 8 * taps + blocks].astype(jnp.int32)
     matrices = blur_matrices(taps, height, notes * (1.0 / TAP_UNIT))
 
-    planes = [piece[:height] for piece in pieces]
-    pairs = [piece[height : 3 * height].reshape(2, height, columns) for piece in pieces]
+    pairs = [pair.reshape(2, height, columns) for pair in pairs]
     keep = [lax.dynamic_index_in_dim(pair, core, 0, keepdims=False) for pair in pairs]
     give = [lax.dynamic_index_in_dim(pair, 1 - core, 0, keepdims=False) for pair in pairs]
     got = lax.ppermute(jnp.concatenate([*planes, *give]), "gz", swap)
@@ -435,13 +437,16 @@
     mine = jnp.concatenate(pieces)
     crossed = [lax.ppermute(pieces[0], "views", swap)]
     crossed.append(lax.ppermute(mine[1:], "views", swap))
-    crossed = jnp.concatenate(crossed)
-    same = jnp.where(straight, mine, crossed)
-    twin = lax.ppermute(jnp.where(straight, crossed, mine), "gz", swap)
-    even, odd = jnp.where(core == 0, same, twin), jnp.where(core == 0, twin, same)
-    result = [jnp.stack([even[k], odd[k]]) for k in range(tiles)]
-    result = jnp.concatenate(ordered(result, lax.bitwise_xor(tile, end_of(core))))
-    return result.astype(jnp.float32)
+    crossed = [crossed[0][0], *[crossed[1][k] for k in range(tiles - 1)]]
+    mine = [mine[k] for k in range(tiles)]
+    here = lax.bitwise_xor(tile, end_of(core))
+    send = [jnp.where(straight, c, m) for c, m in zip(crossed, mine)]
+    send = jnp.stack(ordered(send, lax.bitwise_xor(tile, end_of(1 - core))))
+    twin = lax.ppermute(send, "gz", swap)
+    same = jnp.stack(ordered([jnp.where(straight, m, c) for c, m in zip(crossed, mine)], here))
+    parity = lax.broadcasted_iota(jnp.int32, (tiles, 2, height, columns), 1)
+    result = jnp.where(parity == core, same[:, None], twin[:, None])
+    return result.astype(jnp.float32).reshape(2 * tiles, height, columns)
 
 
 def one_plane_each(mesh, view_data, estimate, psf_taps, offsets):

time: 52 us -> 57.3 us (1.10)
  starting transfers between devices: 29.2 us -> 35 us
    ppermute x5 -> x7, starting transfers between devices: 5.19 us -> 11.4 us  [the longest x6 11.3 us: transfer(): return lax.ppermute(piece, square, pairs)]
    ppermute x1, starting transfers between devices: 7.49 us -> 4.51 us  [plane_shards(): twin = lax.ppermute(current, 'gz', swap)]
    ppermute x1, starting transfers between devices: 2.63 us -> 5.28 us  [plane_shards(): got = lax.ppermute(jnp.concatenate([*planes, *give]), 'gz', swap)]
    ppermute x5 -> x7, waiting for transfers between devices: 6.66 us -> 5.52 us  [the longest x6 4.29 us: transfer(): return lax.ppermute(piece, square, pairs)]
    ppermute x1, waiting for transfers between devices: 0.32 us -> 1.04 us  [plane_shards(): got = lax.ppermute(jnp.concatenate([*planes, *give]), 'gz', swap)]
    unnamed x14 -> x12, local copies, waits for them, and re-layouts: 1.32 us -> 1.3 us
  transfers between devices with their start and end apart: 15 -> 17, of which waited for: 7 -> 7; matrix products, arithmetic and copies ran while one was open for 1% -> 1% of each run, Pallas kernels for 5% -> 5%
where the time goes in v8:
time: 57.3 us; the launch traced here: 57.1 us
  starting transfers between devices  35 us (61%)
  waiting for transfers between devices  11.1 us (19%)
  Pallas kernels  5.56 us (10%)
  other arithmetic  3.21 us (6%)
  local copies, waits for them, and re-layouts  1.77 us (3%)
    ppermute x6, starting transfers between devices, transfer(): return lax.ppermute(piece, square, pairs)  11.3 us
    ppermute x1, starting transfers between devices, plane_shards(): got = lax.ppermute(jnp.concatenate([*planes, *give]), 'gz', swap)  5.28 us
    ppermute x1, starting transfers between devices, plane_shards(): twin = lax.ppermute(current, 'gz', swap)  4.51 us
    ppermute x3, starting transfers between devices, plane_shards(): lax.ppermute(piece, 'tiles', [(t, t ^ k) for t in range(tiles)])  4.45 us
    ppermute x6, waiting for transfers between devices, transfer(): return lax.ppermute(piece, square, pairs)  4.29 us
    pallas_call x2, Pallas kernels, correction_logs(): pl.pallas_call(functools.partial(correction_kernel, tiles), out_shape=jax...  3.39 us
    ppermute x1, starting transfers between devices, plane_shards(): note = lax.ppermute(info, 'views', swap)  3.03 us
    ppermute x1, waiting for transfers between devices, plane_shards(): crossed.append(lax.ppermute(mine[1:], 'views', swap))  2.96 us
  transfers between devices with their start and end apart: 17, of which 7 were waited for; matrix products, arithmetic and copies ran while one was open for 1% of the time, Pallas kernels for 5%

profile of v8, /device:TPU:0, one launch (start us, length us, event | category | flops | bytes accessed | tf_op | source)
XLA Modules:
  0.0 57.1 jit_solution(16928886737510090781)
XLA Ops:
  0.0 1.1 %multiply_convert_fusion = s16[1,1,8,128,128]{4,3,2,1,0:T(8,128)(2,1)S(1)} fusion(bf16[1,1,8,128,128]{4,3,2,1,0:T(8,128)(2,1)} %param.4), kind=kLoop, calls=%fused_computation | loop fusion | flops 393216 | bytes 524288 | tf_op jit(solution)/shard_map/convert_element_type | solution.py:366
  2.9 3.0 %collective-permute-start.8 = (s16[16,128]{1,0:T(8,128)(2,1)S(1)}, s16[16,128]{1,0:T(8,128)(2,1)S(1)}, u32[]{:S(2)}, u32[]{:S(2)}) collective-permute-start(s16[16,128]{1,0:T(8,128)(2,1)S(1)} %broadcast_in_dim.31), channel_id=1, source_target_pairs={{0,2},{2,0},{1,3},{3,1},{4,6},{6,4},{5,7},{7,5},{8,10},{10,8},{9,1... | collective-permute-start | bytes 12296 | tf_op jit(solution)/shard_map/ppermute | solution.py:387
  5.9 3.6 %collective-permute-start = (s16[128,128]{1,0:T(8,128)(2,1)S(1)}, s16[128,128]{1,0:T(8,128)(2,1)S(1)}, u32[]{:S(2)}, u32[]{:S(2)}) collective-permute-start(s16[128,128]{1,0:T(8,128)(2,1)S(1)} %get-tuple-element.29), channel_id=1, source_target_pairs={{0,12},{1,14},{2,13},{3,15},{4,8},{5,10},{6,9},{7,11},{8,4},{9,6},... | collective-permute-start | bytes 98312 | tf_op jit(solution)/shard_map/ppermute | solution.py:354
  10.2 0.8 %collective-permute-start.2 = (s16[384,128]{1,0:T(8,128)(2,1)S(1)}, s16[384,128]{1,0:T(8,128)(2,1)S(1)}, u32[]{:S(2)}, u32[]{:S(2)}) collective-permute-start(s16[384,128]{1,0:T(8,128)(2,1)S(1)} %get-tuple-element.27), channel_id=1, source_target_pairs={{0,4},{1,6},{2,5},{3,7},{4,0},{5,2},{6,1},{7,3},{8,12},{9,14},{10,... | collective-permute-start | bytes 294920 | tf_op jit(solution)/shard_map/ppermute | solution.py:354
  11.1 2.2 %collective-permute-start.4 = (s16[256,128]{1,0:T(8,128)(2,1)S(1)}, s16[256,128]{1,0:T(8,128)(2,1)S(1)}, u32[]{:S(2)}, u32[]{:S(2)}) collective-permute-start(s16[256,128]{1,0:T(8,128)(2,1)S(1)} %get-tuple-element.26), channel_id=1, source_target_pairs={{0,8},{1,10},{2,9},{3,11},{4,12},{5,14},{6,13},{7,15},{8,0},{9,2},... | collective-permute-start | bytes 196616 | tf_op jit(solution)/shard_map/ppermute | solution.py:354
  13.4 1.0 %blur_matrices.1.matrices_ref = bf16[2,4,256,128]{3,2,1,0:T(8,128)(2,1)S(1)} custom-call(f32[2,128]{1,0:T(2,128)S(1)} %broadcast_multiply_fusion.info_ref), custom_call_target="tpu_custom_call" | custom-call | tf_op jit(solution)/shard_map/blur_matrices/pallas_call | solution.py:192
  14.4 2.0 %collective-permute-done.4 = s16[256,128]{1,0:T(8,128)(2,1)S(1)} collective-permute-done((s16[256,128]{1,0:T(8,128)(2,1)S(1)}, s16[256,128]{1,0:T(8,128)(2,1)S(1)}, u32[]{:S(2)}, u32[]{:S(2)}) %collective-permute-start.4) | collective-permute-done | bytes 65568 | tf_op jit(solution)/shard_map/ppermute | solution.py:354
  16.4 4.0 %collective-permute-start.5 = (s16[256,128]{1,0:T(8,128)(2,1)S(1)}, s16[256,128]{1,0:T(8,128)(2,1)S(1)}, u32[]{:S(2)}, u32[]{:S(2)}) collective-permute-start(s16[256,128]{1,0:T(8,128)(2,1)S(1)} %get-tuple-element.25), channel_id=1, source_target_pairs={{0,12},{1,14},{2,13},{3,15},{4,8},{5,10},{6,9},{7,11},{8,4},{9,6},... | collective-permute-start | bytes 196616 | tf_op jit(solution)/shard_map/ppermute | solution.py:354
  20.4 2.3 %collective-permute-done.5 = s16[256,128]{1,0:T(8,128)(2,1)S(1)} collective-permute-done((s16[256,128]{1,0:T(8,128)(2,1)S(1)}, s16[256,128]{1,0:T(8,128)(2,1)S(1)}, u32[]{:S(2)}, u32[]{:S(2)}) %collective-permute-start.5) | collective-permute-done | bytes 65568 | tf_op jit(solution)/shard_map/ppermute | solution.py:354
  23.1 0.7 %collective-permute-start.7 = (s16[512,128]{1,0:T(8,128)(2,1)S(1)}, s16[512,128]{1,0:T(8,128)(2,1)S(1)}, u32[]{:S(2)}, u32[]{:S(2)}) collective-permute-start(s16[512,128]{1,0:T(8,128)(2,1)S(1)} %pad_add_fusion.1), channel_id=1, source_target_pairs={{1,4},{4,1},{5,8},{8,5},{9,12},{12,9},{13,14},{14,13},{15,10},{10,... | collective-permute-start | bytes 393224 | tf_op jit(solution)/shard_map/ppermute | solution.py:420
  23.8 5.3 %collective-permute-start.6 = (s16[1024,128]{1,0:T(8,128)(2,1)S(1)}, s16[1024,128]{1,0:T(8,128)(2,1)S(1)}, u32[]{:S(2)}, u32[]{:S(2)}) collective-permute-start(s16[1024,128]{1,0:T(8,128)(2,1)S(1)} %bitcast_dynamic-update-slice_fusion), channel_id=1, source_target_pairs={{0,1},{1,0},{2,3},{3,2},{4,5},{5,4},{6,7},{7,6},{8,9},{9,8},{10,11... | collective-permute-start | bytes 786440 | tf_op jit(solution)/shard_map/ppermute | solution.py:397
  29.2 1.0 %collective-permute-done.6 = s16[1024,128]{1,0:T(8,128)(2,1)S(1)} collective-permute-done((s16[1024,128]{1,0:T(8,128)(2,1)S(1)}, s16[1024,128]{1,0:T(8,128)(2,1)S(1)}, u32[]{:S(2)}, u32[]{:S(2)}) %collective-permute-start.6) | collective-permute-done | bytes 262176 | tf_op jit(solution)/shard_map/ppermute | solution.py:397
  30.4 1.7 %correction.2.log_ref = f32[512,128]{1,0:T(8,128)S(1)} custom-call(s32[1]{0:T(128)} %bitcast.18.tile_ref, s32[2,8]{1,0:T(2,128)S(1)} %slice_convert_fusion.offsets_ref, bf16[4,128,128]{2,1,0:T(8,128)(2,1)S(1)} %bitcast.58, bf16[2,4,256,128]{3,2,1,0:T(8,128)(2,1)S(1)} %blur_matrices.1.matrices_ref, bf16[128,128]{1,0:T(8,128)(2,1)S(1)} %get-tuple-element.63.refs_0_, ...), custom_call_target="tpu_custom_call" | custom-call | flops 300000000 | bytes 1500000 | tf_op jit(solution)/shard_map/correction/pallas_call | solution.py:260
  33.4 4.5 %collective-permute-start.9 = (f32[512,128]{1,0:T(8,128)S(1)}, f32[512,128]{1,0:T(8,128)S(1)}, u32[]{:S(2)}, u32[]{:S(2)}) collective-permute-start(f32[512,128]{1,0:T(8,128)S(1)} %get-tuple-element.13.current_ref), channel_id=1, source_target_pairs={{0,1},{1,0},{2,3},{3,2},{4,5},{5,4},{6,7},{7,6},{8,9},{9,8},{10,11... | collective-permute-start | bytes 786440 | tf_op jit(solution)/shard_map/ppermute | solution.py:422
  37.9 1.7 %correction.3.log_ref = f32[512,128]{1,0:T(8,128)S(1)} custom-call(s32[1]{0:T(128)} %bitcast.18.tile_ref, s32[2,8]{1,0:T(2,128)S(1)} %slice_convert_fusion.offsets_ref, bf16[4,128,128]{2,1,0:T(8,128)(2,1)S(1)} %bitcast.59, bf16[2,4,256,128]{3,2,1,0:T(8,128)(2,1)S(1)} %blur_matrices.1.matrices_ref, bf16[128,128]{1,0:T(8,128)(2,1)S(1)} %get-tuple-element.63.refs_0_, ...), custom_call_target="tpu_custom_call" | custom-call | flops 300000000 | bytes 1500000 | tf_op jit(solution)/shard_map/correction/pallas_call | solution.py:260
  40.4 3.7 %collective-permute-start.11 = (f16[1,128,128]{2,1,0:T(8,128)(2,1)S(1)}, f16[1,128,128]{2,1,0:T(8,128)(2,1)S(1)}, u32[]{:S(2)}, u32[]{:S(2)}) collective-permute-start(f16[1,128,128]{2,1,0:T(8,128)(2,1)S(1)} %get-tuple-element.57), channel_id=1, source_target_pairs={{0,12},{4,8},{8,4},{12,0},{1,13},{5,9},{9,5},{13,1},{2,14},{6,10},... | collective-permute-start | bytes 98312 | tf_op jit(solution)/shard_map/ppermute | solution.py:436
  44.1 0.7 %collective-permute-start.13 = (f16[1,128,128]{2,1,0:T(8,128)(2,1)S(1)}, f16[1,128,128]{2,1,0:T(8,128)(2,1)S(1)}, u32[]{:S(2)}, u32[]{:S(2)}) collective-permute-start(f16[1,128,128]{2,1,0:T(8,128)(2,1)S(1)} %get-tuple-element.55), channel_id=1, source_target_pairs={{0,8},{4,12},{8,0},{12,4},{1,9},{5,13},{9,1},{13,5},{2,10},{6,14},... | collective-permute-start | bytes 98312 | tf_op jit(solution)/shard_map/ppermute | solution.py:436
  44.8 2.5 %collective-permute-start.15 = (f16[1,128,128]{2,1,0:T(8,128)(2,1)S(1)}, f16[1,128,128]{2,1,0:T(8,128)(2,1)S(1)}, u32[]{:S(2)}, u32[]{:S(2)}) collective-permute-start(f16[1,128,128]{2,1,0:T(8,128)(2,1)S(1)} %get-tuple-element.54), channel_id=1, source_target_pairs={{0,2},{2,0},{1,3},{3,1},{4,6},{6,4},{5,7},{7,5},{8,10},{10,8},{9,1... | collective-permute-start | bytes 98312 | tf_op jit(solution)/shard_map/ppermute | solution.py:438
  47.4 0.9 %collective-permute-done.12 = f16[1,128,128]{2,1,0:T(8,128)(2,1)S(1)} collective-permute-done((f16[1,128,128]{2,1,0:T(8,128)(2,1)S(1)}, f16[1,128,128]{2,1,0:T(8,128)(2,1)S(1)}, u32[]{:S(2)}, u32[]{:S(2)}) %collective-permute-start.12) | collective-permute-done | bytes 32800 | tf_op jit(solution)/shard_map/ppermute | solution.py:436
  48.2 0.7 %collective-permute-done.13 = f16[1,128,128]{2,1,0:T(8,128)(2,1)S(1)} collective-permute-done((f16[1,128,128]{2,1,0:T(8,128)(2,1)S(1)}, f16[1,128,128]{2,1,0:T(8,128)(2,1)S(1)}, u32[]{:S(2)}, u32[]{:S(2)}) %collective-permute-start.13) | collective-permute-done | bytes 32800 | tf_op jit(solution)/shard_map/ppermute | solution.py:436
  48.9 2.5 %collective-permute-start.14 = (f16[3,128,128]{2,1,0:T(8,128)(2,1)S(1)}, f16[3,128,128]{2,1,0:T(8,128)(2,1)S(1)}, u32[]{:S(2)}, u32[]{:S(2)}) collective-permute-start(f16[3,128,128]{2,1,0:T(8,128)(2,1)S(1)} %pad_maximum_fusion.2), channel_id=1, source_target_pairs={{0,2},{2,0},{1,3},{3,1},{4,6},{6,4},{5,7},{7,5},{8,10},{10,8},{9,1... | collective-permute-start | bytes 294920 | tf_op jit(solution)/shard_map/ppermute | solution.py:439
  51.6 3.0 %collective-permute-done.14 = f16[3,128,128]{2,1,0:T(8,128)(2,1)S(1)} collective-permute-done((f16[3,128,128]{2,1,0:T(8,128)(2,1)S(1)}, f16[3,128,128]{2,1,0:T(8,128)(2,1)S(1)}, u32[]{:S(2)}, u32[]{:S(2)}) %collective-permute-start.14) | collective-permute-done | bytes 98336 | tf_op jit(solution)/shard_map/ppermute | solution.py:439
  54.9 1.2 %collective-permute-done.16 = f16[4,128,128]{2,1,0:T(8,128)(2,1)S(1)} collective-permute-done((f16[4,128,128]{2,1,0:T(8,128)(2,1)S(1)}, f16[4,128,128]{2,1,0:T(8,128)(2,1)S(1)}, u32[]{:S(2)}, u32[]{:S(2)}) %collective-permute-start.16) | collective-permute-done | bytes 131104 | tf_op jit(solution)/shard_map/ppermute | solution.py:445
  56.2 0.9 %fusion = f32[8,128,128]{2,1,0:T(8,128)} fusion(pred[8]{0:T(512)(128)(4,1)S(1)} %iota.12, f16[4,128,128]{2,1,0:T(8,128)(2,1)S(1)} %collective-permute-done.16, f16[4,128,128]{2,1,0:T(8,128)(2,1)S(1)} %pad_maximum_fusion), kind=kLoop, calls=%fused_computation.3 | loop fusion | flops 262144 | bytes 786440 | tf_op jit(solution)/shard_map/convert_element_type | solution.py:449
  (73 shorter events, 5.5 us)
Async XLA Ops:
  0.0 1.1 %copy-start = (f32[8,128,128]{2,1,0:T(8,128)S(1)}, f32[8,128,128]{2,1,0:T(8,128)}, u32[]{:S(2)}) copy-start(f32[8,128,128]{2,1,0:T(8,128)} %param.5) | copy-start | bytes 1572868
  1.2 0.7 %copy-start.1 = (f32[1,2,2,9]{3,2,1,0:T(2,128)S(1)}, f32[1,2,2,9]{3,2,1,0:T(2,128)}, u32[]{:S(2)}) copy-start(f32[1,2,2,9]{3,2,1,0:T(2,128)} %param.6) | copy-start | bytes 436
  2.1 0.7 %copy-start.2 = (s32[1,8]{1,0:T(1,128)S(1)}, s32[1,8]{1,0:T(1,128)}, u32[]{:S(2)}) copy-start(s32[1,8]{1,0:T(1,128)} %param.7) | copy-start | bytes 100
  2.9 8.2 %collective-permute-start.8 = (s16[16,128]{1,0:T(8,128)(2,1)S(1)}, s16[16,128]{1,0:T(8,128)(2,1)S(1)}, u32[]{:S(2)}, u32[]{:S(2)}) collective-permute-start(s16[16,128]{1,0:T(8,128)(2,1)S(1)} %broadcast_in_dim.31), channel_id=1, source_target_pairs={{0,2},{2,0},{1,3},{3,1},{4,6},{6,4},{5,7},{7,5},{8,10},{10,8},{9,1... | collective-permute-start | bytes 12296 | tf_op jit(solution)/shard_map/ppermute | solution.py:387
  5.9 16.8 %collective-permute-start = (s16[128,128]{1,0:T(8,128)(2,1)S(1)}, s16[128,128]{1,0:T(8,128)(2,1)S(1)}, u32[]{:S(2)}, u32[]{:S(2)}) collective-permute-start(s16[128,128]{1,0:T(8,128)(2,1)S(1)} %get-tuple-element.29), channel_id=1, source_target_pairs={{0,12},{1,14},{2,13},{3,15},{4,8},{5,10},{6,9},{7,11},{8,4},{9,6},... | collective-permute-start | bytes 98312 | tf_op jit(solution)/shard_map/ppermute | solution.py:354
  9.5 13.3 %collective-permute-start.1 = (s16[128,128]{1,0:T(8,128)(2,1)S(1)}, s16[128,128]{1,0:T(8,128)(2,1)S(1)}, u32[]{:S(2)}, u32[]{:S(2)}) collective-permute-start(s16[128,128]{1,0:T(8,128)(2,1)S(1)} %get-tuple-element.30), channel_id=1, source_target_pairs={{0,8},{1,10},{2,9},{3,11},{4,12},{5,14},{6,13},{7,15},{8,0},{9,2},... | collective-permute-start | bytes 98312 | tf_op jit(solution)/shard_map/ppermute | solution.py:354
  9.5 13.2 %collective-permute-start.3 = (s16[384,128]{1,0:T(8,128)(2,1)S(1)}, s16[384,128]{1,0:T(8,128)(2,1)S(1)}, u32[]{:S(2)}, u32[]{:S(2)}) collective-permute-start(s16[384,128]{1,0:T(8,128)(2,1)S(1)} %get-tuple-element.28), channel_id=1, source_target_pairs={{0,0},{1,2},{2,1},{3,3},{4,4},{5,6},{6,5},{7,7},{8,8},{9,10},{10,9... | collective-permute-start | bytes 294920 | tf_op jit(solution)/shard_map/ppermute | solution.py:354
  10.2 12.6 %collective-permute-start.2 = (s16[384,128]{1,0:T(8,128)(2,1)S(1)}, s16[384,128]{1,0:T(8,128)(2,1)S(1)}, u32[]{:S(2)}, u32[]{:S(2)}) collective-permute-start(s16[384,128]{1,0:T(8,128)(2,1)S(1)} %get-tuple-element.27), channel_id=1, source_target_pairs={{0,4},{1,6},{2,5},{3,7},{4,0},{5,2},{6,1},{7,3},{8,12},{9,14},{10,... | collective-permute-start | bytes 294920 | tf_op jit(solution)/shard_map/ppermute | solution.py:354
  11.1 5.3 %collective-permute-start.4 = (s16[256,128]{1,0:T(8,128)(2,1)S(1)}, s16[256,128]{1,0:T(8,128)(2,1)S(1)}, u32[]{:S(2)}, u32[]{:S(2)}) collective-permute-start(s16[256,128]{1,0:T(8,128)(2,1)S(1)} %get-tuple-element.26), channel_id=1, source_target_pairs={{0,8},{1,10},{2,9},{3,11},{4,12},{5,14},{6,13},{7,15},{8,0},{9,2},... | collective-permute-start | bytes 196616 | tf_op jit(solution)/shard_map/ppermute | solution.py:354
  16.4 6.3 %collective-permute-start.5 = (s16[256,128]{1,0:T(8,128)(2,1)S(1)}, s16[256,128]{1,0:T(8,128)(2,1)S(1)}, u32[]{:S(2)}, u32[]{:S(2)}) collective-permute-start(s16[256,128]{1,0:T(8,128)(2,1)S(1)} %get-tuple-element.25), channel_id=1, source_target_pairs={{0,12},{1,14},{2,13},{3,15},{4,8},{5,10},{6,9},{7,11},{8,4},{9,6},... | collective-permute-start | bytes 196616 | tf_op jit(solution)/shard_map/ppermute | solution.py:354
  23.1 6.0 %collective-permute-start.7 = (s16[512,128]{1,0:T(8,128)(2,1)S(1)}, s16[512,128]{1,0:T(8,128)(2,1)S(1)}, u32[]{:S(2)}, u32[]{:S(2)}) collective-permute-start(s16[512,128]{1,0:T(8,128)(2,1)S(1)} %pad_add_fusion.1), channel_id=1, source_target_pairs={{1,4},{4,1},{5,8},{8,5},{9,12},{12,9},{13,14},{14,13},{15,10},{10,... | collective-permute-start | bytes 393224 | tf_op jit(solution)/shard_map/ppermute | solution.py:420
  23.8 6.4 %collective-permute-start.6 = (s16[1024,128]{1,0:T(8,128)(2,1)S(1)}, s16[1024,128]{1,0:T(8,128)(2,1)S(1)}, u32[]{:S(2)}, u32[]{:S(2)}) collective-permute-start(s16[1024,128]{1,0:T(8,128)(2,1)S(1)} %bitcast_dynamic-update-slice_fusion), channel_id=1, source_target_pairs={{0,1},{1,0},{2,3},{3,2},{4,5},{5,4},{6,7},{7,6},{8,9},{9,8},{10,11... | collective-permute-start | bytes 786440 | tf_op jit(solution)/shard_map/ppermute | solution.py:397
  32.7 6.9 %collective-permute-start.10 = (f16[512,128]{1,0:T(8,128)(2,1)S(1)}, f16[512,128]{1,0:T(8,128)(2,1)S(1)}, u32[]{:S(2)}, u32[]{:S(2)}) collective-permute-start(f16[512,128]{1,0:T(8,128)(2,1)S(1)} %add_convert_fusion), channel_id=1, source_target_pairs={{1,4},{4,1},{5,8},{8,5},{9,12},{12,9},{13,14},{14,13},{15,10},{10,... | collective-permute-start | bytes 393224 | tf_op jit(solution)/shard_map/ppermute | solution.py:420
  33.4 6.3 %collective-permute-start.9 = (f32[512,128]{1,0:T(8,128)S(1)}, f32[512,128]{1,0:T(8,128)S(1)}, u32[]{:S(2)}, u32[]{:S(2)}) collective-permute-start(f32[512,128]{1,0:T(8,128)S(1)} %get-tuple-element.13.current_ref), channel_id=1, source_target_pairs={{0,1},{1,0},{2,3},{3,2},{4,5},{5,4},{6,7},{7,6},{8,9},{9,8},{10,11... | collective-permute-start | bytes 786440 | tf_op jit(solution)/shard_map/ppermute | solution.py:422
  40.4 7.0 %collective-permute-start.11 = (f16[1,128,128]{2,1,0:T(8,128)(2,1)S(1)}, f16[1,128,128]{2,1,0:T(8,128)(2,1)S(1)}, u32[]{:S(2)}, u32[]{:S(2)}) collective-permute-start(f16[1,128,128]{2,1,0:T(8,128)(2,1)S(1)} %get-tuple-element.57), channel_id=1, source_target_pairs={{0,12},{4,8},{8,4},{12,0},{1,13},{5,9},{9,5},{13,1},{2,14},{6,10},... | collective-permute-start | bytes 98312 | tf_op jit(solution)/shard_map/ppermute | solution.py:436
  44.1 4.1 %collective-permute-start.12 = (f16[1,128,128]{2,1,0:T(8,128)(2,1)S(1)}, f16[1,128,128]{2,1,0:T(8,128)(2,1)S(1)}, u32[]{:S(2)}, u32[]{:S(2)}) collective-permute-start(f16[1,128,128]{2,1,0:T(8,128)(2,1)S(1)} %get-tuple-element.56), channel_id=1, source_target_pairs={{0,4},{4,0},{8,12},{12,8},{1,5},{5,1},{9,13},{13,9},{2,6},{6,2},{1... | collective-permute-start | bytes 98312 | tf_op jit(solution)/shard_map/ppermute | solution.py:436
  44.1 4.8 %collective-permute-start.13 = (f16[1,128,128]{2,1,0:T(8,128)(2,1)S(1)}, f16[1,128,128]{2,1,0:T(8,128)(2,1)S(1)}, u32[]{:S(2)}, u32[]{:S(2)}) collective-permute-start(f16[1,128,128]{2,1,0:T(8,128)(2,1)S(1)} %get-tuple-element.55), channel_id=1, source_target_pairs={{0,8},{4,12},{8,0},{12,4},{1,9},{5,13},{9,1},{13,5},{2,10},{6,14},... | collective-permute-start | bytes 98312 | tf_op jit(solution)/shard_map/ppermute | solution.py:436
  44.8 6.7 %collective-permute-start.15 = (f16[1,128,128]{2,1,0:T(8,128)(2,1)S(1)}, f16[1,128,128]{2,1,0:T(8,128)(2,1)S(1)}, u32[]{:S(2)}, u32[]{:S(2)}) collective-permute-start(f16[1,128,128]{2,1,0:T(8,128)(2,1)S(1)} %get-tuple-element.54), channel_id=1, source_target_pairs={{0,2},{2,0},{1,3},{3,1},{4,6},{6,4},{5,7},{7,5},{8,10},{10,8},{9,1... | collective-permute-start | bytes 98312 | tf_op jit(solution)/shard_map/ppermute | solution.py:438
  48.9 5.6 %collective-permute-start.14 = (f16[3,128,128]{2,1,0:T(8,128)(2,1)S(1)}, f16[3,128,128]{2,1,0:T(8,128)(2,1)S(1)}, u32[]{:S(2)}, u32[]{:S(2)}) collective-permute-start(f16[3,128,128]{2,1,0:T(8,128)(2,1)S(1)} %pad_maximum_fusion.2), channel_id=1, source_target_pairs={{0,2},{2,0},{1,3},{3,1},{4,6},{6,4},{5,7},{7,5},{8,10},{10,8},{9,1... | collective-permute-start | bytes 294920 | tf_op jit(solution)/shard_map/ppermute | solution.py:439
  54.7 1.4 %collective-permute-start.16 = (f16[4,128,128]{2,1,0:T(8,128)(2,1)S(1)}, f16[4,128,128]{2,1,0:T(8,128)(2,1)S(1)}, u32[]{:S(2)}, u32[]{:S(2)}) collective-permute-start(f16[4,128,128]{2,1,0:T(8,128)(2,1)S(1)} %pad_maximum_fusion.1), channel_id=1, source_target_pairs={{0,1},{1,0},{2,3},{3,2},{4,5},{5,4},{6,7},{7,6},{8,9},{9,8},{10,11... | collective-permute-start | bytes 393224 | tf_op jit(solution)/shard_map/ppermute | solution.py:445

commit v9 on v4

--- a/solution.py
+++ b/solution.py
@@ -435,13 +435,16 @@
     mine = jnp.concatenate(pieces)
     crossed = [lax.ppermute(pieces[0], "views", swap)]
     crossed.append(lax.ppermute(mine[1:], "views", swap))
-    crossed = jnp.concatenate(crossed)
-    same = jnp.where(straight, mine, crossed)
-    twin = lax.ppermute(jnp.where(straight, crossed, mine), "gz", swap)
-    even, odd = jnp.where(core == 0, same, twin), jnp.where(core == 0, twin, same)
-    result = [jnp.stack([even[k], odd[k]]) for k in range(tiles)]
-    result = jnp.concatenate(ordered(result, lax.bitwise_xor(tile, end_of(core))))
-    return result.astype(jnp.float32)
+    crossed = [crossed[0][0], *[crossed[1][k] for k in range(tiles - 1)]]
+    mine = [mine[k] for k in range(tiles)]
+    here = lax.bitwise_xor(tile, end_of(core))
+    send = [jnp.where(straight, c, m) for c, m in zip(crossed, mine)]
+    send = jnp.stack(ordered(send, lax.bitwise_xor(tile, end_of(1 - core))))
+    twin = lax.ppermute(send, "gz", swap)
+    same = jnp.stack(ordered([jnp.where(straight, m, c) for c, m in zip(crossed, mine)], here))
+    parity = lax.broadcasted_iota(jnp.int32, (tiles, 2, height, columns), 1)
+    result = jnp.where(parity == core, same[:, None], twin[:, None])
+    return result.astype(jnp.float32).reshape(2 * tiles, height, columns)
 
 
 def one_plane_each(mesh, view_data, estimate, psf_taps, offsets):

time: 52 us -> 52.2 us (level)
    unnamed x14 -> x13, local copies, waits for them, and re-layouts: 1.32 us -> 1.31 us
where the time goes in v9:
time: 52.2 us; the launch traced here: 52 us
  starting transfers between devices  29.7 us (57%)
  waiting for transfers between devices  11.3 us (22%)
  Pallas kernels  5.57 us (11%)
  other arithmetic  3.21 us (6%)
  local copies, waits for them, and re-layouts  1.79 us (3%)
    ppermute x1, starting transfers between devices, plane_shards(): twin = lax.ppermute(current, 'gz', swap)  7.49 us
    ppermute x4, waiting for transfers between devices, exchange(): pieces.append(lax.ppermute(pick(k), square, pairs))  5.34 us
    ppermute x4, starting transfers between devices, exchange(): pieces.append(lax.ppermute(pick(k), square, pairs))  5.12 us
    ppermute x3, starting transfers between devices, plane_shards(): lax.ppermute(piece, 'tiles', [(t, t ^ k) for t in range(tiles)])  4.95 us
    pallas_call x2, Pallas kernels, correction_logs(): pl.pallas_call(functools.partial(correction_kernel, tiles), out_shape=jax...  3.39 us
    ppermute x1, starting transfers between devices, plane_shards(): note = lax.ppermute(info, 'views', swap)  3.03 us
    ppermute x1, starting transfers between devices, plane_shards(): got = lax.ppermute(jnp.concatenate([*planes, *give]), 'gz', swap)  2.63 us
    ppermute x1, starting transfers between devices, plane_shards(): crossed = [lax.ppermute(pieces[0], 'views', swap)]  2.56 us
  transfers between devices with their start and end apart: 15, of which 7 were waited for; matrix products, arithmetic and copies ran while one was open for 1% of the time, Pallas kernels for 5%

profile of v9, /device:TPU:0, one launch (start us, length us, event | category | flops | bytes accessed | tf_op | source)
XLA Modules:
  0.0 52.0 jit_solution(4603732577898377117)
XLA Ops:
  0.0 1.1 %multiply_convert_fusion = s16[1,1,8,128,128]{4,3,2,1,0:T(8,128)(2,1)S(1)} fusion(bf16[1,1,8,128,128]{4,3,2,1,0:T(8,128)(2,1)} %param.4), kind=kLoop, calls=%fused_computation | loop fusion | flops 393216 | bytes 524288 | tf_op jit(solution)/shard_map/convert_element_type | solution.py:369
  1.3 0.6 %copy-done.1 = f32[1,2,2,9]{3,2,1,0:T(2,128)S(1)} copy-done((f32[1,2,2,9]{3,2,1,0:T(2,128)S(1)}, f32[1,2,2,9]{3,2,1,0:T(2,128)}, u32[]{:S(2)}) %copy-start.1) | copy-done | bytes 168
  2.9 3.0 %collective-permute-start.6 = (s16[16,128]{1,0:T(8,128)(2,1)S(1)}, s16[16,128]{1,0:T(8,128)(2,1)S(1)}, u32[]{:S(2)}, u32[]{:S(2)}) collective-permute-start(s16[16,128]{1,0:T(8,128)(2,1)S(1)} %broadcast_in_dim.31), channel_id=1, source_target_pairs={{0,2},{2,0},{1,3},{3,1},{4,6},{6,4},{5,7},{7,5},{8,10},{10,8},{9,1... | collective-permute-start | bytes 12296 | tf_op jit(solution)/shard_map/ppermute | solution.py:384
  5.9 0.7 %collective-permute-start.3 = (s16[384,128]{1,0:T(8,128)(2,1)S(1)}, s16[384,128]{1,0:T(8,128)(2,1)S(1)}, u32[]{:S(2)}, u32[]{:S(2)}) collective-permute-start(s16[384,128]{1,0:T(8,128)(2,1)S(1)} %get-tuple-element.30), channel_id=1, source_target_pairs={{0,0},{1,2},{2,1},{3,3},{4,4},{5,6},{6,5},{7,7},{8,8},{9,10},{10,9... | collective-permute-start | bytes 294920 | tf_op jit(solution)/shard_map/ppermute | solution.py:356
  6.6 1.6 %collective-permute-start.2 = (s16[384,128]{1,0:T(8,128)(2,1)S(1)}, s16[384,128]{1,0:T(8,128)(2,1)S(1)}, u32[]{:S(2)}, u32[]{:S(2)}) collective-permute-start(s16[384,128]{1,0:T(8,128)(2,1)S(1)} %get-tuple-element.31), channel_id=1, source_target_pairs={{0,4},{1,6},{2,5},{3,7},{4,0},{5,2},{6,1},{7,3},{8,12},{9,14},{10,... | collective-permute-start | bytes 294920 | tf_op jit(solution)/shard_map/ppermute | solution.py:356
  8.2 2.6 %collective-permute-start.1 = (s16[384,128]{1,0:T(8,128)(2,1)S(1)}, s16[384,128]{1,0:T(8,128)(2,1)S(1)}, u32[]{:S(2)}, u32[]{:S(2)}) collective-permute-start(s16[384,128]{1,0:T(8,128)(2,1)S(1)} %get-tuple-element.32), channel_id=1, source_target_pairs={{0,8},{1,10},{2,9},{3,11},{4,12},{5,14},{6,13},{7,15},{8,0},{9,2},... | collective-permute-start | bytes 294920 | tf_op jit(solution)/shard_map/ppermute | solution.py:356
  11.2 1.0 %blur_matrices.1.matrices_ref = bf16[2,4,256,128]{3,2,1,0:T(8,128)(2,1)S(1)} custom-call(f32[2,128]{1,0:T(2,128)S(1)} %broadcast_multiply_fusion.info_ref), custom_call_target="tpu_custom_call" | custom-call | tf_op jit(solution)/shard_map/blur_matrices/pallas_call | solution.py:192
  12.2 2.2 %collective-permute-done.1 = s16[384,128]{1,0:T(8,128)(2,1)S(1)} collective-permute-done((s16[384,128]{1,0:T(8,128)(2,1)S(1)}, s16[384,128]{1,0:T(8,128)(2,1)S(1)}, u32[]{:S(2)}, u32[]{:S(2)}) %collective-permute-start.1) | collective-permute-done | bytes 98336 | tf_op jit(solution)/shard_map/ppermute | solution.py:356
  14.4 3.1 %collective-permute-done = s16[384,128]{1,0:T(8,128)(2,1)S(1)} collective-permute-done((s16[384,128]{1,0:T(8,128)(2,1)S(1)}, s16[384,128]{1,0:T(8,128)(2,1)S(1)}, u32[]{:S(2)}, u32[]{:S(2)}) %collective-permute-start) | collective-permute-done | bytes 98336 | tf_op jit(solution)/shard_map/ppermute | solution.py:356
  17.9 2.6 %collective-permute-start.4 = (s16[1024,128]{1,0:T(8,128)(2,1)S(1)}, s16[1024,128]{1,0:T(8,128)(2,1)S(1)}, u32[]{:S(2)}, u32[]{:S(2)}) collective-permute-start(s16[1024,128]{1,0:T(8,128)(2,1)S(1)} %bitcast_dynamic-update-slice_fusion), channel_id=1, source_target_pairs={{0,1},{1,0},{2,3},{3,2},{4,5},{5,4},{6,7},{7,6},{8,9},{9,8},{10,11... | collective-permute-start | bytes 786440 | tf_op jit(solution)/shard_map/ppermute | solution.py:395
  20.5 0.7 %collective-permute-start.5 = (s16[512,128]{1,0:T(8,128)(2,1)S(1)}, s16[512,128]{1,0:T(8,128)(2,1)S(1)}, u32[]{:S(2)}, u32[]{:S(2)}) collective-permute-start(s16[512,128]{1,0:T(8,128)(2,1)S(1)} %pad_add_fusion.1), channel_id=1, source_target_pairs={{1,4},{4,1},{5,8},{8,5},{9,12},{12,9},{13,14},{14,13},{15,10},{10,... | collective-permute-start | bytes 393224 | tf_op jit(solution)/shard_map/ppermute | solution.py:418
  21.8 1.7 %correction.2.log_ref = f32[512,128]{1,0:T(8,128)S(1)} custom-call(s32[1]{0:T(128)} %bitcast.16.tile_ref, s32[2,8]{1,0:T(2,128)S(1)} %slice_convert_fusion.offsets_ref, bf16[4,128,128]{2,1,0:T(8,128)(2,1)S(1)} %bitcast.54, bf16[2,4,256,128]{3,2,1,0:T(8,128)(2,1)S(1)} %blur_matrices.1.matrices_ref, bf16[128,128]{1,0:T(8,128)(2,1)S(1)} %get-tuple-element.60.refs_0_, ...), custom_call_target="tpu_custom_call" | custom-call | flops 300000000 | bytes 1500000 | tf_op jit(solution)/shard_map/correction/pallas_call | solution.py:260
  24.2 0.7 %collective-permute-start.8 = (f16[512,128]{1,0:T(8,128)(2,1)S(1)}, f16[512,128]{1,0:T(8,128)(2,1)S(1)}, u32[]{:S(2)}, u32[]{:S(2)}) collective-permute-start(f16[512,128]{1,0:T(8,128)(2,1)S(1)} %add_convert_fusion), channel_id=1, source_target_pairs={{1,4},{4,1},{5,8},{8,5},{9,12},{12,9},{13,14},{14,13},{15,10},{10,... | collective-permute-start | bytes 393224 | tf_op jit(solution)/shard_map/ppermute | solution.py:418
  24.9 7.5 %collective-permute-start.7 = (f32[512,128]{1,0:T(8,128)S(1)}, f32[512,128]{1,0:T(8,128)S(1)}, u32[]{:S(2)}, u32[]{:S(2)}) collective-permute-start(f32[512,128]{1,0:T(8,128)S(1)} %get-tuple-element.13.current_ref), channel_id=1, source_target_pairs={{0,1},{1,0},{2,3},{3,2},{4,5},{5,4},{6,7},{7,6},{8,9},{9,8},{10,11... | collective-permute-start | bytes 786440 | tf_op jit(solution)/shard_map/ppermute | solution.py:420
  32.4 1.7 %correction.3.log_ref = f32[512,128]{1,0:T(8,128)S(1)} custom-call(s32[1]{0:T(128)} %bitcast.16.tile_ref, s32[2,8]{1,0:T(2,128)S(1)} %slice_convert_fusion.offsets_ref, bf16[4,128,128]{2,1,0:T(8,128)(2,1)S(1)} %bitcast.55, bf16[2,4,256,128]{3,2,1,0:T(8,128)(2,1)S(1)} %blur_matrices.1.matrices_ref, bf16[128,128]{1,0:T(8,128)(2,1)S(1)} %get-tuple-element.60.refs_0_, ...), custom_call_target="tpu_custom_call" | custom-call | flops 300000000 | bytes 1500000 | tf_op jit(solution)/shard_map/correction/pallas_call | solution.py:260
  34.8 2.5 %collective-permute-start.10 = (f16[1,128,128]{2,1,0:T(8,128)(2,1)S(1)}, f16[1,128,128]{2,1,0:T(8,128)(2,1)S(1)}, u32[]{:S(2)}, u32[]{:S(2)}) collective-permute-start(f16[1,128,128]{2,1,0:T(8,128)(2,1)S(1)} %get-tuple-element.54), channel_id=1, source_target_pairs={{0,4},{4,0},{8,12},{12,8},{1,5},{5,1},{9,13},{13,9},{2,6},{6,2},{1... | collective-permute-start | bytes 98312 | tf_op jit(solution)/shard_map/ppermute | solution.py:434
  37.3 1.2 %collective-permute-start.11 = (f16[1,128,128]{2,1,0:T(8,128)(2,1)S(1)}, f16[1,128,128]{2,1,0:T(8,128)(2,1)S(1)}, u32[]{:S(2)}, u32[]{:S(2)}) collective-permute-start(f16[1,128,128]{2,1,0:T(8,128)(2,1)S(1)} %get-tuple-element.53), channel_id=1, source_target_pairs={{0,8},{4,12},{8,0},{12,4},{1,9},{5,13},{9,1},{13,5},{2,10},{6,14},... | collective-permute-start | bytes 98312 | tf_op jit(solution)/shard_map/ppermute | solution.py:434
  38.6 1.2 %collective-permute-start.9 = (f16[1,128,128]{2,1,0:T(8,128)(2,1)S(1)}, f16[1,128,128]{2,1,0:T(8,128)(2,1)S(1)}, u32[]{:S(2)}, u32[]{:S(2)}) collective-permute-start(f16[1,128,128]{2,1,0:T(8,128)(2,1)S(1)} %get-tuple-element.55), channel_id=1, source_target_pairs={{0,12},{4,8},{8,4},{12,0},{1,13},{5,9},{9,5},{13,1},{2,14},{6,10},... | collective-permute-start | bytes 98312 | tf_op jit(solution)/shard_map/ppermute | solution.py:434
  39.8 2.6 %collective-permute-start.13 = (f16[1,128,128]{2,1,0:T(8,128)(2,1)S(1)}, f16[1,128,128]{2,1,0:T(8,128)(2,1)S(1)}, u32[]{:S(2)}, u32[]{:S(2)}) collective-permute-start(f16[1,128,128]{2,1,0:T(8,128)(2,1)S(1)} %get-tuple-element.52), channel_id=1, source_target_pairs={{0,2},{2,0},{1,3},{3,1},{4,6},{6,4},{5,7},{7,5},{8,10},{10,8},{9,1... | collective-permute-start | bytes 98312 | tf_op jit(solution)/shard_map/ppermute | solution.py:436
  42.8 1.5 %collective-permute-done.9 = f16[1,128,128]{2,1,0:T(8,128)(2,1)S(1)} collective-permute-done((f16[1,128,128]{2,1,0:T(8,128)(2,1)S(1)}, f16[1,128,128]{2,1,0:T(8,128)(2,1)S(1)}, u32[]{:S(2)}, u32[]{:S(2)}) %collective-permute-start.9) | collective-permute-done | bytes 32800 | tf_op jit(solution)/shard_map/ppermute | solution.py:434
  44.3 2.5 %collective-permute-start.12 = (f16[3,128,128]{2,1,0:T(8,128)(2,1)S(1)}, f16[3,128,128]{2,1,0:T(8,128)(2,1)S(1)}, u32[]{:S(2)}, u32[]{:S(2)}) collective-permute-start(f16[3,128,128]{2,1,0:T(8,128)(2,1)S(1)} %pad_maximum_fusion.2), channel_id=1, source_target_pairs={{0,2},{2,0},{1,3},{3,1},{4,6},{6,4},{5,7},{7,5},{8,10},{10,8},{9,1... | collective-permute-start | bytes 294920 | tf_op jit(solution)/shard_map/ppermute | solution.py:437
  46.9 2.5 %collective-permute-done.12 = f16[3,128,128]{2,1,0:T(8,128)(2,1)S(1)} collective-permute-done((f16[3,128,128]{2,1,0:T(8,128)(2,1)S(1)}, f16[3,128,128]{2,1,0:T(8,128)(2,1)S(1)}, u32[]{:S(2)}, u32[]{:S(2)}) %collective-permute-start.12) | collective-permute-done | bytes 98336 | tf_op jit(solution)/shard_map/ppermute | solution.py:437
  49.8 1.2 %collective-permute-done.14 = f16[4,128,128]{2,1,0:T(8,128)(2,1)S(1)} collective-permute-done((f16[4,128,128]{2,1,0:T(8,128)(2,1)S(1)}, f16[4,128,128]{2,1,0:T(8,128)(2,1)S(1)}, u32[]{:S(2)}, u32[]{:S(2)}) %collective-permute-start.14) | collective-permute-done | bytes 131104 | tf_op jit(solution)/shard_map/ppermute | solution.py:443
  51.1 0.9 %fusion = f32[8,128,128]{2,1,0:T(8,128)} fusion(pred[8]{0:T(512)(128)(4,1)S(1)} %iota.12, f16[4,128,128]{2,1,0:T(8,128)(2,1)S(1)} %collective-permute-done.14, f16[4,128,128]{2,1,0:T(8,128)(2,1)S(1)} %pad_maximum_fusion), kind=kLoop, calls=%fused_computation.3 | loop fusion | flops 262144 | bytes 786440 | tf_op jit(solution)/shard_map/convert_element_type | solution.py:447
  (69 shorter events, 4.6 us)
Async XLA Ops:
  0.0 1.1 %copy-start = (f32[8,128,128]{2,1,0:T(8,128)S(1)}, f32[8,128,128]{2,1,0:T(8,128)}, u32[]{:S(2)}) copy-start(f32[8,128,128]{2,1,0:T(8,128)} %param.5) | copy-start | bytes 1572868
  1.2 0.7 %copy-start.1 = (f32[1,2,2,9]{3,2,1,0:T(2,128)S(1)}, f32[1,2,2,9]{3,2,1,0:T(2,128)}, u32[]{:S(2)}) copy-start(f32[1,2,2,9]{3,2,1,0:T(2,128)} %param.6) | copy-start | bytes 436
  2.1 0.7 %copy-start.2 = (s32[1,8]{1,0:T(1,128)S(1)}, s32[1,8]{1,0:T(1,128)}, u32[]{:S(2)}) copy-start(s32[1,8]{1,0:T(1,128)} %param.7) | copy-start | bytes 100
  2.9 8.2 %collective-permute-start.6 = (s16[16,128]{1,0:T(8,128)(2,1)S(1)}, s16[16,128]{1,0:T(8,128)(2,1)S(1)}, u32[]{:S(2)}, u32[]{:S(2)}) collective-permute-start(s16[16,128]{1,0:T(8,128)(2,1)S(1)} %broadcast_in_dim.31), channel_id=1, source_target_pairs={{0,2},{2,0},{1,3},{3,1},{4,6},{6,4},{5,7},{7,5},{8,10},{10,8},{9,1... | collective-permute-start | bytes 12296 | tf_op jit(solution)/shard_map/ppermute | solution.py:384
  5.9 6.2 %collective-permute-start.3 = (s16[384,128]{1,0:T(8,128)(2,1)S(1)}, s16[384,128]{1,0:T(8,128)(2,1)S(1)}, u32[]{:S(2)}, u32[]{:S(2)}) collective-permute-start(s16[384,128]{1,0:T(8,128)(2,1)S(1)} %get-tuple-element.30), channel_id=1, source_target_pairs={{0,0},{1,2},{2,1},{3,3},{4,4},{5,6},{6,5},{7,7},{8,8},{9,10},{10,9... | collective-permute-start | bytes 294920 | tf_op jit(solution)/shard_map/ppermute | solution.py:356
  6.6 5.6 %collective-permute-start.2 = (s16[384,128]{1,0:T(8,128)(2,1)S(1)}, s16[384,128]{1,0:T(8,128)(2,1)S(1)}, u32[]{:S(2)}, u32[]{:S(2)}) collective-permute-start(s16[384,128]{1,0:T(8,128)(2,1)S(1)} %get-tuple-element.31), channel_id=1, source_target_pairs={{0,4},{1,6},{2,5},{3,7},{4,0},{5,2},{6,1},{7,3},{8,12},{9,14},{10,... | collective-permute-start | bytes 294920 | tf_op jit(solution)/shard_map/ppermute | solution.py:356
  8.2 6.2 %collective-permute-start.1 = (s16[384,128]{1,0:T(8,128)(2,1)S(1)}, s16[384,128]{1,0:T(8,128)(2,1)S(1)}, u32[]{:S(2)}, u32[]{:S(2)}) collective-permute-start(s16[384,128]{1,0:T(8,128)(2,1)S(1)} %get-tuple-element.32), channel_id=1, source_target_pairs={{0,8},{1,10},{2,9},{3,11},{4,12},{5,14},{6,13},{7,15},{8,0},{9,2},... | collective-permute-start | bytes 294920 | tf_op jit(solution)/shard_map/ppermute | solution.py:356
  10.8 6.7 %collective-permute-start = (s16[384,128]{1,0:T(8,128)(2,1)S(1)}, s16[384,128]{1,0:T(8,128)(2,1)S(1)}, u32[]{:S(2)}, u32[]{:S(2)}) collective-permute-start(s16[384,128]{1,0:T(8,128)(2,1)S(1)} %get-tuple-element.29), channel_id=1, source_target_pairs={{0,12},{1,14},{2,13},{3,15},{4,8},{5,10},{6,9},{7,11},{8,4},{9,6},... | collective-permute-start | bytes 294920 | tf_op jit(solution)/shard_map/ppermute | solution.py:356
  17.9 3.8 %collective-permute-start.4 = (s16[1024,128]{1,0:T(8,128)(2,1)S(1)}, s16[1024,128]{1,0:T(8,128)(2,1)S(1)}, u32[]{:S(2)}, u32[]{:S(2)}) collective-permute-start(s16[1024,128]{1,0:T(8,128)(2,1)S(1)} %bitcast_dynamic-update-slice_fusion), channel_id=1, source_target_pairs={{0,1},{1,0},{2,3},{3,2},{4,5},{5,4},{6,7},{7,6},{8,9},{9,8},{10,11... | collective-permute-start | bytes 786440 | tf_op jit(solution)/shard_map/ppermute | solution.py:395
  20.5 0.8 %collective-permute-start.5 = (s16[512,128]{1,0:T(8,128)(2,1)S(1)}, s16[512,128]{1,0:T(8,128)(2,1)S(1)}, u32[]{:S(2)}, u32[]{:S(2)}) collective-permute-start(s16[512,128]{1,0:T(8,128)(2,1)S(1)} %pad_add_fusion.1), channel_id=1, source_target_pairs={{1,4},{4,1},{5,8},{8,5},{9,12},{12,9},{13,14},{14,13},{15,10},{10,... | collective-permute-start | bytes 393224 | tf_op jit(solution)/shard_map/ppermute | solution.py:418
  24.2 9.9 %collective-permute-start.8 = (f16[512,128]{1,0:T(8,128)(2,1)S(1)}, f16[512,128]{1,0:T(8,128)(2,1)S(1)}, u32[]{:S(2)}, u32[]{:S(2)}) collective-permute-start(f16[512,128]{1,0:T(8,128)(2,1)S(1)} %add_convert_fusion), channel_id=1, source_target_pairs={{1,4},{4,1},{5,8},{8,5},{9,12},{12,9},{13,14},{14,13},{15,10},{10,... | collective-permute-start | bytes 393224 | tf_op jit(solution)/shard_map/ppermute | solution.py:418
  24.9 9.3 %collective-permute-start.7 = (f32[512,128]{1,0:T(8,128)S(1)}, f32[512,128]{1,0:T(8,128)S(1)}, u32[]{:S(2)}, u32[]{:S(2)}) collective-permute-start(f32[512,128]{1,0:T(8,128)S(1)} %get-tuple-element.13.current_ref), channel_id=1, source_target_pairs={{0,1},{1,0},{2,3},{3,2},{4,5},{5,4},{6,7},{7,6},{8,9},{9,8},{10,11... | collective-permute-start | bytes 786440 | tf_op jit(solution)/shard_map/ppermute | solution.py:420
  34.8 7.5 %collective-permute-start.10 = (f16[1,128,128]{2,1,0:T(8,128)(2,1)S(1)}, f16[1,128,128]{2,1,0:T(8,128)(2,1)S(1)}, u32[]{:S(2)}, u32[]{:S(2)}) collective-permute-start(f16[1,128,128]{2,1,0:T(8,128)(2,1)S(1)} %get-tuple-element.54), channel_id=1, source_target_pairs={{0,4},{4,0},{8,12},{12,8},{1,5},{5,1},{9,13},{13,9},{2,6},{6,2},{1... | collective-permute-start | bytes 98312 | tf_op jit(solution)/shard_map/ppermute | solution.py:434
  37.3 5.5 %collective-permute-start.11 = (f16[1,128,128]{2,1,0:T(8,128)(2,1)S(1)}, f16[1,128,128]{2,1,0:T(8,128)(2,1)S(1)}, u32[]{:S(2)}, u32[]{:S(2)}) collective-permute-start(f16[1,128,128]{2,1,0:T(8,128)(2,1)S(1)} %get-tuple-element.53), channel_id=1, source_target_pairs={{0,8},{4,12},{8,0},{12,4},{1,9},{5,13},{9,1},{13,5},{2,10},{6,14},... | collective-permute-start | bytes 98312 | tf_op jit(solution)/shard_map/ppermute | solution.py:434
  38.6 5.7 %collective-permute-start.9 = (f16[1,128,128]{2,1,0:T(8,128)(2,1)S(1)}, f16[1,128,128]{2,1,0:T(8,128)(2,1)S(1)}, u32[]{:S(2)}, u32[]{:S(2)}) collective-permute-start(f16[1,128,128]{2,1,0:T(8,128)(2,1)S(1)} %get-tuple-element.55), channel_id=1, source_target_pairs={{0,12},{4,8},{8,4},{12,0},{1,13},{5,9},{9,5},{13,1},{2,14},{6,10},... | collective-permute-start | bytes 98312 | tf_op jit(solution)/shard_map/ppermute | solution.py:434
  39.8 7.2 %collective-permute-start.13 = (f16[1,128,128]{2,1,0:T(8,128)(2,1)S(1)}, f16[1,128,128]{2,1,0:T(8,128)(2,1)S(1)}, u32[]{:S(2)}, u32[]{:S(2)}) collective-permute-start(f16[1,128,128]{2,1,0:T(8,128)(2,1)S(1)} %get-tuple-element.52), channel_id=1, source_target_pairs={{0,2},{2,0},{1,3},{3,1},{4,6},{6,4},{5,7},{7,5},{8,10},{10,8},{9,1... | collective-permute-start | bytes 98312 | tf_op jit(solution)/shard_map/ppermute | solution.py:436
  44.3 5.1 %collective-permute-start.12 = (f16[3,128,128]{2,1,0:T(8,128)(2,1)S(1)}, f16[3,128,128]{2,1,0:T(8,128)(2,1)S(1)}, u32[]{:S(2)}, u32[]{:S(2)}) collective-permute-start(f16[3,128,128]{2,1,0:T(8,128)(2,1)S(1)} %pad_maximum_fusion.2), channel_id=1, source_target_pairs={{0,2},{2,0},{1,3},{3,1},{4,6},{6,4},{5,7},{7,5},{8,10},{10,8},{9,1... | collective-permute-start | bytes 294920 | tf_op jit(solution)/shard_map/ppermute | solution.py:437
  49.7 1.4 %collective-permute-start.14 = (f16[4,128,128]{2,1,0:T(8,128)(2,1)S(1)}, f16[4,128,128]{2,1,0:T(8,128)(2,1)S(1)}, u32[]{:S(2)}, u32[]{:S(2)}) collective-permute-start(f16[4,128,128]{2,1,0:T(8,128)(2,1)S(1)} %pad_maximum_fusion.1), channel_id=1, source_target_pairs={{0,1},{1,0},{2,3},{3,2},{4,5},{5,4},{6,7},{7,6},{8,9},{9,8},{10,11... | collective-permute-start | bytes 393224 | tf_op jit(solution)/shard_map/ppermute | solution.py:443

commit v10 on v6

--- a/solution.py
+++ b/solution.py
@@ -200,27 +200,21 @@
 
 
 def pack_kernel(where_ref, *refs):
-    pieces, (plane_ref, give_ref) = refs[:-2], refs[-2:]
-    height = plane_ref.shape[1]
+    pieces, give_ref = refs[:-1], refs[-1]
+    height = give_ref.shape[2]
     other = pl.multiple_of((2 - where_ref[1]) * height, height)
     for k, piece in enumerate(pieces):
-        plane = piece[0:height, :]
-        plane_ref[lax.bitwise_xor(where_ref[0], k)] = plane
-        give_ref[k, 0] = plane
+        give_ref[k, 0] = piece[0:height, :]
         give_ref[k, 1] = piece[pl.ds(other, height), :]
 
 
 def pack(where, pieces):
     rows, columns = pieces[0].shape
-    shape = (len(pieces), rows // 3, columns)
     return pl.pallas_call(
         pack_kernel,
-        out_shape=[
-            jax.ShapeDtypeStruct(shape, pieces[0].dtype),
-            jax.ShapeDtypeStruct((shape[0], 2, *shape[1:]), pieces[0].dtype),
-        ],
+        out_shape=jax.ShapeDtypeStruct((len(pieces), 2, rows // 3, columns), pieces[0].dtype),
         in_specs=[SMEM] + [VMEM] * len(pieces),
-        out_specs=[VMEM] * 2,
+        out_specs=VMEM,
         compiler_params=LIMIT,
         name="pack",
     )(where, *pieces)
@@ -418,7 +412,7 @@
     shifts = notes[:, 8 * taps : 8 * taps + blocks].astype(jnp.int32)
     matrices = blur_matrices(taps, height, notes * (1.0 / TAP_UNIT))
 
-    plane, give = pack(where, pieces)
+    give = pack(where, pieces)
     swapped = lax.ppermute(give, "gz", swap)
 
     path = [(t, 0) for t in range(tiles)] + [(t, 1) for t in reversed(range(tiles))]
@@ -430,7 +424,7 @@
     def plane_of(coded):
         return coded.astype(jnp.float32) * (1.0 / PLANE_UNIT) + 1.0
 
-    plane = plane.reshape(tiles * height, columns)
+    plane = jnp.concatenate(ordered([piece[:height] for piece in pieces], tile))
     twin = plane_of(jnp.concatenate(ordered([swapped[k, 0] for k in range(tiles)], tile)))
     current = plane_of(plane)
     narrow = current.astype(jnp.bfloat16)
@@ -457,13 +451,16 @@
     mine = jnp.concatenate(pieces)
     crossed = [lax.ppermute(pieces[0], "views", swap)]
     crossed.append(lax.ppermute(mine[1:], "views", swap))
-    crossed = jnp.concatenate(crossed)
-    same = jnp.where(straight, mine, crossed)
-    twin = lax.ppermute(jnp.where(straight, crossed, mine), "gz", swap)
-    even, odd = jnp.where(core == 0, same, twin), jnp.where(core == 0, twin, same)
-    result = [jnp.stack([even[k], odd[k]]) for k in range(tiles)]
-    result = jnp.concatenate(ordered(result, lax.bitwise_xor(tile, end_of(core))))
-    return result.astype(jnp.float32)
+    crossed = [crossed[0][0], *[crossed[1][k] for k in range(tiles - 1)]]
+    mine = [mine[k] for k in range(tiles)]
+    here = lax.bitwise_xor(tile, end_of(core))
+    send = [jnp.where(straight, c, m) for c, m in zip(crossed, mine)]
+    send = jnp.stack(ordered(send, lax.bitwise_xor(tile, end_of(1 - core))))
+    twin = lax.ppermute(send, "gz", swap)
+    same = jnp.stack(ordered([jnp.where(straight, m, c) for c, m in zip(crossed, mine)], here))
+    parity = lax.broadcasted_iota(jnp.int32, (tiles, 2, height, columns), 1)
+    result = jnp.where(parity == core, same[:, None], twin[:, None])
+    return result.astype(jnp.float32).reshape(2 * tiles, height, columns)
 
 
 def one_plane_each(mesh, view_data, estimate, psf_taps, offsets):

time: 52.2 us -> 50.6 us (0.969)
  starting transfers between devices: 29.3 us -> 22.9 us
  waiting for transfers between devices: 11.5 us -> 16.2 us
    ppermute x1, starting transfers between devices: 7.56 us -> 2.95 us  [plane_shards(): twin = lax.ppermute(current, 'gz', swap)]
    ppermute x4, waiting for transfers between devices: 5.26 us -> 7.17 us  [exchange(): pieces.append(lax.ppermute(pick(k), square, pairs))]
    ppermute x1, starting transfers between devices: 2.44 us -> 1.07 us  [plane_shards(): crossed.append(lax.ppermute(mine[1:], 'views', swap))]
    ppermute x3, waiting for transfers between devices: 2.04 us -> 3.31 us  [plane_shards(): lax.ppermute(piece, 'tiles', [(t, t ^ k) for t in range(tiles)])]
    ppermute x1, waiting for transfers between devices: 2.58 us -> 3.51 us  [plane_shards(): crossed.append(lax.ppermute(mine[1:], 'views', swap))]
    ppermute x1, waiting for transfers between devices: 0.26 us -> 1.01 us  [plane_shards(): swapped = lax.ppermute(give, 'gz', swap)]
    ppermute x1, starting transfers between devices: 2.63 us -> 1.94 us  [plane_shards(): swapped = lax.ppermute(give, 'gz', swap)]
    unnamed x7 -> x6, local copies, waits for them, and re-layouts: 1.23 us -> 1.22 us
  transfers between devices with their start and end apart: 15 -> 15, of which waited for: 7 -> 7; matrix products, arithmetic and copies ran while one was open for 1% -> 1% of each run, Pallas kernels for 5% -> 6%
where the time goes in v10:
time: 50.6 us; the launch traced here: 50.4 us
  starting transfers between devices  22.9 us (45%)
  waiting for transfers between devices  16.2 us (32%)
  Pallas kernels  6.13 us (12%)
  other arithmetic  3.15 us (6%)
  local copies, waits for them, and re-layouts  1.66 us (3%)
    ppermute x4, waiting for transfers between devices, exchange(): pieces.append(lax.ppermute(pick(k), square, pairs))  7.17 us
    ppermute x4, starting transfers between devices, exchange(): pieces.append(lax.ppermute(pick(k), square, pairs))  5.11 us
    ppermute x3, starting transfers between devices, plane_shards(): lax.ppermute(piece, 'tiles', [(t, t ^ k) for t in range(tiles)])  5.03 us
    ppermute x1, waiting for transfers between devices, plane_shards(): crossed.append(lax.ppermute(mine[1:], 'views', swap))  3.51 us
    pallas_call x2, Pallas kernels, correction_logs(): pl.pallas_call(correction_kernel, out_shape=jax.ShapeDtypeStruct((tiles *...  3.39 us
    ppermute x3, waiting for transfers between devices, plane_shards(): lax.ppermute(piece, 'tiles', [(t, t ^ k) for t in range(tiles)])  3.31 us
    ppermute x1, starting transfers between devices, plane_shards(): note = lax.ppermute(info, 'views', swap)  3.03 us
    ppermute x1, starting transfers between devices, plane_shards(): twin = lax.ppermute(current, 'gz', swap)  2.95 us
  transfers between devices with their start and end apart: 15, of which 7 were waited for; matrix products, arithmetic and copies ran while one was open for 1% of the time, Pallas kernels for 6%

profile of v10, /device:TPU:0, one launch (start us, length us, event | category | flops | bytes accessed | tf_op | source)
XLA Modules:
  0.0 50.4 jit_solution(14583504744972526433)
XLA Ops:
  0.0 1.1 %multiply_convert_fusion = s16[1,1,8,128,128]{4,3,2,1,0:T(8,128)(2,1)S(1)} fusion(bf16[1,1,8,128,128]{4,3,2,1,0:T(8,128)(2,1)} %param.4), kind=kLoop, calls=%fused_computation | loop fusion | flops 393216 | bytes 524288 | tf_op jit(solution)/shard_map/convert_element_type | solution.py:393
  1.3 0.6 %copy-done.1 = f32[1,2,2,9]{3,2,1,0:T(2,128)S(1)} copy-done((f32[1,2,2,9]{3,2,1,0:T(2,128)S(1)}, f32[1,2,2,9]{3,2,1,0:T(2,128)}, u32[]{:S(2)}) %copy-start.1) | copy-done | bytes 168
  2.9 3.0 %collective-permute-start.6 = (s16[16,128]{1,0:T(8,128)(2,1)S(1)}, s16[16,128]{1,0:T(8,128)(2,1)S(1)}, u32[]{:S(2)}, u32[]{:S(2)}) collective-permute-start(s16[16,128]{1,0:T(8,128)(2,1)S(1)} %broadcast_in_dim.31), channel_id=1, source_target_pairs={{0,2},{2,0},{1,3},{3,1},{4,6},{6,4},{5,7},{7,5},{8,10},{10,8},{9,1... | collective-permute-start | bytes 12296 | tf_op jit(solution)/shard_map/ppermute | solution.py:408
  5.9 3.7 %collective-permute-start = (s16[384,128]{1,0:T(8,128)(2,1)S(1)}, s16[384,128]{1,0:T(8,128)(2,1)S(1)}, u32[]{:S(2)}, u32[]{:S(2)}) collective-permute-start(s16[384,128]{1,0:T(8,128)(2,1)S(1)} %get-tuple-element.29), channel_id=1, source_target_pairs={{0,12},{1,14},{2,13},{3,15},{4,8},{5,10},{6,9},{7,11},{8,4},{9,6},... | collective-permute-start | bytes 294920 | tf_op jit(solution)/shard_map/ppermute | solution.py:380
  9.6 0.8 %collective-permute-start.2 = (s16[384,128]{1,0:T(8,128)(2,1)S(1)}, s16[384,128]{1,0:T(8,128)(2,1)S(1)}, u32[]{:S(2)}, u32[]{:S(2)}) collective-permute-start(s16[384,128]{1,0:T(8,128)(2,1)S(1)} %get-tuple-element.31), channel_id=1, source_target_pairs={{0,4},{1,6},{2,5},{3,7},{4,0},{5,2},{6,1},{7,3},{8,12},{9,14},{10,... | collective-permute-start | bytes 294920 | tf_op jit(solution)/shard_map/ppermute | solution.py:380
  10.4 0.7 %collective-permute-start.3 = (s16[384,128]{1,0:T(8,128)(2,1)S(1)}, s16[384,128]{1,0:T(8,128)(2,1)S(1)}, u32[]{:S(2)}, u32[]{:S(2)}) collective-permute-start(s16[384,128]{1,0:T(8,128)(2,1)S(1)} %get-tuple-element.30), channel_id=1, source_target_pairs={{0,0},{1,2},{2,1},{3,3},{4,4},{5,6},{6,5},{7,7},{8,8},{9,10},{10,9... | collective-permute-start | bytes 294920 | tf_op jit(solution)/shard_map/ppermute | solution.py:380
  11.2 1.6 %collective-permute-done.refs_3_ = s16[384,128]{1,0:T(8,128)(2,1)S(1)} collective-permute-done((s16[384,128]{1,0:T(8,128)(2,1)S(1)}, s16[384,128]{1,0:T(8,128)(2,1)S(1)}, u32[]{:S(2)}, u32[]{:S(2)}) %collective-permute-start) | collective-permute-done | bytes 98336 | tf_op jit(solution)/shard_map/ppermute | solution.py:380
  12.8 5.6 %collective-permute-done.1.refs_2_ = s16[384,128]{1,0:T(8,128)(2,1)S(1)} collective-permute-done((s16[384,128]{1,0:T(8,128)(2,1)S(1)}, s16[384,128]{1,0:T(8,128)(2,1)S(1)}, u32[]{:S(2)}, u32[]{:S(2)}) %collective-permute-start.1) | collective-permute-done | bytes 98336 | tf_op jit(solution)/shard_map/ppermute | solution.py:380
  18.5 0.7 %collective-permute-start.5 = (s16[512,128]{1,0:T(8,128)(2,1)S(1)}, s16[512,128]{1,0:T(8,128)(2,1)S(1)}, u32[]{:S(2)}, u32[]{:S(2)}) collective-permute-start(s16[512,128]{1,0:T(8,128)(2,1)S(1)} %pad_add_fusion.1), channel_id=1, source_target_pairs={{1,4},{4,1},{5,8},{8,5},{9,12},{12,9},{13,14},{14,13},{15,10},{10,... | collective-permute-start | bytes 393224 | tf_op jit(solution)/shard_map/ppermute | solution.py:434
  19.2 1.0 %blur_matrices.1.matrices_ref = bf16[2,4,256,128]{3,2,1,0:T(8,128)(2,1)S(1)} custom-call(f32[2,128]{1,0:T(2,128)S(1)} %broadcast_multiply_fusion.info_ref), custom_call_target="tpu_custom_call" | custom-call | tf_op jit(solution)/shard_map/blur_matrices/pallas_call | solution.py:192
  20.7 1.9 %collective-permute-start.4 = (s16[4,2,128,128]{3,2,1,0:T(8,128)(2,1)S(1)}, s16[4,2,128,128]{3,2,1,0:T(8,128)(2,1)S(1)}, u32[]{:S(2)}, u32[]{:S(2)}) collective-permute-start(s16[4,2,128,128]{3,2,1,0:T(8,128)(2,1)S(1)} %pack.1), channel_id=1, source_target_pairs={{0,1},{1,0},{2,3},{3,2},{4,5},{5,4},{6,7},{7,6},{8,9},{9,8},{10,11... | collective-permute-start | bytes 786440 | tf_op jit(solution)/shard_map/ppermute | solution.py:416
  22.8 1.0 %collective-permute-done.4.refs_4_ = s16[4,2,128,128]{3,2,1,0:T(8,128)(2,1)S(1)} collective-permute-done((s16[4,2,128,128]{3,2,1,0:T(8,128)(2,1)S(1)}, s16[4,2,128,128]{3,2,1,0:T(8,128)(2,1)S(1)}, u32[]{:S(2)}, u32[]{:S(2)}) %collective-permute-start.4) | collective-permute-done | bytes 262176 | tf_op jit(solution)/shard_map/ppermute | solution.py:416
  24.0 1.7 %correction.2.log_ref = f32[512,128]{1,0:T(8,128)S(1)} custom-call(s32[2]{0:T(128)S(1)} %pad_add_fusion.2.where_ref, s32[2,8]{1,0:T(2,128)S(1)} %slice_convert_fusion.offsets_ref, bf16[4,128,128]{2,1,0:T(8,128)(2,1)S(1)} %bitcast.74, bf16[2,4,256,128]{3,2,1,0:T(8,128)(2,1)S(1)} %blur_matrices.1.matrices_ref, ...), custom_call_target="tpu_custom_call" | custom-call | flops 300000000 | bytes 1500000 | tf_op jit(solution)/shard_map/correction/pallas_call | solution.py:284
  26.3 0.7 %collective-permute-start.8 = (f16[512,128]{1,0:T(8,128)(2,1)S(1)}, f16[512,128]{1,0:T(8,128)(2,1)S(1)}, u32[]{:S(2)}, u32[]{:S(2)}) collective-permute-start(f16[512,128]{1,0:T(8,128)(2,1)S(1)} %add_convert_fusion), channel_id=1, source_target_pairs={{1,4},{4,1},{5,8},{8,5},{9,12},{12,9},{13,14},{14,13},{15,10},{10,... | collective-permute-start | bytes 393224 | tf_op jit(solution)/shard_map/ppermute | solution.py:434
  27.0 3.0 %collective-permute-start.7 = (f32[512,128]{1,0:T(8,128)S(1)}, f32[512,128]{1,0:T(8,128)S(1)}, u32[]{:S(2)}, u32[]{:S(2)}) collective-permute-start(f32[512,128]{1,0:T(8,128)S(1)} %get-tuple-element.13.current_ref), channel_id=1, source_target_pairs={{0,1},{1,0},{2,3},{3,2},{4,5},{5,4},{6,7},{7,6},{8,9},{9,8},{10,11... | collective-permute-start | bytes 786440 | tf_op jit(solution)/shard_map/ppermute | solution.py:436
  30.0 1.7 %correction.3.log_ref = f32[512,128]{1,0:T(8,128)S(1)} custom-call(s32[2]{0:T(128)S(1)} %pad_add_fusion.2.where_ref, s32[2,8]{1,0:T(2,128)S(1)} %slice_convert_fusion.offsets_ref, bf16[4,128,128]{2,1,0:T(8,128)(2,1)S(1)} %bitcast.75, bf16[2,4,256,128]{3,2,1,0:T(8,128)(2,1)S(1)} %blur_matrices.1.matrices_ref, ...), custom_call_target="tpu_custom_call" | custom-call | flops 300000000 | bytes 1500000 | tf_op jit(solution)/shard_map/correction/pallas_call | solution.py:284
  32.4 2.5 %collective-permute-start.10 = (f16[1,128,128]{2,1,0:T(8,128)(2,1)S(1)}, f16[1,128,128]{2,1,0:T(8,128)(2,1)S(1)}, u32[]{:S(2)}, u32[]{:S(2)}) collective-permute-start(f16[1,128,128]{2,1,0:T(8,128)(2,1)S(1)} %get-tuple-element.50), channel_id=1, source_target_pairs={{0,4},{4,0},{8,12},{12,8},{1,5},{5,1},{9,13},{13,9},{2,6},{6,2},{1... | collective-permute-start | bytes 98312 | tf_op jit(solution)/shard_map/ppermute | solution.py:450
  34.9 2.5 %collective-permute-start.11 = (f16[1,128,128]{2,1,0:T(8,128)(2,1)S(1)}, f16[1,128,128]{2,1,0:T(8,128)(2,1)S(1)}, u32[]{:S(2)}, u32[]{:S(2)}) collective-permute-start(f16[1,128,128]{2,1,0:T(8,128)(2,1)S(1)} %get-tuple-element.49), channel_id=1, source_target_pairs={{0,8},{4,12},{8,0},{12,4},{1,9},{5,13},{9,1},{13,5},{2,10},{6,14},... | collective-permute-start | bytes 98312 | tf_op jit(solution)/shard_map/ppermute | solution.py:450
  37.4 2.4 %collective-permute-start.13 = (f16[1,128,128]{2,1,0:T(8,128)(2,1)S(1)}, f16[1,128,128]{2,1,0:T(8,128)(2,1)S(1)}, u32[]{:S(2)}, u32[]{:S(2)}) collective-permute-start(f16[1,128,128]{2,1,0:T(8,128)(2,1)S(1)} %get-tuple-element.48), channel_id=1, source_target_pairs={{0,2},{2,0},{1,3},{3,1},{4,6},{6,4},{5,7},{7,5},{8,10},{10,8},{9,1... | collective-permute-start | bytes 98312 | tf_op jit(solution)/shard_map/ppermute | solution.py:452
  40.3 2.8 %collective-permute-done.9 = f16[1,128,128]{2,1,0:T(8,128)(2,1)S(1)} collective-permute-done((f16[1,128,128]{2,1,0:T(8,128)(2,1)S(1)}, f16[1,128,128]{2,1,0:T(8,128)(2,1)S(1)}, u32[]{:S(2)}, u32[]{:S(2)}) %collective-permute-start.9) | collective-permute-done | bytes 32800 | tf_op jit(solution)/shard_map/ppermute | solution.py:450
  43.2 1.1 %collective-permute-start.12 = (f16[3,128,128]{2,1,0:T(8,128)(2,1)S(1)}, f16[3,128,128]{2,1,0:T(8,128)(2,1)S(1)}, u32[]{:S(2)}, u32[]{:S(2)}) collective-permute-start(f16[3,128,128]{2,1,0:T(8,128)(2,1)S(1)} %pad_maximum_fusion.2), channel_id=1, source_target_pairs={{0,2},{2,0},{1,3},{3,1},{4,6},{6,4},{5,7},{7,5},{8,10},{10,8},{9,1... | collective-permute-start | bytes 294920 | tf_op jit(solution)/shard_map/ppermute | solution.py:453
  44.3 3.5 %collective-permute-done.12 = f16[3,128,128]{2,1,0:T(8,128)(2,1)S(1)} collective-permute-done((f16[3,128,128]{2,1,0:T(8,128)(2,1)S(1)}, f16[3,128,128]{2,1,0:T(8,128)(2,1)S(1)}, u32[]{:S(2)}, u32[]{:S(2)}) %collective-permute-start.12) | collective-permute-done | bytes 98336 | tf_op jit(solution)/shard_map/ppermute | solution.py:453
  48.3 1.2 %collective-permute-done.14 = f16[4,128,128]{2,1,0:T(8,128)(2,1)S(1)} collective-permute-done((f16[4,128,128]{2,1,0:T(8,128)(2,1)S(1)}, f16[4,128,128]{2,1,0:T(8,128)(2,1)S(1)}, u32[]{:S(2)}, u32[]{:S(2)}) %collective-permute-start.14) | collective-permute-done | bytes 131104 | tf_op jit(solution)/shard_map/ppermute | solution.py:459
  49.5 0.9 %fusion = f32[8,128,128]{2,1,0:T(8,128)} fusion(pred[8]{0:T(512)(128)(4,1)S(1)} %iota.12, f16[4,128,128]{2,1,0:T(8,128)(2,1)S(1)} %collective-permute-done.14, f16[4,128,128]{2,1,0:T(8,128)(2,1)S(1)} %pad_maximum_fusion), kind=kLoop, calls=%fused_computation.3 | loop fusion | flops 262144 | bytes 786440 | tf_op jit(solution)/shard_map/convert_element_type | solution.py:463
  (56 shorter events, 4.5 us)
Async XLA Ops:
  0.0 1.1 %copy-start = (f32[8,128,128]{2,1,0:T(8,128)S(1)}, f32[8,128,128]{2,1,0:T(8,128)}, u32[]{:S(2)}) copy-start(f32[8,128,128]{2,1,0:T(8,128)} %param.5) | copy-start | bytes 1572868
  1.2 0.7 %copy-start.1 = (f32[1,2,2,9]{3,2,1,0:T(2,128)S(1)}, f32[1,2,2,9]{3,2,1,0:T(2,128)}, u32[]{:S(2)}) copy-start(f32[1,2,2,9]{3,2,1,0:T(2,128)} %param.6) | copy-start | bytes 436
  2.1 0.7 %copy-start.2 = (s32[1,8]{1,0:T(1,128)S(1)}, s32[1,8]{1,0:T(1,128)}, u32[]{:S(2)}) copy-start(s32[1,8]{1,0:T(1,128)} %param.7) | copy-start | bytes 100
  2.9 8.3 %collective-permute-start.6 = (s16[16,128]{1,0:T(8,128)(2,1)S(1)}, s16[16,128]{1,0:T(8,128)(2,1)S(1)}, u32[]{:S(2)}, u32[]{:S(2)}) collective-permute-start(s16[16,128]{1,0:T(8,128)(2,1)S(1)} %broadcast_in_dim.31), channel_id=1, source_target_pairs={{0,2},{2,0},{1,3},{3,1},{4,6},{6,4},{5,7},{7,5},{8,10},{10,8},{9,1... | collective-permute-start | bytes 12296 | tf_op jit(solution)/shard_map/ppermute | solution.py:408
  5.9 6.9 %collective-permute-start = (s16[384,128]{1,0:T(8,128)(2,1)S(1)}, s16[384,128]{1,0:T(8,128)(2,1)S(1)}, u32[]{:S(2)}, u32[]{:S(2)}) collective-permute-start(s16[384,128]{1,0:T(8,128)(2,1)S(1)} %get-tuple-element.29), channel_id=1, source_target_pairs={{0,12},{1,14},{2,13},{3,15},{4,8},{5,10},{6,9},{7,11},{8,4},{9,6},... | collective-permute-start | bytes 294920 | tf_op jit(solution)/shard_map/ppermute | solution.py:380
  9.6 8.8 %collective-permute-start.1 = (s16[384,128]{1,0:T(8,128)(2,1)S(1)}, s16[384,128]{1,0:T(8,128)(2,1)S(1)}, u32[]{:S(2)}, u32[]{:S(2)}) collective-permute-start(s16[384,128]{1,0:T(8,128)(2,1)S(1)} %get-tuple-element.32), channel_id=1, source_target_pairs={{0,8},{1,10},{2,9},{3,11},{4,12},{5,14},{6,13},{7,15},{8,0},{9,2},... | collective-permute-start | bytes 294920 | tf_op jit(solution)/shard_map/ppermute | solution.py:380
  9.6 8.8 %collective-permute-start.2 = (s16[384,128]{1,0:T(8,128)(2,1)S(1)}, s16[384,128]{1,0:T(8,128)(2,1)S(1)}, u32[]{:S(2)}, u32[]{:S(2)}) collective-permute-start(s16[384,128]{1,0:T(8,128)(2,1)S(1)} %get-tuple-element.31), channel_id=1, source_target_pairs={{0,4},{1,6},{2,5},{3,7},{4,0},{5,2},{6,1},{7,3},{8,12},{9,14},{10,... | collective-permute-start | bytes 294920 | tf_op jit(solution)/shard_map/ppermute | solution.py:380
  10.4 8.0 %collective-permute-start.3 = (s16[384,128]{1,0:T(8,128)(2,1)S(1)}, s16[384,128]{1,0:T(8,128)(2,1)S(1)}, u32[]{:S(2)}, u32[]{:S(2)}) collective-permute-start(s16[384,128]{1,0:T(8,128)(2,1)S(1)} %get-tuple-element.30), channel_id=1, source_target_pairs={{0,0},{1,2},{2,1},{3,3},{4,4},{5,6},{6,5},{7,7},{8,8},{9,10},{10,9... | collective-permute-start | bytes 294920 | tf_op jit(solution)/shard_map/ppermute | solution.py:380
  18.5 4.3 %collective-permute-start.5 = (s16[512,128]{1,0:T(8,128)(2,1)S(1)}, s16[512,128]{1,0:T(8,128)(2,1)S(1)}, u32[]{:S(2)}, u32[]{:S(2)}) collective-permute-start(s16[512,128]{1,0:T(8,128)(2,1)S(1)} %pad_add_fusion.1), channel_id=1, source_target_pairs={{1,4},{4,1},{5,8},{8,5},{9,12},{12,9},{13,14},{14,13},{15,10},{10,... | collective-permute-start | bytes 393224 | tf_op jit(solution)/shard_map/ppermute | solution.py:434
  20.7 3.1 %collective-permute-start.4 = (s16[4,2,128,128]{3,2,1,0:T(8,128)(2,1)S(1)}, s16[4,2,128,128]{3,2,1,0:T(8,128)(2,1)S(1)}, u32[]{:S(2)}, u32[]{:S(2)}) collective-permute-start(s16[4,2,128,128]{3,2,1,0:T(8,128)(2,1)S(1)} %pack.1), channel_id=1, source_target_pairs={{0,1},{1,0},{2,3},{3,2},{4,5},{5,4},{6,7},{7,6},{8,9},{9,8},{10,11... | collective-permute-start | bytes 786440 | tf_op jit(solution)/shard_map/ppermute | solution.py:416
  26.3 5.4 %collective-permute-start.8 = (f16[512,128]{1,0:T(8,128)(2,1)S(1)}, f16[512,128]{1,0:T(8,128)(2,1)S(1)}, u32[]{:S(2)}, u32[]{:S(2)}) collective-permute-start(f16[512,128]{1,0:T(8,128)(2,1)S(1)} %add_convert_fusion), channel_id=1, source_target_pairs={{1,4},{4,1},{5,8},{8,5},{9,12},{12,9},{13,14},{14,13},{15,10},{10,... | collective-permute-start | bytes 393224 | tf_op jit(solution)/shard_map/ppermute | solution.py:434
  27.0 4.7 %collective-permute-start.7 = (f32[512,128]{1,0:T(8,128)S(1)}, f32[512,128]{1,0:T(8,128)S(1)}, u32[]{:S(2)}, u32[]{:S(2)}) collective-permute-start(f32[512,128]{1,0:T(8,128)S(1)} %get-tuple-element.13.current_ref), channel_id=1, source_target_pairs={{0,1},{1,0},{2,3},{3,2},{4,5},{5,4},{6,7},{7,6},{8,9},{9,8},{10,11... | collective-permute-start | bytes 786440 | tf_op jit(solution)/shard_map/ppermute | solution.py:436
  32.4 7.4 %collective-permute-start.10 = (f16[1,128,128]{2,1,0:T(8,128)(2,1)S(1)}, f16[1,128,128]{2,1,0:T(8,128)(2,1)S(1)}, u32[]{:S(2)}, u32[]{:S(2)}) collective-permute-start(f16[1,128,128]{2,1,0:T(8,128)(2,1)S(1)} %get-tuple-element.50), channel_id=1, source_target_pairs={{0,4},{4,0},{8,12},{12,8},{1,5},{5,1},{9,13},{13,9},{2,6},{6,2},{1... | collective-permute-start | bytes 98312 | tf_op jit(solution)/shard_map/ppermute | solution.py:450
  34.9 5.4 %collective-permute-start.11 = (f16[1,128,128]{2,1,0:T(8,128)(2,1)S(1)}, f16[1,128,128]{2,1,0:T(8,128)(2,1)S(1)}, u32[]{:S(2)}, u32[]{:S(2)}) collective-permute-start(f16[1,128,128]{2,1,0:T(8,128)(2,1)S(1)} %get-tuple-element.49), channel_id=1, source_target_pairs={{0,8},{4,12},{8,0},{12,4},{1,9},{5,13},{9,1},{13,5},{2,10},{6,14},... | collective-permute-start | bytes 98312 | tf_op jit(solution)/shard_map/ppermute | solution.py:450
  37.4 5.7 %collective-permute-start.9 = (f16[1,128,128]{2,1,0:T(8,128)(2,1)S(1)}, f16[1,128,128]{2,1,0:T(8,128)(2,1)S(1)}, u32[]{:S(2)}, u32[]{:S(2)}) collective-permute-start(f16[1,128,128]{2,1,0:T(8,128)(2,1)S(1)} %get-tuple-element.51), channel_id=1, source_target_pairs={{0,12},{4,8},{8,4},{12,0},{1,13},{5,9},{9,5},{13,1},{2,14},{6,10},... | collective-permute-start | bytes 98312 | tf_op jit(solution)/shard_map/ppermute | solution.py:450
  37.4 6.9 %collective-permute-start.13 = (f16[1,128,128]{2,1,0:T(8,128)(2,1)S(1)}, f16[1,128,128]{2,1,0:T(8,128)(2,1)S(1)}, u32[]{:S(2)}, u32[]{:S(2)}) collective-permute-start(f16[1,128,128]{2,1,0:T(8,128)(2,1)S(1)} %get-tuple-element.48), channel_id=1, source_target_pairs={{0,2},{2,0},{1,3},{3,1},{4,6},{6,4},{5,7},{7,5},{8,10},{10,8},{9,1... | collective-permute-start | bytes 98312 | tf_op jit(solution)/shard_map/ppermute | solution.py:452
  43.2 4.7 %collective-permute-start.12 = (f16[3,128,128]{2,1,0:T(8,128)(2,1)S(1)}, f16[3,128,128]{2,1,0:T(8,128)(2,1)S(1)}, u32[]{:S(2)}, u32[]{:S(2)}) collective-permute-start(f16[3,128,128]{2,1,0:T(8,128)(2,1)S(1)} %pad_maximum_fusion.2), channel_id=1, source_target_pairs={{0,2},{2,0},{1,3},{3,1},{4,6},{6,4},{5,7},{7,5},{8,10},{10,8},{9,1... | collective-permute-start | bytes 294920 | tf_op jit(solution)/shard_map/ppermute | solution.py:453
  48.1 1.4 %collective-permute-start.14 = (f16[4,128,128]{2,1,0:T(8,128)(2,1)S(1)}, f16[4,128,128]{2,1,0:T(8,128)(2,1)S(1)}, u32[]{:S(2)}, u32[]{:S(2)}) collective-permute-start(f16[4,128,128]{2,1,0:T(8,128)(2,1)S(1)} %pad_maximum_fusion.1), channel_id=1, source_target_pairs={{0,1},{1,0},{2,3},{3,2},{4,5},{5,4},{6,7},{7,6},{8,9},{9,8},{10,11... | collective-permute-start | bytes 393224 | tf_op jit(solution)/shard_map/ppermute | solution.py:459

commit v11 on v9

--- a/solution.py
+++ b/solution.py
@@ -360,10 +360,12 @@
         return jnp.where(chain == 0, 0, tiles - 1)
 
     me = tile.reshape(1).astype(jnp.int32)
-    flag = core.reshape(1).astype(jnp.int32)
+    mine_is = lax.bitwise_xor(core, lax.bitwise_xor(tile, end_of(view)) % 2)
+    flag = mine_is.reshape(1).astype(jnp.int32)
 
     wide = estimate.reshape(tiles, 2, height, columns)
-    wide = lax.dynamic_index_in_dim(wide, view, 1, keepdims=True)
+    even, odd = (lax.dynamic_index_in_dim(wide, q, 1, keepdims=True) for q in (view, 1 - view))
+    wide = jnp.where(lax.broadcasted_iota(jnp.int32, even.shape, 0) % 2 == 0, even, odd)
     wide = jnp.round((wide - 1.0) * PLANE_UNIT).astype(jnp.int16)
     data = view_data.reshape(tiles, 2, height, columns).astype(jnp.float32)
     data = (data * DATA_UNIT).astype(jnp.int16)
@@ -390,8 +392,8 @@
 
     planes = [piece[:height] for piece in pieces]
     pairs = [piece[height : 3 * height].reshape(2, height, columns) for piece in pieces]
-    keep = [lax.dynamic_index_in_dim(pair, core, 0, keepdims=False) for pair in pairs]
-    give = [lax.dynamic_index_in_dim(pair, 1 - core, 0, keepdims=False) for pair in pairs]
+    keep = [lax.dynamic_index_in_dim(pair, mine_is, 0, keepdims=False) for pair in pairs]
+    give = [lax.dynamic_index_in_dim(pair, 1 - mine_is, 0, keepdims=False) for pair in pairs]
     got = lax.ppermute(jnp.concatenate([*planes, *give]), "gz", swap)
     length = tiles * height
     twin = got[:length].reshape(tiles, height, columns)
@@ -401,8 +403,8 @@
 
     path = [(t, 0) for t in range(tiles)] + [(t, 1) for t in reversed(range(tiles))]
     hops = []
-    for here, there in zip(path[:-1], path[1:]):
-        one, two = device(*here, 1), device(*there, 0)
+    for p, (here, there) in enumerate(zip(path[:-1], path[1:])):
+        one, two = device(*here, (p + 1) % 2), device(*there, (p + 1) % 2)
         hops += [(one, two), (two, one)]
 
     def plane_of(coded):
@@ -412,7 +414,7 @@
     twin = plane_of(jnp.concatenate(ordered([twin[k] for k in range(tiles)], tile)))
     current = plane_of(plane)
     narrow = current.astype(jnp.bfloat16)
-    at_end = (tile == 0) & (core == view)
+    at_end = (tile == 0) & (core == 0)
     for iteration in range(ITERS):
         first, last = iteration == 0, iteration == ITERS - 1
         other = lax.ppermute(plane, square, hops)
@@ -443,7 +445,8 @@
     twin = lax.ppermute(send, "gz", swap)
     same = jnp.stack(ordered([jnp.where(straight, m, c) for c, m in zip(crossed, mine)], here))
     parity = lax.broadcasted_iota(jnp.int32, (tiles, 2, height, columns), 1)
-    result = jnp.where(parity == core, same[:, None], twin[:, None])
+    turn = lax.broadcasted_iota(jnp.int32, parity.shape, 0) % 2
+    result = jnp.where(parity == lax.bitwise_xor(core, turn), same[:, None], twin[:, None])
     return result.astype(jnp.float32).reshape(2 * tiles, height, columns)
 
 
@@ -455,6 +458,7 @@
         depth == 2
         and views == 2
         and planes == 2 * tiles
+        and tiles > 1
         and tiles & (tiles - 1) == 0
         and height == columns
         and height % (16 * offsets.shape[1]) == 0

time: 52.2 us -> 54.8 us (1.050)
  waiting for transfers between devices: 11.3 us -> 16.1 us
  starting transfers between devices: 29.7 us -> 26.9 us
    ppermute x1, starting transfers between devices: 7.49 us -> 4.22 us  [plane_shards(): twin = lax.ppermute(current, 'gz', swap)]
    ppermute x1, waiting for transfers between devices: 0.01 us -> 3.27 us  [plane_shards(): crossed = [lax.ppermute(pieces[0], 'views', swap)]]
    ppermute x3, waiting for transfers between devices: 1.96 us -> 5.18 us  [plane_shards(): lax.ppermute(piece, 'tiles', [(t, t ^ k) for t in range(tiles)])]
    ppermute x1, waiting for transfers between devices: 2.49 us -> 0.01 us  [plane_shards(): crossed.append(lax.ppermute(mine[1:], 'views', swap))]
    ppermute x1, starting transfers between devices: 2.56 us -> 0.08 us  [plane_shards(): crossed = [lax.ppermute(pieces[0], 'views', swap)]]
    ppermute x1, starting transfers between devices: 2.63 us -> 4.46 us  [plane_shards(): got = lax.ppermute(jnp.concatenate([*planes, *give]), 'gz', swap)]
    ppermute x3, starting transfers between devices: 4.95 us -> 6.54 us  [plane_shards(): lax.ppermute(piece, 'tiles', [(t, t ^ k) for t in range(tiles)])]
    ppermute x1, waiting for transfers between devices: 0.32 us -> 1.06 us  [plane_shards(): got = lax.ppermute(jnp.concatenate([*planes, *give]), 'gz', swap)]
  transfers between devices with their start and end apart: 15 -> 15, of which waited for: 7 -> 7; matrix products, arithmetic and copies ran while one was open for 1% -> 2% of each run, Pallas kernels for 5% -> 5%
where the time goes in v11:
time: 54.8 us; the launch traced here: 54.6 us
  starting transfers between devices  26.9 us (49%)
  waiting for transfers between devices  16.1 us (29%)
  Pallas kernels  5.56 us (10%)
  other arithmetic  3.31 us (6%)
  local copies, waits for them, and re-layouts  2.25 us (4%)
    ppermute x3, starting transfers between devices, plane_shards(): lax.ppermute(piece, 'tiles', [(t, t ^ k) for t in range(tiles)])  6.54 us
    ppermute x4, waiting for transfers between devices, exchange(): pieces.append(lax.ppermute(pick(k), square, pairs))  5.34 us
    ppermute x3, waiting for transfers between devices, plane_shards(): lax.ppermute(piece, 'tiles', [(t, t ^ k) for t in range(tiles)])  5.18 us
    ppermute x4, starting transfers between devices, exchange(): pieces.append(lax.ppermute(pick(k), square, pairs))  5.12 us
    ppermute x1, starting transfers between devices, plane_shards(): got = lax.ppermute(jnp.concatenate([*planes, *give]), 'gz', swap)  4.46 us
    ppermute x1, starting transfers between devices, plane_shards(): twin = lax.ppermute(current, 'gz', swap)  4.22 us
    pallas_call x2, Pallas kernels, correction_logs(): pl.pallas_call(functools.partial(correction_kernel, tiles), out_shape=jax...  3.39 us
    ppermute x1, waiting for transfers between devices, plane_shards(): crossed = [lax.ppermute(pieces[0], 'views', swap)]  3.27 us
  transfers between devices with their start and end apart: 15, of which 7 were waited for; matrix products, arithmetic and copies ran while one was open for 2% of the time, Pallas kernels for 5%

profile of v11, /device:TPU:0, one launch (start us, length us, event | category | flops | bytes accessed | tf_op | source)
XLA Modules:
  0.0 54.6 jit_solution(13255622698093812159)
XLA Ops:
  0.0 1.1 %multiply_convert_fusion = s16[1,1,8,128,128]{4,3,2,1,0:T(8,128)(2,1)S(1)} fusion(bf16[1,1,8,128,128]{4,3,2,1,0:T(8,128)(2,1)} %param.4), kind=kLoop, calls=%fused_computation | loop fusion | flops 393216 | bytes 524288 | tf_op jit(solution)/shard_map/convert_element_type | solution.py:371
  1.3 0.6 %copy-done.1 = f32[1,2,2,9]{3,2,1,0:T(2,128)S(1)} copy-done((f32[1,2,2,9]{3,2,1,0:T(2,128)S(1)}, f32[1,2,2,9]{3,2,1,0:T(2,128)}, u32[]{:S(2)}) %copy-start.1) | copy-done | bytes 168
  3.0 3.0 %collective-permute-start.6 = (s16[16,128]{1,0:T(8,128)(2,1)S(1)}, s16[16,128]{1,0:T(8,128)(2,1)S(1)}, u32[]{:S(2)}, u32[]{:S(2)}) collective-permute-start(s16[16,128]{1,0:T(8,128)(2,1)S(1)} %broadcast_in_dim.31), channel_id=1, source_target_pairs={{0,2},{2,0},{1,3},{3,1},{4,6},{6,4},{5,7},{7,5},{8,10},{10,8},{9,1... | collective-permute-start | bytes 12296 | tf_op jit(solution)/shard_map/ppermute | solution.py:386
  6.0 0.7 %collective-permute-start.3 = (s16[384,128]{1,0:T(8,128)(2,1)S(1)}, s16[384,128]{1,0:T(8,128)(2,1)S(1)}, u32[]{:S(2)}, u32[]{:S(2)}) collective-permute-start(s16[384,128]{1,0:T(8,128)(2,1)S(1)} %get-tuple-element.30), channel_id=1, source_target_pairs={{0,0},{1,2},{2,1},{3,3},{4,4},{5,6},{6,5},{7,7},{8,8},{9,10},{10,9... | collective-permute-start | bytes 294920 | tf_op jit(solution)/shard_map/ppermute | solution.py:356
  6.7 1.6 %collective-permute-start.2 = (s16[384,128]{1,0:T(8,128)(2,1)S(1)}, s16[384,128]{1,0:T(8,128)(2,1)S(1)}, u32[]{:S(2)}, u32[]{:S(2)}) collective-permute-start(s16[384,128]{1,0:T(8,128)(2,1)S(1)} %get-tuple-element.31), channel_id=1, source_target_pairs={{0,4},{1,6},{2,5},{3,7},{4,0},{5,2},{6,1},{7,3},{8,12},{9,14},{10,... | collective-permute-start | bytes 294920 | tf_op jit(solution)/shard_map/ppermute | solution.py:356
  8.3 2.6 %collective-permute-start.1 = (s16[384,128]{1,0:T(8,128)(2,1)S(1)}, s16[384,128]{1,0:T(8,128)(2,1)S(1)}, u32[]{:S(2)}, u32[]{:S(2)}) collective-permute-start(s16[384,128]{1,0:T(8,128)(2,1)S(1)} %get-tuple-element.32), channel_id=1, source_target_pairs={{0,8},{1,10},{2,9},{3,11},{4,12},{5,14},{6,13},{7,15},{8,0},{9,2},... | collective-permute-start | bytes 294920 | tf_op jit(solution)/shard_map/ppermute | solution.py:356
  11.3 1.0 %blur_matrices.1.matrices_ref = bf16[2,4,256,128]{3,2,1,0:T(8,128)(2,1)S(1)} custom-call(f32[2,128]{1,0:T(2,128)S(1)} %broadcast_multiply_fusion.info_ref), custom_call_target="tpu_custom_call" | custom-call | tf_op jit(solution)/shard_map/blur_matrices/pallas_call | solution.py:192
  12.3 2.2 %collective-permute-done.1 = s16[384,128]{1,0:T(8,128)(2,1)S(1)} collective-permute-done((s16[384,128]{1,0:T(8,128)(2,1)S(1)}, s16[384,128]{1,0:T(8,128)(2,1)S(1)}, u32[]{:S(2)}, u32[]{:S(2)}) %collective-permute-start.1) | collective-permute-done | bytes 98336 | tf_op jit(solution)/shard_map/ppermute | solution.py:356
  14.5 3.1 %collective-permute-done = s16[384,128]{1,0:T(8,128)(2,1)S(1)} collective-permute-done((s16[384,128]{1,0:T(8,128)(2,1)S(1)}, s16[384,128]{1,0:T(8,128)(2,1)S(1)}, u32[]{:S(2)}, u32[]{:S(2)}) %collective-permute-start) | collective-permute-done | bytes 98336 | tf_op jit(solution)/shard_map/ppermute | solution.py:356
  18.0 0.7 %collective-permute-start.5 = (s16[512,128]{1,0:T(8,128)(2,1)S(1)}, s16[512,128]{1,0:T(8,128)(2,1)S(1)}, u32[]{:S(2)}, u32[]{:S(2)}) collective-permute-start(s16[512,128]{1,0:T(8,128)(2,1)S(1)} %pad_add_fusion.1), channel_id=1, source_target_pairs={{1,5},{5,1},{4,8},{8,4},{9,13},{13,9},{12,14},{14,12},{15,11},{11,... | collective-permute-start | bytes 393224 | tf_op jit(solution)/shard_map/ppermute | solution.py:420
  18.7 4.5 %collective-permute-start.4 = (s16[1024,128]{1,0:T(8,128)(2,1)S(1)}, s16[1024,128]{1,0:T(8,128)(2,1)S(1)}, u32[]{:S(2)}, u32[]{:S(2)}) collective-permute-start(s16[1024,128]{1,0:T(8,128)(2,1)S(1)} %bitcast_dynamic-update-slice_fusion), channel_id=1, source_target_pairs={{0,1},{1,0},{2,3},{3,2},{4,5},{5,4},{6,7},{7,6},{8,9},{9,8},{10,11... | collective-permute-start | bytes 786440 | tf_op jit(solution)/shard_map/ppermute | solution.py:397
  23.3 1.1 %collective-permute-done.4 = s16[1024,128]{1,0:T(8,128)(2,1)S(1)} collective-permute-done((s16[1024,128]{1,0:T(8,128)(2,1)S(1)}, s16[1024,128]{1,0:T(8,128)(2,1)S(1)}, u32[]{:S(2)}, u32[]{:S(2)}) %collective-permute-start.4) | collective-permute-done | bytes 262176 | tf_op jit(solution)/shard_map/ppermute | solution.py:397
  24.5 1.7 %correction.2.log_ref = f32[512,128]{1,0:T(8,128)S(1)} custom-call(s32[1]{0:T(128)} %bitcast.16.tile_ref, s32[2,8]{1,0:T(2,128)S(1)} %slice_convert_fusion.offsets_ref, bf16[4,128,128]{2,1,0:T(8,128)(2,1)S(1)} %bitcast.52, bf16[2,4,256,128]{3,2,1,0:T(8,128)(2,1)S(1)} %blur_matrices.1.matrices_ref, bf16[128,128]{1,0:T(8,128)(2,1)S(1)} %fusion.3.refs_0_, ...), custom_call_target="tpu_custom_call" | custom-call | flops 300000000 | bytes 1500000 | tf_op jit(solution)/shard_map/correction/pallas_call | solution.py:260
  26.9 0.7 %collective-permute-start.8 = (f16[512,128]{1,0:T(8,128)(2,1)S(1)}, f16[512,128]{1,0:T(8,128)(2,1)S(1)}, u32[]{:S(2)}, u32[]{:S(2)}) collective-permute-start(f16[512,128]{1,0:T(8,128)(2,1)S(1)} %add_convert_fusion), channel_id=1, source_target_pairs={{1,5},{5,1},{4,8},{8,4},{9,13},{13,9},{12,14},{14,12},{15,11},{11,... | collective-permute-start | bytes 393224 | tf_op jit(solution)/shard_map/ppermute | solution.py:420
  27.6 4.2 %collective-permute-start.7 = (f32[512,128]{1,0:T(8,128)S(1)}, f32[512,128]{1,0:T(8,128)S(1)}, u32[]{:S(2)}, u32[]{:S(2)}) collective-permute-start(f32[512,128]{1,0:T(8,128)S(1)} %get-tuple-element.13.current_ref), channel_id=1, source_target_pairs={{0,1},{1,0},{2,3},{3,2},{4,5},{5,4},{6,7},{7,6},{8,9},{9,8},{10,11... | collective-permute-start | bytes 786440 | tf_op jit(solution)/shard_map/ppermute | solution.py:422
  31.8 1.7 %correction.3.log_ref = f32[512,128]{1,0:T(8,128)S(1)} custom-call(s32[1]{0:T(128)} %bitcast.16.tile_ref, s32[2,8]{1,0:T(2,128)S(1)} %slice_convert_fusion.offsets_ref, bf16[4,128,128]{2,1,0:T(8,128)(2,1)S(1)} %bitcast.53, bf16[2,4,256,128]{3,2,1,0:T(8,128)(2,1)S(1)} %blur_matrices.1.matrices_ref, bf16[128,128]{1,0:T(8,128)(2,1)S(1)} %fusion.3.refs_0_, ...), custom_call_target="tpu_custom_call" | custom-call | flops 300000000 | bytes 1500000 | tf_op jit(solution)/shard_map/correction/pallas_call | solution.py:260
  34.2 4.0 %collective-permute-start.10 = (f16[1,128,128]{2,1,0:T(8,128)(2,1)S(1)}, f16[1,128,128]{2,1,0:T(8,128)(2,1)S(1)}, u32[]{:S(2)}, u32[]{:S(2)}) collective-permute-start(f16[1,128,128]{2,1,0:T(8,128)(2,1)S(1)} %get-tuple-element.54), channel_id=1, source_target_pairs={{0,4},{4,0},{8,12},{12,8},{1,5},{5,1},{9,13},{13,9},{2,6},{6,2},{1... | collective-permute-start | bytes 98312 | tf_op jit(solution)/shard_map/ppermute | solution.py:436
  38.2 2.0 %collective-permute-start.11 = (f16[1,128,128]{2,1,0:T(8,128)(2,1)S(1)}, f16[1,128,128]{2,1,0:T(8,128)(2,1)S(1)}, u32[]{:S(2)}, u32[]{:S(2)}) collective-permute-start(f16[1,128,128]{2,1,0:T(8,128)(2,1)S(1)} %get-tuple-element.53), channel_id=1, source_target_pairs={{0,8},{4,12},{8,0},{12,4},{1,9},{5,13},{9,1},{13,5},{2,10},{6,14},... | collective-permute-start | bytes 98312 | tf_op jit(solution)/shard_map/ppermute | solution.py:436
  40.8 2.6 %collective-permute-done.11 = f16[1,128,128]{2,1,0:T(8,128)(2,1)S(1)} collective-permute-done((f16[1,128,128]{2,1,0:T(8,128)(2,1)S(1)}, f16[1,128,128]{2,1,0:T(8,128)(2,1)S(1)}, u32[]{:S(2)}, u32[]{:S(2)}) %collective-permute-start.11) | collective-permute-done | bytes 32800 | tf_op jit(solution)/shard_map/ppermute | solution.py:436
  43.4 2.6 %collective-permute-done.9 = f16[1,128,128]{2,1,0:T(8,128)(2,1)S(1)} collective-permute-done((f16[1,128,128]{2,1,0:T(8,128)(2,1)S(1)}, f16[1,128,128]{2,1,0:T(8,128)(2,1)S(1)}, u32[]{:S(2)}, u32[]{:S(2)}) %collective-permute-start.9) | collective-permute-done | bytes 32800 | tf_op jit(solution)/shard_map/ppermute | solution.py:436
  46.0 2.1 %collective-permute-start.12 = (f16[3,128,128]{2,1,0:T(8,128)(2,1)S(1)}, f16[3,128,128]{2,1,0:T(8,128)(2,1)S(1)}, u32[]{:S(2)}, u32[]{:S(2)}) collective-permute-start(f16[3,128,128]{2,1,0:T(8,128)(2,1)S(1)} %pad_maximum_fusion.2), channel_id=1, source_target_pairs={{0,2},{2,0},{1,3},{3,1},{4,6},{6,4},{5,7},{7,5},{8,10},{10,8},{9,1... | collective-permute-start | bytes 294920 | tf_op jit(solution)/shard_map/ppermute | solution.py:439
  48.7 3.3 %collective-permute-done.13 = f16[1,128,128]{2,1,0:T(8,128)(2,1)S(1)} collective-permute-done((f16[1,128,128]{2,1,0:T(8,128)(2,1)S(1)}, f16[1,128,128]{2,1,0:T(8,128)(2,1)S(1)}, u32[]{:S(2)}, u32[]{:S(2)}) %collective-permute-start.13) | collective-permute-done | bytes 32800 | tf_op jit(solution)/shard_map/ppermute | solution.py:438
  52.4 1.2 %collective-permute-done.14 = f16[4,128,128]{2,1,0:T(8,128)(2,1)S(1)} collective-permute-done((f16[4,128,128]{2,1,0:T(8,128)(2,1)S(1)}, f16[4,128,128]{2,1,0:T(8,128)(2,1)S(1)}, u32[]{:S(2)}, u32[]{:S(2)}) %collective-permute-start.14) | collective-permute-done | bytes 131104 | tf_op jit(solution)/shard_map/ppermute | solution.py:445
  53.6 0.9 %fusion.1 = f32[8,128,128]{2,1,0:T(8,128)} fusion(s32[8]{0:T(128)S(1)} %iota.51, s32[8]{0:T(128)S(1)} %iota.48, s32[]{:T(128)S(6)} %axis_index.32, s32[8]{0:T(128)S(1)} %iota.42, pred[8]{0:T(512)(128)(4,1)S(1)} %and.30, f16[4,128,128]{2,1,0:T(8,128)(2,1)S(1)} %collective-permute-done.14, f16[4,128,128]{2,1,0:T(8,128)(2,1)S(1)} %pad_maximum_fusion), kind=kLoop, calls=%fused_computation.4 | loop fusion | flops 655360 | bytes 786540 | tf_op jit(solution)/shard_map/convert_element_type | solution.py:450
  (78 shorter events, 5.0 us)
Async XLA Ops:
  0.0 1.1 %copy-start = (f32[8,128,128]{2,1,0:T(8,128)S(1)}, f32[8,128,128]{2,1,0:T(8,128)}, u32[]{:S(2)}) copy-start(f32[8,128,128]{2,1,0:T(8,128)} %param.5) | copy-start | bytes 1572868
  1.3 0.7 %copy-start.1 = (f32[1,2,2,9]{3,2,1,0:T(2,128)S(1)}, f32[1,2,2,9]{3,2,1,0:T(2,128)}, u32[]{:S(2)}) copy-start(f32[1,2,2,9]{3,2,1,0:T(2,128)} %param.6) | copy-start | bytes 436
  2.2 0.7 %copy-start.2 = (s32[1,8]{1,0:T(1,128)S(1)}, s32[1,8]{1,0:T(1,128)}, u32[]{:S(2)}) copy-start(s32[1,8]{1,0:T(1,128)} %param.7) | copy-start | bytes 100
  3.0 8.2 %collective-permute-start.6 = (s16[16,128]{1,0:T(8,128)(2,1)S(1)}, s16[16,128]{1,0:T(8,128)(2,1)S(1)}, u32[]{:S(2)}, u32[]{:S(2)}) collective-permute-start(s16[16,128]{1,0:T(8,128)(2,1)S(1)} %broadcast_in_dim.31), channel_id=1, source_target_pairs={{0,2},{2,0},{1,3},{3,1},{4,6},{6,4},{5,7},{7,5},{8,10},{10,8},{9,1... | collective-permute-start | bytes 12296 | tf_op jit(solution)/shard_map/ppermute | solution.py:386
  6.0 6.2 %collective-permute-start.3 = (s16[384,128]{1,0:T(8,128)(2,1)S(1)}, s16[384,128]{1,0:T(8,128)(2,1)S(1)}, u32[]{:S(2)}, u32[]{:S(2)}) collective-permute-start(s16[384,128]{1,0:T(8,128)(2,1)S(1)} %get-tuple-element.30), channel_id=1, source_target_pairs={{0,0},{1,2},{2,1},{3,3},{4,4},{5,6},{6,5},{7,7},{8,8},{9,10},{10,9... | collective-permute-start | bytes 294920 | tf_op jit(solution)/shard_map/ppermute | solution.py:356
  6.7 5.6 %collective-permute-start.2 = (s16[384,128]{1,0:T(8,128)(2,1)S(1)}, s16[384,128]{1,0:T(8,128)(2,1)S(1)}, u32[]{:S(2)}, u32[]{:S(2)}) collective-permute-start(s16[384,128]{1,0:T(8,128)(2,1)S(1)} %get-tuple-element.31), channel_id=1, source_target_pairs={{0,4},{1,6},{2,5},{3,7},{4,0},{5,2},{6,1},{7,3},{8,12},{9,14},{10,... | collective-permute-start | bytes 294920 | tf_op jit(solution)/shard_map/ppermute | solution.py:356
  8.3 6.2 %collective-permute-start.1 = (s16[384,128]{1,0:T(8,128)(2,1)S(1)}, s16[384,128]{1,0:T(8,128)(2,1)S(1)}, u32[]{:S(2)}, u32[]{:S(2)}) collective-permute-start(s16[384,128]{1,0:T(8,128)(2,1)S(1)} %get-tuple-element.32), channel_id=1, source_target_pairs={{0,8},{1,10},{2,9},{3,11},{4,12},{5,14},{6,13},{7,15},{8,0},{9,2},... | collective-permute-start | bytes 294920 | tf_op jit(solution)/shard_map/ppermute | solution.py:356
  10.9 6.7 %collective-permute-start = (s16[384,128]{1,0:T(8,128)(2,1)S(1)}, s16[384,128]{1,0:T(8,128)(2,1)S(1)}, u32[]{:S(2)}, u32[]{:S(2)}) collective-permute-start(s16[384,128]{1,0:T(8,128)(2,1)S(1)} %get-tuple-element.29), channel_id=1, source_target_pairs={{0,12},{1,14},{2,13},{3,15},{4,8},{5,10},{6,9},{7,11},{8,4},{9,6},... | collective-permute-start | bytes 294920 | tf_op jit(solution)/shard_map/ppermute | solution.py:356
  18.0 5.2 %collective-permute-start.5 = (s16[512,128]{1,0:T(8,128)(2,1)S(1)}, s16[512,128]{1,0:T(8,128)(2,1)S(1)}, u32[]{:S(2)}, u32[]{:S(2)}) collective-permute-start(s16[512,128]{1,0:T(8,128)(2,1)S(1)} %pad_add_fusion.1), channel_id=1, source_target_pairs={{1,5},{5,1},{4,8},{8,4},{9,13},{13,9},{12,14},{14,12},{15,11},{11,... | collective-permute-start | bytes 393224 | tf_op jit(solution)/shard_map/ppermute | solution.py:420
  18.7 5.6 %collective-permute-start.4 = (s16[1024,128]{1,0:T(8,128)(2,1)S(1)}, s16[1024,128]{1,0:T(8,128)(2,1)S(1)}, u32[]{:S(2)}, u32[]{:S(2)}) collective-permute-start(s16[1024,128]{1,0:T(8,128)(2,1)S(1)} %bitcast_dynamic-update-slice_fusion), channel_id=1, source_target_pairs={{0,1},{1,0},{2,3},{3,2},{4,5},{5,4},{6,7},{7,6},{8,9},{9,8},{10,11... | collective-permute-start | bytes 786440 | tf_op jit(solution)/shard_map/ppermute | solution.py:397
  26.9 6.6 %collective-permute-start.8 = (f16[512,128]{1,0:T(8,128)(2,1)S(1)}, f16[512,128]{1,0:T(8,128)(2,1)S(1)}, u32[]{:S(2)}, u32[]{:S(2)}) collective-permute-start(f16[512,128]{1,0:T(8,128)(2,1)S(1)} %add_convert_fusion), channel_id=1, source_target_pairs={{1,5},{5,1},{4,8},{8,4},{9,13},{13,9},{12,14},{14,12},{15,11},{11,... | collective-permute-start | bytes 393224 | tf_op jit(solution)/shard_map/ppermute | solution.py:420
  27.6 6.0 %collective-permute-start.7 = (f32[512,128]{1,0:T(8,128)S(1)}, f32[512,128]{1,0:T(8,128)S(1)}, u32[]{:S(2)}, u32[]{:S(2)}) collective-permute-start(f32[512,128]{1,0:T(8,128)S(1)} %get-tuple-element.13.current_ref), channel_id=1, source_target_pairs={{0,1},{1,0},{2,3},{3,2},{4,5},{5,4},{6,7},{7,6},{8,9},{9,8},{10,11... | collective-permute-start | bytes 786440 | tf_op jit(solution)/shard_map/ppermute | solution.py:422
  34.2 6.5 %collective-permute-start.10 = (f16[1,128,128]{2,1,0:T(8,128)(2,1)S(1)}, f16[1,128,128]{2,1,0:T(8,128)(2,1)S(1)}, u32[]{:S(2)}, u32[]{:S(2)}) collective-permute-start(f16[1,128,128]{2,1,0:T(8,128)(2,1)S(1)} %get-tuple-element.54), channel_id=1, source_target_pairs={{0,4},{4,0},{8,12},{12,8},{1,5},{5,1},{9,13},{13,9},{2,6},{6,2},{1... | collective-permute-start | bytes 98312 | tf_op jit(solution)/shard_map/ppermute | solution.py:436
  38.2 5.1 %collective-permute-start.11 = (f16[1,128,128]{2,1,0:T(8,128)(2,1)S(1)}, f16[1,128,128]{2,1,0:T(8,128)(2,1)S(1)}, u32[]{:S(2)}, u32[]{:S(2)}) collective-permute-start(f16[1,128,128]{2,1,0:T(8,128)(2,1)S(1)} %get-tuple-element.53), channel_id=1, source_target_pairs={{0,8},{4,12},{8,0},{12,4},{1,9},{5,13},{9,1},{13,5},{2,10},{6,14},... | collective-permute-start | bytes 98312 | tf_op jit(solution)/shard_map/ppermute | solution.py:436
  40.2 5.7 %collective-permute-start.9 = (f16[1,128,128]{2,1,0:T(8,128)(2,1)S(1)}, f16[1,128,128]{2,1,0:T(8,128)(2,1)S(1)}, u32[]{:S(2)}, u32[]{:S(2)}) collective-permute-start(f16[1,128,128]{2,1,0:T(8,128)(2,1)S(1)} %get-tuple-element.55), channel_id=1, source_target_pairs={{0,12},{4,8},{8,4},{12,0},{1,13},{5,9},{9,5},{13,1},{2,14},{6,10},... | collective-permute-start | bytes 98312 | tf_op jit(solution)/shard_map/ppermute | solution.py:436
  46.0 6.0 %collective-permute-start.12 = (f16[3,128,128]{2,1,0:T(8,128)(2,1)S(1)}, f16[3,128,128]{2,1,0:T(8,128)(2,1)S(1)}, u32[]{:S(2)}, u32[]{:S(2)}) collective-permute-start(f16[3,128,128]{2,1,0:T(8,128)(2,1)S(1)} %pad_maximum_fusion.2), channel_id=1, source_target_pairs={{0,2},{2,0},{1,3},{3,1},{4,6},{6,4},{5,7},{7,5},{8,10},{10,8},{9,1... | collective-permute-start | bytes 294920 | tf_op jit(solution)/shard_map/ppermute | solution.py:439
  48.1 3.9 %collective-permute-start.13 = (f16[1,128,128]{2,1,0:T(8,128)(2,1)S(1)}, f16[1,128,128]{2,1,0:T(8,128)(2,1)S(1)}, u32[]{:S(2)}, u32[]{:S(2)}) collective-permute-start(f16[1,128,128]{2,1,0:T(8,128)(2,1)S(1)} %get-tuple-element.52), channel_id=1, source_target_pairs={{0,2},{2,0},{1,3},{3,1},{4,6},{6,4},{5,7},{7,5},{8,10},{10,8},{9,1... | collective-permute-start | bytes 98312 | tf_op jit(solution)/shard_map/ppermute | solution.py:438
  52.2 1.4 %collective-permute-start.14 = (f16[4,128,128]{2,1,0:T(8,128)(2,1)S(1)}, f16[4,128,128]{2,1,0:T(8,128)(2,1)S(1)}, u32[]{:S(2)}, u32[]{:S(2)}) collective-permute-start(f16[4,128,128]{2,1,0:T(8,128)(2,1)S(1)} %pad_maximum_fusion.1), channel_id=1, source_target_pairs={{0,1},{1,0},{2,3},{3,2},{4,5},{5,4},{6,7},{7,6},{8,9},{9,8},{10,11... | collective-permute-start | bytes 393224 | tf_op jit(solution)/shard_map/ppermute | solution.py:445

commit v12 on v9

--- a/solution.py
+++ b/solution.py
@@ -432,11 +432,11 @@
     for k in range(tiles):
         piece = lax.dynamic_index_in_dim(result, lax.bitwise_xor(tile, k), 0)
         pieces.append(lax.ppermute(piece, "tiles", [(t, t ^ k) for t in range(tiles)]) if k else piece)
-    mine = jnp.concatenate(pieces)
-    crossed = [lax.ppermute(pieces[0], "views", swap)]
-    crossed.append(lax.ppermute(mine[1:], "views", swap))
-    crossed = [crossed[0][0], *[crossed[1][k] for k in range(tiles - 1)]]
-    mine = [mine[k] for k in range(tiles)]
+    far = [k for k in range(tiles) if k != 1]
+    came = lax.ppermute(jnp.concatenate([pieces[k] for k in far]), "views", swap)
+    near = lax.ppermute(pieces[1], "views", swap)
+    crossed = [near[0] if k == 1 else came[far.index(k)] for k in range(tiles)]
+    mine = [piece[0] for piece in pieces]
     here = lax.bitwise_xor(tile, end_of(core))
     send = [jnp.where(straight, c, m) for c, m in zip(crossed, mine)]
     send = jnp.stack(ordered(send, lax.bitwise_xor(tile, end_of(1 - core))))

time: 52.2 us -> 53.1 us (1.017)
  waiting for transfers between devices: 11.3 us -> 14.8 us
  starting transfers between devices: 29.7 us -> 27.1 us
    ppermute x2, starting transfers between devices: 5.08 us -> 2.59 us  [the longest x1 2.5 us: plane_shards(): lax.ppermute(jnp.concatenate([pieces[k] for k in far]), 'views', swap)]
    ppermute x3, waiting for transfers between devices: 1.96 us -> 4.21 us  [plane_shards(): lax.ppermute(piece, 'tiles', [(t, t ^ k) for t in range(tiles)])]
    ppermute x2, waiting for transfers between devices: 2.49 us -> 3.73 us  [the longest x1 3.73 us: plane_shards(): near = lax.ppermute(pieces[1], 'views', swap)]
where the time goes in v12:
time: 53.1 us; the launch traced here: 52.9 us
  starting transfers between devices  27.1 us (51%)
  waiting for transfers between devices  14.8 us (28%)
  Pallas kernels  5.57 us (10%)
  other arithmetic  3.21 us (6%)
  local copies, waits for them, and re-layouts  1.79 us (3%)
    ppermute x1, starting transfers between devices, plane_shards(): twin = lax.ppermute(current, 'gz', swap)  7.49 us
    ppermute x4, waiting for transfers between devices, exchange(): pieces.append(lax.ppermute(pick(k), square, pairs))  5.34 us
    ppermute x4, starting transfers between devices, exchange(): pieces.append(lax.ppermute(pick(k), square, pairs))  5.12 us
    ppermute x3, starting transfers between devices, plane_shards(): lax.ppermute(piece, 'tiles', [(t, t ^ k) for t in range(tiles)])  4.87 us
    ppermute x3, waiting for transfers between devices, plane_shards(): lax.ppermute(piece, 'tiles', [(t, t ^ k) for t in range(tiles)])  4.21 us
    ppermute x1, waiting for transfers between devices, plane_shards(): near = lax.ppermute(pieces[1], 'views', swap)  3.73 us
    pallas_call x2, Pallas kernels, correction_logs(): pl.pallas_call(functools.partial(correction_kernel, tiles), out_shape=jax...  3.39 us
    ppermute x1, starting transfers between devices, plane_shards(): note = lax.ppermute(info, 'views', swap)  3.03 us
  transfers between devices with their start and end apart: 15, of which 7 were waited for; matrix products, arithmetic and copies ran while one was open for 1% of the time, Pallas kernels for 5%

profile of v12, /device:TPU:0, one launch (start us, length us, event | category | flops | bytes accessed | tf_op | source)
XLA Modules:
  0.0 52.9 jit_solution(15642000430852224608)
XLA Ops:
  0.0 1.1 %multiply_convert_fusion = s16[1,1,8,128,128]{4,3,2,1,0:T(8,128)(2,1)S(1)} fusion(bf16[1,1,8,128,128]{4,3,2,1,0:T(8,128)(2,1)} %param.4), kind=kLoop, calls=%fused_computation | loop fusion | flops 393216 | bytes 524288 | tf_op jit(solution)/shard_map/convert_element_type | solution.py:369
  1.3 0.6 %copy-done.1 = f32[1,2,2,9]{3,2,1,0:T(2,128)S(1)} copy-done((f32[1,2,2,9]{3,2,1,0:T(2,128)S(1)}, f32[1,2,2,9]{3,2,1,0:T(2,128)}, u32[]{:S(2)}) %copy-start.1) | copy-done | bytes 168
  2.9 3.0 %collective-permute-start.6 = (s16[16,128]{1,0:T(8,128)(2,1)S(1)}, s16[16,128]{1,0:T(8,128)(2,1)S(1)}, u32[]{:S(2)}, u32[]{:S(2)}) collective-permute-start(s16[16,128]{1,0:T(8,128)(2,1)S(1)} %broadcast_in_dim.31), channel_id=1, source_target_pairs={{0,2},{2,0},{1,3},{3,1},{4,6},{6,4},{5,7},{7,5},{8,10},{10,8},{9,1... | collective-permute-start | bytes 12296 | tf_op jit(solution)/shard_map/ppermute | solution.py:384
  5.9 0.7 %collective-permute-start.3 = (s16[384,128]{1,0:T(8,128)(2,1)S(1)}, s16[384,128]{1,0:T(8,128)(2,1)S(1)}, u32[]{:S(2)}, u32[]{:S(2)}) collective-permute-start(s16[384,128]{1,0:T(8,128)(2,1)S(1)} %get-tuple-element.30), channel_id=1, source_target_pairs={{0,0},{1,2},{2,1},{3,3},{4,4},{5,6},{6,5},{7,7},{8,8},{9,10},{10,9... | collective-permute-start | bytes 294920 | tf_op jit(solution)/shard_map/ppermute | solution.py:356
  6.6 1.6 %collective-permute-start.2 = (s16[384,128]{1,0:T(8,128)(2,1)S(1)}, s16[384,128]{1,0:T(8,128)(2,1)S(1)}, u32[]{:S(2)}, u32[]{:S(2)}) collective-permute-start(s16[384,128]{1,0:T(8,128)(2,1)S(1)} %get-tuple-element.31), channel_id=1, source_target_pairs={{0,4},{1,6},{2,5},{3,7},{4,0},{5,2},{6,1},{7,3},{8,12},{9,14},{10,... | collective-permute-start | bytes 294920 | tf_op jit(solution)/shard_map/ppermute | solution.py:356
  8.2 2.6 %collective-permute-start.1 = (s16[384,128]{1,0:T(8,128)(2,1)S(1)}, s16[384,128]{1,0:T(8,128)(2,1)S(1)}, u32[]{:S(2)}, u32[]{:S(2)}) collective-permute-start(s16[384,128]{1,0:T(8,128)(2,1)S(1)} %get-tuple-element.32), channel_id=1, source_target_pairs={{0,8},{1,10},{2,9},{3,11},{4,12},{5,14},{6,13},{7,15},{8,0},{9,2},... | collective-permute-start | bytes 294920 | tf_op jit(solution)/shard_map/ppermute | solution.py:356
  11.2 1.0 %blur_matrices.1.matrices_ref = bf16[2,4,256,128]{3,2,1,0:T(8,128)(2,1)S(1)} custom-call(f32[2,128]{1,0:T(2,128)S(1)} %broadcast_multiply_fusion.info_ref), custom_call_target="tpu_custom_call" | custom-call | tf_op jit(solution)/shard_map/blur_matrices/pallas_call | solution.py:192
  12.2 2.2 %collective-permute-done.1 = s16[384,128]{1,0:T(8,128)(2,1)S(1)} collective-permute-done((s16[384,128]{1,0:T(8,128)(2,1)S(1)}, s16[384,128]{1,0:T(8,128)(2,1)S(1)}, u32[]{:S(2)}, u32[]{:S(2)}) %collective-permute-start.1) | collective-permute-done | bytes 98336 | tf_op jit(solution)/shard_map/ppermute | solution.py:356
  14.4 3.1 %collective-permute-done = s16[384,128]{1,0:T(8,128)(2,1)S(1)} collective-permute-done((s16[384,128]{1,0:T(8,128)(2,1)S(1)}, s16[384,128]{1,0:T(8,128)(2,1)S(1)}, u32[]{:S(2)}, u32[]{:S(2)}) %collective-permute-start) | collective-permute-done | bytes 98336 | tf_op jit(solution)/shard_map/ppermute | solution.py:356
  17.9 2.6 %collective-permute-start.4 = (s16[1024,128]{1,0:T(8,128)(2,1)S(1)}, s16[1024,128]{1,0:T(8,128)(2,1)S(1)}, u32[]{:S(2)}, u32[]{:S(2)}) collective-permute-start(s16[1024,128]{1,0:T(8,128)(2,1)S(1)} %bitcast_dynamic-update-slice_fusion), channel_id=1, source_target_pairs={{0,1},{1,0},{2,3},{3,2},{4,5},{5,4},{6,7},{7,6},{8,9},{9,8},{10,11... | collective-permute-start | bytes 786440 | tf_op jit(solution)/shard_map/ppermute | solution.py:395
  20.5 0.7 %collective-permute-start.5 = (s16[512,128]{1,0:T(8,128)(2,1)S(1)}, s16[512,128]{1,0:T(8,128)(2,1)S(1)}, u32[]{:S(2)}, u32[]{:S(2)}) collective-permute-start(s16[512,128]{1,0:T(8,128)(2,1)S(1)} %pad_add_fusion.1), channel_id=1, source_target_pairs={{1,4},{4,1},{5,8},{8,5},{9,12},{12,9},{13,14},{14,13},{15,10},{10,... | collective-permute-start | bytes 393224 | tf_op jit(solution)/shard_map/ppermute | solution.py:418
  21.8 1.7 %correction.2.log_ref = f32[512,128]{1,0:T(8,128)S(1)} custom-call(s32[1]{0:T(128)} %bitcast.16.tile_ref, s32[2,8]{1,0:T(2,128)S(1)} %slice_convert_fusion.offsets_ref, bf16[4,128,128]{2,1,0:T(8,128)(2,1)S(1)} %bitcast.54, bf16[2,4,256,128]{3,2,1,0:T(8,128)(2,1)S(1)} %blur_matrices.1.matrices_ref, bf16[128,128]{1,0:T(8,128)(2,1)S(1)} %get-tuple-element.60.refs_0_, ...), custom_call_target="tpu_custom_call" | custom-call | flops 300000000 | bytes 1500000 | tf_op jit(solution)/shard_map/correction/pallas_call | solution.py:260
  23.5 0.6 %update.2 = (f32[512,128]{1,0:T(8,128)S(1)}, bf16[512,128]{1,0:T(8,128)(2,1)S(1)}) custom-call(s32[1]{0:T(128)} %bitcast.core_ref, f32[512,128]{1,0:T(8,128)S(1)} %get-tuple-element.57.current_ref, f32[512,128]{1,0:T(8,128)S(1)} %multiply_add_fusion.twin_ref, f32[512,128]{1,0:T(8,128)S(1)} %add_select_fusion.1.other_ref, f32[512,128]{1,0:T(8,128)S(1)} %correction.2.log_ref), custom_call_target="tpu_custom_call" | custom-call | tf_op jit(solution)/shard_map/update/pallas_call | solution.py:321
  24.2 0.7 %collective-permute-start.8 = (f16[512,128]{1,0:T(8,128)(2,1)S(1)}, f16[512,128]{1,0:T(8,128)(2,1)S(1)}, u32[]{:S(2)}, u32[]{:S(2)}) collective-permute-start(f16[512,128]{1,0:T(8,128)(2,1)S(1)} %add_convert_fusion), channel_id=1, source_target_pairs={{1,4},{4,1},{5,8},{8,5},{9,12},{12,9},{13,14},{14,13},{15,10},{10,... | collective-permute-start | bytes 393224 | tf_op jit(solution)/shard_map/ppermute | solution.py:418
  24.9 7.5 %collective-permute-start.7 = (f32[512,128]{1,0:T(8,128)S(1)}, f32[512,128]{1,0:T(8,128)S(1)}, u32[]{:S(2)}, u32[]{:S(2)}) collective-permute-start(f32[512,128]{1,0:T(8,128)S(1)} %get-tuple-element.13.current_ref), channel_id=1, source_target_pairs={{0,1},{1,0},{2,3},{3,2},{4,5},{5,4},{6,7},{7,6},{8,9},{9,8},{10,11... | collective-permute-start | bytes 786440 | tf_op jit(solution)/shard_map/ppermute | solution.py:420
  32.4 1.7 %correction.3.log_ref = f32[512,128]{1,0:T(8,128)S(1)} custom-call(s32[1]{0:T(128)} %bitcast.16.tile_ref, s32[2,8]{1,0:T(2,128)S(1)} %slice_convert_fusion.offsets_ref, bf16[4,128,128]{2,1,0:T(8,128)(2,1)S(1)} %bitcast.55, bf16[2,4,256,128]{3,2,1,0:T(8,128)(2,1)S(1)} %blur_matrices.1.matrices_ref, bf16[128,128]{1,0:T(8,128)(2,1)S(1)} %get-tuple-element.60.refs_0_, ...), custom_call_target="tpu_custom_call" | custom-call | flops 300000000 | bytes 1500000 | tf_op jit(solution)/shard_map/correction/pallas_call | solution.py:260
  34.1 0.6 %update.3 = f32[512,128]{1,0:T(8,128)S(1)} custom-call(s32[1]{0:T(128)} %bitcast.core_ref, f32[512,128]{1,0:T(8,128)S(1)} %get-tuple-element.13.current_ref, f32[512,128]{1,0:T(8,128)S(1)} %collective-permute-done.7.twin_ref, f32[512,128]{1,0:T(8,128)S(1)} %add_select_fusion.other_ref, f32[512,128]{1,0:T(8,128)S(1)} %correction.3.log_ref), custom_call_target="tpu_custom_call" | custom-call | tf_op jit(solution)/shard_map/update/pallas_call | solution.py:321
  34.8 3.3 %collective-permute-start.10 = (f16[1,128,128]{2,1,0:T(8,128)(2,1)S(1)}, f16[1,128,128]{2,1,0:T(8,128)(2,1)S(1)}, u32[]{:S(2)}, u32[]{:S(2)}) collective-permute-start(f16[1,128,128]{2,1,0:T(8,128)(2,1)S(1)} %get-tuple-element.53), channel_id=1, source_target_pairs={{0,8},{4,12},{8,0},{12,4},{1,9},{5,13},{9,1},{13,5},{2,10},{6,14},... | collective-permute-start | bytes 98312 | tf_op jit(solution)/shard_map/ppermute | solution.py:434
  38.1 1.6 %collective-permute-start.9 = (f16[1,128,128]{2,1,0:T(8,128)(2,1)S(1)}, f16[1,128,128]{2,1,0:T(8,128)(2,1)S(1)}, u32[]{:S(2)}, u32[]{:S(2)}) collective-permute-start(f16[1,128,128]{2,1,0:T(8,128)(2,1)S(1)} %get-tuple-element.55), channel_id=1, source_target_pairs={{0,12},{4,8},{8,4},{12,0},{1,13},{5,9},{9,5},{13,1},{2,14},{6,10},... | collective-permute-start | bytes 98312 | tf_op jit(solution)/shard_map/ppermute | solution.py:434
  40.0 3.9 %collective-permute-done.9 = f16[1,128,128]{2,1,0:T(8,128)(2,1)S(1)} collective-permute-done((f16[1,128,128]{2,1,0:T(8,128)(2,1)S(1)}, f16[1,128,128]{2,1,0:T(8,128)(2,1)S(1)}, u32[]{:S(2)}, u32[]{:S(2)}) %collective-permute-start.9) | collective-permute-done | bytes 32800 | tf_op jit(solution)/shard_map/ppermute | solution.py:434
  43.9 2.5 %collective-permute-start.11 = (f16[3,128,128]{2,1,0:T(8,128)(2,1)S(1)}, f16[3,128,128]{2,1,0:T(8,128)(2,1)S(1)}, u32[]{:S(2)}, u32[]{:S(2)}) collective-permute-start(f16[3,128,128]{2,1,0:T(8,128)(2,1)S(1)} %pad_maximum_fusion.2), channel_id=1, source_target_pairs={{0,2},{2,0},{1,3},{3,1},{4,6},{6,4},{5,7},{7,5},{8,10},{10,8},{9,1... | collective-permute-start | bytes 294920 | tf_op jit(solution)/shard_map/ppermute | solution.py:436
  46.6 3.7 %collective-permute-done.13 = f16[1,128,128]{2,1,0:T(8,128)(2,1)S(1)} collective-permute-done((f16[1,128,128]{2,1,0:T(8,128)(2,1)S(1)}, f16[1,128,128]{2,1,0:T(8,128)(2,1)S(1)}, u32[]{:S(2)}, u32[]{:S(2)}) %collective-permute-start.13) | collective-permute-done | bytes 32800 | tf_op jit(solution)/shard_map/ppermute | solution.py:437
  50.8 1.2 %collective-permute-done.14 = f16[4,128,128]{2,1,0:T(8,128)(2,1)S(1)} collective-permute-done((f16[4,128,128]{2,1,0:T(8,128)(2,1)S(1)}, f16[4,128,128]{2,1,0:T(8,128)(2,1)S(1)}, u32[]{:S(2)}, u32[]{:S(2)}) %collective-permute-start.14) | collective-permute-done | bytes 131104 | tf_op jit(solution)/shard_map/ppermute | solution.py:443
  52.0 0.9 %fusion = f32[8,128,128]{2,1,0:T(8,128)} fusion(pred[8]{0:T(512)(128)(4,1)S(1)} %iota.12, f16[4,128,128]{2,1,0:T(8,128)(2,1)S(1)} %collective-permute-done.14, f16[4,128,128]{2,1,0:T(8,128)(2,1)S(1)} %pad_maximum_fusion), kind=kLoop, calls=%fused_computation.3 | loop fusion | flops 262144 | bytes 786440 | tf_op jit(solution)/shard_map/convert_element_type | solution.py:447
  (69 shorter events, 3.3 us)
Async XLA Ops:
  0.0 1.1 %copy-start = (f32[8,128,128]{2,1,0:T(8,128)S(1)}, f32[8,128,128]{2,1,0:T(8,128)}, u32[]{:S(2)}) copy-start(f32[8,128,128]{2,1,0:T(8,128)} %param.5) | copy-start | bytes 1572868
  1.2 0.7 %copy-start.1 = (f32[1,2,2,9]{3,2,1,0:T(2,128)S(1)}, f32[1,2,2,9]{3,2,1,0:T(2,128)}, u32[]{:S(2)}) copy-start(f32[1,2,2,9]{3,2,1,0:T(2,128)} %param.6) | copy-start | bytes 436
  2.1 0.7 %copy-start.2 = (s32[1,8]{1,0:T(1,128)S(1)}, s32[1,8]{1,0:T(1,128)}, u32[]{:S(2)}) copy-start(s32[1,8]{1,0:T(1,128)} %param.7) | copy-start | bytes 100
  2.9 8.2 %collective-permute-start.6 = (s16[16,128]{1,0:T(8,128)(2,1)S(1)}, s16[16,128]{1,0:T(8,128)(2,1)S(1)}, u32[]{:S(2)}, u32[]{:S(2)}) collective-permute-start(s16[16,128]{1,0:T(8,128)(2,1)S(1)} %broadcast_in_dim.31), channel_id=1, source_target_pairs={{0,2},{2,0},{1,3},{3,1},{4,6},{6,4},{5,7},{7,5},{8,10},{10,8},{9,1... | collective-permute-start | bytes 12296 | tf_op jit(solution)/shard_map/ppermute | solution.py:384
  5.9 6.2 %collective-permute-start.3 = (s16[384,128]{1,0:T(8,128)(2,1)S(1)}, s16[384,128]{1,0:T(8,128)(2,1)S(1)}, u32[]{:S(2)}, u32[]{:S(2)}) collective-permute-start(s16[384,128]{1,0:T(8,128)(2,1)S(1)} %get-tuple-element.30), channel_id=1, source_target_pairs={{0,0},{1,2},{2,1},{3,3},{4,4},{5,6},{6,5},{7,7},{8,8},{9,10},{10,9... | collective-permute-start | bytes 294920 | tf_op jit(solution)/shard_map/ppermute | solution.py:356
  6.6 5.6 %collective-permute-start.2 = (s16[384,128]{1,0:T(8,128)(2,1)S(1)}, s16[384,128]{1,0:T(8,128)(2,1)S(1)}, u32[]{:S(2)}, u32[]{:S(2)}) collective-permute-start(s16[384,128]{1,0:T(8,128)(2,1)S(1)} %get-tuple-element.31), channel_id=1, source_target_pairs={{0,4},{1,6},{2,5},{3,7},{4,0},{5,2},{6,1},{7,3},{8,12},{9,14},{10,... | collective-permute-start | bytes 294920 | tf_op jit(solution)/shard_map/ppermute | solution.py:356
  8.2 6.2 %collective-permute-start.1 = (s16[384,128]{1,0:T(8,128)(2,1)S(1)}, s16[384,128]{1,0:T(8,128)(2,1)S(1)}, u32[]{:S(2)}, u32[]{:S(2)}) collective-permute-start(s16[384,128]{1,0:T(8,128)(2,1)S(1)} %get-tuple-element.32), channel_id=1, source_target_pairs={{0,8},{1,10},{2,9},{3,11},{4,12},{5,14},{6,13},{7,15},{8,0},{9,2},... | collective-permute-start | bytes 294920 | tf_op jit(solution)/shard_map/ppermute | solution.py:356
  10.8 6.7 %collective-permute-start = (s16[384,128]{1,0:T(8,128)(2,1)S(1)}, s16[384,128]{1,0:T(8,128)(2,1)S(1)}, u32[]{:S(2)}, u32[]{:S(2)}) collective-permute-start(s16[384,128]{1,0:T(8,128)(2,1)S(1)} %get-tuple-element.29), channel_id=1, source_target_pairs={{0,12},{1,14},{2,13},{3,15},{4,8},{5,10},{6,9},{7,11},{8,4},{9,6},... | collective-permute-start | bytes 294920 | tf_op jit(solution)/shard_map/ppermute | solution.py:356
  17.9 3.8 %collective-permute-start.4 = (s16[1024,128]{1,0:T(8,128)(2,1)S(1)}, s16[1024,128]{1,0:T(8,128)(2,1)S(1)}, u32[]{:S(2)}, u32[]{:S(2)}) collective-permute-start(s16[1024,128]{1,0:T(8,128)(2,1)S(1)} %bitcast_dynamic-update-slice_fusion), channel_id=1, source_target_pairs={{0,1},{1,0},{2,3},{3,2},{4,5},{5,4},{6,7},{7,6},{8,9},{9,8},{10,11... | collective-permute-start | bytes 786440 | tf_op jit(solution)/shard_map/ppermute | solution.py:395
  20.5 0.8 %collective-permute-start.5 = (s16[512,128]{1,0:T(8,128)(2,1)S(1)}, s16[512,128]{1,0:T(8,128)(2,1)S(1)}, u32[]{:S(2)}, u32[]{:S(2)}) collective-permute-start(s16[512,128]{1,0:T(8,128)(2,1)S(1)} %pad_add_fusion.1), channel_id=1, source_target_pairs={{1,4},{4,1},{5,8},{8,5},{9,12},{12,9},{13,14},{14,13},{15,10},{10,... | collective-permute-start | bytes 393224 | tf_op jit(solution)/shard_map/ppermute | solution.py:418
  24.2 9.9 %collective-permute-start.8 = (f16[512,128]{1,0:T(8,128)(2,1)S(1)}, f16[512,128]{1,0:T(8,128)(2,1)S(1)}, u32[]{:S(2)}, u32[]{:S(2)}) collective-permute-start(f16[512,128]{1,0:T(8,128)(2,1)S(1)} %add_convert_fusion), channel_id=1, source_target_pairs={{1,4},{4,1},{5,8},{8,5},{9,12},{12,9},{13,14},{14,13},{15,10},{10,... | collective-permute-start | bytes 393224 | tf_op jit(solution)/shard_map/ppermute | solution.py:418
  24.9 9.3 %collective-permute-start.7 = (f32[512,128]{1,0:T(8,128)S(1)}, f32[512,128]{1,0:T(8,128)S(1)}, u32[]{:S(2)}, u32[]{:S(2)}) collective-permute-start(f32[512,128]{1,0:T(8,128)S(1)} %get-tuple-element.13.current_ref), channel_id=1, source_target_pairs={{0,1},{1,0},{2,3},{3,2},{4,5},{5,4},{6,7},{7,6},{8,9},{9,8},{10,11... | collective-permute-start | bytes 786440 | tf_op jit(solution)/shard_map/ppermute | solution.py:420
  34.8 5.2 %collective-permute-start.10 = (f16[1,128,128]{2,1,0:T(8,128)(2,1)S(1)}, f16[1,128,128]{2,1,0:T(8,128)(2,1)S(1)}, u32[]{:S(2)}, u32[]{:S(2)}) collective-permute-start(f16[1,128,128]{2,1,0:T(8,128)(2,1)S(1)} %get-tuple-element.53), channel_id=1, source_target_pairs={{0,8},{4,12},{8,0},{12,4},{1,9},{5,13},{9,1},{13,5},{2,10},{6,14},... | collective-permute-start | bytes 98312 | tf_op jit(solution)/shard_map/ppermute | solution.py:434
  38.1 5.8 %collective-permute-start.9 = (f16[1,128,128]{2,1,0:T(8,128)(2,1)S(1)}, f16[1,128,128]{2,1,0:T(8,128)(2,1)S(1)}, u32[]{:S(2)}, u32[]{:S(2)}) collective-permute-start(f16[1,128,128]{2,1,0:T(8,128)(2,1)S(1)} %get-tuple-element.55), channel_id=1, source_target_pairs={{0,12},{4,8},{8,4},{12,0},{1,13},{5,9},{9,5},{13,1},{2,14},{6,10},... | collective-permute-start | bytes 98312 | tf_op jit(solution)/shard_map/ppermute | solution.py:434
  39.7 6.8 %collective-permute-start.12 = (f16[1,128,128]{2,1,0:T(8,128)(2,1)S(1)}, f16[1,128,128]{2,1,0:T(8,128)(2,1)S(1)}, u32[]{:S(2)}, u32[]{:S(2)}) collective-permute-start(f16[1,128,128]{2,1,0:T(8,128)(2,1)S(1)} %get-tuple-element.52), channel_id=1, source_target_pairs={{0,4},{4,0},{8,12},{12,8},{1,5},{5,1},{9,13},{13,9},{2,6},{6,2},{1... | collective-permute-start | bytes 98312 | tf_op jit(solution)/shard_map/ppermute | solution.py:434
  43.9 6.4 %collective-permute-start.11 = (f16[3,128,128]{2,1,0:T(8,128)(2,1)S(1)}, f16[3,128,128]{2,1,0:T(8,128)(2,1)S(1)}, u32[]{:S(2)}, u32[]{:S(2)}) collective-permute-start(f16[3,128,128]{2,1,0:T(8,128)(2,1)S(1)} %pad_maximum_fusion.2), channel_id=1, source_target_pairs={{0,2},{2,0},{1,3},{3,1},{4,6},{6,4},{5,7},{7,5},{8,10},{10,8},{9,1... | collective-permute-start | bytes 294920 | tf_op jit(solution)/shard_map/ppermute | solution.py:436
  46.4 3.9 %collective-permute-start.13 = (f16[1,128,128]{2,1,0:T(8,128)(2,1)S(1)}, f16[1,128,128]{2,1,0:T(8,128)(2,1)S(1)}, u32[]{:S(2)}, u32[]{:S(2)}) collective-permute-start(f16[1,128,128]{2,1,0:T(8,128)(2,1)S(1)} %collective-permute-done.12), channel_id=1, source_target_pairs={{0,2},{2,0},{1,3},{3,1},{4,6},{6,4},{5,7},{7,5},{8,10},{10,8},{9,1... | collective-permute-start | bytes 98312 | tf_op jit(solution)/shard_map/ppermute | solution.py:437
  50.6 1.4 %collective-permute-start.14 = (f16[4,128,128]{2,1,0:T(8,128)(2,1)S(1)}, f16[4,128,128]{2,1,0:T(8,128)(2,1)S(1)}, u32[]{:S(2)}, u32[]{:S(2)}) collective-permute-start(f16[4,128,128]{2,1,0:T(8,128)(2,1)S(1)} %pad_maximum_fusion.1), channel_id=1, source_target_pairs={{0,1},{1,0},{2,3},{3,2},{4,5},{5,4},{6,7},{7,6},{8,9},{9,8},{10,11... | collective-permute-start | bytes 393224 | tf_op jit(solution)/shard_map/ppermute | solution.py:443
